TPU v7x, 128 devices: a whole 4x4x4 slice. The times are simulated.
128 devices in a mesh: img: 16 (over z_lo, x, core), head: 2 (over z_hi), txt: 4 (over y).
Axes of the slice: x: 4, y: 4, z: 4 (z_hi: 2, z_lo: 2; z = z_hi * 2 + z_lo), core: 2. Of those that a mesh axis runs over, the one named last changes fastest.
Arguments:
- image_feats: bfloat16 [16384, 7680], P(('img', 'txt'), 'head'), may hold values from -6 to 6
- key_weight: bfloat16 [7680, 512], P('head'), may hold values from -0.0625 to 0.0625
- value_weight: bfloat16 [7680, 512], P('head'), may hold values from -0.0625 to 0.0625
- queries: bfloat16 [1024, 4096], P('txt', 'head'), may hold values from -21 to 21
- grad_out: bfloat16 [1024, 4096], P('txt', 'head'), may hold values from -768 to 768
- tile_image: int32 [128], P('img'), may hold values from 0 to 7, never falling along the last dimension, each value on 1 to 32 neighbouring positions
- text_sees: int32 [8, 8], replicated, may hold values from 0 to 1, as said below
Outputs:
- attn_out: bfloat16 [1024, 4096], P('txt', 'head')
- grad_feats: bfloat16 [16384, 7680], P(('img', 'txt'), 'head')
Inputs may be any that keep to these rules, and one draw needn't show every extreme that they name: `text_sees`: every row holds at least one 1.
All inputs are finite; a program needn't handle non-finite values.
Results may differ from a plain program's by a relative error of at most 0.012.
The roundings to bfloat16 on the way count: a program that leaves them out, or rounds other values in their place, can miss the bound.
Values may be sent and summed in bfloat16 or wider, within the bound.
No kernel may reach another device: no remote copies, remote signals or barrier semaphores. Data moves between devices by JAX's collectives and lax.ppermute only.
A program may use at most 128 MiB of HBM per device.

v0:
```python
import math

import jax
import jax.numpy as jnp
from jax import lax
from jax.sharding import PartitionSpec as P

HD = 128
TILE = 128
TBLK = 128


def in_blocks(array, dim, length):
    before, after = (array.shape[:dim], array.shape[dim + 1 :])
    return jnp.moveaxis(array.reshape(*before, length, -1, *after), dim, 0)


def summed_on_arrival(array, axis, dim):
    length = lax.axis_size(axis)
    blocks = lax.all_to_all(in_blocks(array, dim, length), axis, 0, 0, tiled=True)
    return jnp.sum(blocks, axis=0)


def in_one_piece(arrays, axis, dim, along):
    ends, at = ([], 0)
    for a in arrays[:-1]:
        at += a.shape[along]
        ends.append(at)
    both = jnp.concatenate(arrays, axis=along)
    return tuple(jnp.split(summed_on_arrival(both, axis, dim), ends, axis=along))


def sent_to_all(array, axis):
    copies = jnp.broadcast_to(array, (lax.axis_size(axis), *array.shape))
    return lax.all_to_all(copies, axis, split_axis=0, concat_axis=0, tiled=True)


def of_everyone(array, axis):
    everything = sent_to_all(array, axis)
    return jnp.max(everything, axis=0)


def of_everyone_2(array, axis):
    everything = sent_to_all(array, axis)
    return jnp.sum(everything, axis=0)


def joined_along(blocks, dim):
    blocks = jnp.moveaxis(blocks, 0, dim)
    shape = blocks.shape
    return blocks.reshape(*shape[:dim], shape[dim] * shape[dim + 1], *shape[dim + 2 :])


def gather_directly(array, axis, dim):
    return joined_along(sent_to_all(array, axis), dim)


def side_by_side(arrays, axis, dim, along):
    widths = [a.shape[along] for a in arrays]
    both = jnp.concatenate(arrays, axis=along)
    out = lax.all_gather(both, axis, axis=dim, tiled=True)
    return tuple(jnp.split(out, [sum(widths[:k]) for k in range(1, len(widths))], axis=along))


def build_mask(text_sees, tile_image, text_count):
    blocks_total = text_sees.shape[0]
    images_total = text_sees.shape[1]
    text_rows = lax.axis_index("txt") * text_count + jnp.arange(text_count, dtype=jnp.int32)
    text_block = text_rows // TBLK
    block_onehot = (
        text_block[:, None] == jnp.arange(blocks_total, dtype=jnp.int32)[None, :]
    ).astype(jnp.float32)
    row_sees = jnp.dot(block_onehot, text_sees.astype(jnp.float32))
    tile_onehot = (
        tile_image[:, None] == jnp.arange(images_total, dtype=jnp.int32)[None, :]
    ).astype(jnp.float32)
    tile_allowed = jnp.dot(row_sees, tile_onehot.T) > 0.5
    return jnp.repeat(tile_allowed, TILE, axis=1)


def shards(image_feats, key_weight, value_weight, queries, grad_out, tile_image, text_sees):
    key_part = jnp.dot(image_feats, key_weight, preferred_element_type=jnp.float32)
    value_part = jnp.dot(image_feats, value_weight, preferred_element_type=jnp.float32)
    key_own, value_own = in_one_piece((key_part, value_part), "head", 1, 0)
    keys, values = (
        lax.all_gather(key_own.astype(jnp.bfloat16), "txt", axis=0, tiled=True),
        lax.all_gather(value_own.astype(jnp.bfloat16), "txt", axis=0, tiled=True),
    )
    text_count = queries.shape[0]
    key_count = keys.shape[0]
    groups = keys.shape[1] // HD
    repeats = queries.shape[1] // (groups * HD)
    scale_factor = 1.0 / math.sqrt(HD)
    allowed = build_mask(text_sees, tile_image, text_count)
    query_heads = queries.reshape(text_count, groups, repeats, HD)
    grad_heads = grad_out.reshape(text_count, groups, repeats, HD)
    key_heads = keys.reshape(key_count, groups, HD)
    value_heads = values.reshape(key_count, groups, HD)
    scores = (
        jnp.einsum("tgrd,jgd->grtj", query_heads, key_heads, preferred_element_type=jnp.float32)
        * scale_factor
    )
    masked = jnp.where(allowed[None, None], scores, -1e30)
    row_max = of_everyone(jnp.max(masked, axis=-1), "img")
    weights = jnp.exp(masked - row_max[..., None]).astype(jnp.bfloat16)
    local_totals = (
        jnp.sum(weights, axis=-1, dtype=jnp.float32)
        .transpose(2, 0, 1)
        .reshape(text_count, groups * repeats)
    )
    numerator = jnp.einsum(
        "grtj,jgd->tgrd", weights, value_heads, preferred_element_type=jnp.float32
    )
    numerator = numerator.reshape(text_count, groups * repeats, HD)
    num_rows = summed_on_arrival(numerator, "img", 0)
    totals = of_everyone_2(local_totals, "img")
    share_rows = num_rows.shape[0]
    row_totals = lax.dynamic_slice_in_dim(totals, lax.axis_index("img") * share_rows, share_rows, 0)
    out_rows = (
        (num_rows / row_totals[..., None])
        .astype(jnp.bfloat16)
        .reshape(share_rows, groups * repeats * HD)
    )
    attn_out = gather_directly(out_rows, "img", 0)
    log_total = row_max + jnp.log(totals.reshape(text_count, groups, repeats).transpose(1, 2, 0))
    products = grad_out.astype(jnp.float32) * attn_out.astype(jnp.float32)
    row_delta = jnp.sum(products.reshape(text_count, groups, repeats, HD), axis=-1).transpose(
        1, 2, 0
    )
    key_grads = []
    value_grads = []
    for group_index in range(groups):
        probabilities = jnp.exp(masked[group_index] - log_total[group_index][..., None])
        grad_probs = jnp.einsum(
            "trd,jd->rtj",
            grad_heads[:, group_index],
            value_heads[:, group_index],
            preferred_element_type=jnp.float32,
        )
        grad_scores = (
            probabilities * (grad_probs - row_delta[group_index][..., None]) * scale_factor
        ).astype(jnp.bfloat16)
        value_grads.append(
            jnp.einsum(
                "rtj,trd->jd",
                probabilities.astype(jnp.bfloat16),
                grad_heads[:, group_index],
                preferred_element_type=jnp.float32,
            )
        )
        key_grads.append(
            jnp.einsum(
                "rtj,trd->jd",
                grad_scores,
                query_heads[:, group_index],
                preferred_element_type=jnp.float32,
            )
        )
    key_grad = jnp.concatenate(key_grads, axis=1)
    value_grad = jnp.concatenate(value_grads, axis=1)
    key_own_grad, value_own_grad = in_one_piece((key_grad, value_grad), "txt", 0, 1)
    key_all, value_all = side_by_side(
        (key_own_grad.astype(jnp.bfloat16), value_own_grad.astype(jnp.bfloat16)), "head", 1, 0
    )
    contract = (((1,), (1,)), ((), ()))
    grad_feats = lax.dot_general(key_all, key_weight, contract, preferred_element_type=jnp.float32)
    grad_feats = grad_feats + lax.dot_general(
        value_all, value_weight, contract, preferred_element_type=jnp.float32
    )
    return (attn_out, grad_feats.astype(jnp.bfloat16))


def solution(mesh):
    placed = (
        P(("img", "txt"), "head"),
        P("head", None),
        P("head", None),
        P("txt", "head"),
        P("txt", "head"),
        P("img"),
        P(),
    )
    return jax.shard_map(
        shards,
        mesh=mesh,
        in_specs=placed,
        out_specs=(P("txt", "head"), P(("img", "txt"), "head")),
        check_vma=False,
    )
```

profile of v0, /device:TPU:1, one launch (start us, length us, event | category | flops | bytes accessed | tf_op | source)
XLA Modules:
  0.0 226.5 jit_solution(16640007711787524154)
XLA Ops:
  0.6 0.0 copy-start
  0.6 0.0 copy-start.3
  0.7 1.5 copy-done
  2.2 3.5 %fusion.59 = f32[256,512]{1,0:T(8,128)S(1)} fusion(bf16[256,3840]{1,0:T(8,128)(2,1)S(1)} %copy-done, bf16[3840,512]{1,0:T(8,128)(2,1)} %param.8), kind=kOutput, calls=%fused_computation.72 | convolution fusion | flops 1006632960 | bytes 6422528 | tf_op jit(solution)/shard_map/dot_general | solution.py:82
  5.7 0.0 copy-done.3
  5.7 1.2 fusion.60
  6.8 0.0 copy-start.7
  6.9 0.0 copy-start.8
  6.9 0.1 pad_maximum_fusion.1
  7.0 1.1 copy.131
  8.0 5.7 %all-to-all-start = ((f32[2,512,256]{2,1,0:T(8,128)}), f32[2,512,256]{2,1,0:T(8,128)S(1)}, u32[]{:S(2)}, u32[]{:S(2)}) async-start(f32[2,512,256]{2,1,0:T(8,128)} %bitcast.154), calls=%async_computation | async-start | bytes 2097152 | tf_op jit(solution)/shard_map/all_to_all | solution.py:20
  13.7 1.5 copy.82
  15.2 0.0 copy-done.7
  15.2 0.0 copy-done.8
  15.2 0.3 fusion.42
  15.6 12.3 %all-to-all-done = f32[2,512,256]{2,1,0:T(8,128)S(1)} async-done(((f32[2,512,256]{2,1,0:T(8,128)}), f32[2,512,256]{2,1,0:T(8,128)S(1)}, u32[]{:S(2)}, u32[]{:S(2)}) %all-to-all-start) | async-done | bytes 1048608 | tf_op jit(solution)/shard_map/all_to_all | solution.py:20
  27.9 0.1 reduce_sum.54
  28.0 10.4 %all_gather.10 = bf16[1024,256]{1,0:T(8,128)(2,1)S(1)} all-gather(bf16[256,256]{1,0:T(8,128)(2,1)S(1)} %get-tuple-element.6), channel_id=1, replica_groups=mesh['img'=16,'head'=2,'txt'=4] {'txt'}, dimensions={0}, use_global_device_ids=true | all-gather | bytes 655360 | tf_op jit(solution)/shard_map/all_gather | solution.py:86
  38.4 0.2 copy.81
  38.6 0.1 broadcast_in_dim.32
  38.7 7.3 %fusion.58 = (f32[2,8,256]{2,1,0:T(8,128)S(1)}, f32[2,8,256,1024]{2,3,1,0:T(8,128)}) fusion(bf16[1024,2,128,1]{0,2,3,1:T(8,128)(2,1)S(1)} %bitcast.166, bf16[256,2,8,128]{0,3,2,1:T(8,128)(2,1)S(1)} %bitcast.161, pred[256,1024]{0,1:T(8,128)(4,1)S(1)} %bitcast.164), kind=kOutput, calls=%fused_computation.71 | convolution fusion | flops 1086320640 | bytes 18628608 | tf_op jit(solution)/shard_map/tgrd,jgd->grtj/dot_general | solution.py:100
  46.0 0.7 broadcast_in_dim.36
  46.7 10.1 %all-to-all-start.1 = ((f32[16,2,8,256]{3,2,1,0:T(8,128)}), f32[16,2,8,256]{3,2,1,0:T(8,128)S(1)}, u32[]{:S(2)}, u32[]{:S(2)}) async-start(f32[16,2,8,256]{3,2,1,0:T(8,128)} %broadcast_in_dim.36), calls=%async_computation.1 | async-start | bytes 524288 | tf_op jit(solution)/shard_map/all_to_all | solution.py:35
  56.8 10.5 %all_gather.9 = bf16[1024,256]{1,0:T(8,128)(2,1)S(1)} all-gather(bf16[256,256]{1,0:T(8,128)(2,1)S(1)} %get-tuple-element.7), channel_id=1, replica_groups=mesh['img'=16,'head'=2,'txt'=4] {'txt'}, dimensions={0}, use_global_device_ids=true | all-gather | bytes 655360 | tf_op jit(solution)/shard_map/all_gather | solution.py:87
  67.3 0.2 copy.80
  67.5 0.0 all-to-all-done.1
  67.5 8.0 %convert_reduce_fusion = f32[2,8,256]{2,1,0:T(8,128)S(1)} fusion(f32[2,8,256,1024]{2,3,1,0:T(8,128)} %get-tuple-element.11, f32[2,8,256]{2,1,0:T(8,128)S(1)} %reduce_max.19), kind=kLoop, calls=%fused_computation.1 | loop fusion | flops 16773120 | bytes 16809984 | tf_op jit(solution)/shard_map/reduce_sum | solution.py:107
  75.5 0.7 broadcast_in_dim.37
  76.2 8.0 %all-to-all-start.3 = ((f32[16,256,16]{1,2,0:T(8,128)}), f32[16,256,16]{1,2,0:T(8,128)S(1)}, u32[]{:S(2)}, u32[]{:S(2)}) async-start(f32[16,256,16]{1,2,0:T(8,128)} %broadcast_in_dim.37), calls=%async_computation.3 | async-start | bytes 524288 | tf_op jit(solution)/shard_map/all_to_all | solution.py:35
  84.2 10.0 %fusion.26 = f32[256,2,8,128]{0,3,2,1:T(8,128)} fusion(bf16[1024,2,128,1]{0,2,3,1:T(8,128)(2,1)S(1)} %bitcast.167, f32[2,8,256,1024]{2,3,1,0:T(8,128)} %get-tuple-element.11, f32[2,8,256]{2,1,0:T(8,128)S(1)} %reduce_max.19), kind=kOutput, calls=%fused_computation.31 | convolution fusion | flops 1082130432 | bytes 19415040 | tf_op jit(solution)/shard_map/grtj,jgd->tgrd/dot_general | solution.py:111
  94.2 3.2 %copy.86 = f32[256,2,8,128]{3,2,1,0:T(8,128)} copy(f32[256,2,8,128]{0,3,2,1:T(8,128)} %fusion.26) | data formatting | bytes 4194304 | tf_op jit(solution)/shard_map/grtj,jgd->tgrd/transpose | solution.py:111
  97.4 0.0 all-to-all-done.3
  97.4 5.7 %all-to-all-start.2 = ((f32[16,16,16,128]{3,2,1,0:T(8,128)}), f32[16,16,16,128]{3,2,1,0:T(8,128)}, u32[]{:S(2)}, u32[]{:S(2)}) async-start(f32[16,16,16,128]{3,2,1,0:T(8,128)} %bitcast.158), calls=%async_computation.2 | async-start | bytes 4194304 | tf_op jit(solution)/shard_map/all_to_all | solution.py:20
  103.1 1.3 copy.88
  104.5 0.1 constant_dynamic-slice_fusion
  104.5 0.1 copy.87
  104.6 26.2 %all-to-all-done.2 = f32[16,16,16,128]{3,2,1,0:T(8,128)} async-done(((f32[16,16,16,128]{3,2,1,0:T(8,128)}), f32[16,16,16,128]{3,2,1,0:T(8,128)}, u32[]{:S(2)}, u32[]{:S(2)}) %all-to-all-start.2) | async-done | bytes 2097184 | tf_op jit(solution)/shard_map/all_to_all | solution.py:20
  130.8 1.7 reduce_sum.55
  132.5 0.1 divide_convert_fusion
  132.7 1.1 broadcast_in_dim.38
  133.8 5.1 %all-to-all-start.4 = ((bf16[16,16,2048]{2,1,0:T(8,128)(2,1)}), bf16[16,16,2048]{2,1,0:T(8,128)(2,1)S(1)}, u32[]{:S(2)}, u32[]{:S(2)}) async-start(bf16[16,16,2048]{2,1,0:T(8,128)(2,1)} %broadcast_in_dim.38), calls=%async_computation.4 | async-start | bytes 2097152 | tf_op jit(solution)/shard_map/all_to_all | solution.py:35
  138.8 5.9 %fusion.33 = f32[1024,128]{0,1:T(8,128)} fusion(f32[2,8,256,1024]{2,3,1,0:T(8,128)} %get-tuple-element.11, f32[8,256]{1,0:T(8,128)S(1)} %get-tuple-element.8, bf16[256,2,8,128]{0,3,2,1:T(8,128)(2,1)} %bitcast.171), kind=kOutput, calls=%fused_computation.34 | convolution fusion | flops 541065216 | bytes 9445376 | tf_op jit(solution)/shard_map/rtj,trd->jd/dot_general | solution.py:144
  144.7 0.0 copy-done.5
  144.7 5.7 %fusion.36 = f32[1024,128]{0,1:T(8,128)} fusion(f32[2,8,256,1024]{2,3,1,0:T(8,128)} %get-tuple-element.11, f32[8,256]{1,0:T(8,128)S(1)} %get-tuple-element.9, bf16[256,2,8,128]{0,3,2,1:T(8,128)(2,1)S(1)} %bitcast.174), kind=kOutput, calls=%fused_computation.35 | convolution fusion | flops 541065216 | bytes 9445376 | tf_op jit(solution)/shard_map/rtj,trd->jd/dot_general | solution.py:144
  150.4 4.3 %all-to-all-done.4 = bf16[16,16,2048]{2,1,0:T(8,128)(2,1)S(1)} async-done(((bf16[16,16,2048]{2,1,0:T(8,128)(2,1)}), bf16[16,16,2048]{2,1,0:T(8,128)(2,1)S(1)}, u32[]{:S(2)}, u32[]{:S(2)}) %all-to-all-start.4) | async-done | bytes 1048608 | tf_op jit(solution)/shard_map/all_to_all | solution.py:35
  154.7 1.6 multiply_bitcast_fusion
  156.3 1.7 copy.126
  158.0 2.4 %reduce_sum.58 = f32[256,2,8]{2,1,0:T(2,128)S(1)} reduce(f32[256,2,8,128]{3,2,1,0:T(8,128)} %bitcast.157, f32[]{:T(128)} %constant.14.clone.1), dimensions={3}, to_apply=%region_6.7 | reduce | flops 520192 | bytes 2113540 | tf_op jit(solution)/shard_map/reduce_sum | solution.py:127
  160.4 0.2 fusion.56
  160.6 0.1 copy.91
  160.6 0.1 copy.95
  160.7 7.6 %fusion.30 = f32[1024,128]{0,1:T(8,128)} fusion(f32[2,8,256,1024]{2,3,1,0:T(8,128)} %get-tuple-element.11, f32[8,256]{1,0:T(8,128)S(1)} %copy.91, f32[8,256]{1,0:T(8,128)S(1)} %get-tuple-element.8, bf16[256,2,8,128]{0,3,2,1:T(8,128)(2,1)S(1)} %bitcast.162, bf16[256,2,8,128]{0,3,2,1:T(8,128)(2,1)} %bitcast.172, bf16[1024,2,128]{0,2,1:T(8,128)(2,1)S(1)} %bitcast.168), kind=kOutput, calls=%fused_computation.33 | convolution fusion | flops 1084227584 | bytes 10240000 | tf_op jit(solution)/shard_map/rtj,trd->jd/dot_general | solution.py:152
  168.2 7.6 %fusion.27 = f32[1024,128]{0,1:T(8,128)} fusion(f32[2,8,256,1024]{2,3,1,0:T(8,128)} %get-tuple-element.11, f32[8,256]{1,0:T(8,128)S(1)} %copy.95, f32[8,256]{1,0:T(8,128)S(1)} %get-tuple-element.9, bf16[256,2,8,128]{0,3,2,1:T(8,128)(2,1)S(1)} %bitcast.163, bf16[256,2,8,128]{0,3,2,1:T(8,128)(2,1)} %bitcast.173, bf16[1024,2,128]{0,2,1:T(8,128)(2,1)S(1)} %bitcast.169), kind=kOutput, calls=%fused_computation.32 | convolution fusion | flops 1084227584 | bytes 10240000 | tf_op jit(solution)/shard_map/rtj,trd->jd/dot_general | solution.py:152
  175.8 1.6 pad_maximum_fusion
  177.4 1.5 copy.130
  178.9 4.4 %all-to-all-start.5 = ((f32[4,256,512]{1,2,0:T(8,128)}), f32[4,256,512]{1,2,0:T(8,128)}, u32[]{:S(2)}, u32[]{:S(2)}) async-start(f32[4,256,512]{1,2,0:T(8,128)} %bitcast.159), calls=%async_computation.5 | async-start | bytes 4194304 | tf_op jit(solution)/shard_map/all_to_all | solution.py:20
  183.3 25.7 %all-to-all-done.5 = f32[4,256,512]{1,2,0:T(8,128)} async-done(((f32[4,256,512]{1,2,0:T(8,128)}), f32[4,256,512]{1,2,0:T(8,128)}, u32[]{:S(2)}, u32[]{:S(2)}) %all-to-all-start.5) | async-done | bytes 2097184 | tf_op jit(solution)/shard_map/all_to_all | solution.py:20
  209.0 1.7 reduce_sum.59
  210.8 8.6 %all_gather.11 = bf16[512,512]{0,1:T(8,128)(2,1)S(1)} all-gather(bf16[512,256]{0,1:T(8,128)(2,1)S(1)} %pad_maximum_fusion.2), channel_id=1, replica_groups=mesh['img'=16,'head'=2,'txt'=4] {'head'}, dimensions={1}, use_global_device_ids=true | all-gather | bytes 786432 | tf_op jit(solution)/shard_map/all_gather | solution.py:61
  219.5 3.5 %fusion.46 = f32[256,3840]{1,0:T(8,128)S(1)} fusion(bf16[3840,512]{1,0:T(8,128)(2,1)} %param.8, bf16[512,512]{0,1:T(8,128)(2,1)S(1)} %all_gather.11), kind=kOutput, calls=%fused_computation.46 | convolution fusion | flops 1006632960 | bytes 8126464 | tf_op jit(solution)/shard_map/dot_general | solution.py:166
  223.0 0.0 copy-done.4
  223.0 2.5 %fusion.12 = bf16[256,3840]{1,0:T(8,128)(2,1)} fusion(f32[256,3840]{1,0:T(8,128)S(1)} %fusion.46, bf16[3840,512]{1,0:T(8,128)(2,1)S(1)} %copy-done.4, bf16[512,512]{0,1:T(8,128)(2,1)S(1)} %all_gather.11), kind=kOutput, calls=%fused_computation.20 | convolution fusion | flops 1008599040 | bytes 10092544 | tf_op jit(solution)/shard_map/dot_general | solution.py:167
  225.5 1.0 copy.134
  226.5 0.0 copy-done.1
  (16 shorter events, 0.2 us)
Async XLA Ops:
  0.6 1.6 copy-start
  0.6 5.0 %copy-start.3 = (bf16[3840,512]{1,0:T(8,128)(2,1)S(1)}, bf16[3840,512]{1,0:T(8,128)(2,1)}, u32[]{:S(2)}) copy-start(bf16[3840,512]{1,0:T(8,128)(2,1)} %param.9) | copy-start | bytes 11796484
  6.8 8.4 %copy-start.7 = (s32[8,8]{1,0:T(8,128)S(1)}, s32[8,8]{1,0:T(8,128)}, u32[]{:S(2)}) copy-start(s32[8,8]{1,0:T(8,128)} %param.13) | copy-start | bytes 772
  6.9 8.3 %copy-start.8 = (s32[8]{0:T(128)S(1)}, s32[8]{0:T(128)}, u32[]{:S(2)}) copy-start(s32[8]{0:T(128)} %param.12) | copy-start | bytes 100
  8.0 19.9 %all-to-all-start = ((f32[2,512,256]{2,1,0:T(8,128)}), f32[2,512,256]{2,1,0:T(8,128)S(1)}, u32[]{:S(2)}, u32[]{:S(2)}) async-start(f32[2,512,256]{2,1,0:T(8,128)} %bitcast.154), calls=%async_computation | async-start | bytes 2097152 | tf_op jit(solution)/shard_map/all_to_all | solution.py:20
  46.7 20.8 %all-to-all-start.1 = ((f32[16,2,8,256]{3,2,1,0:T(8,128)}), f32[16,2,8,256]{3,2,1,0:T(8,128)S(1)}, u32[]{:S(2)}, u32[]{:S(2)}) async-start(f32[16,2,8,256]{3,2,1,0:T(8,128)} %broadcast_in_dim.36), calls=%async_computation.1 | async-start | bytes 524288 | tf_op jit(solution)/shard_map/all_to_all | solution.py:35
  76.2 21.2 %all-to-all-start.3 = ((f32[16,256,16]{1,2,0:T(8,128)}), f32[16,256,16]{1,2,0:T(8,128)S(1)}, u32[]{:S(2)}, u32[]{:S(2)}) async-start(f32[16,256,16]{1,2,0:T(8,128)} %broadcast_in_dim.37), calls=%async_computation.3 | async-start | bytes 524288 | tf_op jit(solution)/shard_map/all_to_all | solution.py:35
  94.2 8.9 %copy-start.2 = (bf16[256,2048]{1,0:T(8,128)(2,1)S(1)}, bf16[256,2048]{1,0:T(8,128)(2,1)}, u32[]{:S(2)}) copy-start(bf16[256,2048]{1,0:T(8,128)(2,1)} %param.11) | copy-start | bytes 3145732
  97.4 33.4 %all-to-all-start.2 = ((f32[16,16,16,128]{3,2,1,0:T(8,128)}), f32[16,16,16,128]{3,2,1,0:T(8,128)}, u32[]{:S(2)}, u32[]{:S(2)}) async-start(f32[16,16,16,128]{3,2,1,0:T(8,128)} %bitcast.158), calls=%async_computation.2 | async-start | bytes 4194304 | tf_op jit(solution)/shard_map/all_to_all | solution.py:20
  133.8 20.9 %all-to-all-start.4 = ((bf16[16,16,2048]{2,1,0:T(8,128)(2,1)}), bf16[16,16,2048]{2,1,0:T(8,128)(2,1)S(1)}, u32[]{:S(2)}, u32[]{:S(2)}) async-start(bf16[16,16,2048]{2,1,0:T(8,128)(2,1)} %broadcast_in_dim.38), calls=%async_computation.4 | async-start | bytes 2097152 | tf_op jit(solution)/shard_map/all_to_all | solution.py:35
  138.8 5.9 %copy-start.5 = (bf16[256,2048]{0,1:T(8,128)(2,1)S(1)}, bf16[256,2048]{0,1:T(8,128)(2,1)}, u32[]{:S(2)}) copy-start(bf16[256,2048]{0,1:T(8,128)(2,1)} %copy.88) | copy-start | bytes 3145732
  168.2 7.6 %copy-start.6 = (f32[1024,128]{0,1:T(8,128)S(1)}, f32[1024,128]{0,1:T(8,128)}, u32[]{:S(2)}) copy-start(f32[1024,128]{0,1:T(8,128)} %fusion.33) | copy-start | bytes 1572868
  178.9 30.2 %all-to-all-start.5 = ((f32[4,256,512]{1,2,0:T(8,128)}), f32[4,256,512]{1,2,0:T(8,128)}, u32[]{:S(2)}, u32[]{:S(2)}) async-start(f32[4,256,512]{1,2,0:T(8,128)} %bitcast.159), calls=%async_computation.5 | async-start | bytes 4194304 | tf_op jit(solution)/shard_map/all_to_all | solution.py:20
  219.4 3.5 %copy-start.4 = (bf16[3840,512]{1,0:T(8,128)(2,1)S(1)}, bf16[3840,512]{1,0:T(8,128)(2,1)}, u32[]{:S(2)}) copy-start(bf16[3840,512]{1,0:T(8,128)(2,1)} %param.9) | copy-start | bytes 11796484
  219.4 7.0 %copy-start.1 = (bf16[256,3840]{1,0:T(8,128)(2,1)S(1)}, bf16[256,3840]{1,0:T(8,128)(2,1)}, u32[]{:S(2)}) copy-start(bf16[256,3840]{1,0:T(8,128)(2,1)} %param.7) | copy-start | bytes 5898244
where the time goes:
time: 229 us; the launch traced here: 226 us
  waiting for transfers between devices  68.5 us (30%)
  matrix products  55 us (24%)
  starting transfers between devices  39 us (17%)
  blocking collectives  29.5 us (13%)
  other arithmetic  17.3 us (8%)
  local copies, waits for them, and re-layouts  16.3 us (7%)
    all_to_all x3, waiting for transfers between devices, summed_on_arrival(): lax.all_to_all(in_blocks(array, dim, length), axis, 0, 0, tiled=True)  64.2 us
    all_to_all x3, starting transfers between devices, sent_to_all(): return lax.all_to_all(copies, axis, split_axis=0, concat_axis=0, tiled=True)  23.1 us
    all_to_all x3, starting transfers between devices, summed_on_arrival(): lax.all_to_all(in_blocks(array, dim, length), axis, 0, 0, tiled=True)  15.9 us
    dot_general x2, matrix products, shards(): jnp.einsum('rtj,trd->jd', grad_scores, query_heads[:, group_index], prefe...  15.1 us
    dot_general x2, matrix products, shards(): jnp.einsum('rtj,trd->jd', probabilities.astype(jnp.bfloat16), grad_heads[...  11.6 us
    all_gather x1, blocking collectives, shards(): lax.all_gather(value_own.astype(jnp.bfloat16), 'txt', axis=0, tiled=True)  10.5 us
    all_gather x1, blocking collectives, shards(): lax.all_gather(key_own.astype(jnp.bfloat16), 'txt', axis=0, tiled=True)  10.4 us
    dot_general x1, matrix products, shards(): jnp.einsum('grtj,jgd->tgrd', weights, value_heads, preferred_element_type...  10 us
  transfers between devices with their start and end apart: 6, of which 4 were waited for; matrix products, arithmetic and copies ran while one was open for 12% of the time, Pallas kernels for 0%

commit v1 on v0

v1 whole, which is shorter than its diff:
```python
import math

import jax
import jax.numpy as jnp
from jax import lax
from jax.experimental import pallas as pl
from jax.experimental.pallas import tpu as pltpu
from jax.sharding import PartitionSpec as P

HD = 128
TILE = 128
TBLK = 128
BF = jnp.bfloat16
F32 = jnp.float32
SCALE = 1.0 / math.sqrt(HD)
C2 = SCALE * math.log2(math.e)
NEG = -1e30
TOP = 3e38
AXES = ("img", "head", "txt")
NT = (((1,), (1,)), ((), ()))


def dot_nt(a, b):
    return lax.dot_general(a, b, NT, preferred_element_type=F32)


def dot_nn(a, b):
    return jnp.dot(a, b, preferred_element_type=F32)


def moved(sizes, where):
    ni, nh, nt = sizes
    pairs = []
    for i in range(ni):
        for h in range(nh):
            for t in range(nt):
                a, b, c = where(i, h, t)
                pairs.append(((i * nh + h) * nt + t, (a * nh + b) * nt + c))
    return lambda x: lax.ppermute(x, AXES, pairs)


def spec(shape):
    zeros = (0,) * len(shape)
    return pl.BlockSpec(shape, lambda *_: zeros)


def project(idx, feats, weight, own_dtype, sent_dtype, name):
    rows, feat = feats.shape
    cols = weight.shape[1]
    steps = 5
    chunk = feat // steps

    def body(ix, x, w, own, oc, oh, ohc, acc):
        k = pl.program_id(0)
        part = dot_nn(x[...], w[...])

        @pl.when(k == 0)
        def _():
            acc[...] = part

        @pl.when(k > 0)
        def _():
            acc[...] += part

        @pl.when(k == steps - 1)
        def _():
            h = ix[0]
            c = ix[1]

            def piece(hh, cc):
                at = pl.multiple_of((hh * 2 + cc) * HD, HD)
                return acc[:, pl.ds(at, HD)]

            own[...] = piece(h, c).astype(own.dtype)
            oc[...] = piece(h, 1 - c).astype(oc.dtype)
            oh[...] = piece(1 - h, c).astype(oh.dtype)
            ohc[...] = piece(1 - h, 1 - c).astype(ohc.dtype)

    out = lambda dt: jax.ShapeDtypeStruct((rows, HD), dt)
    return pl.pallas_call(
        body,
        out_shape=(out(own_dtype), out(sent_dtype), out(sent_dtype), out(sent_dtype)),
        grid_spec=pltpu.PrefetchScalarGridSpec(
            num_scalar_prefetch=1,
            grid=(steps,),
            in_specs=[
                pl.BlockSpec((rows, chunk), lambda k, ix: (0, k)),
                pl.BlockSpec((chunk, cols), lambda k, ix: (k, 0)),
            ],
            out_specs=[spec((rows, HD))] * 4,
            scratch_shapes=[pltpu.VMEM((rows, cols), F32)],
        ),
        compiler_params=pltpu.CompilerParams(vmem_limit_bytes=24 << 20),
        name=name,
    )(idx, feats, weight)


def tile_cap(ix, tiles, sees, block, chunk, tile):
    half, j = divmod(tile, 2)
    shard = jnp.bitwise_xor(ix[2], chunk)
    image = tiles[half, shard * 2 + j]
    row = ix[2] * 2 + block
    return jnp.where(sees[row, image] > 0, jnp.float32(TOP), jnp.float32(NEG))


def forward(idx, tiles, sees, queries, grad_out, keys, values):
    rows = queries.shape[0]
    heads = 8
    width = heads * HD
    span = keys[0].shape[0]
    n = len(keys)
    total = span * n
    per = span // TILE

    def body(ix, tl, se, q, g, k0, k1, k2, k3, v0, v1, v2, v3, o_out, st_out, y_scr, va, stat):
        ks = (k0, k1, k2, k3)
        vs = (v0, v1, v2, v3)
        for j in range(n):
            va[j * span : (j + 1) * span, :HD] = vs[j][...]
        va[:, HD:] = jnp.ones((total, HD), BF)
        caps = [
            [tile_cap(ix, tl, se, b, j, e) for j in range(n) for e in range(per)]
            for b in range(2)
        ]
        lane = lax.broadcasted_iota(jnp.int32, (rows, HD), 1)
        st = jnp.zeros((rows, HD), F32)
        for h in range(heads):
            cols = slice(h * HD, (h + 1) * HD)
            slot = h % 2
            qh = q[:, cols]
            best = [None, None]
            for j in range(n):
                s = dot_nt(qh, ks[j][...]) * C2
                for b in range(2):
                    for e in range(per):
                        y = jnp.minimum(
                            s[b * TBLK : (b + 1) * TBLK, e * TILE : (e + 1) * TILE],
                            caps[b][j * per + e],
                        )
                        at = j * span + e * TILE
                        y_scr[slot, b * TBLK : (b + 1) * TBLK, at : at + TILE] = y
                        best[b] = y if best[b] is None else jnp.maximum(best[b], y)
            m = jnp.max(jnp.concatenate(best, axis=0), axis=1, keepdims=True)
            p = jnp.exp2(y_scr[slot] - m).astype(BF)
            r = dot_nn(p, va[...])
            den = r[:, HD:]
            o = r[:, :HD] / den
            o_out[:, :, cols] = o.astype(BF).reshape(8, rows // 8, HD)
            lse = m + jnp.log2(den)
            delta = jnp.sum(o * g[:, cols].astype(F32), axis=1, keepdims=True)
            st = jnp.where(lane == h, lse, st)
            st = jnp.where(lane == heads + h, delta, st)
        flat = st.T[: 2 * heads, :]
        for i in range(8):
            st_out[i] = flat

    own = lambda i, ix, tl, se: (0, ix[1])
    return pl.pallas_call(
        body,
        out_shape=(
            jax.ShapeDtypeStruct((8, rows // 8, width), BF),
            jax.ShapeDtypeStruct((8, 2 * heads, rows), F32),
        ),
        grid_spec=pltpu.PrefetchScalarGridSpec(
            num_scalar_prefetch=3,
            grid=(1,),
            in_specs=[pl.BlockSpec((rows, width), own)] * 2 + [spec((span, HD))] * 8,
            out_specs=[spec((8, rows // 8, width)), spec((8, 2 * heads, rows))],
            scratch_shapes=[
                pltpu.VMEM((2, rows, total), F32),
                pltpu.VMEM((total, 2 * HD), BF),
                pltpu.VMEM((rows, HD), F32),
            ],
        ),
        compiler_params=pltpu.CompilerParams(vmem_limit_bytes=40 << 20),
        name="fwd",
    )(idx, tiles, sees, queries, grad_out, *keys, *values)


def merge_weights(stats, heads):
    lses = [stats[i, :heads, :] for i in range(8)]
    top = lses[0]
    for x in lses[1:]:
        top = jnp.maximum(top, x)
    ws = [jnp.exp2(x - top) for x in lses]
    total = ws[0]
    for w in ws[1:]:
        total = total + w
    return top, ws, total


def combine(idx, parts, stats):
    _, share, width = parts.shape
    heads = width // HD
    rows = stats.shape[2]

    def body(ix, x, st, out, w_scr):
        _, ws, total = merge_weights(st, heads)
        inv = 1.0 / total
        stacked = jnp.concatenate([w * inv for w in ws] + [jnp.zeros((HD - 8 * heads, rows), F32)], axis=0)
        w_scr[...] = stacked.T
        w = w_scr[pl.ds(pl.multiple_of(ix[3] * share, share), share), :]
        for h in range(heads):
            cols = slice(h * HD, (h + 1) * HD)
            acc = jnp.zeros((share, HD), F32)
            for i in range(8):
                acc += x[i, :, cols].astype(F32) * w[:, i * heads + h : i * heads + h + 1]
            v = acc.astype(BF)
            for i in range(8):
                out[i, :, cols] = v

    return pl.pallas_call(
        body,
        out_shape=jax.ShapeDtypeStruct((8, share, width), BF),
        grid_spec=pltpu.PrefetchScalarGridSpec(
            num_scalar_prefetch=1,
            grid=(1,),
            in_specs=[spec(parts.shape), spec(stats.shape)],
            out_specs=spec((8, share, width)),
            scratch_shapes=[pltpu.VMEM((rows, HD), F32)],
        ),
        name="combine",
    )(idx, parts, stats)


def backward(idx, tiles, sees, queries, grad_out, key, value, stats, chunk, dtype):
    rows = queries.shape[0]
    heads = 8
    width = heads * HD
    span = key.shape[0]
    per = span // TILE

    def body(ix, tl, se, q, g, k, v, st, out, dk, dv):
        top, ws, total = merge_weights(st, heads)
        inv = 1.0 / total
        lse = top + jnp.log2(total)
        delta = ws[0] * st[0, heads:, :]
        for i in range(1, 8):
            delta += ws[i] * st[i, heads:, :]
        delta = delta * inv
        lane = lax.broadcasted_iota(jnp.int32, (1, rows), 1)
        caps = [
            jnp.where(
                lane < TBLK,
                tile_cap(ix, tl, se, 0, chunk, e),
                tile_cap(ix, tl, se, 1, chunk, e),
            )
            for e in range(per)
        ]
        kk = k[...]
        vv = v[...]
        for h in range(heads):
            cols = slice(h * HD, (h + 1) * HD)
            qh = q[:, cols]
            gh = g[:, cols]
            s = dot_nt(kk, qh) * C2
            d = dot_nt(vv, gh)
            lh = lse[h : h + 1, :]
            dh = delta[h : h + 1, :]
            ps = []
            ds = []
            for e in range(per):
                at = slice(e * TILE, (e + 1) * TILE)
                p = jnp.exp2(jnp.minimum(s[at, :], caps[e]) - lh)
                ps.append(p.astype(BF))
                ds.append((p * (d[at, :] - dh) * SCALE).astype(BF))
            pv = dot_nn(jnp.concatenate(ps, axis=0), gh)
            pk = dot_nn(jnp.concatenate(ds, axis=0), qh)
            if h == 0:
                dv[...] = pv
                dk[...] = pk
            else:
                dv[...] += pv
                dk[...] += pk
        out[:, :HD] = dk[...].astype(out.dtype)
        out[:, HD:] = dv[...].astype(out.dtype)

    own = lambda i, ix, tl, se: (0, ix[1])
    return pl.pallas_call(
        body,
        out_shape=jax.ShapeDtypeStruct((span, 2 * HD), dtype),
        grid_spec=pltpu.PrefetchScalarGridSpec(
            num_scalar_prefetch=3,
            grid=(1,),
            in_specs=[pl.BlockSpec((rows, width), own)] * 2
            + [spec((span, HD))] * 2
            + [spec(stats.shape)],
            out_specs=spec((span, 2 * HD)),
            scratch_shapes=[pltpu.VMEM((span, HD), F32)] * 2,
        ),
        compiler_params=pltpu.CompilerParams(vmem_limit_bytes=32 << 20),
        name=f"grads{chunk}",
    )(idx, tiles, sees, queries, grad_out, key, value, stats)


def feature_grad(idx, own, oc, oh, ohc, key_weight, value_weight):
    rows = own.shape[0]
    feat, cols = key_weight.shape
    steps = 5
    chunk = feat // steps

    def body(ix, a, b, c_, d_, wk, wv, out, both):
        @pl.when(pl.program_id(0) == 0)
        def _():
            h = ix[0]
            c = ix[1]

            def put(hh, cc, x):
                at = pl.multiple_of((hh * 2 + cc) * HD, HD)
                both[0, :, pl.ds(at, HD)] = x[:, :HD]
                both[1, :, pl.ds(at, HD)] = x[:, HD:]

            put(h, c, a)
            put(h, 1 - c, b)
            put(1 - h, c, c_)
            put(1 - h, 1 - c, d_)

        out[...] = (dot_nt(both[0], wk[...]) + dot_nt(both[1], wv[...])).astype(BF)

    piece = spec((rows, 2 * HD))
    return pl.pallas_call(
        body,
        out_shape=jax.ShapeDtypeStruct((rows, feat), BF),
        grid_spec=pltpu.PrefetchScalarGridSpec(
            num_scalar_prefetch=1,
            grid=(steps,),
            in_specs=[piece] * 4 + [pl.BlockSpec((chunk, cols), lambda k, ix: (k, 0))] * 2,
            out_specs=pl.BlockSpec((rows, chunk), lambda k, ix: (0, k)),
            scratch_shapes=[pltpu.VMEM((2, rows, cols), BF)],
        ),
        compiler_params=pltpu.CompilerParams(vmem_limit_bytes=24 << 20),
        name="feats",
    )(idx, own, oc, oh, ohc, key_weight, value_weight)


def solution(mesh):
    sizes = tuple(mesh.shape[a] for a in AXES)
    to_c = moved(sizes, lambda i, h, t: (i ^ 1, h, t))
    to_h = moved(sizes, lambda i, h, t: (i, 1 - h, t))
    to_hc = moved(sizes, lambda i, h, t: (i ^ 1, 1 - h, t))
    to_t = {k: moved(sizes, lambda i, h, t, k=k: (i, h, t ^ k)) for k in (1, 2, 3)}
    chips = [[m * 2 + c for m in range(8)] for c in range(2)]

    def swap8(x):
        return lax.all_to_all(x, "img", 0, 0, axis_index_groups=chips, tiled=True)

    def gathered(own):
        return [own] + [to_t[k](own) for k in (1, 2, 3)]

    def shards(image_feats, key_weight, value_weight, queries, grad_out, tile_image, text_sees):
        img = lax.axis_index("img")
        core = img % 2
        idx = jnp.stack([lax.axis_index("head"), core, lax.axis_index("txt"), img // 2]).astype(jnp.int32)
        tiles = jnp.stack([tile_image, to_c(tile_image)])

        def owned(weight, sent, name):
            own, c, h, hc = project(idx, image_feats, weight, F32, sent, name)
            h, c, hc = to_h(h), to_c(c), to_hc(hc)
            near = own + h.astype(F32)
            far = c.astype(F32) + hc.astype(F32)
            return jnp.concatenate([near.astype(BF), far.astype(BF)], axis=0)

        keys = gathered(owned(key_weight, F32, "keys"))
        values = gathered(owned(value_weight, BF, "values"))
        parts, stats = forward(idx, tiles, text_sees, queries, grad_out, keys, values)
        stats = swap8(stats)

        def grads(k, dtype):
            return backward(idx, tiles, text_sees, queries, grad_out, keys[k], values[k], stats, k, dtype)

        far = [to_t[k](grads(k, BF)) for k in (2, 1, 3)]
        total = grads(0, F32)
        for x in far:
            total = total + x.astype(F32)
        total = total.astype(BF)
        rows = total.shape[0] // 2
        near, other = total[:rows], total[rows:]
        grad_feats = feature_grad(
            idx, near, to_c(other), to_h(near), to_hc(other), key_weight, value_weight
        )

        merged = combine(idx, swap8(parts), stats)
        mine = swap8(merged).reshape(queries.shape[0], -1)
        theirs = to_c(mine)
        attn_out = jnp.where(
            core == 0,
            jnp.concatenate([mine, theirs], axis=1),
            jnp.concatenate([theirs, mine], axis=1),
        )
        return attn_out, grad_feats

    placed = (
        P(("img", "txt"), "head"),
        P("head", None),
        P("head", None),
        P("txt", "head"),
        P("txt", "head"),
        P("img"),
        P(),
    )
    return jax.shard_map(
        shards,
        mesh=mesh,
        in_specs=placed,
        out_specs=(P("txt", "head"), P(("img", "txt"), "head")),
        check_vma=False,
    )
```

time: 229 us -> 119 us (0.52); the launches traced: 226 us -> 119 us
  waiting for transfers between devices: 68.5 us -> 13.3 us
  matrix products: 55 us -> 0 us
  Pallas kernels: 0 us -> 33.5 us
  other arithmetic: 17.3 us -> 4.01 us
  local copies, waits for them, and re-layouts: 16.3 us -> 7.94 us
  blocking collectives: 29.5 us -> 21.4 us
    all_to_all x6 -> x1, waiting for transfers between devices: 68.5 us -> 0.01 us  [swap8(): return lax.all_to_all(x, 'img', 0, 0, axis_index_groups=chips, tiled=True)]
    dot_general x11 -> x0, matrix products: 55 us -> none  [the longest x2 15.1 us: shards(): jnp.einsum('rtj,trd->jd', grad_scores, query_heads[:, group_index], prefe...]
    all_to_all x6 -> x1, starting transfers between devices: 39 us -> 4.32 us  [swap8(): return lax.all_to_all(x, 'img', 0, 0, axis_index_groups=chips, tiled=True)]
    ppermute x0 -> x20, starting transfers between devices: none -> 33.6 us  [moved(): return lambda x: lax.ppermute(x, AXES, pairs)]
    pallas_call x0 -> x9, Pallas kernels: none -> 33.5 us  [the longest x4 12.8 us: backward(): pl.pallas_call(body, out_shape=jax.ShapeDtypeStruct((span, 2 * HD), dtype...]
    all_gather x3 -> x0, blocking collectives: 29.5 us -> none  [the longest x1 10.5 us: shards(): lax.all_gather(value_own.astype(jnp.bfloat16), 'txt', axis=0, tiled=True)]
    all_to_all x0 -> x2, blocking collectives: none -> 21.4 us  [swap8(): return lax.all_to_all(x, 'img', 0, 0, axis_index_groups=chips, tiled=True)]
    reduce_sum x6 -> x0, other arithmetic: 13.9 us -> none  [the longest x1 7.97 us: shards(): jnp.sum(weights, axis=-1, dtype=jnp.float32).transpose(2, 0, 1)]
  transfers between devices with their start and end apart: 6 -> 21, of which waited for: 4 -> 8; matrix products, arithmetic and copies ran while one was open for 12% -> 1% of each run, Pallas kernels for 0% -> 17%
where the time goes in v1:
time: 119 us
  starting transfers between devices  38 us (32%)
  Pallas kernels  33.5 us (28%)
  blocking collectives  21.4 us (18%)
  waiting for transfers between devices  13.3 us (11%)
  local copies, waits for them, and re-layouts  7.94 us (7%)
  other arithmetic  4.01 us (3%)
    ppermute x20, starting transfers between devices, moved(): return lambda x: lax.ppermute(x, AXES, pairs)  33.6 us
    all_to_all x2, blocking collectives, swap8(): return lax.all_to_all(x, 'img', 0, 0, axis_index_groups=chips, tiled=True)  21.4 us
    ppermute x20, waiting for transfers between devices, moved(): return lambda x: lax.ppermute(x, AXES, pairs)  13.3 us
    pallas_call x4, Pallas kernels, backward(): pl.pallas_call(body, out_shape=jax.ShapeDtypeStruct((span, 2 * HD), dtype...  12.8 us
    unnamed x24, local copies, waits for them, and re-layouts  7.92 us
    pallas_call x1, Pallas kernels, forward(): pl.pallas_call(body, out_shape=(jax.ShapeDtypeStruct((8, rows // 8, width...  6.93 us
    pallas_call x2, Pallas kernels, project(): pl.pallas_call(body, out_shape=(out(own_dtype), out(sent_dtype), out(sent...  5.81 us
    pallas_call x1, Pallas kernels, feature_grad(): pl.pallas_call(body, out_shape=jax.ShapeDtypeStruct((rows, feat), BF), gr...  4.73 us
  transfers between devices with their start and end apart: 21, of which 8 were waited for; matrix products, arithmetic and copies ran while one was open for 1% of the time, Pallas kernels for 17%

profile of v1, /device:TPU:1, one launch (start us, length us, event | category | flops | bytes accessed | tf_op | source)
XLA Modules:
  0.0 118.9 jit_solution(12365060043006403005)
XLA Ops:
  0.6 0.1 pad_add_fusion.1.ix
  0.7 2.1 %copy-done.4 = bf16[3840,512]{1,0:T(8,128)(2,1)S(1)} copy-done((bf16[3840,512]{1,0:T(8,128)(2,1)S(1)}, bf16[3840,512]{1,0:T(8,128)(2,1)}, u32[]{:S(2)}) %copy-start.4) | copy-done | bytes 3932184
  2.8 1.5 %copy-done.6 = bf16[256,3840]{1,0:T(8,128)(2,1)S(1)} copy-done((bf16[256,3840]{1,0:T(8,128)(2,1)S(1)}, bf16[256,3840]{1,0:T(8,128)(2,1)}, u32[]{:S(2)}) %copy-start.6) | copy-done | bytes 1966104
  4.4 2.9 %values.1 = (f32[256,128]{1,0:T(8,128)S(1)}, bf16[256,128]{1,0:T(8,128)(2,1)S(1)}, bf16[256,128]{1,0:T(8,128)(2,1)S(1)}, bf16[256,128]{1,0:T(8,128)(2,1)S(1)}) custom-call(s32[4]{0:T(128)S(1)} %pad_add_fusion.1.ix, bf16[256,3840]{1,0:T(8,128)(2,1)S(1)} %copy-done.6, bf16[3840,512]{1,0:T(8,128)(2,1)S(1)} %copy-done.4), custom_call_target="tpu_custom_call" | custom-call | tf_op jit(solution)/shard_map/values/pallas_call | solution.py:80
  7.3 4.5 %collective-permute-start.7 = (bf16[256,128]{1,0:T(8,128)(2,1)S(1)}, bf16[256,128]{1,0:T(8,128)(2,1)S(1)}, u32[]{:S(2)}, u32[]{:S(2)}) collective-permute-start(bf16[256,128]{1,0:T(8,128)(2,1)S(1)} %get-tuple-element.17), channel_id=1, source_target_pairs={{0,4},{1,5},{2,6},{3,7},{4,0},{5,1},{6,2},{7,3},{8,12},{9,13},{10,... | collective-permute-start | bytes 196616 | tf_op jit(solution)/shard_map/ppermute | solution.py:39
  11.8 0.0 copy-done.11
  11.8 1.0 collective-permute-start
  12.8 0.0 collective-permute-start.8
  12.8 0.2 collective-permute-start.9
  13.0 0.0 copy-done.2
  13.0 2.9 %keys.1 = (f32[256,128]{1,0:T(8,128)S(1)}, f32[256,128]{1,0:T(8,128)S(1)}, f32[256,128]{1,0:T(8,128)S(1)}, f32[256,128]{1,0:T(8,128)S(1)}) custom-call(s32[4]{0:T(128)S(1)} %pad_add_fusion.1.ix, bf16[256,3840]{1,0:T(8,128)(2,1)S(1)} %copy-done.6, bf16[3840,512]{1,0:T(8,128)(2,1)S(1)} %copy-done.2), custom_call_target="tpu_custom_call" | custom-call | tf_op jit(solution)/shard_map/keys/pallas_call | solution.py:80
  15.9 0.0 copy-start
  15.9 3.2 %collective-permute-start.1 = (f32[256,128]{1,0:T(8,128)S(1)}, f32[256,128]{1,0:T(8,128)S(1)}, u32[]{:S(2)}, u32[]{:S(2)}) collective-permute-start(f32[256,128]{1,0:T(8,128)S(1)} %get-tuple-element.13), channel_id=1, source_target_pairs={{0,4},{1,5},{2,6},{3,7},{4,0},{5,1},{6,2},{7,3},{8,12},{9,13},{10,... | collective-permute-start | bytes 393224 | tf_op jit(solution)/shard_map/ppermute | solution.py:39
  19.2 0.0 collective-permute-done.7
  19.2 0.3 collective-permute-start.2
  19.5 0.0 collective-permute-done.8
  19.5 0.3 collective-permute-start.3
  19.8 0.0 collective-permute-done.9
  19.8 2.8 %collective-permute-start.12 = (bf16[512,128]{1,0:T(8,128)(2,1)S(1)}, bf16[512,128]{1,0:T(8,128)(2,1)S(1)}, u32[]{:S(2)}, u32[]{:S(2)}) collective-permute-start(bf16[512,128]{1,0:T(8,128)(2,1)S(1)} %pad_maximum_fusion.1.v0.v), channel_id=1, source_target_pairs={{0,3},{1,2},{2,1},{3,0},{4,7},{5,6},{6,5},{7,4},{8,11},{9,10},{10,... | collective-permute-start | bytes 393224 | tf_op jit(solution)/shard_map/ppermute | solution.py:39
  22.6 0.1 collective-permute-done.1
  22.7 2.9 %collective-permute-start.11 = (bf16[512,128]{1,0:T(8,128)(2,1)S(1)}, bf16[512,128]{1,0:T(8,128)(2,1)S(1)}, u32[]{:S(2)}, u32[]{:S(2)}) collective-permute-start(bf16[512,128]{1,0:T(8,128)(2,1)S(1)} %pad_maximum_fusion.1.v0.v), channel_id=1, source_target_pairs={{0,2},{1,3},{2,0},{3,1},{4,6},{5,7},{6,4},{7,5},{8,10},{9,11},{10,... | collective-permute-start | bytes 393224 | tf_op jit(solution)/shard_map/ppermute | solution.py:39
  25.6 0.0 collective-permute-done.2
  25.6 0.5 collective-permute-start.10
  26.1 0.3 collective-permute-done.3
  26.4 2.8 %collective-permute-start.6 = (bf16[512,128]{1,0:T(8,128)(2,1)S(1)}, bf16[512,128]{1,0:T(8,128)(2,1)S(1)}, u32[]{:S(2)}, u32[]{:S(2)}) collective-permute-start(bf16[512,128]{1,0:T(8,128)(2,1)S(1)} %pad_maximum_fusion.k0.k), channel_id=1, source_target_pairs={{0,3},{1,2},{2,1},{3,0},{4,7},{5,6},{6,5},{7,4},{8,11},{9,10},{10,... | collective-permute-start | bytes 393224 | tf_op jit(solution)/shard_map/ppermute | solution.py:39
  29.2 0.0 collective-permute-done
  29.2 0.4 collective-permute-start.5
  29.6 0.0 collective-permute-done.12.v3.v
  29.6 0.3 collective-permute-start.4
  29.9 0.0 collective-permute-done.11.v2.v
  29.9 1.2 %collective-permute-done.10.v1.v = bf16[512,128]{1,0:T(8,128)(2,1)S(1)} collective-permute-done((bf16[512,128]{1,0:T(8,128)(2,1)S(1)}, bf16[512,128]{1,0:T(8,128)(2,1)S(1)}, u32[]{:S(2)}, u32[]{:S(2)}) %collective-permute-start.10) | collective-permute-done | bytes 131104 | tf_op jit(solution)/shard_map/ppermute | solution.py:39
  31.1 3.0 %collective-permute-done.6.k3.k = bf16[512,128]{1,0:T(8,128)(2,1)S(1)} collective-permute-done((bf16[512,128]{1,0:T(8,128)(2,1)S(1)}, bf16[512,128]{1,0:T(8,128)(2,1)S(1)}, u32[]{:S(2)}, u32[]{:S(2)}) %collective-permute-start.6) | collective-permute-done | bytes 131104 | tf_op jit(solution)/shard_map/ppermute | solution.py:39
  34.1 1.1 collective-permute-done.5.k2.k
  35.2 1.8 %collective-permute-done.4.k1.k = bf16[512,128]{1,0:T(8,128)(2,1)S(1)} collective-permute-done((bf16[512,128]{1,0:T(8,128)(2,1)S(1)}, bf16[512,128]{1,0:T(8,128)(2,1)S(1)}, u32[]{:S(2)}, u32[]{:S(2)}) %collective-permute-start.4) | collective-permute-done | bytes 131104 | tf_op jit(solution)/shard_map/ppermute | solution.py:39
  37.1 0.0 copy-done.9
  37.1 6.9 %fwd.1 = (bf16[8,32,1024]{2,1,0:T(8,128)(2,1)S(1)}, f32[8,16,256]{2,1,0:T(8,128)S(1)}) custom-call(s32[4]{0:T(128)S(1)} %pad_add_fusion.1.ix, s32[2,8]{1,0:T(2,128)S(1)} %pad_add_fusion.tl, s32[8,8]{1,0:T(8,128)S(1)} %copy-done.8, bf16[256,2048]{1,0:T(8,128)(2,1)S(1)} %copy-done, bf16[256,2048]{1,0:T(8,128)(2,1)S(1)} %copy-done.1, ...), custom_call_target="tpu_custom_call" | custom-call | tf_op jit(solution)/shard_map/fwd/pallas_call | solution.py:158
  44.0 10.5 %all_to_all.15.st = f32[8,16,256]{2,1,0:T(8,128)} all-to-all(f32[8,16,256]{2,1,0:T(8,128)S(1)} %get-tuple-element.21), channel_id=1, replica_groups={{0,16,32,48,64,80,96,112},{8,24,40,56,72,88,104,120},{1,17,33,49,65,81,..., dimensions={0} | all-to-all | bytes 262144 | tf_op jit(solution)/shard_map/all_to_all | solution.py:345
  54.5 10.9 %all_to_all.16.x = bf16[8,32,1024]{2,1,0:T(8,128)(2,1)} all-to-all(bf16[8,32,1024]{2,1,0:T(8,128)(2,1)S(1)} %get-tuple-element.20), channel_id=1, replica_groups={{0,16,32,48,64,80,96,112},{8,24,40,56,72,88,104,120},{1,17,33,49,65,81,..., dimensions={0} | all-to-all | bytes 1048576 | tf_op jit(solution)/shard_map/all_to_all | solution.py:345
  65.4 3.1 %combine.1 = bf16[8,32,1024]{2,1,0:T(8,128)(2,1)} custom-call(s32[4]{0:T(128)} %copy-done.9, bf16[8,32,1024]{2,1,0:T(8,128)(2,1)} %all_to_all.16.x, f32[8,16,256]{2,1,0:T(8,128)} %all_to_all.15.st), custom_call_target="tpu_custom_call" | custom-call | tf_op jit(solution)/shard_map/combine/pallas_call | solution.py:212
  68.6 4.3 %all-to-all-start.2 = ((bf16[8,32,1024]{2,1,0:T(8,128)(2,1)}), bf16[8,32,1024]{2,1,0:T(8,128)(2,1)}, u32[]{:S(2)}, u32[]{:S(2)}) async-start(bf16[8,32,1024]{2,1,0:T(8,128)(2,1)} %combine.1), calls=%async_computation.2 | async-start | bytes 1048576 | tf_op jit(solution)/shard_map/all_to_all | solution.py:345
  72.9 3.0 %grads2.1 = bf16[512,256]{1,0:T(8,128)(2,1)S(1)} custom-call(s32[4]{0:T(128)S(1)} %copy-done.10, s32[2,8]{1,0:T(2,128)S(1)} %pad_add_fusion.tl, s32[8,8]{1,0:T(8,128)S(1)} %copy-done.8, bf16[256,2048]{1,0:T(8,128)(2,1)S(1)} %copy-done, bf16[256,2048]{1,0:T(8,128)(2,1)S(1)} %copy-done.1, bf16[512,128]{1,0:T(8,128)(2,1)S(1)} %collective-permute-done.5.k2.k, ...), custom_call_target="tpu_custom_call" | custom-call | tf_op jit(solution)/shard_map/grads2/pallas_call | solution.py:279
  76.0 2.4 %collective-permute-start.14 = (bf16[512,256]{1,0:T(8,128)(2,1)S(1)}, bf16[512,256]{1,0:T(8,128)(2,1)}, u32[]{:S(2)}, u32[]{:S(2)}) collective-permute-start(bf16[512,256]{1,0:T(8,128)(2,1)S(1)} %grads2.1), channel_id=1, source_target_pairs={{0,2},{1,3},{2,0},{3,1},{4,6},{5,7},{6,4},{7,5},{8,10},{9,11},{10,... | collective-permute-start | bytes 786440 | tf_op jit(solution)/shard_map/ppermute | solution.py:39
  78.3 3.7 %grads1.1 = bf16[512,256]{1,0:T(8,128)(2,1)} custom-call(s32[4]{0:T(128)S(1)} %copy-done.10, s32[2,8]{1,0:T(2,128)S(1)} %pad_add_fusion.tl, s32[8,8]{1,0:T(8,128)S(1)} %copy-done.8, bf16[256,2048]{1,0:T(8,128)(2,1)S(1)} %copy-done, bf16[256,2048]{1,0:T(8,128)(2,1)S(1)} %copy-done.1, bf16[512,128]{1,0:T(8,128)(2,1)S(1)} %collective-permute-done.4.k1.k, ...), custom_call_target="tpu_custom_call" | custom-call | tf_op jit(solution)/shard_map/grads1/pallas_call | solution.py:279
  82.1 0.0 collective-permute-start.15
  82.1 3.0 %grads3.1 = bf16[512,256]{1,0:T(8,128)(2,1)S(1)} custom-call(s32[4]{0:T(128)S(1)} %copy-done.10, s32[2,8]{1,0:T(2,128)S(1)} %pad_add_fusion.tl, s32[8,8]{1,0:T(8,128)S(1)} %copy-done.8, bf16[256,2048]{1,0:T(8,128)(2,1)S(1)} %copy-done, bf16[256,2048]{1,0:T(8,128)(2,1)S(1)} %copy-done.1, bf16[512,128]{1,0:T(8,128)(2,1)S(1)} %collective-permute-done.6.k3.k, ...), custom_call_target="tpu_custom_call" | custom-call | tf_op jit(solution)/shard_map/grads3/pallas_call | solution.py:279
  85.1 1.3 %collective-permute-start.16 = (bf16[512,256]{1,0:T(8,128)(2,1)S(1)}, bf16[512,256]{1,0:T(8,128)(2,1)}, u32[]{:S(2)}, u32[]{:S(2)}) collective-permute-start(bf16[512,256]{1,0:T(8,128)(2,1)S(1)} %grads3.1), channel_id=1, source_target_pairs={{0,3},{1,2},{2,1},{3,0},{4,7},{5,6},{6,5},{7,4},{8,11},{9,10},{10,... | collective-permute-start | bytes 786440 | tf_op jit(solution)/shard_map/ppermute | solution.py:39
  86.4 3.0 %grads0.1 = f32[512,256]{1,0:T(8,128)S(1)} custom-call(s32[4]{0:T(128)S(1)} %copy-done.10, s32[2,8]{1,0:T(2,128)S(1)} %pad_add_fusion.tl, s32[8,8]{1,0:T(8,128)S(1)} %copy-done.8, bf16[256,2048]{1,0:T(8,128)(2,1)S(1)} %copy-done, bf16[256,2048]{1,0:T(8,128)(2,1)S(1)} %copy-done.1, bf16[512,128]{1,0:T(8,128)(2,1)S(1)} %pad_maximum_fusion.k0.k, ...), custom_call_target="tpu_custom_call" | custom-call | tf_op jit(solution)/shard_map/grads0/pallas_call | solution.py:279
  89.4 0.0 all-to-all-done.2
  89.4 4.7 %collective-permute-start.13 = (bf16[256,1024]{1,0:T(8,128)(2,1)}, bf16[256,1024]{1,0:T(8,128)(2,1)S(1)}, u32[]{:S(2)}, u32[]{:S(2)}) collective-permute-start(bf16[256,1024]{1,0:T(8,128)(2,1)} %bitcast.6), channel_id=1, source_target_pairs={{0,8},{1,9},{2,10},{3,11},{4,12},{5,13},{6,14},{7,15},{8,0},{9,1},... | collective-permute-start | bytes 1572872 | tf_op jit(solution)/shard_map/ppermute | solution.py:39
  94.2 0.0 collective-permute-done.14
  94.2 0.0 collective-permute-done.15
  94.2 0.0 collective-permute-done.16
  94.2 1.2 %add_convert_fusion = bf16[512,256]{1,0:T(8,128)(2,1)S(1)} fusion(bf16[512,256]{1,0:T(8,128)(2,1)} %collective-permute-done.16, bf16[512,256]{1,0:T(8,128)(2,1)} %collective-permute-done.15, f32[512,256]{1,0:T(8,128)S(1)} %grads0.1, bf16[512,256]{1,0:T(8,128)(2,1)} %collective-permute-done.14), kind=kLoop, calls=%fused_computation.1 | loop fusion | flops 917504 | bytes 1572864 | tf_op jit(solution)/shard_map/convert_element_type | solution.py:375
  95.4 5.9 %collective-permute-start.19 = (bf16[256,256]{1,0:T(8,128)(2,1)S(1)}, bf16[256,256]{1,0:T(8,128)(2,1)S(1)}, u32[]{:S(2)}, u32[]{:S(2)}) collective-permute-start(bf16[256,256]{1,0:T(8,128)(2,1)S(1)} %get-tuple-element.22), channel_id=1, source_target_pairs={{0,12},{1,13},{2,14},{3,15},{4,8},{5,9},{6,10},{7,11},{8,4},{9,5},... | collective-permute-start | bytes 393224 | tf_op jit(solution)/shard_map/ppermute | solution.py:39
  101.3 0.0 collective-permute-start.17
  101.3 0.2 collective-permute-start.18
  101.5 3.1 %collective-permute-done.19.d_ = bf16[256,256]{1,0:T(8,128)(2,1)S(1)} collective-permute-done((bf16[256,256]{1,0:T(8,128)(2,1)S(1)}, bf16[256,256]{1,0:T(8,128)(2,1)S(1)}, u32[]{:S(2)}, u32[]{:S(2)}) %collective-permute-start.19) | collective-permute-done | bytes 131104 | tf_op jit(solution)/shard_map/ppermute | solution.py:39
  104.6 0.0 collective-permute-done.17.b
  104.6 2.8 %collective-permute-done.18.c_ = bf16[256,256]{1,0:T(8,128)(2,1)S(1)} collective-permute-done((bf16[256,256]{1,0:T(8,128)(2,1)S(1)}, bf16[256,256]{1,0:T(8,128)(2,1)S(1)}, u32[]{:S(2)}, u32[]{:S(2)}) %collective-permute-start.18) | collective-permute-done | bytes 131104 | tf_op jit(solution)/shard_map/ppermute | solution.py:39
  107.4 2.1 %copy-done.3 = bf16[3840,512]{1,0:T(8,128)(2,1)S(1)} copy-done((bf16[3840,512]{1,0:T(8,128)(2,1)S(1)}, bf16[3840,512]{1,0:T(8,128)(2,1)}, u32[]{:S(2)}) %copy-start.3) | copy-done | bytes 3932184
  109.5 2.1 %copy-done.5 = bf16[3840,512]{1,0:T(8,128)(2,1)S(1)} copy-done((bf16[3840,512]{1,0:T(8,128)(2,1)S(1)}, bf16[3840,512]{1,0:T(8,128)(2,1)}, u32[]{:S(2)}) %copy-start.5) | copy-done | bytes 3932184
  111.6 4.7 %feats.1 = bf16[256,3840]{1,0:T(8,128)(2,1)} custom-call(s32[4]{0:T(128)S(1)} %copy-done.10, bf16[256,256]{1,0:T(8,128)(2,1)S(1)} %get-tuple-element.23.a, bf16[256,256]{1,0:T(8,128)(2,1)S(1)} %collective-permute-done.17.b, bf16[256,256]{1,0:T(8,128)(2,1)S(1)} %collective-permute-done.18.c_, bf16[256,256]{1,0:T(8,128)(2,1)S(1)} %collective-permute-done.19.d_, ...), custom_call_target="tpu_custom_call" | custom-call | tf_op jit(solution)/shard_map/feats/pallas_call | solution.py:321
  116.3 0.0 collective-permute-done.13
  116.3 2.6 %maximum_select_fusion = bf16[256,2048]{1,0:T(8,128)(2,1)} fusion(bf16[256,1024]{1,0:T(8,128)(2,1)S(1)} %collective-permute-done.13, bf16[256,1024]{1,0:T(8,128)(2,1)} %bitcast.6, pred[]{:T(512)S(6)} %eq.5), kind=kLoop, calls=%fused_computation | loop fusion | flops 4718592 | bytes 2097153 | tf_op jit(solution)/shard_map/jit(_where)/select_n | solution.py:385
  (24 shorter events, 0.2 us)
Async XLA Ops:
  0.7 2.1 %copy-start.4 = (bf16[3840,512]{1,0:T(8,128)(2,1)S(1)}, bf16[3840,512]{1,0:T(8,128)(2,1)}, u32[]{:S(2)}) copy-start(bf16[3840,512]{1,0:T(8,128)(2,1)} %wv.1) | copy-start | bytes 11796484
  2.8 1.5 %copy-start.6 = (bf16[256,3840]{1,0:T(8,128)(2,1)S(1)}, bf16[256,3840]{1,0:T(8,128)(2,1)}, u32[]{:S(2)}) copy-start(bf16[256,3840]{1,0:T(8,128)(2,1)} %x.3) | copy-start | bytes 5898244
  4.4 32.7 %copy-start.9 = (s32[4]{0:T(128)}, s32[4]{0:T(128)S(1)}, u32[]{:S(2)}) copy-start(s32[4]{0:T(128)S(1)} %pad_add_fusion.1.ix) | copy-start | bytes 52
  4.4 7.4 %copy-start.11 = (s32[8]{0:T(128)S(1)}, s32[8]{0:T(128)}, u32[]{:S(2)}) copy-start(s32[8]{0:T(128)} %param.12) | copy-start | bytes 100
  4.4 8.6 %copy-start.2 = (bf16[3840,512]{1,0:T(8,128)(2,1)S(1)}, bf16[3840,512]{1,0:T(8,128)(2,1)}, u32[]{:S(2)}) copy-start(bf16[3840,512]{1,0:T(8,128)(2,1)} %wk.1) | copy-start | bytes 11796484
  7.3 11.8 %collective-permute-start.7 = (bf16[256,128]{1,0:T(8,128)(2,1)S(1)}, bf16[256,128]{1,0:T(8,128)(2,1)S(1)}, u32[]{:S(2)}, u32[]{:S(2)}) collective-permute-start(bf16[256,128]{1,0:T(8,128)(2,1)S(1)} %get-tuple-element.17), channel_id=1, source_target_pairs={{0,4},{1,5},{2,6},{3,7},{4,0},{5,1},{6,2},{7,3},{8,12},{9,13},{10,... | collective-permute-start | bytes 196616 | tf_op jit(solution)/shard_map/ppermute | solution.py:39
  11.8 17.4 %collective-permute-start = (s32[8]{0:T(128)S(1)}, s32[8]{0:T(128)S(1)}, u32[]{:S(2)}, u32[]{:S(2)}) collective-permute-start(s32[8]{0:T(128)S(1)} %copy-done.11), channel_id=1, source_target_pairs={{0,8},{1,9},{2,10},{3,11},{4,12},{5,13},{6,14},{7,15},{8,0},{9,1},... | collective-permute-start | bytes 104 | tf_op jit(solution)/shard_map/ppermute | solution.py:39
  12.8 6.7 %collective-permute-start.8 = (bf16[256,128]{1,0:T(8,128)(2,1)S(1)}, bf16[256,128]{1,0:T(8,128)(2,1)S(1)}, u32[]{:S(2)}, u32[]{:S(2)}) collective-permute-start(bf16[256,128]{1,0:T(8,128)(2,1)S(1)} %get-tuple-element.18), channel_id=1, source_target_pairs={{0,8},{1,9},{2,10},{3,11},{4,12},{5,13},{6,14},{7,15},{8,0},{9,1},... | collective-permute-start | bytes 196616 | tf_op jit(solution)/shard_map/ppermute | solution.py:39
  12.8 24.3 %copy-start.8 = (s32[8,8]{1,0:T(8,128)S(1)}, s32[8,8]{1,0:T(8,128)}, u32[]{:S(2)}) copy-start(s32[8,8]{1,0:T(8,128)} %se.9) | copy-start | bytes 772
  12.8 7.0 %collective-permute-start.9 = (bf16[256,128]{1,0:T(8,128)(2,1)S(1)}, bf16[256,128]{1,0:T(8,128)(2,1)S(1)}, u32[]{:S(2)}, u32[]{:S(2)}) collective-permute-start(bf16[256,128]{1,0:T(8,128)(2,1)S(1)} %get-tuple-element.19), channel_id=1, source_target_pairs={{0,12},{1,13},{2,14},{3,15},{4,8},{5,9},{6,10},{7,11},{8,4},{9,5},... | collective-permute-start | bytes 196616 | tf_op jit(solution)/shard_map/ppermute | solution.py:39
  13.0 24.1 %copy-start.1 = (bf16[256,2048]{1,0:T(8,128)(2,1)S(1)}, bf16[256,2048]{1,0:T(8,128)(2,1)}, u32[]{:S(2)}) copy-start(bf16[256,2048]{1,0:T(8,128)(2,1)} %g.9) | copy-start | bytes 3145732
  15.9 21.2 %copy-start = (bf16[256,2048]{1,0:T(8,128)(2,1)S(1)}, bf16[256,2048]{1,0:T(8,128)(2,1)}, u32[]{:S(2)}) copy-start(bf16[256,2048]{1,0:T(8,128)(2,1)} %q.9) | copy-start | bytes 3145732
  15.9 6.8 %collective-permute-start.1 = (f32[256,128]{1,0:T(8,128)S(1)}, f32[256,128]{1,0:T(8,128)S(1)}, u32[]{:S(2)}, u32[]{:S(2)}) collective-permute-start(f32[256,128]{1,0:T(8,128)S(1)} %get-tuple-element.13), channel_id=1, source_target_pairs={{0,4},{1,5},{2,6},{3,7},{4,0},{5,1},{6,2},{7,3},{8,12},{9,13},{10,... | collective-permute-start | bytes 393224 | tf_op jit(solution)/shard_map/ppermute | solution.py:39
  19.2 6.5 %collective-permute-start.2 = (f32[256,128]{1,0:T(8,128)S(1)}, f32[256,128]{1,0:T(8,128)S(1)}, u32[]{:S(2)}, u32[]{:S(2)}) collective-permute-start(f32[256,128]{1,0:T(8,128)S(1)} %get-tuple-element.14), channel_id=1, source_target_pairs={{0,8},{1,9},{2,10},{3,11},{4,12},{5,13},{6,14},{7,15},{8,0},{9,1},... | collective-permute-start | bytes 393224 | tf_op jit(solution)/shard_map/ppermute | solution.py:39
  19.5 6.9 %collective-permute-start.3 = (f32[256,128]{1,0:T(8,128)S(1)}, f32[256,128]{1,0:T(8,128)S(1)}, u32[]{:S(2)}, u32[]{:S(2)}) collective-permute-start(f32[256,128]{1,0:T(8,128)S(1)} %get-tuple-element.15), channel_id=1, source_target_pairs={{0,12},{1,13},{2,14},{3,15},{4,8},{5,9},{6,10},{7,11},{8,4},{9,5},... | collective-permute-start | bytes 393224 | tf_op jit(solution)/shard_map/ppermute | solution.py:39
  19.8 9.8 %collective-permute-start.12 = (bf16[512,128]{1,0:T(8,128)(2,1)S(1)}, bf16[512,128]{1,0:T(8,128)(2,1)S(1)}, u32[]{:S(2)}, u32[]{:S(2)}) collective-permute-start(bf16[512,128]{1,0:T(8,128)(2,1)S(1)} %pad_maximum_fusion.1.v0.v), channel_id=1, source_target_pairs={{0,3},{1,2},{2,1},{3,0},{4,7},{5,6},{6,5},{7,4},{8,11},{9,10},{10,... | collective-permute-start | bytes 393224 | tf_op jit(solution)/shard_map/ppermute | solution.py:39
  22.7 7.3 %collective-permute-start.11 = (bf16[512,128]{1,0:T(8,128)(2,1)S(1)}, bf16[512,128]{1,0:T(8,128)(2,1)S(1)}, u32[]{:S(2)}, u32[]{:S(2)}) collective-permute-start(bf16[512,128]{1,0:T(8,128)(2,1)S(1)} %pad_maximum_fusion.1.v0.v), channel_id=1, source_target_pairs={{0,2},{1,3},{2,0},{3,1},{4,6},{5,7},{6,4},{7,5},{8,10},{9,11},{10,... | collective-permute-start | bytes 393224 | tf_op jit(solution)/shard_map/ppermute | solution.py:39
  25.6 5.5 %collective-permute-start.10 = (bf16[512,128]{1,0:T(8,128)(2,1)S(1)}, bf16[512,128]{1,0:T(8,128)(2,1)S(1)}, u32[]{:S(2)}, u32[]{:S(2)}) collective-permute-start(bf16[512,128]{1,0:T(8,128)(2,1)S(1)} %pad_maximum_fusion.1.v0.v), channel_id=1, source_target_pairs={{0,1},{1,0},{2,3},{3,2},{4,5},{5,4},{6,7},{7,6},{8,9},{9,8},{10,11... | collective-permute-start | bytes 393224 | tf_op jit(solution)/shard_map/ppermute | solution.py:39
  26.4 7.7 %collective-permute-start.6 = (bf16[512,128]{1,0:T(8,128)(2,1)S(1)}, bf16[512,128]{1,0:T(8,128)(2,1)S(1)}, u32[]{:S(2)}, u32[]{:S(2)}) collective-permute-start(bf16[512,128]{1,0:T(8,128)(2,1)S(1)} %pad_maximum_fusion.k0.k), channel_id=1, source_target_pairs={{0,3},{1,2},{2,1},{3,0},{4,7},{5,6},{6,5},{7,4},{8,11},{9,10},{10,... | collective-permute-start | bytes 393224 | tf_op jit(solution)/shard_map/ppermute | solution.py:39
  29.2 6.0 %collective-permute-start.5 = (bf16[512,128]{1,0:T(8,128)(2,1)S(1)}, bf16[512,128]{1,0:T(8,128)(2,1)S(1)}, u32[]{:S(2)}, u32[]{:S(2)}) collective-permute-start(bf16[512,128]{1,0:T(8,128)(2,1)S(1)} %pad_maximum_fusion.k0.k), channel_id=1, source_target_pairs={{0,2},{1,3},{2,0},{3,1},{4,6},{5,7},{6,4},{7,5},{8,10},{9,11},{10,... | collective-permute-start | bytes 393224 | tf_op jit(solution)/shard_map/ppermute | solution.py:39
  29.6 7.4 %collective-permute-start.4 = (bf16[512,128]{1,0:T(8,128)(2,1)S(1)}, bf16[512,128]{1,0:T(8,128)(2,1)S(1)}, u32[]{:S(2)}, u32[]{:S(2)}) collective-permute-start(bf16[512,128]{1,0:T(8,128)(2,1)S(1)} %pad_maximum_fusion.k0.k), channel_id=1, source_target_pairs={{0,1},{1,0},{2,3},{3,2},{4,5},{5,4},{6,7},{7,6},{8,9},{9,8},{10,11... | collective-permute-start | bytes 393224 | tf_op jit(solution)/shard_map/ppermute | solution.py:39
  44.0 28.9 %copy-start.10 = (s32[4]{0:T(128)S(1)}, s32[4]{0:T(128)}, u32[]{:S(2)}) copy-start(s32[4]{0:T(128)} %copy-done.9) | copy-start | bytes 52
  54.5 18.4 %copy-start.7 = (f32[8,16,256]{2,1,0:T(8,128)S(1)}, f32[8,16,256]{2,1,0:T(8,128)}, u32[]{:S(2)}) copy-start(f32[8,16,256]{2,1,0:T(8,128)} %all_to_all.15.st) | copy-start | bytes 393220
  68.6 20.9 %all-to-all-start.2 = ((bf16[8,32,1024]{2,1,0:T(8,128)(2,1)}), bf16[8,32,1024]{2,1,0:T(8,128)(2,1)}, u32[]{:S(2)}, u32[]{:S(2)}) async-start(bf16[8,32,1024]{2,1,0:T(8,128)(2,1)} %combine.1), calls=%async_computation.2 | async-start | bytes 1048576 | tf_op jit(solution)/shard_map/all_to_all | solution.py:345
  76.0 18.2 %collective-permute-start.14 = (bf16[512,256]{1,0:T(8,128)(2,1)S(1)}, bf16[512,256]{1,0:T(8,128)(2,1)}, u32[]{:S(2)}, u32[]{:S(2)}) collective-permute-start(bf16[512,256]{1,0:T(8,128)(2,1)S(1)} %grads2.1), channel_id=1, source_target_pairs={{0,2},{1,3},{2,0},{3,1},{4,6},{5,7},{6,4},{7,5},{8,10},{9,11},{10,... | collective-permute-start | bytes 786440 | tf_op jit(solution)/shard_map/ppermute | solution.py:39
  82.1 12.1 %collective-permute-start.15 = (bf16[512,256]{1,0:T(8,128)(2,1)}, bf16[512,256]{1,0:T(8,128)(2,1)}, u32[]{:S(2)}, u32[]{:S(2)}) collective-permute-start(bf16[512,256]{1,0:T(8,128)(2,1)} %grads1.1), channel_id=1, source_target_pairs={{0,1},{1,0},{2,3},{3,2},{4,5},{5,4},{6,7},{7,6},{8,9},{9,8},{10,11... | collective-permute-start | bytes 786440 | tf_op jit(solution)/shard_map/ppermute | solution.py:39
  85.1 9.1 %collective-permute-start.16 = (bf16[512,256]{1,0:T(8,128)(2,1)S(1)}, bf16[512,256]{1,0:T(8,128)(2,1)}, u32[]{:S(2)}, u32[]{:S(2)}) collective-permute-start(bf16[512,256]{1,0:T(8,128)(2,1)S(1)} %grads3.1), channel_id=1, source_target_pairs={{0,3},{1,2},{2,1},{3,0},{4,7},{5,6},{6,5},{7,4},{8,11},{9,10},{10,... | collective-permute-start | bytes 786440 | tf_op jit(solution)/shard_map/ppermute | solution.py:39
  89.4 26.9 %collective-permute-start.13 = (bf16[256,1024]{1,0:T(8,128)(2,1)}, bf16[256,1024]{1,0:T(8,128)(2,1)S(1)}, u32[]{:S(2)}, u32[]{:S(2)}) collective-permute-start(bf16[256,1024]{1,0:T(8,128)(2,1)} %bitcast.6), channel_id=1, source_target_pairs={{0,8},{1,9},{2,10},{3,11},{4,12},{5,13},{6,14},{7,15},{8,0},{9,1},... | collective-permute-start | bytes 1572872 | tf_op jit(solution)/shard_map/ppermute | solution.py:39
  95.4 9.1 %collective-permute-start.19 = (bf16[256,256]{1,0:T(8,128)(2,1)S(1)}, bf16[256,256]{1,0:T(8,128)(2,1)S(1)}, u32[]{:S(2)}, u32[]{:S(2)}) collective-permute-start(bf16[256,256]{1,0:T(8,128)(2,1)S(1)} %get-tuple-element.22), channel_id=1, source_target_pairs={{0,12},{1,13},{2,14},{3,15},{4,8},{5,9},{6,10},{7,11},{8,4},{9,5},... | collective-permute-start | bytes 393224 | tf_op jit(solution)/shard_map/ppermute | solution.py:39
  101.3 3.3 %collective-permute-start.17 = (bf16[256,256]{1,0:T(8,128)(2,1)S(1)}, bf16[256,256]{1,0:T(8,128)(2,1)S(1)}, u32[]{:S(2)}, u32[]{:S(2)}) collective-permute-start(bf16[256,256]{1,0:T(8,128)(2,1)S(1)} %get-tuple-element.22), channel_id=1, source_target_pairs={{0,8},{1,9},{2,10},{3,11},{4,12},{5,13},{6,14},{7,15},{8,0},{9,1},... | collective-permute-start | bytes 393224 | tf_op jit(solution)/shard_map/ppermute | solution.py:39
  101.3 6.1 %collective-permute-start.18 = (bf16[256,256]{1,0:T(8,128)(2,1)S(1)}, bf16[256,256]{1,0:T(8,128)(2,1)S(1)}, u32[]{:S(2)}, u32[]{:S(2)}) collective-permute-start(bf16[256,256]{1,0:T(8,128)(2,1)S(1)} %get-tuple-element.23.a), channel_id=1, source_target_pairs={{0,4},{1,5},{2,6},{3,7},{4,0},{5,1},{6,2},{7,3},{8,12},{9,13},{10,... | collective-permute-start | bytes 393224 | tf_op jit(solution)/shard_map/ppermute | solution.py:39
  107.4 2.1 %copy-start.3 = (bf16[3840,512]{1,0:T(8,128)(2,1)S(1)}, bf16[3840,512]{1,0:T(8,128)(2,1)}, u32[]{:S(2)}) copy-start(bf16[3840,512]{1,0:T(8,128)(2,1)} %wk.1) | copy-start | bytes 11796484
  109.5 2.1 %copy-start.5 = (bf16[3840,512]{1,0:T(8,128)(2,1)S(1)}, bf16[3840,512]{1,0:T(8,128)(2,1)}, u32[]{:S(2)}) copy-start(bf16[3840,512]{1,0:T(8,128)(2,1)} %wv.1) | copy-start | bytes 11796484

commit v2 on v1

v2 whole, which is shorter than its diff:
```python
import math

import jax
import jax.numpy as jnp
from jax import lax
from jax.experimental import pallas as pl
from jax.experimental.pallas import tpu as pltpu
from jax.sharding import PartitionSpec as P

HD = 128
TILE = 128
TBLK = 128
BF = jnp.bfloat16
F32 = jnp.float32
SCALE = 1.0 / math.sqrt(HD)
C2 = SCALE * math.log2(math.e)
NEG = -1e30
TOP = 3e38
AXES = ("img", "head", "txt")
NT = (((1,), (1,)), ((), ()))


def dot_nt(a, b):
    return lax.dot_general(a, b, NT, preferred_element_type=F32)


def dot_nn(a, b):
    return jnp.dot(a, b, preferred_element_type=F32)


def moved(sizes, where):
    ni, nh, nt = sizes
    pairs = []
    for i in range(ni):
        for h in range(nh):
            for t in range(nt):
                a, b, c = where(i, h, t)
                pairs.append(((i * nh + h) * nt + t, (a * nh + b) * nt + c))
    return lambda x: lax.ppermute(x, AXES, pairs)


def cost(us):
    return pl.CostEstimate(flops=int(us * 1.1e9), transcendentals=0, bytes_accessed=1 << 16)


def spec(shape):
    zeros = (0,) * len(shape)
    return pl.BlockSpec(shape, lambda *_: zeros)


def in_hbm(x):
    return pltpu.with_memory_space_constraint(x, pltpu.HBM)


def project(idx, feats, key_weight, value_weight):
    rows, feat = feats.shape
    cols = key_weight.shape[1]
    steps = 5
    chunk = feat // steps

    def body(ix, x, wk, wv, own, oc, oh, ohc, acc):
        k = pl.program_id(0)
        key = dot_nn(x[...], wk[...])
        value = dot_nn(x[...], wv[...])

        @pl.when(k == 0)
        def _():
            acc[0] = key
            acc[1] = value

        @pl.when(k > 0)
        def _():
            acc[0] += key
            acc[1] += value

        @pl.when(k == steps - 1)
        def _():
            h = ix[0]
            c = ix[1]

            def piece(which, hh, cc):
                at = pl.multiple_of((hh * 2 + cc) * HD, HD)
                return acc[which, :, pl.ds(at, HD)]

            own[:, :HD] = piece(0, h, c)
            own[:, HD:] = piece(1, h, c)
            for ref, hh, cc in ((oh, 1 - h, c), (ohc, 1 - h, 1 - c), (oc, h, 1 - c)):
                kp = piece(0, hh, cc)
                high = kp.astype(BF)
                ref[:, :HD] = high
                ref[:, HD : 2 * HD] = (kp - high.astype(F32)).astype(BF)
                ref[:, 2 * HD :] = piece(1, hh, cc).astype(BF)

    sent = jax.ShapeDtypeStruct((rows, 3 * HD), BF)
    return pl.pallas_call(
        body,
        out_shape=(jax.ShapeDtypeStruct((rows, 2 * HD), F32), sent, sent, sent),
        grid_spec=pltpu.PrefetchScalarGridSpec(
            num_scalar_prefetch=1,
            grid=(steps,),
            in_specs=[
                pl.BlockSpec((rows, chunk), lambda k, ix: (0, k)),
                pl.BlockSpec((chunk, cols), lambda k, ix: (k, 0)),
                pl.BlockSpec((chunk, cols), lambda k, ix: (k, 0)),
            ],
            out_specs=[spec((rows, 2 * HD))] + [spec((rows, 3 * HD))] * 3,
            scratch_shapes=[pltpu.VMEM((2, rows, cols), F32)],
        ),
        compiler_params=pltpu.CompilerParams(vmem_limit_bytes=24 << 20),
        name="project",
        cost_estimate=cost(4),
    )(idx, in_hbm(feats), in_hbm(key_weight), in_hbm(value_weight))


def tile_cap(ix, tiles, sees, block, chunk, tile):
    half, j = divmod(tile, 2)
    shard = jnp.bitwise_xor(ix[2], chunk)
    image = tiles[half, shard * 2 + j]
    row = ix[2] * 2 + block
    return jnp.where(sees[row, image] > 0, jnp.float32(TOP), jnp.float32(NEG))


def forward(idx, tiles, sees, queries, grad_out, kvs):
    rows = queries.shape[0]
    heads = 8
    width = heads * HD
    span = kvs[0].shape[0]
    n = len(kvs)
    total = span * n
    share = rows // 8
    per = span // TILE

    def body(ix, tl, se, q, g, k0, k1, k2, k3, out, y_scr, va):
        ks = (k0, k1, k2, k3)
        for j in range(n):
            va[j * span : (j + 1) * span, :HD] = ks[j][:, HD:]
        va[:, HD:] = jnp.ones((total, HD), BF)
        caps = [
            [tile_cap(ix, tl, se, b, j, e) for j in range(n) for e in range(per)]
            for b in range(2)
        ]
        lane = lax.broadcasted_iota(jnp.int32, (rows, HD), 1)
        st = jnp.zeros((rows, HD), F32)
        for h in range(heads):
            cols = slice(h * HD, (h + 1) * HD)
            slot = h % 2
            qh = q[:, cols]
            best = [None, None]
            for j in range(n):
                s = dot_nt(qh, ks[j][:, :HD]) * C2
                for b in range(2):
                    for e in range(per):
                        y = jnp.minimum(
                            s[b * TBLK : (b + 1) * TBLK, e * TILE : (e + 1) * TILE],
                            caps[b][j * per + e],
                        )
                        at = j * span + e * TILE
                        y_scr[slot, b * TBLK : (b + 1) * TBLK, at : at + TILE] = y
                        best[b] = y if best[b] is None else jnp.maximum(best[b], y)
            m = jnp.max(jnp.concatenate(best, axis=0), axis=1, keepdims=True)
            p = jnp.exp2(y_scr[slot] - m).astype(BF)
            r = dot_nn(p, va[...])
            den = r[:, HD:]
            o = r[:, :HD] / den
            out[:, :share, cols] = o.astype(BF).reshape(8, share, HD)
            lse = m + jnp.log2(den)
            delta = jnp.sum(o * g[:, cols].astype(F32), axis=1, keepdims=True)
            st = jnp.where(lane == h, lse, st)
            st = jnp.where(lane == heads + h, delta, st)
        left = st.T[: 2 * heads, :]
        terms = []
        for _ in range(3):
            terms.append(left.astype(BF))
            left = left - terms[-1].astype(F32)
        note = jnp.concatenate(terms + [jnp.zeros((2 * heads, width - 3 * rows), BF)], axis=1)
        for i in range(8):
            out[i, share:, :] = note

    own = lambda i, ix, tl, se: (0, ix[1])
    return pl.pallas_call(
        body,
        out_shape=jax.ShapeDtypeStruct((8, share + 2 * heads, width), BF),
        grid_spec=pltpu.PrefetchScalarGridSpec(
            num_scalar_prefetch=3,
            grid=(1,),
            in_specs=[pl.BlockSpec((rows, width), own)] * 2 + [spec((span, 2 * HD))] * 4,
            out_specs=spec((8, share + 2 * heads, width)),
            scratch_shapes=[
                pltpu.VMEM((2, rows, total), F32),
                pltpu.VMEM((total, 2 * HD), BF),
            ],
        ),
        compiler_params=pltpu.CompilerParams(vmem_limit_bytes=40 << 20),
        name="fwd",
        cost_estimate=cost(7),
    )(idx, tiles, sees, queries, grad_out, *kvs)


def merge_weights(note, heads, rows):
    stats = []
    for i in range(8):
        x = note[i].astype(F32)
        stats.append(x[:, :rows] + x[:, rows : 2 * rows] + x[:, 2 * rows : 3 * rows])
    top = stats[0][:heads]
    for x in stats[1:]:
        top = jnp.maximum(top, x[:heads])
    ws = [jnp.exp2(x[:heads] - top) for x in stats]
    total = ws[0]
    delta = ws[0] * stats[0][heads:]
    for w, x in zip(ws[1:], stats[1:]):
        total = total + w
        delta = delta + w * x[heads:]
    inv = 1.0 / total
    return top + jnp.log2(total), delta * inv, [w * inv for w in ws]


def merge_parts(ix, x, ws, out, w_scr):
    _, share, width = x.shape
    heads = width // HD
    rows = w_scr.shape[0]
    pad = [jnp.zeros((HD - 8 * heads, rows), F32)]
    w_scr[...] = jnp.concatenate(ws + pad, axis=0).T
    w = w_scr[pl.ds(pl.multiple_of(ix[3] * share, share), share), :]
    for h in range(heads):
        cols = slice(h * HD, (h + 1) * HD)
        acc = jnp.zeros((share, HD), F32)
        for i in range(8):
            acc += x[i, :, cols].astype(F32) * w[:, i * heads + h : i * heads + h + 1]
        out[:, cols] = acc.astype(BF)


def backward(idx, tiles, sees, queries, grad_out, kv, notes, chunk, dtype, merging=False):
    rows = queries.shape[0]
    heads = 8
    width = heads * HD
    span = kv.shape[0]
    per = span // TILE

    def body(ix, tl, se, q, g, kv_ref, st, *refs):
        lse, delta, ws = merge_weights(st, heads, rows)
        if merging:
            x, out, merged, dk, dv, w_scr = refs
            merge_parts(ix, x, ws, merged, w_scr)
        else:
            out, dk, dv = refs
        lane = lax.broadcasted_iota(jnp.int32, (1, rows), 1)
        caps = [
            jnp.where(
                lane < TBLK,
                tile_cap(ix, tl, se, 0, chunk, e),
                tile_cap(ix, tl, se, 1, chunk, e),
            )
            for e in range(per)
        ]
        kk = kv_ref[:, :HD]
        vv = kv_ref[:, HD:]
        for h in range(heads):
            cols = slice(h * HD, (h + 1) * HD)
            qh = q[:, cols]
            gh = g[:, cols]
            s = dot_nt(kk, qh) * C2
            d = dot_nt(vv, gh)
            lh = lse[h : h + 1, :]
            dh = delta[h : h + 1, :]
            ps = []
            ds = []
            for e in range(per):
                at = slice(e * TILE, (e + 1) * TILE)
                p = jnp.exp2(jnp.minimum(s[at, :], caps[e]) - lh)
                ps.append(p.astype(BF))
                ds.append((p * (d[at, :] - dh) * SCALE).astype(BF))
            pv = dot_nn(jnp.concatenate(ps, axis=0), gh)
            pk = dot_nn(jnp.concatenate(ds, axis=0), qh)
            if h == 0:
                dv[...] = pv
                dk[...] = pk
            else:
                dv[...] += pv
                dk[...] += pk
        out[:, :HD] = dk[...].astype(out.dtype)
        out[:, HD:] = dv[...].astype(out.dtype)

    own = lambda i, ix, tl, se: (0, ix[1])
    out_shape = [jax.ShapeDtypeStruct((span, 2 * HD), dtype)]
    share = rows // 8
    in_specs = [pl.BlockSpec((rows, width), own)] * 2 + [
        spec((span, 2 * HD)),
        pl.BlockSpec((8, 2 * heads, width), lambda *_: (0, share // (2 * heads), 0)),
    ]
    out_specs = [spec((span, 2 * HD))]
    scratch = [pltpu.VMEM((span, HD), F32)] * 2
    more = []
    if merging:
        more = [notes]
        in_specs.append(spec((8, share, width)))
        out_shape.append(jax.ShapeDtypeStruct((share, width), BF))
        out_specs.append(spec((share, width)))
        scratch.append(pltpu.VMEM((rows, HD), F32))
    return pl.pallas_call(
        body,
        out_shape=out_shape,
        grid_spec=pltpu.PrefetchScalarGridSpec(
            num_scalar_prefetch=3,
            grid=(1,),
            in_specs=in_specs,
            out_specs=out_specs,
            scratch_shapes=scratch,
        ),
        compiler_params=pltpu.CompilerParams(vmem_limit_bytes=32 << 20),
        name=f"grads{chunk}",
        cost_estimate=cost(3),
    )(idx, tiles, sees, queries, grad_out, kv, notes, *more)


def feature_grad(idx, own, oc, oh, ohc, key_weight, value_weight, gathered):
    rows = own.shape[0]
    feat, cols = key_weight.shape
    steps = 5
    chunk = feat // steps
    chips, cores, share, half = gathered.shape

    def body(ix, a, b, c_, d_, wk, wv, all_ref, out, attn, both, sems):
        h = ix[0]
        c = ix[1]
        step = pl.program_id(0)

        def place(cc):
            return pltpu.make_async_copy(
                all_ref.at[:, cc], attn.at[:, :, cc * half : (cc + 1) * half], sems.at[cc]
            )

        @pl.when(step == 0)
        def _():
            for cc in range(cores):
                place(cc).start()

            def put(hh, cc, x):
                at = pl.multiple_of((hh * 2 + cc) * HD, HD)
                both[0, :, pl.ds(at, HD)] = x[:, :HD]
                both[1, :, pl.ds(at, HD)] = x[:, HD:]

            put(h, c, a)
            put(h, 1 - c, b)
            put(1 - h, c, c_)
            put(1 - h, 1 - c, d_)

        out[...] = (dot_nt(both[0], wk[...]) + dot_nt(both[1], wv[...])).astype(BF)

        @pl.when(step == steps - 1)
        def _():
            for cc in range(cores):
                place(cc).wait()

    piece = spec((rows, 2 * HD))
    whole = pl.BlockSpec(memory_space=pltpu.HBM)
    return pl.pallas_call(
        body,
        out_shape=(
            jax.ShapeDtypeStruct((rows, feat), BF),
            jax.ShapeDtypeStruct((chips, share, cores * half), BF),
        ),
        grid_spec=pltpu.PrefetchScalarGridSpec(
            num_scalar_prefetch=1,
            grid=(steps,),
            in_specs=[piece] * 4
            + [pl.BlockSpec((chunk, cols), lambda k, ix: (k, 0))] * 2
            + [whole],
            out_specs=[pl.BlockSpec((rows, chunk), lambda k, ix: (0, k)), whole],
            scratch_shapes=[pltpu.VMEM((2, rows, cols), BF), pltpu.SemaphoreType.DMA((2,))],
        ),
        compiler_params=pltpu.CompilerParams(vmem_limit_bytes=24 << 20),
        name="feats",
        cost_estimate=cost(4),
    )(idx, own, oc, oh, ohc, in_hbm(key_weight), in_hbm(value_weight), gathered)


def solution(mesh):
    sizes = tuple(mesh.shape[a] for a in AXES)
    to_c = moved(sizes, lambda i, h, t: (i ^ 1, h, t))
    to_h = moved(sizes, lambda i, h, t: (i, 1 - h, t))
    to_hc = moved(sizes, lambda i, h, t: (i ^ 1, 1 - h, t))
    to_t = {k: moved(sizes, lambda i, h, t, k=k: (i, h, t ^ k)) for k in (1, 2, 3)}
    chips = [[m * 2 + c for m in range(8)] for c in range(2)]

    def swap8(x):
        return lax.all_to_all(x, "img", 0, 0, axis_index_groups=chips, tiled=True)

    def gathered(own):
        return [own] + [to_t[k](own) for k in (1, 2, 3)]

    def shards(image_feats, key_weight, value_weight, queries, grad_out, tile_image, text_sees):
        img = lax.axis_index("img")
        core = img % 2
        idx = jnp.stack([lax.axis_index("head"), core, lax.axis_index("txt"), img // 2]).astype(jnp.int32)
        tiles = jnp.stack([tile_image, to_c(tile_image)])

        own, c, h, hc = project(idx, image_feats, key_weight, value_weight)
        h, hc, c = to_h(h), to_hc(hc), to_c(c)

        def wide(x):
            x = x.astype(F32)
            return x[:, :HD] + x[:, HD : 2 * HD], x[:, 2 * HD :]

        hk, hv = wide(h)
        ck, cv = wide(c)
        hck, hcv = wide(hc)
        near = jnp.concatenate([own[:, :HD] + hk, own[:, HD:] + hv], axis=1).astype(BF)
        far = jnp.concatenate([ck + hck, cv + hcv], axis=1).astype(BF)
        kvs = gathered(jnp.concatenate([near, far], axis=0))
        notes = swap8(forward(idx, tiles, text_sees, queries, grad_out, kvs))

        def grads(k, dtype, merging=False):
            return backward(idx, tiles, text_sees, queries, grad_out, kvs[k], notes, k, dtype, merging)

        far = []
        for k in (2, 1, 3):
            if k == 2:
                sent, merged = grads(k, BF, True)
                every = lax.all_gather(merged, "img").reshape(8, 2, *merged.shape)
            else:
                (sent,) = grads(k, BF)
            far.append(to_t[k](sent))
        (total,) = grads(0, F32)
        for x in far:
            total = total + x.astype(F32)
        total = total.astype(BF)
        rows = total.shape[0] // 2
        near, other = total[:rows], total[rows:]
        grad_feats, attn_out = feature_grad(
            idx, near, to_c(other), to_h(near), to_hc(other), key_weight, value_weight, every
        )
        return attn_out.reshape(queries.shape), grad_feats

    placed = (
        P(("img", "txt"), "head"),
        P("head", None),
        P("head", None),
        P("txt", "head"),
        P("txt", "head"),
        P("img"),
        P(),
    )
    return jax.shard_map(
        shards,
        mesh=mesh,
        in_specs=placed,
        out_specs=(P("txt", "head"), P(("img", "txt"), "head")),
        check_vma=False,
    )
```

time: 119 us -> 123 us (1.034)
  waiting for transfers between devices: 13.3 us -> 32.2 us
  starting transfers between devices: 38 us -> 21.5 us
  between operations: 0.83 us -> 14.2 us
  local copies, waits for them, and re-layouts: 7.94 us -> 2.93 us
  blocking collectives: 21.4 us -> 16.5 us
  other arithmetic: 4.01 us -> 0.46 us
    ppermute x20 -> x13, waiting for transfers between devices: 13.3 us -> 29.1 us  [moved(): return lambda x: lax.ppermute(x, AXES, pairs)]
    ppermute x20 -> x13, starting transfers between devices: 33.6 us -> 21.5 us  [moved(): return lambda x: lax.ppermute(x, AXES, pairs)]
    unnamed x24 -> x16, local copies, waits for them, and re-layouts: 7.92 us -> 2.91 us
    all_to_all x2 -> x1, blocking collectives: 21.4 us -> 16.5 us  [swap8(): return lax.all_to_all(x, 'img', 0, 0, axis_index_groups=chips, tiled=True)]
    all_to_all x1 -> x0, starting transfers between devices: 4.32 us -> none  [swap8(): return lax.all_to_all(x, 'img', 0, 0, axis_index_groups=chips, tiled=True)]
    all_gather x0 -> x1, waiting for transfers between devices: none -> 3.11 us  [shards(): every = lax.all_gather(merged, 'img').reshape(8, 2, *merged.shape)]
    select_n x1 -> x0, other arithmetic: 2.6 us -> none  [shards(): jnp.where(core == 0, jnp.concatenate([mine, theirs], axis=1), jnp.concate...]
    pallas_call x9 -> x7, Pallas kernels: 33.5 us -> 34.5 us  [the longest x4 12.5 us: backward(): pl.pallas_call(body, out_shape=out_shape, grid_spec=pltpu.PrefetchScalarG...]
  transfers between devices with their start and end apart: 21 -> 14, of which waited for: 8 -> 9; matrix products, arithmetic and copies ran while one was open for 1% -> 0% of each run, Pallas kernels for 17% -> 7%
where the time goes in v2:
time: 123 us; the launch traced here: 122 us
  Pallas kernels  34.5 us (28%)
  waiting for transfers between devices  32.2 us (26%)
  starting transfers between devices  21.5 us (17%)
  blocking collectives  16.5 us (13%)
  between operations  14.2 us (12%)
  local copies, waits for them, and re-layouts  2.93 us (2%)
    ppermute x13, waiting for transfers between devices, moved(): return lambda x: lax.ppermute(x, AXES, pairs)  29.1 us
    ppermute x13, starting transfers between devices, moved(): return lambda x: lax.ppermute(x, AXES, pairs)  21.5 us
    all_to_all x1, blocking collectives, swap8(): return lax.all_to_all(x, 'img', 0, 0, axis_index_groups=chips, tiled=True)  16.5 us
    pallas_call x4, Pallas kernels, backward(): pl.pallas_call(body, out_shape=out_shape, grid_spec=pltpu.PrefetchScalarG...  12.5 us
    pallas_call x1, Pallas kernels, feature_grad(): pl.pallas_call(body, out_shape=(jax.ShapeDtypeStruct((rows, feat), BF), j...  7.69 us
    pallas_call x1, Pallas kernels, project(): pl.pallas_call(body, out_shape=(jax.ShapeDtypeStruct((rows, 2 * HD), F32)...  7.21 us
    pallas_call x1, Pallas kernels, forward(): pl.pallas_call(body, out_shape=jax.ShapeDtypeStruct((8, share + 2 * heads...  7.16 us
    all_gather x1, waiting for transfers between devices, shards(): every = lax.all_gather(merged, 'img').reshape(8, 2, *merged.shape)  3.11 us
  transfers between devices with their start and end apart: 14, of which 9 were waited for; matrix products, arithmetic and copies ran while one was open for 0% of the time, Pallas kernels for 7%

profile of v2, /device:TPU:1, one launch (start us, length us, event | category | flops | bytes accessed | tf_op | source)
XLA Modules:
  0.0 122.4 jit_solution(3103327515472771933)
XLA Ops:
  7.2 0.0 all-gather.3.cloned.1.call-start
  7.2 0.1 pad_add_fusion.1.ix
  7.3 7.2 %project.1 = (f32[256,256]{1,0:T(8,128)S(1)}, bf16[256,384]{1,0:T(8,128)(2,1)S(1)}, bf16[256,384]{1,0:T(8,128)(2,1)S(1)}, bf16[256,384]{1,0:T(8,128)(2,1)S(1)}) custom-call(s32[4]{0:T(128)S(1)} %pad_add_fusion.1.ix, bf16[256,3840]{1,0:T(8,128)(2,1)} %x.1, bf16[3840,512]{1,0:T(8,128)(2,1)} %wk.3, bf16[3840,512]{1,0:T(8,128)(2,1)} %wv.3), custom_call_target="tpu_custom_call" | custom-call | flops 4400000000 | bytes 65536 | tf_op jit(solution)/shard_map/project/pallas_call | solution.py:95
  14.5 0.0 copy-start.7
  14.5 0.0 copy-start
  14.6 0.0 copy-start.1
  14.6 0.0 copy-start.6
  14.6 4.5 %collective-permute-start.1 = (bf16[256,384]{1,0:T(8,128)(2,1)S(1)}, bf16[256,384]{1,0:T(8,128)(2,1)S(1)}, u32[]{:S(2)}, u32[]{:S(2)}) collective-permute-start(bf16[256,384]{1,0:T(8,128)(2,1)S(1)} %get-tuple-element.11), channel_id=1, source_target_pairs={{0,4},{1,5},{2,6},{3,7},{4,0},{5,1},{6,2},{7,3},{8,12},{9,13},{10,... | collective-permute-start | bytes 589832 | tf_op jit(solution)/shard_map/ppermute | solution.py:39
  19.1 1.0 collective-permute-start.2
  20.0 0.0 collective-permute-start.3
  20.0 3.7 %collective-permute-done.1 = bf16[256,384]{1,0:T(8,128)(2,1)S(1)} collective-permute-done((bf16[256,384]{1,0:T(8,128)(2,1)S(1)}, bf16[256,384]{1,0:T(8,128)(2,1)S(1)}, u32[]{:S(2)}, u32[]{:S(2)}) %collective-permute-start.1) | collective-permute-done | bytes 196640 | tf_op jit(solution)/shard_map/ppermute | solution.py:39
  23.7 0.0 collective-permute-done.2
  23.8 0.1 fusion.5
  23.8 4.6 %collective-permute-done.3 = bf16[256,384]{1,0:T(8,128)(2,1)S(1)} collective-permute-done((bf16[256,384]{1,0:T(8,128)(2,1)S(1)}, bf16[256,384]{1,0:T(8,128)(2,1)S(1)}, u32[]{:S(2)}, u32[]{:S(2)}) %collective-permute-start.3) | collective-permute-done | bytes 196640 | tf_op jit(solution)/shard_map/ppermute | solution.py:39
  28.5 0.1 fusion.2
  28.6 2.8 %collective-permute-start.6 = (bf16[512,256]{1,0:T(8,128)(2,1)S(1)}, bf16[512,256]{1,0:T(8,128)(2,1)S(1)}, u32[]{:S(2)}, u32[]{:S(2)}) collective-permute-start(bf16[512,256]{1,0:T(8,128)(2,1)S(1)} %maximum_maximum_fusion.k0.kv_ref), channel_id=1, source_target_pairs={{0,3},{1,2},{2,1},{3,0},{4,7},{5,6},{6,5},{7,4},{8,11},{9,10},{10,... | collective-permute-start | bytes 786440 | tf_op jit(solution)/shard_map/ppermute | solution.py:39
  31.4 0.3 collective-permute-start.5
  31.8 0.3 collective-permute-start.4
  32.1 0.0 copy-done.7
  32.1 1.0 collective-permute-start
  33.1 0.8 collective-permute-done
  34.0 9.2 %collective-permute-done.6.k3.kv_ref = bf16[512,256]{1,0:T(8,128)(2,1)S(1)} collective-permute-done((bf16[512,256]{1,0:T(8,128)(2,1)S(1)}, bf16[512,256]{1,0:T(8,128)(2,1)S(1)}, u32[]{:S(2)}, u32[]{:S(2)}) %collective-permute-start.6) | collective-permute-done | bytes 262176 | tf_op jit(solution)/shard_map/ppermute | solution.py:39
  43.2 0.0 collective-permute-done.5.k2.kv_ref
  43.2 0.5 collective-permute-done.4.k1.kv_ref
  43.7 0.0 copy-done
  43.7 0.0 copy-done.1
  43.7 0.0 copy-done.6
  43.7 0.0 copy-start.3
  43.7 7.2 %fwd.1 = bf16[8,48,1024]{2,1,0:T(8,128)(2,1)S(1)} custom-call(s32[4]{0:T(128)S(1)} %pad_add_fusion.1.ix, s32[2,8]{1,0:T(2,128)S(1)} %pad_add_fusion.tl, s32[8,8]{1,0:T(8,128)S(1)} %copy-done.6, bf16[256,2048]{1,0:T(8,128)(2,1)S(1)} %copy-done, bf16[256,2048]{1,0:T(8,128)(2,1)S(1)} %copy-done.1, bf16[512,256]{1,0:T(8,128)(2,1)S(1)} %maximum_maximum_fusion.k0.kv_ref, ...), custom_call_target="tpu_custom_call" | custom-call | flops 7699999744 | bytes 65536 | tf_op jit(solution)/shard_map/fwd/pallas_call | solution.py:180
  50.9 0.0 copy-done.3
  50.9 16.5 %all_to_all.5.st.refs_0_ = bf16[8,48,1024]{2,1,0:T(8,128)(2,1)S(1)} all-to-all(bf16[8,48,1024]{2,1,0:T(8,128)(2,1)S(1)} %fwd.1), channel_id=1, replica_groups={{0,16,32,48,64,80,96,112},{8,24,40,56,72,88,104,120},{1,17,33,49,65,81,..., dimensions={0} | all-to-all | bytes 1572864 | tf_op jit(solution)/shard_map/all_to_all | solution.py:386
  67.4 3.4 %grads2.1 = (bf16[512,256]{1,0:T(8,128)(2,1)S(1)}, bf16[32,1024]{1,0:T(8,128)(2,1)}) custom-call(s32[4]{0:T(128)S(1)} %pad_add_fusion.1.ix, s32[2,8]{1,0:T(2,128)S(1)} %pad_add_fusion.tl, s32[8,8]{1,0:T(8,128)S(1)} %copy-done.6, bf16[256,2048]{1,0:T(8,128)(2,1)S(1)} %copy-done, bf16[256,2048]{1,0:T(8,128)(2,1)S(1)} %copy-done.1, ...), custom_call_target="tpu_custom_call" | custom-call | flops 3300000000 | bytes 65536 | tf_op jit(solution)/shard_map/grads2/pallas_call | solution.py:299
  70.8 0.0 copy-start.5
  70.8 0.7 copy-done.5
  71.5 0.0 all-gather.3.cloned.1.call-update
  71.5 2.7 %collective-permute-start.7 = (bf16[512,256]{1,0:T(8,128)(2,1)}, bf16[512,256]{1,0:T(8,128)(2,1)S(1)}, u32[]{:S(2)}, u32[]{:S(2)}) collective-permute-start(bf16[512,256]{1,0:T(8,128)(2,1)} %copy-done.5), channel_id=1, source_target_pairs={{0,2},{1,3},{2,0},{3,1},{4,6},{5,7},{6,4},{7,5},{8,10},{9,11},{10,... | collective-permute-start | bytes 786440 | tf_op jit(solution)/shard_map/ppermute | solution.py:39
  74.2 0.0 copy-start.4
  74.2 0.9 copy-done.4
  75.1 3.0 %grads1.1 = bf16[512,256]{1,0:T(8,128)(2,1)S(1)} custom-call(s32[4]{0:T(128)S(1)} %pad_add_fusion.1.ix, s32[2,8]{1,0:T(2,128)S(1)} %pad_add_fusion.tl, s32[8,8]{1,0:T(8,128)S(1)} %copy-done.6, bf16[256,2048]{1,0:T(8,128)(2,1)S(1)} %copy-done, bf16[256,2048]{1,0:T(8,128)(2,1)S(1)} %copy-done.1, bf16[512,256]{1,0:T(8,128)(2,1)S(1)} %copy-done.4, ...), custom_call_target="tpu_custom_call" | custom-call | flops 3300000000 | bytes 65536 | tf_op jit(solution)/shard_map/grads1/pallas_call | solution.py:299
  78.2 0.5 collective-permute-start.8
  78.7 3.0 %grads3.1 = bf16[512,256]{1,0:T(8,128)(2,1)S(1)} custom-call(s32[4]{0:T(128)S(1)} %pad_add_fusion.1.ix, s32[2,8]{1,0:T(2,128)S(1)} %pad_add_fusion.tl, s32[8,8]{1,0:T(8,128)S(1)} %copy-done.6, bf16[256,2048]{1,0:T(8,128)(2,1)S(1)} %copy-done, bf16[256,2048]{1,0:T(8,128)(2,1)S(1)} %copy-done.1, bf16[512,256]{1,0:T(8,128)(2,1)S(1)} %collective-permute-done.6.k3.kv_ref, ...), custom_call_target="tpu_custom_call" | custom-call | flops 3300000000 | bytes 65536 | tf_op jit(solution)/shard_map/grads3/pallas_call | solution.py:299
  81.7 0.5 collective-permute-start.9
  82.2 3.0 %grads0.1 = f32[512,256]{1,0:T(8,128)S(1)} custom-call(s32[4]{0:T(128)S(1)} %pad_add_fusion.1.ix, s32[2,8]{1,0:T(2,128)S(1)} %pad_add_fusion.tl, s32[8,8]{1,0:T(8,128)S(1)} %copy-done.6, bf16[256,2048]{1,0:T(8,128)(2,1)S(1)} %copy-done, bf16[256,2048]{1,0:T(8,128)(2,1)S(1)} %copy-done.1, bf16[512,256]{1,0:T(8,128)(2,1)S(1)} %maximum_maximum_fusion.k0.kv_ref, ...), custom_call_target="tpu_custom_call" | custom-call | flops 3300000000 | bytes 65536 | tf_op jit(solution)/shard_map/grads0/pallas_call | solution.py:299
  85.2 0.0 collective-permute-done.7
  85.2 0.0 collective-permute-done.8
  85.2 3.0 %collective-permute-done.9 = bf16[512,256]{1,0:T(8,128)(2,1)S(1)} collective-permute-done((bf16[512,256]{1,0:T(8,128)(2,1)S(1)}, bf16[512,256]{1,0:T(8,128)(2,1)S(1)}, u32[]{:S(2)}, u32[]{:S(2)}) %collective-permute-start.9) | collective-permute-done | bytes 262176 | tf_op jit(solution)/shard_map/ppermute | solution.py:39
  88.2 0.1 add_convert_fusion
  88.4 7.6 %collective-permute-start.12 = (bf16[256,256]{1,0:T(8,128)(2,1)S(1)}, bf16[256,256]{1,0:T(8,128)(2,1)S(1)}, u32[]{:S(2)}, u32[]{:S(2)}) collective-permute-start(bf16[256,256]{1,0:T(8,128)(2,1)S(1)} %get-tuple-element.22), channel_id=1, source_target_pairs={{0,12},{1,13},{2,14},{3,15},{4,8},{5,9},{6,10},{7,11},{8,4},{9,5},... | collective-permute-start | bytes 393224 | tf_op jit(solution)/shard_map/ppermute | solution.py:39
  96.0 0.0 collective-permute-start.10
  96.0 0.2 collective-permute-start.11
  96.2 3.8 %collective-permute-done.12.d_ = bf16[256,256]{1,0:T(8,128)(2,1)S(1)} collective-permute-done((bf16[256,256]{1,0:T(8,128)(2,1)S(1)}, bf16[256,256]{1,0:T(8,128)(2,1)S(1)}, u32[]{:S(2)}, u32[]{:S(2)}) %collective-permute-start.12) | collective-permute-done | bytes 131104 | tf_op jit(solution)/shard_map/ppermute | solution.py:39
  100.0 0.0 collective-permute-done.10.b
  100.0 3.5 %collective-permute-done.11.c_ = bf16[256,256]{1,0:T(8,128)(2,1)S(1)} collective-permute-done((bf16[256,256]{1,0:T(8,128)(2,1)S(1)}, bf16[256,256]{1,0:T(8,128)(2,1)S(1)}, u32[]{:S(2)}, u32[]{:S(2)}) %collective-permute-start.11) | collective-permute-done | bytes 131104 | tf_op jit(solution)/shard_map/ppermute | solution.py:39
  103.5 3.1 %all-gather.3.cloned.1.call-done = bf16[512,1024]{1,0:T(8,128)(2,1)} async-done(((bf16[32,1024]{1,0:T(8,128)(2,1)}), bf16[512,1024]{1,0:T(8,128)(2,1)}) %all-gather.3.cloned.1.call-update) | async-done | bytes 1048592 | tf_op jit(solution)/shard_map/all_gather | solution.py:419
  106.6 0.0 copy-start.2
  106.6 1.2 copy-done.2
  107.9 7.7 %feats.1 = (bf16[256,3840]{1,0:T(8,128)(2,1)}, bf16[8,32,2048]{2,1,0:T(8,128)(2,1)}) custom-call(s32[4]{0:T(128)S(1)} %pad_add_fusion.1.ix, bf16[256,256]{1,0:T(8,128)(2,1)S(1)} %get-tuple-element.23.a, bf16[256,256]{1,0:T(8,128)(2,1)S(1)} %collective-permute-done.10.b, bf16[256,256]{1,0:T(8,128)(2,1)S(1)} %collective-permute-done.11.c_, ...), custom_call_target="tpu_custom_call" | custom-call | flops 4400000000 | bytes 65536 | tf_op jit(solution)/shard_map/feats/pallas_call | solution.py:356
  (6 shorter events, 0.1 us)
Async XLA Ops:
  7.2 99.5 %all-gather.3.cloned.1.call-start = ((), (), s32[]{:S(2)}) async-start(), calls=%async_computation.1 | async-start | bytes 1114112 | tf_op jit(solution)/shard_map/all_gather | solution.py:419
  14.5 17.6 %copy-start.7 = (s32[8]{0:T(128)S(1)}, s32[8]{0:T(128)}, u32[]{:S(2)}) copy-start(s32[8]{0:T(128)} %param.12) | copy-start | bytes 100
  14.5 29.1 %copy-start = (bf16[256,2048]{1,0:T(8,128)(2,1)S(1)}, bf16[256,2048]{1,0:T(8,128)(2,1)}, u32[]{:S(2)}) copy-start(bf16[256,2048]{1,0:T(8,128)(2,1)} %q.9) | copy-start | bytes 3145732
  14.6 29.1 %copy-start.1 = (bf16[256,2048]{1,0:T(8,128)(2,1)S(1)}, bf16[256,2048]{1,0:T(8,128)(2,1)}, u32[]{:S(2)}) copy-start(bf16[256,2048]{1,0:T(8,128)(2,1)} %g.9) | copy-start | bytes 3145732
  14.6 29.1 %copy-start.6 = (s32[8,8]{1,0:T(8,128)S(1)}, s32[8,8]{1,0:T(8,128)}, u32[]{:S(2)}) copy-start(s32[8,8]{1,0:T(8,128)} %se.9) | copy-start | bytes 772
  14.6 9.1 %collective-permute-start.1 = (bf16[256,384]{1,0:T(8,128)(2,1)S(1)}, bf16[256,384]{1,0:T(8,128)(2,1)S(1)}, u32[]{:S(2)}, u32[]{:S(2)}) collective-permute-start(bf16[256,384]{1,0:T(8,128)(2,1)S(1)} %get-tuple-element.11), channel_id=1, source_target_pairs={{0,4},{1,5},{2,6},{3,7},{4,0},{5,1},{6,2},{7,3},{8,12},{9,13},{10,... | collective-permute-start | bytes 589832 | tf_op jit(solution)/shard_map/ppermute | solution.py:39
  19.1 4.7 %collective-permute-start.2 = (bf16[256,384]{1,0:T(8,128)(2,1)S(1)}, bf16[256,384]{1,0:T(8,128)(2,1)S(1)}, u32[]{:S(2)}, u32[]{:S(2)}) collective-permute-start(bf16[256,384]{1,0:T(8,128)(2,1)S(1)} %get-tuple-element.12), channel_id=1, source_target_pairs={{0,8},{1,9},{2,10},{3,11},{4,12},{5,13},{6,14},{7,15},{8,0},{9,1},... | collective-permute-start | bytes 589832 | tf_op jit(solution)/shard_map/ppermute | solution.py:39
  20.0 8.4 %collective-permute-start.3 = (bf16[256,384]{1,0:T(8,128)(2,1)S(1)}, bf16[256,384]{1,0:T(8,128)(2,1)S(1)}, u32[]{:S(2)}, u32[]{:S(2)}) collective-permute-start(bf16[256,384]{1,0:T(8,128)(2,1)S(1)} %get-tuple-element.13), channel_id=1, source_target_pairs={{0,12},{1,13},{2,14},{3,15},{4,8},{5,9},{6,10},{7,11},{8,4},{9,5},... | collective-permute-start | bytes 589832 | tf_op jit(solution)/shard_map/ppermute | solution.py:39
  28.6 14.6 %collective-permute-start.6 = (bf16[512,256]{1,0:T(8,128)(2,1)S(1)}, bf16[512,256]{1,0:T(8,128)(2,1)S(1)}, u32[]{:S(2)}, u32[]{:S(2)}) collective-permute-start(bf16[512,256]{1,0:T(8,128)(2,1)S(1)} %maximum_maximum_fusion.k0.kv_ref), channel_id=1, source_target_pairs={{0,3},{1,2},{2,1},{3,0},{4,7},{5,6},{6,5},{7,4},{8,11},{9,10},{10,... | collective-permute-start | bytes 786440 | tf_op jit(solution)/shard_map/ppermute | solution.py:39
  31.4 11.8 %collective-permute-start.5 = (bf16[512,256]{1,0:T(8,128)(2,1)S(1)}, bf16[512,256]{1,0:T(8,128)(2,1)S(1)}, u32[]{:S(2)}, u32[]{:S(2)}) collective-permute-start(bf16[512,256]{1,0:T(8,128)(2,1)S(1)} %maximum_maximum_fusion.k0.kv_ref), channel_id=1, source_target_pairs={{0,2},{1,3},{2,0},{3,1},{4,6},{5,7},{6,4},{7,5},{8,10},{9,11},{10,... | collective-permute-start | bytes 786440 | tf_op jit(solution)/shard_map/ppermute | solution.py:39
  31.8 11.9 %collective-permute-start.4 = (bf16[512,256]{1,0:T(8,128)(2,1)S(1)}, bf16[512,256]{1,0:T(8,128)(2,1)S(1)}, u32[]{:S(2)}, u32[]{:S(2)}) collective-permute-start(bf16[512,256]{1,0:T(8,128)(2,1)S(1)} %maximum_maximum_fusion.k0.kv_ref), channel_id=1, source_target_pairs={{0,1},{1,0},{2,3},{3,2},{4,5},{5,4},{6,7},{7,6},{8,9},{9,8},{10,11... | collective-permute-start | bytes 786440 | tf_op jit(solution)/shard_map/ppermute | solution.py:39
  32.1 1.9 %collective-permute-start = (s32[8]{0:T(128)S(1)}, s32[8]{0:T(128)S(1)}, u32[]{:S(2)}, u32[]{:S(2)}) collective-permute-start(s32[8]{0:T(128)S(1)} %copy-done.7), channel_id=1, source_target_pairs={{0,8},{1,9},{2,10},{3,11},{4,12},{5,13},{6,14},{7,15},{8,0},{9,1},... | collective-permute-start | bytes 104 | tf_op jit(solution)/shard_map/ppermute | solution.py:39
  43.7 7.2 %copy-start.3 = (bf16[512,256]{1,0:T(8,128)(2,1)}, bf16[512,256]{1,0:T(8,128)(2,1)S(1)}, u32[]{:S(2)}) copy-start(bf16[512,256]{1,0:T(8,128)(2,1)S(1)} %collective-permute-done.4.k1.kv_ref) | copy-start | bytes 786436
  70.8 0.7 copy-start.5
  71.5 13.7 %collective-permute-start.7 = (bf16[512,256]{1,0:T(8,128)(2,1)}, bf16[512,256]{1,0:T(8,128)(2,1)S(1)}, u32[]{:S(2)}, u32[]{:S(2)}) collective-permute-start(bf16[512,256]{1,0:T(8,128)(2,1)} %copy-done.5), channel_id=1, source_target_pairs={{0,2},{1,3},{2,0},{3,1},{4,6},{5,7},{6,4},{7,5},{8,10},{9,11},{10,... | collective-permute-start | bytes 786440 | tf_op jit(solution)/shard_map/ppermute | solution.py:39
  74.2 0.9 copy-start.4
  78.2 7.0 %collective-permute-start.8 = (bf16[512,256]{1,0:T(8,128)(2,1)S(1)}, bf16[512,256]{1,0:T(8,128)(2,1)S(1)}, u32[]{:S(2)}, u32[]{:S(2)}) collective-permute-start(bf16[512,256]{1,0:T(8,128)(2,1)S(1)} %grads1.1), channel_id=1, source_target_pairs={{0,1},{1,0},{2,3},{3,2},{4,5},{5,4},{6,7},{7,6},{8,9},{9,8},{10,11... | collective-permute-start | bytes 786440 | tf_op jit(solution)/shard_map/ppermute | solution.py:39
  81.7 6.5 %collective-permute-start.9 = (bf16[512,256]{1,0:T(8,128)(2,1)S(1)}, bf16[512,256]{1,0:T(8,128)(2,1)S(1)}, u32[]{:S(2)}, u32[]{:S(2)}) collective-permute-start(bf16[512,256]{1,0:T(8,128)(2,1)S(1)} %grads3.1), channel_id=1, source_target_pairs={{0,3},{1,2},{2,1},{3,0},{4,7},{5,6},{6,5},{7,4},{8,11},{9,10},{10,... | collective-permute-start | bytes 786440 | tf_op jit(solution)/shard_map/ppermute | solution.py:39
  88.4 11.6 %collective-permute-start.12 = (bf16[256,256]{1,0:T(8,128)(2,1)S(1)}, bf16[256,256]{1,0:T(8,128)(2,1)S(1)}, u32[]{:S(2)}, u32[]{:S(2)}) collective-permute-start(bf16[256,256]{1,0:T(8,128)(2,1)S(1)} %get-tuple-element.22), channel_id=1, source_target_pairs={{0,12},{1,13},{2,14},{3,15},{4,8},{5,9},{6,10},{7,11},{8,4},{9,5},... | collective-permute-start | bytes 393224 | tf_op jit(solution)/shard_map/ppermute | solution.py:39
  96.0 4.0 %collective-permute-start.10 = (bf16[256,256]{1,0:T(8,128)(2,1)S(1)}, bf16[256,256]{1,0:T(8,128)(2,1)S(1)}, u32[]{:S(2)}, u32[]{:S(2)}) collective-permute-start(bf16[256,256]{1,0:T(8,128)(2,1)S(1)} %get-tuple-element.22), channel_id=1, source_target_pairs={{0,8},{1,9},{2,10},{3,11},{4,12},{5,13},{6,14},{7,15},{8,0},{9,1},... | collective-permute-start | bytes 393224 | tf_op jit(solution)/shard_map/ppermute | solution.py:39
  96.0 7.5 %collective-permute-start.11 = (bf16[256,256]{1,0:T(8,128)(2,1)S(1)}, bf16[256,256]{1,0:T(8,128)(2,1)S(1)}, u32[]{:S(2)}, u32[]{:S(2)}) collective-permute-start(bf16[256,256]{1,0:T(8,128)(2,1)S(1)} %get-tuple-element.23.a), channel_id=1, source_target_pairs={{0,4},{1,5},{2,6},{3,7},{4,0},{5,1},{6,2},{7,3},{8,12},{9,13},{10,... | collective-permute-start | bytes 393224 | tf_op jit(solution)/shard_map/ppermute | solution.py:39
  106.6 1.2 %copy-start.2 = (bf16[512,1024]{1,0:T(8,128)(2,1)S(1)}, bf16[512,1024]{1,0:T(8,128)(2,1)}, u32[]{:S(2)}) copy-start(bf16[512,1024]{1,0:T(8,128)(2,1)} %all-gather.3.cloned.1.call-done) | copy-start | bytes 3145732
Sparse Core Ops, SparseCore 0:
  71.6 34.9 all-gather.2

commit v3 on v2

--- a/solution.py
+++ b/solution.py
@@ -58,38 +58,45 @@
     steps = 5
     chunk = feat // steps
 
-    def body(ix, x, wk, wv, own, oc, oh, ohc, acc):
-        k = pl.program_id(0)
-        key = dot_nn(x[...], wk[...])
-        value = dot_nn(x[...], wv[...])
-
-        @pl.when(k == 0)
-        def _():
-            acc[0] = key
-            acc[1] = value
-
-        @pl.when(k > 0)
-        def _():
-            acc[0] += key
-            acc[1] += value
-
-        @pl.when(k == steps - 1)
-        def _():
-            h = ix[0]
-            c = ix[1]
-
-            def piece(which, hh, cc):
-                at = pl.multiple_of((hh * 2 + cc) * HD, HD)
-                return acc[which, :, pl.ds(at, HD)]
-
-            own[:, :HD] = piece(0, h, c)
-            own[:, HD:] = piece(1, h, c)
-            for ref, hh, cc in ((oh, 1 - h, c), (ohc, 1 - h, 1 - c), (oc, h, 1 - c)):
-                kp = piece(0, hh, cc)
-                high = kp.astype(BF)
-                ref[:, :HD] = high
-                ref[:, HD : 2 * HD] = (kp - high.astype(F32)).astype(BF)
-                ref[:, 2 * HD :] = piece(1, hh, cc).astype(BF)
+    def body(ix, x_hbm, wk_hbm, wv_hbm, own, oc, oh, ohc, x, wk, wv, acc, sems):
+        copies = []
+        for s in range(steps):
+            at = slice(s * chunk, (s + 1) * chunk)
+            copies.append(
+                (
+                    pltpu.make_async_copy(x_hbm.at[:, at], x.at[s], sems.at[0, s]),
+                    pltpu.make_async_copy(wk_hbm.at[at, :], wk.at[s], sems.at[1, s]),
+                    pltpu.make_async_copy(wv_hbm.at[at, :], wv.at[s], sems.at[2, s]),
+                )
+            )
+            for copy in copies[s]:
+                copy.start()
+        for s in range(steps):
+            for copy in copies[s]:
+                copy.wait()
+            key = dot_nn(x[s], wk[s])
+            value = dot_nn(x[s], wv[s])
+            if s == 0:
+                acc[0] = key
+                acc[1] = value
+            else:
+                acc[0] += key
+                acc[1] += value
+        h = ix[0]
+        c = ix[1]
+
+        def piece(which, hh, cc):
+            at = pl.multiple_of((hh * 2 + cc) * HD, HD)
+            return acc[which, :, pl.ds(at, HD)]
+
+        own[:, :HD] = piece(0, h, c)
+        own[:, HD:] = piece(1, h, c)
+        for ref, hh, cc in ((oh, 1 - h, c), (ohc, 1 - h, 1 - c), (oc, h, 1 - c)):
+            kp = piece(0, hh, cc)
+            high = kp.astype(BF)
+            ref[:, :HD] = high
+            ref[:, HD : 2 * HD] = (kp - high.astype(F32)).astype(BF)
+            ref[:, 2 * HD :] = piece(1, hh, cc).astype(BF)
 
     sent = jax.ShapeDtypeStruct((rows, 3 * HD), BF)
     return pl.pallas_call(
@@ -97,14 +104,16 @@
         out_shape=(jax.ShapeDtypeStruct((rows, 2 * HD), F32), sent, sent, sent),
         grid_spec=pltpu.PrefetchScalarGridSpec(
             num_scalar_prefetch=1,
-            grid=(steps,),
-            in_specs=[
-                pl.BlockSpec((rows, chunk), lambda k, ix: (0, k)),
-                pl.BlockSpec((chunk, cols), lambda k, ix: (k, 0)),
-                pl.BlockSpec((chunk, cols), lambda k, ix: (k, 0)),
+            grid=(1,),
+            in_specs=[pl.BlockSpec(memory_space=pltpu.HBM)] * 3,
+            out_specs=[spec((rows, 2 * HD))] + [spec((rows, 3 * HD))] * 3,
+            scratch_shapes=[
+                pltpu.VMEM((steps, rows, chunk), BF),
+                pltpu.VMEM((steps, chunk, cols), BF),
+                pltpu.VMEM((steps, chunk, cols), BF),
+                pltpu.VMEM((2, rows, cols), F32),
+                pltpu.SemaphoreType.DMA((3, steps)),
             ],
-            out_specs=[spec((rows, 2 * HD))] + [spec((rows, 3 * HD))] * 3,
-            scratch_shapes=[pltpu.VMEM((2, rows, cols), F32)],
         ),
         compiler_params=pltpu.CompilerParams(vmem_limit_bytes=24 << 20),
         name="project",
@@ -130,7 +139,7 @@
     share = rows // 8
     per = span // TILE
 
-    def body(ix, tl, se, q, g, k0, k1, k2, k3, out, y_scr, va):
+    def body(ix, tl, se, q, g, k0, k1, k2, k3, out, st_out, y_scr, va):
         ks = (k0, k1, k2, k3)
         for j in range(n):
             va[j * span : (j + 1) * span, :HD] = ks[j][:, HD:]
@@ -162,29 +171,27 @@
             r = dot_nn(p, va[...])
             den = r[:, HD:]
             o = r[:, :HD] / den
-            out[:, :share, cols] = o.astype(BF).reshape(8, share, HD)
+            out[:, :, cols] = o.astype(BF).reshape(8, share, HD)
             lse = m + jnp.log2(den)
             delta = jnp.sum(o * g[:, cols].astype(F32), axis=1, keepdims=True)
             st = jnp.where(lane == h, lse, st)
             st = jnp.where(lane == heads + h, delta, st)
-        left = st.T[: 2 * heads, :]
-        terms = []
-        for _ in range(3):
-            terms.append(left.astype(BF))
-            left = left - terms[-1].astype(F32)
-        note = jnp.concatenate(terms + [jnp.zeros((2 * heads, width - 3 * rows), BF)], axis=1)
+        flat = st.T[: 2 * heads, :]
         for i in range(8):
-            out[i, share:, :] = note
+            st_out[i] = flat
 
     own = lambda i, ix, tl, se: (0, ix[1])
     return pl.pallas_call(
         body,
-        out_shape=jax.ShapeDtypeStruct((8, share + 2 * heads, width), BF),
+        out_shape=(
+            jax.ShapeDtypeStruct((8, share, width), BF),
+            jax.ShapeDtypeStruct((8, 2 * heads, rows), F32),
+        ),
         grid_spec=pltpu.PrefetchScalarGridSpec(
             num_scalar_prefetch=3,
             grid=(1,),
             in_specs=[pl.BlockSpec((rows, width), own)] * 2 + [spec((span, 2 * HD))] * 4,
-            out_specs=spec((8, share + 2 * heads, width)),
+            out_specs=[spec((8, share, width)), spec((8, 2 * heads, rows))],
             scratch_shapes=[
                 pltpu.VMEM((2, rows, total), F32),
                 pltpu.VMEM((total, 2 * HD), BF),
@@ -196,11 +203,8 @@
     )(idx, tiles, sees, queries, grad_out, *kvs)
 
 
-def merge_weights(note, heads, rows):
-    stats = []
-    for i in range(8):
-        x = note[i].astype(F32)
-        stats.append(x[:, :rows] + x[:, rows : 2 * rows] + x[:, 2 * rows : 3 * rows])
+def merge_weights(st, heads):
+    stats = [st[i] for i in range(8)]
     top = stats[0][:heads]
     for x in stats[1:]:
         top = jnp.maximum(top, x[:heads])
@@ -226,10 +230,12 @@
         acc = jnp.zeros((share, HD), F32)
         for i in range(8):
             acc += x[i, :, cols].astype(F32) * w[:, i * heads + h : i * heads + h + 1]
-        out[:, cols] = acc.astype(BF)
-
-
-def backward(idx, tiles, sees, queries, grad_out, kv, notes, chunk, dtype, merging=False):
+        v = acc.astype(BF)
+        for i in range(8):
+            out[i, :, cols] = v
+
+
+def backward(idx, tiles, sees, queries, grad_out, kv, stats, chunk, dtype, parts=None):
     rows = queries.shape[0]
     heads = 8
     width = heads * HD
@@ -237,12 +243,12 @@
     per = span // TILE
 
     def body(ix, tl, se, q, g, kv_ref, st, *refs):
-        lse, delta, ws = merge_weights(st, heads, rows)
-        if merging:
+        lse, delta, ws = merge_weights(st, heads)
+        if parts is None:
+            out, dk, dv = refs
+        else:
             x, out, merged, dk, dv, w_scr = refs
             merge_parts(ix, x, ws, merged, w_scr)
-        else:
-            out, dk, dv = refs
         lane = lax.broadcasted_iota(jnp.int32, (1, rows), 1)
         caps = [
             jnp.where(
@@ -282,19 +288,15 @@
 
     own = lambda i, ix, tl, se: (0, ix[1])
     out_shape = [jax.ShapeDtypeStruct((span, 2 * HD), dtype)]
-    share = rows // 8
-    in_specs = [pl.BlockSpec((rows, width), own)] * 2 + [
-        spec((span, 2 * HD)),
-        pl.BlockSpec((8, 2 * heads, width), lambda *_: (0, share // (2 * heads), 0)),
-    ]
+    in_specs = [pl.BlockSpec((rows, width), own)] * 2 + [spec((span, 2 * HD)), spec(stats.shape)]
     out_specs = [spec((span, 2 * HD))]
     scratch = [pltpu.VMEM((span, HD), F32)] * 2
     more = []
-    if merging:
-        more = [notes]
-        in_specs.append(spec((8, share, width)))
-        out_shape.append(jax.ShapeDtypeStruct((share, width), BF))
-        out_specs.append(spec((share, width)))
+    if parts is not None:
+        more = [parts]
+        in_specs.append(spec(parts.shape))
+        out_shape.append(jax.ShapeDtypeStruct(parts.shape, BF))
+        out_specs.append(spec(parts.shape))
         scratch.append(pltpu.VMEM((rows, HD), F32))
     return pl.pallas_call(
         body,
@@ -309,69 +311,86 @@
         compiler_params=pltpu.CompilerParams(vmem_limit_bytes=32 << 20),
         name=f"grads{chunk}",
         cost_estimate=cost(3),
-    )(idx, tiles, sees, queries, grad_out, kv, notes, *more)
-
-
-def feature_grad(idx, own, oc, oh, ohc, key_weight, value_weight, gathered):
+    )(idx, tiles, sees, queries, grad_out, kv, stats, *more)
+
+
+def feature_grad(idx, own, oc, oh, ohc, key_weight, value_weight, mine, theirs):
     rows = own.shape[0]
     feat, cols = key_weight.shape
     steps = 5
     chunk = feat // steps
-    chips, cores, share, half = gathered.shape
-
-    def body(ix, a, b, c_, d_, wk, wv, all_ref, out, attn, both, sems):
+    half = mine.shape[1]
+
+    def body(ix, a, b, c_, d_, wk_hbm, wv_hbm, m_ref, t_ref, out_hbm, attn, wk, wv, both, out, sems):
         h = ix[0]
         c = ix[1]
-        step = pl.program_id(0)
-
-        def place(cc):
-            return pltpu.make_async_copy(
-                all_ref.at[:, cc], attn.at[:, :, cc * half : (cc + 1) * half], sems.at[cc]
+
+        def load(s):
+            at = slice(s * chunk, (s + 1) * chunk)
+            return (
+                pltpu.make_async_copy(wk_hbm.at[at, :], wk.at[s], sems.at[0, s]),
+                pltpu.make_async_copy(wv_hbm.at[at, :], wv.at[s], sems.at[1, s]),
             )
 
-        @pl.when(step == 0)
-        def _():
-            for cc in range(cores):
-                place(cc).start()
-
-            def put(hh, cc, x):
-                at = pl.multiple_of((hh * 2 + cc) * HD, HD)
-                both[0, :, pl.ds(at, HD)] = x[:, :HD]
-                both[1, :, pl.ds(at, HD)] = x[:, HD:]
-
-            put(h, c, a)
-            put(h, 1 - c, b)
-            put(1 - h, c, c_)
-            put(1 - h, 1 - c, d_)
-
-        out[...] = (dot_nt(both[0], wk[...]) + dot_nt(both[1], wv[...])).astype(BF)
-
-        @pl.when(step == steps - 1)
-        def _():
-            for cc in range(cores):
-                place(cc).wait()
+        def place(src, cc, s):
+            at = pl.multiple_of(cc * half, half)
+            return pltpu.make_async_copy(src, attn.at[:, pl.ds(at, half)], sems.at[3, s])
+
+        def store(s):
+            at = slice(s * chunk, (s + 1) * chunk)
+            return pltpu.make_async_copy(out.at[s], out_hbm.at[:, at], sems.at[2, s])
+
+        for s in range(steps):
+            for copy in load(s):
+                copy.start()
+        place(m_ref, c, 0).start()
+        place(t_ref, 1 - c, 1).start()
+
+        def put(hh, cc, x):
+            at = pl.multiple_of((hh * 2 + cc) * HD, HD)
+            both[0, :, pl.ds(at, HD)] = x[:, :HD]
+            both[1, :, pl.ds(at, HD)] = x[:, HD:]
+
+        put(h, c, a)
+        put(h, 1 - c, b)
+        put(1 - h, c, c_)
+        put(1 - h, 1 - c, d_)
+        for s in range(steps):
+            for copy in load(s):
+                copy.wait()
+            out[s] = (dot_nt(both[0], wk[s]) + dot_nt(both[1], wv[s])).astype(BF)
+            store(s).start()
+        for s in range(steps):
+            store(s).wait()
+        place(m_ref, c, 0).wait()
+        place(t_ref, 1 - c, 1).wait()
 
     piece = spec((rows, 2 * HD))
-    whole = pl.BlockSpec(memory_space=pltpu.HBM)
+    hbm = pl.BlockSpec(memory_space=pltpu.HBM)
+    anywhere = pl.BlockSpec(memory_space=pl.ANY)
     return pl.pallas_call(
         body,
         out_shape=(
             jax.ShapeDtypeStruct((rows, feat), BF),
-            jax.ShapeDtypeStruct((chips, share, cores * half), BF),
+            jax.ShapeDtypeStruct((rows, 2 * half), BF),
         ),
         grid_spec=pltpu.PrefetchScalarGridSpec(
             num_scalar_prefetch=1,
-            grid=(steps,),
-            in_specs=[piece] * 4
-            + [pl.BlockSpec((chunk, cols), lambda k, ix: (k, 0))] * 2
-            + [whole],
-            out_specs=[pl.BlockSpec((rows, chunk), lambda k, ix: (0, k)), whole],
-            scratch_shapes=[pltpu.VMEM((2, rows, cols), BF), pltpu.SemaphoreType.DMA((2,))],
+            grid=(1,),
+            in_specs=[piece] * 4 + [hbm] * 2 + [anywhere] * 2,
+            out_specs=[hbm, hbm],
+            scratch_shapes=[
+                pltpu.VMEM((steps, chunk, cols), BF),
+                pltpu.VMEM((steps, chunk, cols), BF),
+                pltpu.VMEM((2, rows, cols), BF),
+                pltpu.VMEM((steps, rows, chunk), BF),
+                pltpu.SemaphoreType.DMA((4, steps)),
+            ],
         ),
         compiler_params=pltpu.CompilerParams(vmem_limit_bytes=24 << 20),
         name="feats",
         cost_estimate=cost(4),
-    )(idx, own, oc, oh, ohc, in_hbm(key_weight), in_hbm(value_weight), gathered)
+    )(idx, own, oc, oh, ohc, in_hbm(key_weight), in_hbm(value_weight), mine, theirs)
 
 
 def solution(mesh):
@@ -407,29 +426,28 @@
         near = jnp.concatenate([own[:, :HD] + hk, own[:, HD:] + hv], axis=1).astype(BF)
         far = jnp.concatenate([ck + hck, cv + hcv], axis=1).astype(BF)
         kvs = gathered(jnp.concatenate([near, far], axis=0))
-        notes = swap8(forward(idx, tiles, text_sees, queries, grad_out, kvs))
-
-        def grads(k, dtype, merging=False):
-            return backward(idx, tiles, text_sees, queries, grad_out, kvs[k], notes, k, dtype, merging)
+        parts, stats = forward(idx, tiles, text_sees, queries, grad_out, kvs)
+        stats = swap8(stats)
+        parts = swap8(parts)
+
+        def grads(k, dtype, *more):
+            return backward(idx, tiles, text_sees, queries, grad_out, kvs[k], stats, k, dtype, *more)
 
         far = []
         for k in (2, 1, 3):
-            if k == 2:
-                sent, merged = grads(k, BF, True)
-                every = lax.all_gather(merged, "img").reshape(8, 2, *merged.shape)
-            else:
-                (sent,) = grads(k, BF)
+            (sent,) = grads(k, BF)
             far.append(to_t[k](sent))
-        (total,) = grads(0, F32)
+        total, merged = grads(0, F32, parts)
+        mine = swap8(merged).reshape(queries.shape[0], -1)
         for x in far:
             total = total + x.astype(F32)
         total = total.astype(BF)
         rows = total.shape[0] // 2
         near, other = total[:rows], total[rows:]
         grad_feats, attn_out = feature_grad(
-            idx, near, to_c(other), to_h(near), to_hc(other), key_weight, value_weight, every
+            idx, near, to_c(other), to_h(near), to_hc(other), key_weight, value_weight, mine, to_c(mine)
         )
-        return attn_out.reshape(queries.shape), grad_feats
+        return attn_out, grad_feats
 
     placed = (
         P(("img", "txt"), "head"),

time: 123 us -> 110 us (0.89)
  between operations: 14.2 us -> 0.97 us
  starting transfers between devices: 21.5 us -> 34 us
  blocking collectives: 16.5 us -> 10.3 us
  waiting for transfers between devices: 32.2 us -> 27.3 us
  local copies, waits for them, and re-layouts: 2.93 us -> 1 us
    all_to_all x0 -> x2, starting transfers between devices: none -> 8.58 us  [swap8(): return lax.all_to_all(x, 'img', 0, 0, axis_index_groups=chips, tiled=True)]
    all_to_all x1, blocking collectives: 16.5 us -> 10.3 us  [swap8(): return lax.all_to_all(x, 'img', 0, 0, axis_index_groups=chips, tiled=True)]
    ppermute x13 -> x14, waiting for transfers between devices: 29.1 us -> 24.7 us  [moved(): return lambda x: lax.ppermute(x, AXES, pairs)]
    ppermute x13 -> x14, starting transfers between devices: 21.5 us -> 25.4 us  [moved(): return lambda x: lax.ppermute(x, AXES, pairs)]
    all_gather x1 -> x0, waiting for transfers between devices: 3.11 us -> none  [shards(): every = lax.all_gather(merged, 'img').reshape(8, 2, *merged.shape)]
    all_to_all x0 -> x2, waiting for transfers between devices: none -> 2.58 us  [swap8(): return lax.all_to_all(x, 'img', 0, 0, axis_index_groups=chips, tiled=True)]
    pallas_call x4, Pallas kernels: 12.5 us -> 14.8 us  [backward(): pl.pallas_call(body, out_shape=out_shape, grid_spec=pltpu.PrefetchScalarG...]
    pallas_call x1, Pallas kernels: 7.21 us -> 5.22 us  [project(): pl.pallas_call(body, out_shape=(jax.ShapeDtypeStruct((rows, 2 * HD), F32)...]
  transfers between devices with their start and end apart: 14 -> 16, of which waited for: 9 -> 8; matrix products, arithmetic and copies ran while one was open for 0% -> 1% of each run, Pallas kernels for 7% -> 14%
where the time goes in v3:
time: 110 us
  Pallas kernels  34.6 us (31%)
  starting transfers between devices  34 us (31%)
  waiting for transfers between devices  27.3 us (25%)
  blocking collectives  10.3 us (9%)
  other arithmetic  1.44 us (1%)
    ppermute x14, starting transfers between devices, moved(): return lambda x: lax.ppermute(x, AXES, pairs)  25.4 us
    ppermute x14, waiting for transfers between devices, moved(): return lambda x: lax.ppermute(x, AXES, pairs)  24.7 us
    pallas_call x4, Pallas kernels, backward(): pl.pallas_call(body, out_shape=out_shape, grid_spec=pltpu.PrefetchScalarG...  14.8 us
    all_to_all x1, blocking collectives, swap8(): return lax.all_to_all(x, 'img', 0, 0, axis_index_groups=chips, tiled=True)  10.3 us
    all_to_all x2, starting transfers between devices, swap8(): return lax.all_to_all(x, 'img', 0, 0, axis_index_groups=chips, tiled=True)  8.58 us
    pallas_call x1, Pallas kernels, forward(): pl.pallas_call(body, out_shape=(jax.ShapeDtypeStruct((8, share, width), B...  7.76 us
    pallas_call x1, Pallas kernels, feature_grad(): pl.pallas_call(body, out_shape=(jax.ShapeDtypeStruct((rows, feat), BF), j...  6.8 us
    pallas_call x1, Pallas kernels, project(): pl.pallas_call(body, out_shape=(jax.ShapeDtypeStruct((rows, 2 * HD), F32)...  5.22 us
  transfers between devices with their start and end apart: 16, of which 8 were waited for; matrix products, arithmetic and copies ran while one was open for 1% of the time, Pallas kernels for 14%

profile of v3, /device:TPU:1, one launch (start us, length us, event | category | flops | bytes accessed | tf_op | source)
XLA Modules:
  0.0 109.5 jit_solution(66750336470008809)
XLA Ops:
  0.6 0.1 pad_add_fusion.1.ix
  0.7 5.2 %project.1 = (f32[256,256]{1,0:T(8,128)S(1)}, bf16[256,384]{1,0:T(8,128)(2,1)S(1)}, bf16[256,384]{1,0:T(8,128)(2,1)S(1)}, bf16[256,384]{1,0:T(8,128)(2,1)S(1)}) custom-call(s32[4]{0:T(128)S(1)} %pad_add_fusion.1.ix, bf16[256,3840]{1,0:T(8,128)(2,1)} %x_hbm.1, bf16[3840,512]{1,0:T(8,128)(2,1)} %wk_hbm.3, bf16[3840,512]{1,0:T(8,128)(2,1)} %wv_hbm.3), custom_call_target="tpu_custom_call" | custom-call | flops 4400000000 | bytes 65536 | tf_op jit(solution)/shard_map/project/pallas_call | solution.py:102
  6.0 0.0 copy-start.5
  6.0 0.0 copy-start
  6.0 0.0 copy-start.1
  6.0 0.0 copy-start.4
  6.0 4.5 %collective-permute-start.1 = (bf16[256,384]{1,0:T(8,128)(2,1)S(1)}, bf16[256,384]{1,0:T(8,128)(2,1)S(1)}, u32[]{:S(2)}, u32[]{:S(2)}) collective-permute-start(bf16[256,384]{1,0:T(8,128)(2,1)S(1)} %get-tuple-element.13), channel_id=1, source_target_pairs={{0,4},{1,5},{2,6},{3,7},{4,0},{5,1},{6,2},{7,3},{8,12},{9,13},{10,... | collective-permute-start | bytes 589832 | tf_op jit(solution)/shard_map/ppermute | solution.py:39
  10.5 1.0 collective-permute-start.2
  11.5 0.0 collective-permute-start.3
  11.5 3.7 %collective-permute-done.1 = bf16[256,384]{1,0:T(8,128)(2,1)S(1)} collective-permute-done((bf16[256,384]{1,0:T(8,128)(2,1)S(1)}, bf16[256,384]{1,0:T(8,128)(2,1)S(1)}, u32[]{:S(2)}, u32[]{:S(2)}) %collective-permute-start.1) | collective-permute-done | bytes 196640 | tf_op jit(solution)/shard_map/ppermute | solution.py:39
  15.2 0.0 collective-permute-done.2
  15.3 4.6 %collective-permute-done.3 = bf16[256,384]{1,0:T(8,128)(2,1)S(1)} collective-permute-done((bf16[256,384]{1,0:T(8,128)(2,1)S(1)}, bf16[256,384]{1,0:T(8,128)(2,1)S(1)}, u32[]{:S(2)}, u32[]{:S(2)}) %collective-permute-start.3) | collective-permute-done | bytes 196640 | tf_op jit(solution)/shard_map/ppermute | solution.py:39
  20.0 2.8 %collective-permute-start.6 = (bf16[512,256]{1,0:T(8,128)(2,1)S(1)}, bf16[512,256]{1,0:T(8,128)(2,1)S(1)}, u32[]{:S(2)}, u32[]{:S(2)}) collective-permute-start(bf16[512,256]{1,0:T(8,128)(2,1)S(1)} %maximum_maximum_fusion.k0.kv_ref), channel_id=1, source_target_pairs={{0,3},{1,2},{2,1},{3,0},{4,7},{5,6},{6,5},{7,4},{8,11},{9,10},{10,... | collective-permute-start | bytes 786440 | tf_op jit(solution)/shard_map/ppermute | solution.py:39
  22.8 0.3 collective-permute-start.5
  23.2 0.3 collective-permute-start.4
  23.5 0.0 copy-done.5
  23.5 1.0 collective-permute-start
  24.5 0.8 collective-permute-done
  25.4 9.2 %collective-permute-done.6.k3.kv_ref = bf16[512,256]{1,0:T(8,128)(2,1)S(1)} collective-permute-done((bf16[512,256]{1,0:T(8,128)(2,1)S(1)}, bf16[512,256]{1,0:T(8,128)(2,1)S(1)}, u32[]{:S(2)}, u32[]{:S(2)}) %collective-permute-start.6) | collective-permute-done | bytes 262176 | tf_op jit(solution)/shard_map/ppermute | solution.py:39
  34.6 0.0 copy-start.2
  34.6 0.0 collective-permute-done.5.k2.kv_ref
  34.6 0.5 collective-permute-done.4.k1.kv_ref
  35.1 0.0 copy-done
  35.1 0.0 copy-done.1
  35.1 0.0 copy-done.4
  35.1 7.8 %fwd.1 = (bf16[8,32,1024]{2,1,0:T(8,128)(2,1)}, f32[8,16,256]{2,1,0:T(8,128)S(1)}) custom-call(s32[4]{0:T(128)S(1)} %pad_add_fusion.1.ix, s32[2,8]{1,0:T(2,128)S(1)} %pad_add_fusion.tl, s32[8,8]{1,0:T(8,128)S(1)} %copy-done.4, bf16[256,2048]{1,0:T(8,128)(2,1)S(1)} %copy-done, bf16[256,2048]{1,0:T(8,128)(2,1)S(1)} %copy-done.1, ...), custom_call_target="tpu_custom_call" | custom-call | flops 7699999744 | bytes 65536 | tf_op jit(solution)/shard_map/fwd/pallas_call | solution.py:184
  42.8 0.0 copy-done.2
  42.9 10.3 %all_to_all.15.st = f32[8,16,256]{2,1,0:T(8,128)S(1)} all-to-all(f32[8,16,256]{2,1,0:T(8,128)S(1)} %get-tuple-element.16), channel_id=1, replica_groups={{0,16,32,48,64,80,96,112},{8,24,40,56,72,88,104,120},{1,17,33,49,65,81,..., dimensions={0} | all-to-all | bytes 262144 | tf_op jit(solution)/shard_map/all_to_all | solution.py:405
  53.1 3.7 %all-to-all-start.1 = ((bf16[8,32,1024]{2,1,0:T(8,128)(2,1)}), bf16[8,32,1024]{2,1,0:T(8,128)(2,1)S(1)}, u32[]{:S(2)}, u32[]{:S(2)}) async-start(bf16[8,32,1024]{2,1,0:T(8,128)(2,1)} %get-tuple-element.17), calls=%async_computation.1 | async-start | bytes 1048576 | tf_op jit(solution)/shard_map/all_to_all | solution.py:405
  56.8 3.8 %grads2.1 = bf16[512,256]{1,0:T(8,128)(2,1)} custom-call(s32[4]{0:T(128)S(1)} %pad_add_fusion.1.ix, s32[2,8]{1,0:T(2,128)S(1)} %pad_add_fusion.tl, s32[8,8]{1,0:T(8,128)S(1)} %copy-done.4, bf16[256,2048]{1,0:T(8,128)(2,1)S(1)} %copy-done, bf16[256,2048]{1,0:T(8,128)(2,1)S(1)} %copy-done.1, bf16[512,256]{1,0:T(8,128)(2,1)S(1)} %collective-permute-done.5.k2.kv_ref, ...), custom_call_target="tpu_custom_call" | custom-call | flops 3300000000 | bytes 65536 | tf_op jit(solution)/shard_map/grads2/pallas_call | solution.py:301
  60.6 2.6 %collective-permute-start.7 = (bf16[512,256]{1,0:T(8,128)(2,1)}, bf16[512,256]{1,0:T(8,128)(2,1)}, u32[]{:S(2)}, u32[]{:S(2)}) collective-permute-start(bf16[512,256]{1,0:T(8,128)(2,1)} %grads2.1), channel_id=1, source_target_pairs={{0,2},{1,3},{2,0},{3,1},{4,6},{5,7},{6,4},{7,5},{8,10},{9,11},{10,... | collective-permute-start | bytes 786440 | tf_op jit(solution)/shard_map/ppermute | solution.py:39
  63.2 3.8 %grads1.1 = bf16[512,256]{1,0:T(8,128)(2,1)} custom-call(s32[4]{0:T(128)S(1)} %pad_add_fusion.1.ix, s32[2,8]{1,0:T(2,128)S(1)} %pad_add_fusion.tl, s32[8,8]{1,0:T(8,128)S(1)} %copy-done.4, bf16[256,2048]{1,0:T(8,128)(2,1)S(1)} %copy-done, bf16[256,2048]{1,0:T(8,128)(2,1)S(1)} %copy-done.1, bf16[512,256]{1,0:T(8,128)(2,1)S(1)} %collective-permute-done.4.k1.kv_ref, ...), custom_call_target="tpu_custom_call" | custom-call | flops 3300000000 | bytes 65536 | tf_op jit(solution)/shard_map/grads1/pallas_call | solution.py:301
  66.9 0.4 collective-permute-start.8
  67.3 0.0 all-to-all-done.1.refs_0_
  67.3 3.6 %grads0.1 = (f32[512,256]{1,0:T(8,128)S(1)}, bf16[8,32,1024]{2,1,0:T(8,128)(2,1)}) custom-call(s32[4]{0:T(128)S(1)} %pad_add_fusion.1.ix, s32[2,8]{1,0:T(2,128)S(1)} %pad_add_fusion.tl, s32[8,8]{1,0:T(8,128)S(1)} %copy-done.4, bf16[256,2048]{1,0:T(8,128)(2,1)S(1)} %copy-done, bf16[256,2048]{1,0:T(8,128)(2,1)S(1)} %copy-done.1, ...), custom_call_target="tpu_custom_call" | custom-call | flops 3300000000 | bytes 65536 | tf_op jit(solution)/shard_map/grads0/pallas_call | solution.py:301
  70.9 4.9 %all-to-all-start.2 = ((bf16[8,32,1024]{2,1,0:T(8,128)(2,1)}), bf16[8,32,1024]{2,1,0:T(8,128)(2,1)S(1)}, u32[]{:S(2)}, u32[]{:S(2)}) async-start(bf16[8,32,1024]{2,1,0:T(8,128)(2,1)} %get-tuple-element.19), calls=%async_computation.2 | async-start | bytes 1048576 | tf_op jit(solution)/shard_map/all_to_all | solution.py:405
  75.8 0.0 copy-start.3
  75.8 0.9 copy-done.3
  76.8 3.7 %grads3.1 = bf16[512,256]{1,0:T(8,128)(2,1)} custom-call(s32[4]{0:T(128)S(1)} %pad_add_fusion.1.ix, s32[2,8]{1,0:T(2,128)S(1)} %pad_add_fusion.tl, s32[8,8]{1,0:T(8,128)S(1)} %copy-done.4, bf16[256,2048]{1,0:T(8,128)(2,1)S(1)} %copy-done, bf16[256,2048]{1,0:T(8,128)(2,1)S(1)} %copy-done.1, bf16[512,256]{1,0:T(8,128)(2,1)S(1)} %copy-done.3, ...), custom_call_target="tpu_custom_call" | custom-call | flops 3300000000 | bytes 65536 | tf_op jit(solution)/shard_map/grads3/pallas_call | solution.py:301
  80.5 0.4 collective-permute-start.9
  80.9 2.6 %all-to-all-done.2 = bf16[8,32,1024]{2,1,0:T(8,128)(2,1)S(1)} async-done(((bf16[8,32,1024]{2,1,0:T(8,128)(2,1)}), bf16[8,32,1024]{2,1,0:T(8,128)(2,1)S(1)}, u32[]{:S(2)}, u32[]{:S(2)}) %all-to-all-start.2) | async-done | bytes 524320 | tf_op jit(solution)/shard_map/all_to_all | solution.py:405
  83.5 4.8 %collective-permute-start.13 = (bf16[256,1024]{1,0:T(8,128)(2,1)S(1)}, bf16[256,1024]{1,0:T(8,128)(2,1)S(1)}, u32[]{:S(2)}, u32[]{:S(2)}) collective-permute-start(bf16[256,1024]{1,0:T(8,128)(2,1)S(1)} %bitcast.7), channel_id=1, source_target_pairs={{0,8},{1,9},{2,10},{3,11},{4,12},{5,13},{6,14},{7,15},{8,0},{9,1},... | collective-permute-start | bytes 1572872 | tf_op jit(solution)/shard_map/ppermute | solution.py:39
  88.2 0.0 collective-permute-done.7
  88.2 0.0 collective-permute-done.8
  88.2 0.0 collective-permute-done.9
  88.2 1.2 %add_convert_fusion = bf16[512,256]{1,0:T(8,128)(2,1)S(1)} fusion(bf16[512,256]{1,0:T(8,128)(2,1)S(1)} %collective-permute-done.9, bf16[512,256]{1,0:T(8,128)(2,1)} %collective-permute-done.8, f32[512,256]{1,0:T(8,128)S(1)} %get-tuple-element.18, bf16[512,256]{1,0:T(8,128)(2,1)} %collective-permute-done.7), kind=kLoop, calls=%fused_computation | loop fusion | flops 917504 | bytes 1572864 | tf_op jit(solution)/shard_map/convert_element_type | solution.py:444
  89.4 7.0 %collective-permute-start.12 = (bf16[256,256]{1,0:T(8,128)(2,1)S(1)}, bf16[256,256]{1,0:T(8,128)(2,1)S(1)}, u32[]{:S(2)}, u32[]{:S(2)}) collective-permute-start(bf16[256,256]{1,0:T(8,128)(2,1)S(1)} %get-tuple-element.26), channel_id=1, source_target_pairs={{0,12},{1,13},{2,14},{3,15},{4,8},{5,9},{6,10},{7,11},{8,4},{9,5},... | collective-permute-start | bytes 393224 | tf_op jit(solution)/shard_map/ppermute | solution.py:39
  96.5 0.0 collective-permute-start.10
  96.5 0.2 collective-permute-start.11
  96.7 3.2 %collective-permute-done.12.d_ = bf16[256,256]{1,0:T(8,128)(2,1)S(1)} collective-permute-done((bf16[256,256]{1,0:T(8,128)(2,1)S(1)}, bf16[256,256]{1,0:T(8,128)(2,1)S(1)}, u32[]{:S(2)}, u32[]{:S(2)}) %collective-permute-start.12) | collective-permute-done | bytes 131104 | tf_op jit(solution)/shard_map/ppermute | solution.py:39
  99.9 0.0 collective-permute-done.10.b
  99.9 2.6 %collective-permute-done.11.c_ = bf16[256,256]{1,0:T(8,128)(2,1)S(1)} collective-permute-done((bf16[256,256]{1,0:T(8,128)(2,1)S(1)}, bf16[256,256]{1,0:T(8,128)(2,1)S(1)}, u32[]{:S(2)}, u32[]{:S(2)}) %collective-permute-start.11) | collective-permute-done | bytes 131104 | tf_op jit(solution)/shard_map/ppermute | solution.py:39
  102.5 0.0 collective-permute-done.13.t_ref
  102.5 6.8 %feats.1 = (bf16[256,3840]{1,0:T(8,128)(2,1)}, bf16[256,2048]{1,0:T(8,128)(2,1)}) custom-call(s32[4]{0:T(128)S(1)} %pad_add_fusion.1.ix, bf16[256,256]{1,0:T(8,128)(2,1)S(1)} %get-tuple-element.27.a, bf16[256,256]{1,0:T(8,128)(2,1)S(1)} %collective-permute-done.10.b, bf16[256,256]{1,0:T(8,128)(2,1)S(1)} %collective-permute-done.11.c_, ...), custom_call_target="tpu_custom_call" | custom-call | flops 4400000000 | bytes 65536 | tf_op jit(solution)/shard_map/feats/pallas_call | solution.py:371
  (8 shorter events, 0.2 us)
Async XLA Ops:
  6.0 17.5 %copy-start.5 = (s32[8]{0:T(128)S(1)}, s32[8]{0:T(128)}, u32[]{:S(2)}) copy-start(s32[8]{0:T(128)} %param.12) | copy-start | bytes 100
  6.0 29.1 %copy-start = (bf16[256,2048]{1,0:T(8,128)(2,1)S(1)}, bf16[256,2048]{1,0:T(8,128)(2,1)}, u32[]{:S(2)}) copy-start(bf16[256,2048]{1,0:T(8,128)(2,1)} %q.9) | copy-start | bytes 3145732
  6.0 29.1 %copy-start.1 = (bf16[256,2048]{1,0:T(8,128)(2,1)S(1)}, bf16[256,2048]{1,0:T(8,128)(2,1)}, u32[]{:S(2)}) copy-start(bf16[256,2048]{1,0:T(8,128)(2,1)} %g.9) | copy-start | bytes 3145732
  6.0 29.1 %copy-start.4 = (s32[8,8]{1,0:T(8,128)S(1)}, s32[8,8]{1,0:T(8,128)}, u32[]{:S(2)}) copy-start(s32[8,8]{1,0:T(8,128)} %se.9) | copy-start | bytes 772
  6.0 9.1 %collective-permute-start.1 = (bf16[256,384]{1,0:T(8,128)(2,1)S(1)}, bf16[256,384]{1,0:T(8,128)(2,1)S(1)}, u32[]{:S(2)}, u32[]{:S(2)}) collective-permute-start(bf16[256,384]{1,0:T(8,128)(2,1)S(1)} %get-tuple-element.13), channel_id=1, source_target_pairs={{0,4},{1,5},{2,6},{3,7},{4,0},{5,1},{6,2},{7,3},{8,12},{9,13},{10,... | collective-permute-start | bytes 589832 | tf_op jit(solution)/shard_map/ppermute | solution.py:39
  10.5 4.7 %collective-permute-start.2 = (bf16[256,384]{1,0:T(8,128)(2,1)S(1)}, bf16[256,384]{1,0:T(8,128)(2,1)S(1)}, u32[]{:S(2)}, u32[]{:S(2)}) collective-permute-start(bf16[256,384]{1,0:T(8,128)(2,1)S(1)} %get-tuple-element.14), channel_id=1, source_target_pairs={{0,8},{1,9},{2,10},{3,11},{4,12},{5,13},{6,14},{7,15},{8,0},{9,1},... | collective-permute-start | bytes 589832 | tf_op jit(solution)/shard_map/ppermute | solution.py:39
  11.5 8.4 %collective-permute-start.3 = (bf16[256,384]{1,0:T(8,128)(2,1)S(1)}, bf16[256,384]{1,0:T(8,128)(2,1)S(1)}, u32[]{:S(2)}, u32[]{:S(2)}) collective-permute-start(bf16[256,384]{1,0:T(8,128)(2,1)S(1)} %get-tuple-element.15), channel_id=1, source_target_pairs={{0,12},{1,13},{2,14},{3,15},{4,8},{5,9},{6,10},{7,11},{8,4},{9,5},... | collective-permute-start | bytes 589832 | tf_op jit(solution)/shard_map/ppermute | solution.py:39
  20.0 14.6 %collective-permute-start.6 = (bf16[512,256]{1,0:T(8,128)(2,1)S(1)}, bf16[512,256]{1,0:T(8,128)(2,1)S(1)}, u32[]{:S(2)}, u32[]{:S(2)}) collective-permute-start(bf16[512,256]{1,0:T(8,128)(2,1)S(1)} %maximum_maximum_fusion.k0.kv_ref), channel_id=1, source_target_pairs={{0,3},{1,2},{2,1},{3,0},{4,7},{5,6},{6,5},{7,4},{8,11},{9,10},{10,... | collective-permute-start | bytes 786440 | tf_op jit(solution)/shard_map/ppermute | solution.py:39
  22.8 11.8 %collective-permute-start.5 = (bf16[512,256]{1,0:T(8,128)(2,1)S(1)}, bf16[512,256]{1,0:T(8,128)(2,1)S(1)}, u32[]{:S(2)}, u32[]{:S(2)}) collective-permute-start(bf16[512,256]{1,0:T(8,128)(2,1)S(1)} %maximum_maximum_fusion.k0.kv_ref), channel_id=1, source_target_pairs={{0,2},{1,3},{2,0},{3,1},{4,6},{5,7},{6,4},{7,5},{8,10},{9,11},{10,... | collective-permute-start | bytes 786440 | tf_op jit(solution)/shard_map/ppermute | solution.py:39
  23.2 11.9 %collective-permute-start.4 = (bf16[512,256]{1,0:T(8,128)(2,1)S(1)}, bf16[512,256]{1,0:T(8,128)(2,1)S(1)}, u32[]{:S(2)}, u32[]{:S(2)}) collective-permute-start(bf16[512,256]{1,0:T(8,128)(2,1)S(1)} %maximum_maximum_fusion.k0.kv_ref), channel_id=1, source_target_pairs={{0,1},{1,0},{2,3},{3,2},{4,5},{5,4},{6,7},{7,6},{8,9},{9,8},{10,11... | collective-permute-start | bytes 786440 | tf_op jit(solution)/shard_map/ppermute | solution.py:39
  23.5 1.9 %collective-permute-start = (s32[8]{0:T(128)S(1)}, s32[8]{0:T(128)S(1)}, u32[]{:S(2)}, u32[]{:S(2)}) collective-permute-start(s32[8]{0:T(128)S(1)} %copy-done.5), channel_id=1, source_target_pairs={{0,8},{1,9},{2,10},{3,11},{4,12},{5,13},{6,14},{7,15},{8,0},{9,1},... | collective-permute-start | bytes 104 | tf_op jit(solution)/shard_map/ppermute | solution.py:39
  34.6 8.3 %copy-start.2 = (bf16[512,256]{1,0:T(8,128)(2,1)}, bf16[512,256]{1,0:T(8,128)(2,1)S(1)}, u32[]{:S(2)}) copy-start(bf16[512,256]{1,0:T(8,128)(2,1)S(1)} %collective-permute-done.6.k3.kv_ref) | copy-start | bytes 786436
  53.1 14.2 %all-to-all-start.1 = ((bf16[8,32,1024]{2,1,0:T(8,128)(2,1)}), bf16[8,32,1024]{2,1,0:T(8,128)(2,1)S(1)}, u32[]{:S(2)}, u32[]{:S(2)}) async-start(bf16[8,32,1024]{2,1,0:T(8,128)(2,1)} %get-tuple-element.17), calls=%async_computation.1 | async-start | bytes 1048576 | tf_op jit(solution)/shard_map/all_to_all | solution.py:405
  60.6 27.7 %collective-permute-start.7 = (bf16[512,256]{1,0:T(8,128)(2,1)}, bf16[512,256]{1,0:T(8,128)(2,1)}, u32[]{:S(2)}, u32[]{:S(2)}) collective-permute-start(bf16[512,256]{1,0:T(8,128)(2,1)} %grads2.1), channel_id=1, source_target_pairs={{0,2},{1,3},{2,0},{3,1},{4,6},{5,7},{6,4},{7,5},{8,10},{9,11},{10,... | collective-permute-start | bytes 786440 | tf_op jit(solution)/shard_map/ppermute | solution.py:39
  66.9 21.3 %collective-permute-start.8 = (bf16[512,256]{1,0:T(8,128)(2,1)}, bf16[512,256]{1,0:T(8,128)(2,1)}, u32[]{:S(2)}, u32[]{:S(2)}) collective-permute-start(bf16[512,256]{1,0:T(8,128)(2,1)} %grads1.1), channel_id=1, source_target_pairs={{0,1},{1,0},{2,3},{3,2},{4,5},{5,4},{6,7},{7,6},{8,9},{9,8},{10,11... | collective-permute-start | bytes 786440 | tf_op jit(solution)/shard_map/ppermute | solution.py:39
  70.9 12.6 %all-to-all-start.2 = ((bf16[8,32,1024]{2,1,0:T(8,128)(2,1)}), bf16[8,32,1024]{2,1,0:T(8,128)(2,1)S(1)}, u32[]{:S(2)}, u32[]{:S(2)}) async-start(bf16[8,32,1024]{2,1,0:T(8,128)(2,1)} %get-tuple-element.19), calls=%async_computation.2 | async-start | bytes 1048576 | tf_op jit(solution)/shard_map/all_to_all | solution.py:405
  75.8 0.9 copy-start.3
  80.5 7.7 %collective-permute-start.9 = (bf16[512,256]{1,0:T(8,128)(2,1)}, bf16[512,256]{1,0:T(8,128)(2,1)S(1)}, u32[]{:S(2)}, u32[]{:S(2)}) collective-permute-start(bf16[512,256]{1,0:T(8,128)(2,1)} %grads3.1), channel_id=1, source_target_pairs={{0,3},{1,2},{2,1},{3,0},{4,7},{5,6},{6,5},{7,4},{8,11},{9,10},{10,... | collective-permute-start | bytes 786440 | tf_op jit(solution)/shard_map/ppermute | solution.py:39
  83.5 19.1 %collective-permute-start.13 = (bf16[256,1024]{1,0:T(8,128)(2,1)S(1)}, bf16[256,1024]{1,0:T(8,128)(2,1)S(1)}, u32[]{:S(2)}, u32[]{:S(2)}) collective-permute-start(bf16[256,1024]{1,0:T(8,128)(2,1)S(1)} %bitcast.7), channel_id=1, source_target_pairs={{0,8},{1,9},{2,10},{3,11},{4,12},{5,13},{6,14},{7,15},{8,0},{9,1},... | collective-permute-start | bytes 1572872 | tf_op jit(solution)/shard_map/ppermute | solution.py:39
  89.4 10.5 %collective-permute-start.12 = (bf16[256,256]{1,0:T(8,128)(2,1)S(1)}, bf16[256,256]{1,0:T(8,128)(2,1)S(1)}, u32[]{:S(2)}, u32[]{:S(2)}) collective-permute-start(bf16[256,256]{1,0:T(8,128)(2,1)S(1)} %get-tuple-element.26), channel_id=1, source_target_pairs={{0,12},{1,13},{2,14},{3,15},{4,8},{5,9},{6,10},{7,11},{8,4},{9,5},... | collective-permute-start | bytes 393224 | tf_op jit(solution)/shard_map/ppermute | solution.py:39
  96.5 3.4 %collective-permute-start.10 = (bf16[256,256]{1,0:T(8,128)(2,1)S(1)}, bf16[256,256]{1,0:T(8,128)(2,1)S(1)}, u32[]{:S(2)}, u32[]{:S(2)}) collective-permute-start(bf16[256,256]{1,0:T(8,128)(2,1)S(1)} %get-tuple-element.26), channel_id=1, source_target_pairs={{0,8},{1,9},{2,10},{3,11},{4,12},{5,13},{6,14},{7,15},{8,0},{9,1},... | collective-permute-start | bytes 393224 | tf_op jit(solution)/shard_map/ppermute | solution.py:39
  96.5 6.1 %collective-permute-start.11 = (bf16[256,256]{1,0:T(8,128)(2,1)S(1)}, bf16[256,256]{1,0:T(8,128)(2,1)S(1)}, u32[]{:S(2)}, u32[]{:S(2)}) collective-permute-start(bf16[256,256]{1,0:T(8,128)(2,1)S(1)} %get-tuple-element.27.a), channel_id=1, source_target_pairs={{0,4},{1,5},{2,6},{3,7},{4,0},{5,1},{6,2},{7,3},{8,12},{9,13},{10,... | collective-permute-start | bytes 393224 | tf_op jit(solution)/shard_map/ppermute | solution.py:39

commit v4 on v3

--- a/solution.py
+++ b/solution.py
@@ -197,7 +197,7 @@
                 pltpu.VMEM((total, 2 * HD), BF),
             ],
         ),
-        compiler_params=pltpu.CompilerParams(vmem_limit_bytes=40 << 20),
+        compiler_params=pltpu.CompilerParams(vmem_limit_bytes=24 << 20),
         name="fwd",
         cost_estimate=cost(7),
     )(idx, tiles, sees, queries, grad_out, *kvs)
@@ -235,65 +235,69 @@
             out[i, :, cols] = v
 
 
-def backward(idx, tiles, sees, queries, grad_out, kv, stats, chunk, dtype, parts=None):
+def backward(idx, tiles, sees, queries, grad_out, kvs, stats, chunks, parts=None):
     rows = queries.shape[0]
     heads = 8
     width = heads * HD
-    span = kv.shape[0]
+    span = kvs[0].shape[0]
     per = span // TILE
-
-    def body(ix, tl, se, q, g, kv_ref, st, *refs):
+    n = len(chunks)
+
+    def body(ix, tl, se, q, g, st, *refs):
+        kv_refs, refs = refs[:n], refs[n:]
         lse, delta, ws = merge_weights(st, heads)
         if parts is None:
-            out, dk, dv = refs
+            outs, (dk, dv) = refs[:n], refs[n:]
         else:
-            x, out, merged, dk, dv, w_scr = refs
+            x, outs, (merged, dk, dv, w_scr) = refs[0], refs[1 : n + 1], refs[n + 1 :]
+        lane = lax.broadcasted_iota(jnp.int32, (1, rows), 1)
+        for chunk, kv_ref, out in zip(chunks, kv_refs, outs):
+            caps = [
+                jnp.where(
+                    lane < TBLK,
+                    tile_cap(ix, tl, se, 0, chunk, e),
+                    tile_cap(ix, tl, se, 1, chunk, e),
+                )
+                for e in range(per)
+            ]
+            kk = kv_ref[:, :HD]
+            vv = kv_ref[:, HD:]
+            for h in range(heads):
+                cols = slice(h * HD, (h + 1) * HD)
+                qh = q[:, cols]
+                gh = g[:, cols]
+                s = dot_nt(kk, qh) * C2
+                d = dot_nt(vv, gh)
+                lh = lse[h : h + 1, :]
+                dh = delta[h : h + 1, :]
+                ps = []
+                ds = []
+                for e in range(per):
+                    at = slice(e * TILE, (e + 1) * TILE)
+                    p = jnp.exp2(jnp.minimum(s[at, :], caps[e]) - lh)
+                    ps.append(p.astype(BF))
+                    ds.append((p * (d[at, :] - dh) * SCALE).astype(BF))
+                pv = dot_nn(jnp.concatenate(ps, axis=0), gh)
+                pk = dot_nn(jnp.concatenate(ds, axis=0), qh)
+                if h == 0:
+                    dv[...] = pv
+                    dk[...] = pk
+                else:
+                    dv[...] += pv
+                    dk[...] += pk
+            out[:, :HD] = dk[...].astype(out.dtype)
+            out[:, HD:] = dv[...].astype(out.dtype)
+        if parts is not None:
             merge_parts(ix, x, ws, merged, w_scr)
-        lane = lax.broadcasted_iota(jnp.int32, (1, rows), 1)
-        caps = [
-            jnp.where(
-                lane < TBLK,
-                tile_cap(ix, tl, se, 0, chunk, e),
-                tile_cap(ix, tl, se, 1, chunk, e),
-            )
-            for e in range(per)
-        ]
-        kk = kv_ref[:, :HD]
-        vv = kv_ref[:, HD:]
-        for h in range(heads):
-            cols = slice(h * HD, (h + 1) * HD)
-            qh = q[:, cols]
-            gh = g[:, cols]
-            s = dot_nt(kk, qh) * C2
-            d = dot_nt(vv, gh)
-            lh = lse[h : h + 1, :]
-            dh = delta[h : h + 1, :]
-            ps = []
-            ds = []
-            for e in range(per):
-                at = slice(e * TILE, (e + 1) * TILE)
-                p = jnp.exp2(jnp.minimum(s[at, :], caps[e]) - lh)
-                ps.append(p.astype(BF))
-                ds.append((p * (d[at, :] - dh) * SCALE).astype(BF))
-            pv = dot_nn(jnp.concatenate(ps, axis=0), gh)
-            pk = dot_nn(jnp.concatenate(ds, axis=0), qh)
-            if h == 0:
-                dv[...] = pv
-                dk[...] = pk
-            else:
-                dv[...] += pv
-                dk[...] += pk
-        out[:, :HD] = dk[...].astype(out.dtype)
-        out[:, HD:] = dv[...].astype(out.dtype)
 
     own = lambda i, ix, tl, se: (0, ix[1])
-    out_shape = [jax.ShapeDtypeStruct((span, 2 * HD), dtype)]
-    in_specs = [pl.BlockSpec((rows, width), own)] * 2 + [spec((span, 2 * HD)), spec(stats.shape)]
-    out_specs = [spec((span, 2 * HD))]
+    out_shape = [jax.ShapeDtypeStruct((span, 2 * HD), BF if k else F32) for k in chunks]
+    in_specs = [pl.BlockSpec((rows, width), own)] * 2 + [spec(stats.shape)] + [spec((span, 2 * HD))] * n
+    out_specs = [spec((span, 2 * HD))] * n
     scratch = [pltpu.VMEM((span, HD), F32)] * 2
     more = []
     if parts is not None:
-        more = [parts]
+        more.append(parts)
         in_specs.append(spec(parts.shape))
         out_shape.append(jax.ShapeDtypeStruct(parts.shape, BF))
         out_specs.append(spec(parts.shape))
@@ -308,10 +312,43 @@
             out_specs=out_specs,
             scratch_shapes=scratch,
         ),
-        compiler_params=pltpu.CompilerParams(vmem_limit_bytes=32 << 20),
-        name=f"grads{chunk}",
-        cost_estimate=cost(3),
-    )(idx, tiles, sees, queries, grad_out, kv, stats, *more)
+        compiler_params=pltpu.CompilerParams(vmem_limit_bytes=20 << 20),
+        name="grads" + "".join(map(str, chunks)),
+        cost_estimate=cost(3 * n),
+    )(idx, tiles, sees, queries, grad_out, stats, *[kvs[k] for k in chunks], *more)
+
+
+def fetch_weights(key_weight, value_weight, token):
+    rows = key_weight.shape[0]
+    steps = 4
+    chunk = rows // steps
+
+    def body(k_hbm, v_hbm, _, k_out, v_out, sems):
+        copies = []
+        for s in range(steps):
+            at = slice(s * chunk, (s + 1) * chunk)
+            copies.append(pltpu.make_async_copy(k_hbm.at[at, :], k_out.at[at, :], sems.at[0, s]))
+            copies.append(pltpu.make_async_copy(v_hbm.at[at, :], v_out.at[at, :], sems.at[1, s]))
+        for copy in copies:
+            copy.start()
+        for copy in copies:
+            copy.wait()
+
+    hbm = pl.BlockSpec(memory_space=pltpu.HBM)
+    vmem = pl.BlockSpec(memory_space=pltpu.VMEM)
+    return pl.pallas_call(
+        body,
+        out_shape=(
+            pltpu.VMEM(key_weight.shape, BF),
+            pltpu.VMEM(value_weight.shape, BF),
+        ),
+        in_specs=[hbm, hbm, pl.BlockSpec(memory_space=pl.ANY)],
+        out_specs=[vmem, vmem],
+        scratch_shapes=[pltpu.SemaphoreType.DMA((2, steps))],
+        compiler_params=pltpu.CompilerParams(vmem_limit_bytes=2 << 20),
+        name="fetch",
+        cost_estimate=cost(4),
+    )(in_hbm(key_weight), in_hbm(value_weight), token)
 
 
 def feature_grad(idx, own, oc, oh, ohc, key_weight, value_weight, mine, theirs):
@@ -321,28 +358,18 @@
     chunk = feat // steps
     half = mine.shape[1]
 
-    def body(ix, a, b, c_, d_, wk_hbm, wv_hbm, m_ref, t_ref, out_hbm, attn, wk, wv, both, out, sems):
+    def body(ix, a, b, c_, d_, wk, wv, m_ref, t_ref, out_hbm, attn, both, out, sems):
         h = ix[0]
         c = ix[1]
 
-        def load(s):
-            at = slice(s * chunk, (s + 1) * chunk)
-            return (
-                pltpu.make_async_copy(wk_hbm.at[at, :], wk.at[s], sems.at[0, s]),
-                pltpu.make_async_copy(wv_hbm.at[at, :], wv.at[s], sems.at[1, s]),
-            )
-
         def place(src, cc, s):
             at = pl.multiple_of(cc * half, half)
-            return pltpu.make_async_copy(src, attn.at[:, pl.ds(at, half)], sems.at[3, s])
+            return pltpu.make_async_copy(src, attn.at[:, pl.ds(at, half)], sems.at[1, s])
 
         def store(s):
             at = slice(s * chunk, (s + 1) * chunk)
-            return pltpu.make_async_copy(out.at[s], out_hbm.at[:, at], sems.at[2, s])
-
-        for s in range(steps):
-            for copy in load(s):
-                copy.start()
+            return pltpu.make_async_copy(out.at[s], out_hbm.at[:, at], sems.at[0, s])
+
         place(m_ref, c, 0).start()
         place(t_ref, 1 - c, 1).start()
 
@@ -356,9 +383,8 @@
         put(1 - h, c, c_)
         put(1 - h, 1 - c, d_)
         for s in range(steps):
-            for copy in load(s):
-                copy.wait()
-            out[s] = (dot_nt(both[0], wk[s]) + dot_nt(both[1], wv[s])).astype(BF)
+            at = slice(s * chunk, (s + 1) * chunk)
+            out[s] = (dot_nt(both[0], wk[at, :]) + dot_nt(both[1], wv[at, :])).astype(BF)
             store(s).start()
         for s in range(steps):
             store(s).wait()
@@ -367,6 +393,7 @@
 
     piece = spec((rows, 2 * HD))
     hbm = pl.BlockSpec(memory_space=pltpu.HBM)
+    vmem = pl.BlockSpec(memory_space=pltpu.VMEM)
     anywhere = pl.BlockSpec(memory_space=pl.ANY)
     return pl.pallas_call(
         body,
@@ -377,20 +404,18 @@
         grid_spec=pltpu.PrefetchScalarGridSpec(
             num_scalar_prefetch=1,
             grid=(1,),
-            in_specs=[piece] * 4 + [hbm] * 2 + [anywhere] * 2,
+            in_specs=[piece] * 4 + [vmem] * 2 + [anywhere] * 2,
             out_specs=[hbm, hbm],
             scratch_shapes=[
-                pltpu.VMEM((steps, chunk, cols), BF),
-                pltpu.VMEM((steps, chunk, cols), BF),
                 pltpu.VMEM((2, rows, cols), BF),
                 pltpu.VMEM((steps, rows, chunk), BF),
-                pltpu.SemaphoreType.DMA((4, steps)),
+                pltpu.SemaphoreType.DMA((2, steps)),
             ],
         ),
-        compiler_params=pltpu.CompilerParams(vmem_limit_bytes=24 << 20),
+        compiler_params=pltpu.CompilerParams(vmem_limit_bytes=8 << 20),
         name="feats",
         cost_estimate=cost(4),
-    )(idx, own, oc, oh, ohc, in_hbm(key_weight), in_hbm(value_weight), mine, theirs)
+    )(idx, own, oc, oh, ohc, key_weight, value_weight, mine, theirs)
 
 
 def solution(mesh):
@@ -430,23 +455,22 @@
         stats = swap8(stats)
         parts = swap8(parts)
 
-        def grads(k, dtype, *more):
-            return backward(idx, tiles, text_sees, queries, grad_out, kvs[k], stats, k, dtype, *more)
-
-        far = []
-        for k in (2, 1, 3):
-            (sent,) = grads(k, BF)
-            far.append(to_t[k](sent))
-        total, merged = grads(0, F32, parts)
+        def grads(chunks, *more):
+            return backward(idx, tiles, text_sees, queries, grad_out, kvs, stats, chunks, *more)
+
+        (second,) = grads((2,))
+        (first,) = grads((1,))
+        third, total, merged = grads((3, 0), parts)
+        far = [to_t[2](second), to_t[1](first), to_t[3](third)]
         mine = swap8(merged).reshape(queries.shape[0], -1)
         for x in far:
             total = total + x.astype(F32)
         total = total.astype(BF)
         rows = total.shape[0] // 2
         near, other = total[:rows], total[rows:]
-        grad_feats, attn_out = feature_grad(
-            idx, near, to_c(other), to_h(near), to_hc(other), key_weight, value_weight, mine, to_c(mine)
-        )
+        pieces = near, to_c(other), to_h(near), to_hc(other)
+        key_near, value_near = fetch_weights(key_weight, value_weight, total)
+        grad_feats, attn_out = feature_grad(idx, *pieces, key_near, value_near, mine, to_c(mine))
         return attn_out, grad_feats
 
     placed = (

time: 110 us -> 107 us (0.973)
  starting transfers between devices: 34 us -> 30.5 us
  Pallas kernels: 34.6 us -> 33.3 us
  waiting for transfers between devices: 27.3 us -> 28.6 us
    ppermute x14, starting transfers between devices: 25.4 us -> 21.9 us  [moved(): return lambda x: lax.ppermute(x, AXES, pairs)]
    pallas_call x0 -> x1, Pallas kernels: none -> 3.32 us  [fetch_weights(): pl.pallas_call(body, out_shape=(pltpu.VMEM(key_weight.shape, BF), pltpu.V...]
    pallas_call x1, Pallas kernels: 6.8 us -> 3.71 us  [feature_grad(): pl.pallas_call(body, out_shape=(jax.ShapeDtypeStruct((rows, feat), BF), j...]
    all_to_all x2, waiting for transfers between devices: 2.58 us -> 5.11 us  [swap8(): return lax.all_to_all(x, 'img', 0, 0, axis_index_groups=chips, tiled=True)]
    pallas_call x4 -> x3, Pallas kernels: 14.8 us -> 13.3 us  [backward(): pl.pallas_call(body, out_shape=out_shape, grid_spec=pltpu.PrefetchScalarG...]
    ppermute x14, waiting for transfers between devices: 24.7 us -> 23.5 us  [moved(): return lambda x: lax.ppermute(x, AXES, pairs)]
  transfers between devices with their start and end apart: 16 -> 16, of which waited for: 8 -> 9; matrix products, arithmetic and copies ran while one was open for 1% -> 1% of each run, Pallas kernels for 14% -> 16%
where the time goes in v4:
time: 107 us
  Pallas kernels  33.3 us (31%)
  starting transfers between devices  30.5 us (29%)
  waiting for transfers between devices  28.6 us (27%)
  blocking collectives  10.3 us (10%)
  local copies, waits for them, and re-layouts  1.94 us (2%)
  other arithmetic  1.44 us (1%)
    ppermute x14, waiting for transfers between devices, moved(): return lambda x: lax.ppermute(x, AXES, pairs)  23.5 us
    ppermute x14, starting transfers between devices, moved(): return lambda x: lax.ppermute(x, AXES, pairs)  21.9 us
    pallas_call x3, Pallas kernels, backward(): pl.pallas_call(body, out_shape=out_shape, grid_spec=pltpu.PrefetchScalarG...  13.3 us
    all_to_all x1, blocking collectives, swap8(): return lax.all_to_all(x, 'img', 0, 0, axis_index_groups=chips, tiled=True)  10.3 us
    all_to_all x2, starting transfers between devices, swap8(): return lax.all_to_all(x, 'img', 0, 0, axis_index_groups=chips, tiled=True)  8.56 us
    pallas_call x1, Pallas kernels, forward(): pl.pallas_call(body, out_shape=(jax.ShapeDtypeStruct((8, share, width), B...  7.73 us
    pallas_call x1, Pallas kernels, project(): pl.pallas_call(body, out_shape=(jax.ShapeDtypeStruct((rows, 2 * HD), F32)...  5.22 us
    all_to_all x2, waiting for transfers between devices, swap8(): return lax.all_to_all(x, 'img', 0, 0, axis_index_groups=chips, tiled=True)  5.11 us
  transfers between devices with their start and end apart: 16, of which 9 were waited for; matrix products, arithmetic and copies ran while one was open for 1% of the time, Pallas kernels for 16%

profile of v4, /device:TPU:1, one launch (start us, length us, event | category | flops | bytes accessed | tf_op | source)
XLA Modules:
  0.0 107.0 jit_solution(4602200339356267525)
XLA Ops:
  0.6 0.1 pad_add_fusion.1.ix
  0.7 5.2 %project.1 = (f32[256,256]{1,0:T(8,128)S(1)}, bf16[256,384]{1,0:T(8,128)(2,1)S(1)}, bf16[256,384]{1,0:T(8,128)(2,1)S(1)}, bf16[256,384]{1,0:T(8,128)(2,1)S(1)}) custom-call(s32[4]{0:T(128)S(1)} %pad_add_fusion.1.ix, bf16[256,3840]{1,0:T(8,128)(2,1)} %x_hbm.1, bf16[3840,512]{1,0:T(8,128)(2,1)} %k_hbm.1, bf16[3840,512]{1,0:T(8,128)(2,1)} %v_hbm.1), custom_call_target="tpu_custom_call" | custom-call | flops 4400000000 | bytes 65536 | tf_op jit(solution)/shard_map/project/pallas_call | solution.py:102
  6.0 0.0 copy-start.7
  6.0 0.0 copy-start
  6.0 0.0 copy-start.1
  6.0 0.0 copy-start.6
  6.0 4.5 %collective-permute-start.1 = (bf16[256,384]{1,0:T(8,128)(2,1)S(1)}, bf16[256,384]{1,0:T(8,128)(2,1)S(1)}, u32[]{:S(2)}, u32[]{:S(2)}) collective-permute-start(bf16[256,384]{1,0:T(8,128)(2,1)S(1)} %get-tuple-element.16), channel_id=1, source_target_pairs={{0,4},{1,5},{2,6},{3,7},{4,0},{5,1},{6,2},{7,3},{8,12},{9,13},{10,... | collective-permute-start | bytes 589832 | tf_op jit(solution)/shard_map/ppermute | solution.py:39
  10.5 1.0 collective-permute-start.2
  11.5 0.0 collective-permute-start.3
  11.5 3.7 %collective-permute-done.1 = bf16[256,384]{1,0:T(8,128)(2,1)S(1)} collective-permute-done((bf16[256,384]{1,0:T(8,128)(2,1)S(1)}, bf16[256,384]{1,0:T(8,128)(2,1)S(1)}, u32[]{:S(2)}, u32[]{:S(2)}) %collective-permute-start.1) | collective-permute-done | bytes 196640 | tf_op jit(solution)/shard_map/ppermute | solution.py:39
  15.2 0.0 collective-permute-done.2
  15.2 4.6 %collective-permute-done.3 = bf16[256,384]{1,0:T(8,128)(2,1)S(1)} collective-permute-done((bf16[256,384]{1,0:T(8,128)(2,1)S(1)}, bf16[256,384]{1,0:T(8,128)(2,1)S(1)}, u32[]{:S(2)}, u32[]{:S(2)}) %collective-permute-start.3) | collective-permute-done | bytes 196640 | tf_op jit(solution)/shard_map/ppermute | solution.py:39
  20.0 2.8 %collective-permute-start.6 = (bf16[512,256]{1,0:T(8,128)(2,1)S(1)}, bf16[512,256]{1,0:T(8,128)(2,1)S(1)}, u32[]{:S(2)}, u32[]{:S(2)}) collective-permute-start(bf16[512,256]{1,0:T(8,128)(2,1)S(1)} %maximum_maximum_fusion.k0.refs_1_), channel_id=1, source_target_pairs={{0,3},{1,2},{2,1},{3,0},{4,7},{5,6},{6,5},{7,4},{8,11},{9,10},{10,... | collective-permute-start | bytes 786440 | tf_op jit(solution)/shard_map/ppermute | solution.py:39
  22.8 0.3 collective-permute-start.5
  23.2 0.3 collective-permute-start.4
  23.5 0.0 copy-done.7
  23.5 1.0 collective-permute-start
  24.5 0.8 collective-permute-done
  25.4 9.2 %collective-permute-done.6.k3.refs_0_ = bf16[512,256]{1,0:T(8,128)(2,1)S(1)} collective-permute-done((bf16[512,256]{1,0:T(8,128)(2,1)S(1)}, bf16[512,256]{1,0:T(8,128)(2,1)S(1)}, u32[]{:S(2)}, u32[]{:S(2)}) %collective-permute-start.6) | collective-permute-done | bytes 262176 | tf_op jit(solution)/shard_map/ppermute | solution.py:39
  34.6 0.0 copy-start.2
  34.6 0.0 collective-permute-done.5.k2.refs_0_
  34.6 0.0 copy-start.4
  34.6 0.5 collective-permute-done.4.k1.refs_0_
  35.1 0.0 copy-done
  35.1 0.0 copy-done.1
  35.1 0.0 copy-done.6
  35.1 7.7 %fwd.1 = (bf16[8,32,1024]{2,1,0:T(8,128)(2,1)}, f32[8,16,256]{2,1,0:T(8,128)S(1)}) custom-call(s32[4]{0:T(128)S(1)} %pad_add_fusion.1.ix, s32[2,8]{1,0:T(2,128)S(1)} %pad_add_fusion.tl, s32[8,8]{1,0:T(8,128)S(1)} %copy-done.6, bf16[256,2048]{1,0:T(8,128)(2,1)S(1)} %copy-done, bf16[256,2048]{1,0:T(8,128)(2,1)S(1)} %copy-done.1, ...), custom_call_target="tpu_custom_call" | custom-call | flops 7699999744 | bytes 65536 | tf_op jit(solution)/shard_map/fwd/pallas_call | solution.py:184
  42.8 0.0 copy-done.2
  42.8 0.0 copy-done.4
  42.8 10.3 %all_to_all.15.st = f32[8,16,256]{2,1,0:T(8,128)S(1)} all-to-all(f32[8,16,256]{2,1,0:T(8,128)S(1)} %get-tuple-element.19), channel_id=1, replica_groups={{0,16,32,48,64,80,96,112},{8,24,40,56,72,88,104,120},{1,17,33,49,65,81,..., dimensions={0} | all-to-all | bytes 262144 | tf_op jit(solution)/shard_map/all_to_all | solution.py:430
  53.1 3.7 %all-to-all-start.1 = ((bf16[8,32,1024]{2,1,0:T(8,128)(2,1)}), bf16[8,32,1024]{2,1,0:T(8,128)(2,1)S(1)}, u32[]{:S(2)}, u32[]{:S(2)}) async-start(bf16[8,32,1024]{2,1,0:T(8,128)(2,1)} %get-tuple-element.20), calls=%async_computation.1 | async-start | bytes 1048576 | tf_op jit(solution)/shard_map/all_to_all | solution.py:430
  56.8 0.0 copy-start.5
  56.8 0.9 copy-done.5
  57.7 3.8 %grads2.1 = bf16[512,256]{1,0:T(8,128)(2,1)} custom-call(s32[4]{0:T(128)S(1)} %pad_add_fusion.1.ix, s32[2,8]{1,0:T(2,128)S(1)} %pad_add_fusion.tl, s32[8,8]{1,0:T(8,128)S(1)} %copy-done.6, bf16[256,2048]{1,0:T(8,128)(2,1)S(1)} %copy-done, bf16[256,2048]{1,0:T(8,128)(2,1)S(1)} %copy-done.1, f32[8,16,256]{2,1,0:T(8,128)S(1)} %all_to_all.15.st, ...), custom_call_target="tpu_custom_call" | custom-call | flops 3300000000 | bytes 65536 | tf_op jit(solution)/shard_map/grads2/pallas_call | solution.py:305
  61.5 2.6 %collective-permute-start.7 = (bf16[512,256]{1,0:T(8,128)(2,1)}, bf16[512,256]{1,0:T(8,128)(2,1)}, u32[]{:S(2)}, u32[]{:S(2)}) collective-permute-start(bf16[512,256]{1,0:T(8,128)(2,1)} %grads2.1), channel_id=1, source_target_pairs={{0,2},{1,3},{2,0},{3,1},{4,6},{5,7},{6,4},{7,5},{8,10},{9,11},{10,... | collective-permute-start | bytes 786440 | tf_op jit(solution)/shard_map/ppermute | solution.py:39
  64.1 3.8 %grads1.1 = bf16[512,256]{1,0:T(8,128)(2,1)} custom-call(s32[4]{0:T(128)S(1)} %pad_add_fusion.1.ix, s32[2,8]{1,0:T(2,128)S(1)} %pad_add_fusion.tl, s32[8,8]{1,0:T(8,128)S(1)} %copy-done.6, bf16[256,2048]{1,0:T(8,128)(2,1)S(1)} %copy-done, bf16[256,2048]{1,0:T(8,128)(2,1)S(1)} %copy-done.1, f32[8,16,256]{2,1,0:T(8,128)S(1)} %all_to_all.15.st, ...), custom_call_target="tpu_custom_call" | custom-call | flops 3300000000 | bytes 65536 | tf_op jit(solution)/shard_map/grads1/pallas_call | solution.py:305
  67.9 0.4 collective-permute-start.8
  68.3 0.0 all-to-all-done.1.refs_2_
  68.3 0.0 copy-start.3
  68.3 0.9 copy-done.3
  69.2 5.8 %grads30.1 = (bf16[512,256]{1,0:T(8,128)(2,1)}, f32[512,256]{1,0:T(8,128)S(1)}, bf16[8,32,1024]{2,1,0:T(8,128)(2,1)}) custom-call(s32[4]{0:T(128)S(1)} %pad_add_fusion.1.ix, s32[2,8]{1,0:T(2,128)S(1)} %pad_add_fusion.tl, s32[8,8]{1,0:T(8,128)S(1)} %copy-done.6, bf16[256,2048]{1,0:T(8,128)(2,1)S(1)} %copy-done, bf16[256,2048]{1,0:T(8,128)(2,1)S(1)} %copy-done.1, ...), custom_call_target="tpu_custom_call" | custom-call | flops 6600000000 | bytes 65536 | tf_op jit(solution)/shard_map/grads30/pallas_call | solution.py:305
  75.0 0.4 collective-permute-start.9
  75.4 4.9 %all-to-all-start.2 = ((bf16[8,32,1024]{2,1,0:T(8,128)(2,1)}), bf16[8,32,1024]{2,1,0:T(8,128)(2,1)S(1)}, u32[]{:S(2)}, u32[]{:S(2)}) async-start(bf16[8,32,1024]{2,1,0:T(8,128)(2,1)} %get-tuple-element.25), calls=%async_computation.2 | async-start | bytes 1048576 | tf_op jit(solution)/shard_map/all_to_all | solution.py:430
  80.3 0.0 collective-permute-done.7
  80.3 0.0 collective-permute-done.8
  80.3 1.4 %collective-permute-done.9 = bf16[512,256]{1,0:T(8,128)(2,1)S(1)} collective-permute-done((bf16[512,256]{1,0:T(8,128)(2,1)}, bf16[512,256]{1,0:T(8,128)(2,1)S(1)}, u32[]{:S(2)}, u32[]{:S(2)}) %collective-permute-start.9) | collective-permute-done | bytes 262176 | tf_op jit(solution)/shard_map/ppermute | solution.py:39
  81.7 1.2 %add_convert_fusion._ = bf16[512,256]{1,0:T(8,128)(2,1)S(1)} fusion(bf16[512,256]{1,0:T(8,128)(2,1)S(1)} %collective-permute-done.9, bf16[512,256]{1,0:T(8,128)(2,1)} %collective-permute-done.8, f32[512,256]{1,0:T(8,128)S(1)} %get-tuple-element.21, bf16[512,256]{1,0:T(8,128)(2,1)} %collective-permute-done.7), kind=kLoop, calls=%fused_computation | loop fusion | flops 917504 | bytes 1572864 | tf_op jit(solution)/shard_map/convert_element_type | solution.py:468
  82.8 5.1 %all-to-all-done.2 = bf16[8,32,1024]{2,1,0:T(8,128)(2,1)S(1)} async-done(((bf16[8,32,1024]{2,1,0:T(8,128)(2,1)}), bf16[8,32,1024]{2,1,0:T(8,128)(2,1)S(1)}, u32[]{:S(2)}, u32[]{:S(2)}) %all-to-all-start.2) | async-done | bytes 524320 | tf_op jit(solution)/shard_map/all_to_all | solution.py:430
  87.9 4.8 %collective-permute-start.13 = (bf16[256,1024]{1,0:T(8,128)(2,1)S(1)}, bf16[256,1024]{1,0:T(8,128)(2,1)S(1)}, u32[]{:S(2)}, u32[]{:S(2)}) collective-permute-start(bf16[256,1024]{1,0:T(8,128)(2,1)S(1)} %bitcast.7), channel_id=1, source_target_pairs={{0,8},{1,9},{2,10},{3,11},{4,12},{5,13},{6,14},{7,15},{8,0},{9,1},... | collective-permute-start | bytes 1572872 | tf_op jit(solution)/shard_map/ppermute | solution.py:39
  92.7 3.2 %collective-permute-start.12 = (bf16[256,256]{1,0:T(8,128)(2,1)S(1)}, bf16[256,256]{1,0:T(8,128)(2,1)S(1)}, u32[]{:S(2)}, u32[]{:S(2)}) collective-permute-start(bf16[256,256]{1,0:T(8,128)(2,1)S(1)} %get-tuple-element.32), channel_id=1, source_target_pairs={{0,12},{1,13},{2,14},{3,15},{4,8},{5,9},{6,10},{7,11},{8,4},{9,5},... | collective-permute-start | bytes 393224 | tf_op jit(solution)/shard_map/ppermute | solution.py:39
  96.0 0.5 collective-permute-start.10
  96.5 0.0 collective-permute-start.11
  96.5 3.3 %fetch.1 = (bf16[3840,512]{1,0:T(8,128)(2,1)S(1)}, bf16[3840,512]{1,0:T(8,128)(2,1)S(1)}) custom-call(bf16[3840,512]{1,0:T(8,128)(2,1)} %k_hbm.1, bf16[3840,512]{1,0:T(8,128)(2,1)} %v_hbm.1, bf16[512,256]{1,0:T(8,128)(2,1)S(1)} %add_convert_fusion._), custom_call_target="tpu_custom_call" | custom-call | flops 4400000000 | bytes 65536 | tf_op jit(solution)/shard_map/fetch/pallas_call | solution.py:339
  99.8 0.1 collective-permute-done.12.d_
  99.9 0.0 collective-permute-done.10.b
  99.9 3.2 %collective-permute-done.11.c_ = bf16[256,256]{1,0:T(8,128)(2,1)S(1)} collective-permute-done((bf16[256,256]{1,0:T(8,128)(2,1)S(1)}, bf16[256,256]{1,0:T(8,128)(2,1)S(1)}, u32[]{:S(2)}, u32[]{:S(2)}) %collective-permute-start.11) | collective-permute-done | bytes 131104 | tf_op jit(solution)/shard_map/ppermute | solution.py:39
  103.1 0.0 collective-permute-done.13.t_ref
  103.1 3.7 %feats.1 = (bf16[256,3840]{1,0:T(8,128)(2,1)}, bf16[256,2048]{1,0:T(8,128)(2,1)}) custom-call(s32[4]{0:T(128)S(1)} %pad_add_fusion.1.ix, bf16[256,256]{1,0:T(8,128)(2,1)S(1)} %get-tuple-element.33.a, bf16[256,256]{1,0:T(8,128)(2,1)S(1)} %collective-permute-done.10.b, bf16[256,256]{1,0:T(8,128)(2,1)S(1)} %collective-permute-done.11.c_, ...), custom_call_target="tpu_custom_call" | custom-call | flops 4400000000 | bytes 65536 | tf_op jit(solution)/shard_map/feats/pallas_call | solution.py:398
  (8 shorter events, 0.2 us)
Async XLA Ops:
  6.0 17.5 %copy-start.7 = (s32[8]{0:T(128)S(1)}, s32[8]{0:T(128)}, u32[]{:S(2)}) copy-start(s32[8]{0:T(128)} %param.12) | copy-start | bytes 100
  6.0 29.1 %copy-start = (bf16[256,2048]{1,0:T(8,128)(2,1)S(1)}, bf16[256,2048]{1,0:T(8,128)(2,1)}, u32[]{:S(2)}) copy-start(bf16[256,2048]{1,0:T(8,128)(2,1)} %q.7) | copy-start | bytes 3145732
  6.0 29.1 %copy-start.1 = (bf16[256,2048]{1,0:T(8,128)(2,1)S(1)}, bf16[256,2048]{1,0:T(8,128)(2,1)}, u32[]{:S(2)}) copy-start(bf16[256,2048]{1,0:T(8,128)(2,1)} %g.7) | copy-start | bytes 3145732
  6.0 29.1 %copy-start.6 = (s32[8,8]{1,0:T(8,128)S(1)}, s32[8,8]{1,0:T(8,128)}, u32[]{:S(2)}) copy-start(s32[8,8]{1,0:T(8,128)} %se.7) | copy-start | bytes 772
  6.0 9.1 %collective-permute-start.1 = (bf16[256,384]{1,0:T(8,128)(2,1)S(1)}, bf16[256,384]{1,0:T(8,128)(2,1)S(1)}, u32[]{:S(2)}, u32[]{:S(2)}) collective-permute-start(bf16[256,384]{1,0:T(8,128)(2,1)S(1)} %get-tuple-element.16), channel_id=1, source_target_pairs={{0,4},{1,5},{2,6},{3,7},{4,0},{5,1},{6,2},{7,3},{8,12},{9,13},{10,... | collective-permute-start | bytes 589832 | tf_op jit(solution)/shard_map/ppermute | solution.py:39
  10.5 4.7 %collective-permute-start.2 = (bf16[256,384]{1,0:T(8,128)(2,1)S(1)}, bf16[256,384]{1,0:T(8,128)(2,1)S(1)}, u32[]{:S(2)}, u32[]{:S(2)}) collective-permute-start(bf16[256,384]{1,0:T(8,128)(2,1)S(1)} %get-tuple-element.17), channel_id=1, source_target_pairs={{0,8},{1,9},{2,10},{3,11},{4,12},{5,13},{6,14},{7,15},{8,0},{9,1},... | collective-permute-start | bytes 589832 | tf_op jit(solution)/shard_map/ppermute | solution.py:39
  11.5 8.4 %collective-permute-start.3 = (bf16[256,384]{1,0:T(8,128)(2,1)S(1)}, bf16[256,384]{1,0:T(8,128)(2,1)S(1)}, u32[]{:S(2)}, u32[]{:S(2)}) collective-permute-start(bf16[256,384]{1,0:T(8,128)(2,1)S(1)} %get-tuple-element.18), channel_id=1, source_target_pairs={{0,12},{1,13},{2,14},{3,15},{4,8},{5,9},{6,10},{7,11},{8,4},{9,5},... | collective-permute-start | bytes 589832 | tf_op jit(solution)/shard_map/ppermute | solution.py:39
  20.0 14.6 %collective-permute-start.6 = (bf16[512,256]{1,0:T(8,128)(2,1)S(1)}, bf16[512,256]{1,0:T(8,128)(2,1)S(1)}, u32[]{:S(2)}, u32[]{:S(2)}) collective-permute-start(bf16[512,256]{1,0:T(8,128)(2,1)S(1)} %maximum_maximum_fusion.k0.refs_1_), channel_id=1, source_target_pairs={{0,3},{1,2},{2,1},{3,0},{4,7},{5,6},{6,5},{7,4},{8,11},{9,10},{10,... | collective-permute-start | bytes 786440 | tf_op jit(solution)/shard_map/ppermute | solution.py:39
  22.8 11.8 %collective-permute-start.5 = (bf16[512,256]{1,0:T(8,128)(2,1)S(1)}, bf16[512,256]{1,0:T(8,128)(2,1)S(1)}, u32[]{:S(2)}, u32[]{:S(2)}) collective-permute-start(bf16[512,256]{1,0:T(8,128)(2,1)S(1)} %maximum_maximum_fusion.k0.refs_1_), channel_id=1, source_target_pairs={{0,2},{1,3},{2,0},{3,1},{4,6},{5,7},{6,4},{7,5},{8,10},{9,11},{10,... | collective-permute-start | bytes 786440 | tf_op jit(solution)/shard_map/ppermute | solution.py:39
  23.2 11.9 %collective-permute-start.4 = (bf16[512,256]{1,0:T(8,128)(2,1)S(1)}, bf16[512,256]{1,0:T(8,128)(2,1)S(1)}, u32[]{:S(2)}, u32[]{:S(2)}) collective-permute-start(bf16[512,256]{1,0:T(8,128)(2,1)S(1)} %maximum_maximum_fusion.k0.refs_1_), channel_id=1, source_target_pairs={{0,1},{1,0},{2,3},{3,2},{4,5},{5,4},{6,7},{7,6},{8,9},{9,8},{10,11... | collective-permute-start | bytes 786440 | tf_op jit(solution)/shard_map/ppermute | solution.py:39
  23.5 1.9 %collective-permute-start = (s32[8]{0:T(128)S(1)}, s32[8]{0:T(128)S(1)}, u32[]{:S(2)}, u32[]{:S(2)}) collective-permute-start(s32[8]{0:T(128)S(1)} %copy-done.7), channel_id=1, source_target_pairs={{0,8},{1,9},{2,10},{3,11},{4,12},{5,13},{6,14},{7,15},{8,0},{9,1},... | collective-permute-start | bytes 104 | tf_op jit(solution)/shard_map/ppermute | solution.py:39
  34.6 8.2 %copy-start.2 = (bf16[512,256]{1,0:T(8,128)(2,1)}, bf16[512,256]{1,0:T(8,128)(2,1)S(1)}, u32[]{:S(2)}) copy-start(bf16[512,256]{1,0:T(8,128)(2,1)S(1)} %collective-permute-done.6.k3.refs_0_) | copy-start | bytes 786436
  34.6 8.2 %copy-start.4 = (bf16[512,256]{1,0:T(8,128)(2,1)}, bf16[512,256]{1,0:T(8,128)(2,1)S(1)}, u32[]{:S(2)}) copy-start(bf16[512,256]{1,0:T(8,128)(2,1)S(1)} %collective-permute-done.5.k2.refs_0_) | copy-start | bytes 786436
  53.1 15.2 %all-to-all-start.1 = ((bf16[8,32,1024]{2,1,0:T(8,128)(2,1)}), bf16[8,32,1024]{2,1,0:T(8,128)(2,1)S(1)}, u32[]{:S(2)}, u32[]{:S(2)}) async-start(bf16[8,32,1024]{2,1,0:T(8,128)(2,1)} %get-tuple-element.20), calls=%async_computation.1 | async-start | bytes 1048576 | tf_op jit(solution)/shard_map/all_to_all | solution.py:430
  56.8 1.0 copy-start.5
  61.5 18.8 %collective-permute-start.7 = (bf16[512,256]{1,0:T(8,128)(2,1)}, bf16[512,256]{1,0:T(8,128)(2,1)}, u32[]{:S(2)}, u32[]{:S(2)}) collective-permute-start(bf16[512,256]{1,0:T(8,128)(2,1)} %grads2.1), channel_id=1, source_target_pairs={{0,2},{1,3},{2,0},{3,1},{4,6},{5,7},{6,4},{7,5},{8,10},{9,11},{10,... | collective-permute-start | bytes 786440 | tf_op jit(solution)/shard_map/ppermute | solution.py:39
  67.9 12.4 %collective-permute-start.8 = (bf16[512,256]{1,0:T(8,128)(2,1)}, bf16[512,256]{1,0:T(8,128)(2,1)}, u32[]{:S(2)}, u32[]{:S(2)}) collective-permute-start(bf16[512,256]{1,0:T(8,128)(2,1)} %grads1.1), channel_id=1, source_target_pairs={{0,1},{1,0},{2,3},{3,2},{4,5},{5,4},{6,7},{7,6},{8,9},{9,8},{10,11... | collective-permute-start | bytes 786440 | tf_op jit(solution)/shard_map/ppermute | solution.py:39
  68.3 1.0 copy-start.3
  75.0 6.6 %collective-permute-start.9 = (bf16[512,256]{1,0:T(8,128)(2,1)}, bf16[512,256]{1,0:T(8,128)(2,1)S(1)}, u32[]{:S(2)}, u32[]{:S(2)}) collective-permute-start(bf16[512,256]{1,0:T(8,128)(2,1)} %get-tuple-element.22), channel_id=1, source_target_pairs={{0,3},{1,2},{2,1},{3,0},{4,7},{5,6},{6,5},{7,4},{8,11},{9,10},{10,... | collective-permute-start | bytes 786440 | tf_op jit(solution)/shard_map/ppermute | solution.py:39
  75.4 12.5 %all-to-all-start.2 = ((bf16[8,32,1024]{2,1,0:T(8,128)(2,1)}), bf16[8,32,1024]{2,1,0:T(8,128)(2,1)S(1)}, u32[]{:S(2)}, u32[]{:S(2)}) async-start(bf16[8,32,1024]{2,1,0:T(8,128)(2,1)} %get-tuple-element.25), calls=%async_computation.2 | async-start | bytes 1048576 | tf_op jit(solution)/shard_map/all_to_all | solution.py:430
  87.9 15.2 %collective-permute-start.13 = (bf16[256,1024]{1,0:T(8,128)(2,1)S(1)}, bf16[256,1024]{1,0:T(8,128)(2,1)S(1)}, u32[]{:S(2)}, u32[]{:S(2)}) collective-permute-start(bf16[256,1024]{1,0:T(8,128)(2,1)S(1)} %bitcast.7), channel_id=1, source_target_pairs={{0,8},{1,9},{2,10},{3,11},{4,12},{5,13},{6,14},{7,15},{8,0},{9,1},... | collective-permute-start | bytes 1572872 | tf_op jit(solution)/shard_map/ppermute | solution.py:39
  92.7 7.1 %collective-permute-start.12 = (bf16[256,256]{1,0:T(8,128)(2,1)S(1)}, bf16[256,256]{1,0:T(8,128)(2,1)S(1)}, u32[]{:S(2)}, u32[]{:S(2)}) collective-permute-start(bf16[256,256]{1,0:T(8,128)(2,1)S(1)} %get-tuple-element.32), channel_id=1, source_target_pairs={{0,12},{1,13},{2,14},{3,15},{4,8},{5,9},{6,10},{7,11},{8,4},{9,5},... | collective-permute-start | bytes 393224 | tf_op jit(solution)/shard_map/ppermute | solution.py:39
  96.0 3.9 %collective-permute-start.10 = (bf16[256,256]{1,0:T(8,128)(2,1)S(1)}, bf16[256,256]{1,0:T(8,128)(2,1)S(1)}, u32[]{:S(2)}, u32[]{:S(2)}) collective-permute-start(bf16[256,256]{1,0:T(8,128)(2,1)S(1)} %get-tuple-element.32), channel_id=1, source_target_pairs={{0,8},{1,9},{2,10},{3,11},{4,12},{5,13},{6,14},{7,15},{8,0},{9,1},... | collective-permute-start | bytes 393224 | tf_op jit(solution)/shard_map/ppermute | solution.py:39
  96.5 6.6 %collective-permute-start.11 = (bf16[256,256]{1,0:T(8,128)(2,1)S(1)}, bf16[256,256]{1,0:T(8,128)(2,1)S(1)}, u32[]{:S(2)}, u32[]{:S(2)}) collective-permute-start(bf16[256,256]{1,0:T(8,128)(2,1)S(1)} %get-tuple-element.33.a), channel_id=1, source_target_pairs={{0,4},{1,5},{2,6},{3,7},{4,0},{5,1},{6,2},{7,3},{8,12},{9,13},{10,... | collective-permute-start | bytes 393224 | tf_op jit(solution)/shard_map/ppermute | solution.py:39

commit v5 on v4

--- a/solution.py
+++ b/solution.py
@@ -52,13 +52,13 @@
     return pltpu.with_memory_space_constraint(x, pltpu.HBM)
 
 
-def project(idx, feats, key_weight, value_weight):
+def project(idx, tiles, feats, key_weight, value_weight):
     rows, feat = feats.shape
     cols = key_weight.shape[1]
     steps = 5
     chunk = feat // steps
 
-    def body(ix, x_hbm, wk_hbm, wv_hbm, own, oc, oh, ohc, x, wk, wv, acc, sems):
+    def body(ix, tl, x_hbm, wk_hbm, wv_hbm, k0, kc, kh, khc, v0, vc, vh, vhc, x, wk, wv, acc, sems):
         copies = []
         for s in range(steps):
             at = slice(s * chunk, (s + 1) * chunk)
@@ -89,24 +89,28 @@
             at = pl.multiple_of((hh * 2 + cc) * HD, HD)
             return acc[which, :, pl.ds(at, HD)]
 
-        own[:, :HD] = piece(0, h, c)
-        own[:, HD:] = piece(1, h, c)
-        for ref, hh, cc in ((oh, 1 - h, c), (ohc, 1 - h, 1 - c), (oc, h, 1 - c)):
-            kp = piece(0, hh, cc)
-            high = kp.astype(BF)
-            ref[:, :HD] = high
-            ref[:, HD : 2 * HD] = (kp - high.astype(F32)).astype(BF)
-            ref[:, 2 * HD :] = piece(1, hh, cc).astype(BF)
-
-    sent = jax.ShapeDtypeStruct((rows, 3 * HD), BF)
+        for which, refs in ((1, (v0, vh, vhc, vc)), (0, (k0, kh, khc, kc))):
+            for ref, (hh, cc) in zip(refs, ((h, c), (1 - h, c), (1 - h, 1 - c), (h, 1 - c))):
+                ref[:rows, :] = piece(which, hh, cc).astype(ref.dtype)
+        lane = lax.broadcasted_iota(jnp.int32, (extra, HD), 1)
+        ids = jnp.zeros((extra, HD), F32)
+        for e in range(tiles.shape[0]):
+            ids = jnp.where(lane == e, tl[e].astype(F32), ids)
+        vc[rows:, :] = ids.astype(BF)
+
+    extra = 16
+    key = jax.ShapeDtypeStruct((rows, HD), F32)
+    value = jax.ShapeDtypeStruct((rows, HD), BF)
+    marked = jax.ShapeDtypeStruct((rows + extra, HD), BF)
+    outs = (key, key, key, key, key, marked, value, value)
     return pl.pallas_call(
         body,
-        out_shape=(jax.ShapeDtypeStruct((rows, 2 * HD), F32), sent, sent, sent),
+        out_shape=outs,
         grid_spec=pltpu.PrefetchScalarGridSpec(
-            num_scalar_prefetch=1,
+            num_scalar_prefetch=2,
             grid=(1,),
             in_specs=[pl.BlockSpec(memory_space=pltpu.HBM)] * 3,
-            out_specs=[spec((rows, 2 * HD))] + [spec((rows, 3 * HD))] * 3,
+            out_specs=[spec(o.shape) for o in outs],
             scratch_shapes=[
                 pltpu.VMEM((steps, rows, chunk), BF),
                 pltpu.VMEM((steps, chunk, cols), BF),
@@ -118,7 +122,7 @@
         compiler_params=pltpu.CompilerParams(vmem_limit_bytes=24 << 20),
         name="project",
         cost_estimate=cost(4),
-    )(idx, in_hbm(feats), in_hbm(key_weight), in_hbm(value_weight))
+    )(idx, tiles, in_hbm(feats), in_hbm(key_weight), in_hbm(value_weight))
 
 
 def tile_cap(ix, tiles, sees, block, chunk, tile):
@@ -129,20 +133,21 @@
     return jnp.where(sees[row, image] > 0, jnp.float32(TOP), jnp.float32(NEG))
 
 
-def forward(idx, tiles, sees, queries, grad_out, kvs):
+def forward(idx, tiles, sees, queries, grad_out, keys, values):
     rows = queries.shape[0]
     heads = 8
     width = heads * HD
-    span = kvs[0].shape[0]
-    n = len(kvs)
+    span = keys[0].shape[0]
+    n = len(keys)
     total = span * n
     share = rows // 8
     per = span // TILE
 
-    def body(ix, tl, se, q, g, k0, k1, k2, k3, out, st_out, y_scr, va):
+    def body(ix, tl, se, q, g, k0, k1, k2, k3, v0, v1, v2, v3, out, st_out, y_scr, va):
         ks = (k0, k1, k2, k3)
+        vs = (v0, v1, v2, v3)
         for j in range(n):
-            va[j * span : (j + 1) * span, :HD] = ks[j][:, HD:]
+            va[j * span : (j + 1) * span, :HD] = vs[j][...]
         va[:, HD:] = jnp.ones((total, HD), BF)
         caps = [
             [tile_cap(ix, tl, se, b, j, e) for j in range(n) for e in range(per)]
@@ -156,7 +161,7 @@
             qh = q[:, cols]
             best = [None, None]
             for j in range(n):
-                s = dot_nt(qh, ks[j][:, :HD]) * C2
+                s = dot_nt(qh, ks[j][...]) * C2
                 for b in range(2):
                     for e in range(per):
                         y = jnp.minimum(
@@ -190,7 +195,7 @@
         grid_spec=pltpu.PrefetchScalarGridSpec(
             num_scalar_prefetch=3,
             grid=(1,),
-            in_specs=[pl.BlockSpec((rows, width), own)] * 2 + [spec((span, 2 * HD))] * 4,
+            in_specs=[pl.BlockSpec((rows, width), own)] * 2 + [spec((span, HD))] * 8,
             out_specs=[spec((8, share, width)), spec((8, 2 * heads, rows))],
             scratch_shapes=[
                 pltpu.VMEM((2, rows, total), F32),
@@ -200,7 +205,7 @@
         compiler_params=pltpu.CompilerParams(vmem_limit_bytes=24 << 20),
         name="fwd",
         cost_estimate=cost(7),
-    )(idx, tiles, sees, queries, grad_out, *kvs)
+    )(idx, tiles, sees, queries, grad_out, *keys, *values)
 
 
 def merge_weights(st, heads):
@@ -235,23 +240,23 @@
             out[i, :, cols] = v
 
 
-def backward(idx, tiles, sees, queries, grad_out, kvs, stats, chunks, parts=None):
+def backward(idx, tiles, sees, queries, grad_out, keys, values, stats, chunks, parts=None):
     rows = queries.shape[0]
     heads = 8
     width = heads * HD
-    span = kvs[0].shape[0]
+    span = keys[0].shape[0]
     per = span // TILE
     n = len(chunks)
 
     def body(ix, tl, se, q, g, st, *refs):
-        kv_refs, refs = refs[:n], refs[n:]
+        k_refs, v_refs, refs = refs[:n], refs[n : 2 * n], refs[2 * n :]
         lse, delta, ws = merge_weights(st, heads)
         if parts is None:
             outs, (dk, dv) = refs[:n], refs[n:]
         else:
             x, outs, (merged, dk, dv, w_scr) = refs[0], refs[1 : n + 1], refs[n + 1 :]
         lane = lax.broadcasted_iota(jnp.int32, (1, rows), 1)
-        for chunk, kv_ref, out in zip(chunks, kv_refs, outs):
+        for chunk, k_ref, v_ref, out in zip(chunks, k_refs, v_refs, outs):
             caps = [
                 jnp.where(
                     lane < TBLK,
@@ -260,8 +265,8 @@
                 )
                 for e in range(per)
             ]
-            kk = kv_ref[:, :HD]
-            vv = kv_ref[:, HD:]
+            kk = k_ref[...]
+            vv = v_ref[...]
             for h in range(heads):
                 cols = slice(h * HD, (h + 1) * HD)
                 qh = q[:, cols]
@@ -292,7 +297,7 @@
 
     own = lambda i, ix, tl, se: (0, ix[1])
     out_shape = [jax.ShapeDtypeStruct((span, 2 * HD), BF if k else F32) for k in chunks]
-    in_specs = [pl.BlockSpec((rows, width), own)] * 2 + [spec(stats.shape)] + [spec((span, 2 * HD))] * n
+    in_specs = [pl.BlockSpec((rows, width), own)] * 2 + [spec(stats.shape)] + [spec((span, HD))] * (2 * n)
     out_specs = [spec((span, 2 * HD))] * n
     scratch = [pltpu.VMEM((span, HD), F32)] * 2
     more = []
@@ -315,7 +320,7 @@
         compiler_params=pltpu.CompilerParams(vmem_limit_bytes=20 << 20),
         name="grads" + "".join(map(str, chunks)),
         cost_estimate=cost(3 * n),
-    )(idx, tiles, sees, queries, grad_out, stats, *[kvs[k] for k in chunks], *more)
+    )(idx, tiles, sees, queries, grad_out, stats, *[keys[k] for k in chunks], *[values[k] for k in chunks], *more)
 
 
 def fetch_weights(key_weight, value_weight, token):
@@ -436,30 +441,33 @@
         img = lax.axis_index("img")
         core = img % 2
         idx = jnp.stack([lax.axis_index("head"), core, lax.axis_index("txt"), img // 2]).astype(jnp.int32)
-        tiles = jnp.stack([tile_image, to_c(tile_image)])
-
-        own, c, h, hc = project(idx, image_feats, key_weight, value_weight)
-        h, hc, c = to_h(h), to_hc(hc), to_c(c)
-
-        def wide(x):
-            x = x.astype(F32)
-            return x[:, :HD] + x[:, HD : 2 * HD], x[:, 2 * HD :]
-
-        hk, hv = wide(h)
-        ck, cv = wide(c)
-        hck, hcv = wide(hc)
-        near = jnp.concatenate([own[:, :HD] + hk, own[:, HD:] + hv], axis=1).astype(BF)
-        far = jnp.concatenate([ck + hck, cv + hcv], axis=1).astype(BF)
-        kvs = gathered(jnp.concatenate([near, far], axis=0))
-        parts, stats = forward(idx, tiles, text_sees, queries, grad_out, kvs)
+        own_k, c_k, h_k, hc_k, own_v, c_v, h_v, hc_v = project(
+            idx, tile_image, image_feats, key_weight, value_weight
+        )
+        h_v, hc_v, c_v = to_h(h_v), to_hc(hc_v), to_c(c_v)
+        h_k, hc_k, c_k = to_h(h_k), to_hc(hc_k), to_c(c_k)
+        rows = h_v.shape[0]
+        others = c_v[rows, : tile_image.shape[0]].astype(jnp.int32)
+        tiles = jnp.stack([tile_image, others])
+
+        def owned(own, h, c, hc):
+            near = own + h.astype(F32)
+            far = c[:rows].astype(F32) + hc.astype(F32)
+            return jnp.concatenate([near.astype(BF), far.astype(BF)], axis=0)
+
+        values = gathered(owned(own_v, h_v, c_v, hc_v))
+        keys = gathered(owned(own_k, h_k, c_k, hc_k))
+        parts, stats = forward(idx, tiles, text_sees, queries, grad_out, keys, values)
         stats = swap8(stats)
         parts = swap8(parts)
 
+        keys = [in_hbm(x) for x in keys]
+        values = [in_hbm(x) for x in values]
+
         def grads(chunks, *more):
-            return backward(idx, tiles, text_sees, queries, grad_out, kvs, stats, chunks, *more)
-
-        (second,) = grads((2,))
-        (first,) = grads((1,))
+            return backward(idx, tiles, text_sees, queries, grad_out, keys, values, stats, chunks, *more)
+
+        second, first = grads((2, 1))
         third, total, merged = grads((3, 0), parts)
         far = [to_t[2](second), to_t[1](first), to_t[3](third)]
         mine = swap8(merged).reshape(queries.shape[0], -1)

time: 107 us -> 103 us (0.963)
  waiting for transfers between devices: 28.6 us -> 17.7 us
  starting transfers between devices: 30.5 us -> 37.5 us
  local copies, waits for them, and re-layouts: 1.94 us -> 0.72 us
    ppermute x14 -> x19, waiting for transfers between devices: 23.5 us -> 12.6 us  [moved(): return lambda x: lax.ppermute(x, AXES, pairs)]
    ppermute x14 -> x19, starting transfers between devices: 21.9 us -> 28.9 us  [moved(): return lambda x: lax.ppermute(x, AXES, pairs)]
    unnamed x16 -> x24, local copies, waits for them, and re-layouts: 1.93 us -> 0.7 us
    pallas_call x3 -> x2, Pallas kernels: 13.3 us -> 13.8 us  [backward(): pl.pallas_call(body, out_shape=out_shape, grid_spec=pltpu.PrefetchScalarG...]
  transfers between devices with their start and end apart: 16 -> 21, of which waited for: 9 -> 11; matrix products, arithmetic and copies ran while one was open for 1% -> 1% of each run, Pallas kernels for 16% -> 17%
where the time goes in v5:
time: 103 us
  starting transfers between devices  37.5 us (36%)
  Pallas kernels  33.8 us (33%)
  waiting for transfers between devices  17.7 us (17%)
  blocking collectives  10.8 us (10%)
  other arithmetic  1.35 us (1%)
    ppermute x19, starting transfers between devices, moved(): return lambda x: lax.ppermute(x, AXES, pairs)  28.9 us
    pallas_call x2, Pallas kernels, backward(): pl.pallas_call(body, out_shape=out_shape, grid_spec=pltpu.PrefetchScalarG...  13.8 us
    ppermute x19, waiting for transfers between devices, moved(): return lambda x: lax.ppermute(x, AXES, pairs)  12.6 us
    all_to_all x1, blocking collectives, swap8(): return lax.all_to_all(x, 'img', 0, 0, axis_index_groups=chips, tiled=True)  10.8 us
    all_to_all x2, starting transfers between devices, swap8(): return lax.all_to_all(x, 'img', 0, 0, axis_index_groups=chips, tiled=True)  8.57 us
    pallas_call x1, Pallas kernels, forward(): pl.pallas_call(body, out_shape=(jax.ShapeDtypeStruct((8, share, width), B...  7.72 us
    pallas_call x1, Pallas kernels, project(): pl.pallas_call(body, out_shape=outs, grid_spec=pltpu.PrefetchScalarGridSp...  5.28 us
    all_to_all x2, waiting for transfers between devices, swap8(): return lax.all_to_all(x, 'img', 0, 0, axis_index_groups=chips, tiled=True)  5.16 us
  transfers between devices with their start and end apart: 21, of which 11 were waited for; matrix products, arithmetic and copies ran while one was open for 1% of the time, Pallas kernels for 17%

profile of v5, /device:TPU:1, one launch (start us, length us, event | category | flops | bytes accessed | tf_op | source)
XLA Modules:
  0.0 102.9 jit_solution(5683481579437773933)
XLA Ops:
  0.6 0.1 pad_add_fusion.1.ix
  0.7 0.7 copy-done.2
  1.4 5.3 %project.1 = (f32[256,128]{1,0:T(8,128)S(1)}, f32[256,128]{1,0:T(8,128)S(1)}, f32[256,128]{1,0:T(8,128)S(1)}, f32[256,128]{1,0:T(8,128)S(1)}, f32[256,128]{1,0:T...) custom-call(s32[4]{0:T(128)S(1)} %pad_add_fusion.1.ix, ...), custom_call_target="tpu_custom_call" | custom-call | flops 4400000000 | bytes 65536 | tf_op jit(solution)/shard_map/project/pallas_call | solution.py:106
  6.7 4.5 %collective-permute-start.7 = (bf16[256,128]{1,0:T(8,128)(2,1)S(1)}, bf16[256,128]{1,0:T(8,128)(2,1)S(1)}, u32[]{:S(2)}, u32[]{:S(2)}) collective-permute-start(bf16[256,128]{1,0:T(8,128)(2,1)S(1)} %get-tuple-element.27), channel_id=1, source_target_pairs={{0,4},{1,5},{2,6},{3,7},{4,0},{5,1},{6,2},{7,3},{8,12},{9,13},{10,... | collective-permute-start | bytes 196616 | tf_op jit(solution)/shard_map/ppermute | solution.py:39
  11.2 0.7 collective-permute-start.8
  11.8 0.3 collective-permute-start
  12.1 2.9 %collective-permute-start.1 = (f32[256,128]{1,0:T(8,128)S(1)}, f32[256,128]{1,0:T(8,128)S(1)}, u32[]{:S(2)}, u32[]{:S(2)}) collective-permute-start(f32[256,128]{1,0:T(8,128)S(1)} %get-tuple-element.23), channel_id=1, source_target_pairs={{0,4},{1,5},{2,6},{3,7},{4,0},{5,1},{6,2},{7,3},{8,12},{9,13},{10,... | collective-permute-start | bytes 393224 | tf_op jit(solution)/shard_map/ppermute | solution.py:39
  15.0 0.8 collective-permute-start.2
  15.8 0.0 collective-permute-done.7
  15.8 2.0 %collective-permute-start.3 = (f32[256,128]{1,0:T(8,128)S(1)}, f32[256,128]{1,0:T(8,128)S(1)}, u32[]{:S(2)}, u32[]{:S(2)}) collective-permute-start(f32[256,128]{1,0:T(8,128)S(1)} %get-tuple-element.25), channel_id=1, source_target_pairs={{0,12},{1,13},{2,14},{3,15},{4,8},{5,9},{6,10},{7,11},{8,4},{9,5},... | collective-permute-start | bytes 393224 | tf_op jit(solution)/shard_map/ppermute | solution.py:39
  17.8 0.0 collective-permute-done.8
  17.8 0.0 collective-permute-done
  17.9 0.0 copy-start
  17.9 2.8 %collective-permute-start.11 = (bf16[512,128]{1,0:T(8,128)(2,1)S(1)}, bf16[512,128]{1,0:T(8,128)(2,1)S(1)}, u32[]{:S(2)}, u32[]{:S(2)}) collective-permute-start(bf16[512,128]{1,0:T(8,128)(2,1)S(1)} %pad_maximum_fusion.1.v0.refs_3_), channel_id=1, source_target_pairs={{0,3},{1,2},{2,1},{3,0},{4,7},{5,6},{6,5},{7,4},{8,11},{9,10},{10,... | collective-permute-start | bytes 393224 | tf_op jit(solution)/shard_map/ppermute | solution.py:39
  20.7 0.3 collective-permute-start.10
  21.1 0.0 collective-permute-done.1
  21.1 0.3 collective-permute-start.9
  21.4 0.0 collective-permute-done.2
  21.4 1.3 %collective-permute-done.3 = f32[256,128]{1,0:T(8,128)S(1)} collective-permute-done((f32[256,128]{1,0:T(8,128)S(1)}, f32[256,128]{1,0:T(8,128)S(1)}, u32[]{:S(2)}, u32[]{:S(2)}) %collective-permute-start.3) | collective-permute-done | bytes 131104 | tf_op jit(solution)/shard_map/ppermute | solution.py:39
  22.7 0.0 copy-start.1
  22.8 2.8 %collective-permute-start.6 = (bf16[512,128]{1,0:T(8,128)(2,1)S(1)}, bf16[512,128]{1,0:T(8,128)(2,1)S(1)}, u32[]{:S(2)}, u32[]{:S(2)}) collective-permute-start(bf16[512,128]{1,0:T(8,128)(2,1)S(1)} %pad_maximum_fusion.k0.refs_1_), channel_id=1, source_target_pairs={{0,3},{1,2},{2,1},{3,0},{4,7},{5,6},{6,5},{7,4},{8,11},{9,10},{10,... | collective-permute-start | bytes 393224 | tf_op jit(solution)/shard_map/ppermute | solution.py:39
  25.6 0.3 collective-permute-start.5
  25.9 0.3 collective-permute-done.11.v3.refs_2_
  26.2 0.0 collective-permute-start.4
  26.3 0.5 collective-permute-done.10.v2.refs_2_
  26.8 0.7 collective-permute-done.9.v1.refs_3_
  27.5 4.4 %collective-permute-done.6.k3.refs_0_ = bf16[512,128]{1,0:T(8,128)(2,1)S(1)} collective-permute-done((bf16[512,128]{1,0:T(8,128)(2,1)S(1)}, bf16[512,128]{1,0:T(8,128)(2,1)S(1)}, u32[]{:S(2)}, u32[]{:S(2)}) %collective-permute-start.6) | collective-permute-done | bytes 131104 | tf_op jit(solution)/shard_map/ppermute | solution.py:39
  31.9 0.8 collective-permute-done.5.k2.refs_0_
  32.7 0.5 collective-permute-done.4.k1.refs_1_
  33.2 0.0 copy-done.3
  33.2 0.0 copy-done.4
  33.2 0.0 copy-done.11
  33.2 0.0 copy-start.10
  33.2 7.7 %fwd.1 = (bf16[8,32,1024]{2,1,0:T(8,128)(2,1)}, f32[8,16,256]{2,1,0:T(8,128)S(1)}) custom-call(s32[4]{0:T(128)S(1)} %pad_add_fusion.1.ix, s32[2,8]{1,0:T(2,128)S(1)} %pad_add_fusion.tl, s32[8,8]{1,0:T(8,128)S(1)} %copy-done.11, bf16[256,2048]{1,0:T(8,128)(2,1)S(1)} %copy-done.3, bf16[256,2048]{1,0:T(8,128)(2,1)S(1)} %copy-done.4, ...), custom_call_target="tpu_custom_call" | custom-call | flops 7699999744 | bytes 65536 | tf_op jit(solution)/shard_map/fwd/pallas_call | solution.py:189
  40.9 0.0 copy-done
  40.9 0.0 copy-done.6
  40.9 0.0 copy-done.8
  40.9 0.0 copy-done.7
  40.9 0.0 copy-done.9
  41.0 0.0 copy-done.10
  41.0 10.8 %all_to_all.15.st = f32[8,16,256]{2,1,0:T(8,128)S(1)} all-to-all(f32[8,16,256]{2,1,0:T(8,128)S(1)} %get-tuple-element.29), channel_id=1, replica_groups={{0,16,32,48,64,80,96,112},{8,24,40,56,72,88,104,120},{1,17,33,49,65,81,..., dimensions={0} | all-to-all | bytes 262144 | tf_op jit(solution)/shard_map/all_to_all | solution.py:435
  51.7 3.7 %all-to-all-start.1 = ((bf16[8,32,1024]{2,1,0:T(8,128)(2,1)}), bf16[8,32,1024]{2,1,0:T(8,128)(2,1)S(1)}, u32[]{:S(2)}, u32[]{:S(2)}) async-start(bf16[8,32,1024]{2,1,0:T(8,128)(2,1)} %get-tuple-element.30), calls=%async_computation.1 | async-start | bytes 1048576 | tf_op jit(solution)/shard_map/all_to_all | solution.py:435
  55.4 7.0 %grads21.1 = (bf16[512,256]{1,0:T(8,128)(2,1)}, bf16[512,256]{1,0:T(8,128)(2,1)}) custom-call(s32[4]{0:T(128)S(1)} %pad_add_fusion.1.ix, s32[2,8]{1,0:T(2,128)S(1)} %pad_add_fusion.tl, s32[8,8]{1,0:T(8,128)S(1)} %copy-done.11, bf16[256,2048]{1,0:T(8,128)(2,1)S(1)} %copy-done.3, bf16[256,2048]{1,0:T(8,128)(2,1)S(1)} %copy-done.4, ...), custom_call_target="tpu_custom_call" | custom-call | flops 6600000000 | bytes 65536 | tf_op jit(solution)/shard_map/grads21/pallas_call | solution.py:310
  62.4 2.6 %collective-permute-start.12 = (bf16[512,256]{1,0:T(8,128)(2,1)}, bf16[512,256]{1,0:T(8,128)(2,1)}, u32[]{:S(2)}, u32[]{:S(2)}) collective-permute-start(bf16[512,256]{1,0:T(8,128)(2,1)} %get-tuple-element.32), channel_id=1, source_target_pairs={{0,2},{1,3},{2,0},{3,1},{4,6},{5,7},{6,4},{7,5},{8,10},{9,11},{10,... | collective-permute-start | bytes 786440 | tf_op jit(solution)/shard_map/ppermute | solution.py:39
  64.9 0.4 collective-permute-start.13
  65.3 0.0 all-to-all-done.1.refs_4_
  65.3 6.8 %grads30.1 = (bf16[512,256]{1,0:T(8,128)(2,1)}, f32[512,256]{1,0:T(8,128)S(1)}, bf16[8,32,1024]{2,1,0:T(8,128)(2,1)}) custom-call(s32[4]{0:T(128)S(1)} %pad_add_fusion.1.ix, s32[2,8]{1,0:T(2,128)S(1)} %pad_add_fusion.tl, s32[8,8]{1,0:T(8,128)S(1)} %copy-done.11, bf16[256,2048]{1,0:T(8,128)(2,1)S(1)} %copy-done.3, bf16[256,2048]{1,0:T(8,128)(2,1)S(1)} %copy-done.4, ...), custom_call_target="tpu_custom_call" | custom-call | flops 6600000000 | bytes 65536 | tf_op jit(solution)/shard_map/grads30/pallas_call | solution.py:310
  72.2 0.5 collective-permute-start.14
  72.6 4.9 %all-to-all-start.2 = ((bf16[8,32,1024]{2,1,0:T(8,128)(2,1)}), bf16[8,32,1024]{2,1,0:T(8,128)(2,1)S(1)}, u32[]{:S(2)}, u32[]{:S(2)}) async-start(bf16[8,32,1024]{2,1,0:T(8,128)(2,1)} %get-tuple-element.37), calls=%async_computation.2 | async-start | bytes 1048576 | tf_op jit(solution)/shard_map/all_to_all | solution.py:435
  77.5 0.0 collective-permute-done.12
  77.5 0.0 collective-permute-done.13
  77.6 1.3 %collective-permute-done.14 = bf16[512,256]{1,0:T(8,128)(2,1)S(1)} collective-permute-done((bf16[512,256]{1,0:T(8,128)(2,1)}, bf16[512,256]{1,0:T(8,128)(2,1)S(1)}, u32[]{:S(2)}, u32[]{:S(2)}) %collective-permute-start.14) | collective-permute-done | bytes 262176 | tf_op jit(solution)/shard_map/ppermute | solution.py:39
  78.8 1.2 %add_convert_fusion._ = bf16[512,256]{1,0:T(8,128)(2,1)S(1)} fusion(bf16[512,256]{1,0:T(8,128)(2,1)S(1)} %collective-permute-done.14, bf16[512,256]{1,0:T(8,128)(2,1)} %collective-permute-done.13, f32[512,256]{1,0:T(8,128)S(1)} %get-tuple-element.31, bf16[512,256]{1,0:T(8,128)(2,1)} %collective-permute-done.12), kind=kLoop, calls=%fused_computation | loop fusion | flops 917504 | bytes 1572864 | tf_op jit(solution)/shard_map/convert_element_type | solution.py:476
  80.0 5.2 %all-to-all-done.2 = bf16[8,32,1024]{2,1,0:T(8,128)(2,1)S(1)} async-done(((bf16[8,32,1024]{2,1,0:T(8,128)(2,1)}), bf16[8,32,1024]{2,1,0:T(8,128)(2,1)S(1)}, u32[]{:S(2)}, u32[]{:S(2)}) %all-to-all-start.2) | async-done | bytes 524320 | tf_op jit(solution)/shard_map/all_to_all | solution.py:435
  85.1 4.3 %collective-permute-start.18 = (bf16[256,1024]{1,0:T(8,128)(2,1)S(1)}, bf16[256,1024]{1,0:T(8,128)(2,1)S(1)}, u32[]{:S(2)}, u32[]{:S(2)}) collective-permute-start(bf16[256,1024]{1,0:T(8,128)(2,1)S(1)} %bitcast.6), channel_id=1, source_target_pairs={{0,8},{1,9},{2,10},{3,11},{4,12},{5,13},{6,14},{7,15},{8,0},{9,1},... | collective-permute-start | bytes 1572872 | tf_op jit(solution)/shard_map/ppermute | solution.py:39
  89.5 2.1 %collective-permute-start.17 = (bf16[256,256]{1,0:T(8,128)(2,1)S(1)}, bf16[256,256]{1,0:T(8,128)(2,1)S(1)}, u32[]{:S(2)}, u32[]{:S(2)}) collective-permute-start(bf16[256,256]{1,0:T(8,128)(2,1)S(1)} %get-tuple-element.40), channel_id=1, source_target_pairs={{0,12},{1,13},{2,14},{3,15},{4,8},{5,9},{6,10},{7,11},{8,4},{9,5},... | collective-permute-start | bytes 393224 | tf_op jit(solution)/shard_map/ppermute | solution.py:39
  91.5 0.5 collective-permute-start.15
  92.0 0.9 collective-permute-start.16
  92.9 3.3 %fetch.1 = (bf16[3840,512]{1,0:T(8,128)(2,1)S(1)}, bf16[3840,512]{1,0:T(8,128)(2,1)S(1)}) custom-call(bf16[3840,512]{1,0:T(8,128)(2,1)} %k_hbm.1, bf16[3840,512]{1,0:T(8,128)(2,1)} %v_hbm.1, bf16[512,256]{1,0:T(8,128)(2,1)S(1)} %add_convert_fusion._), custom_call_target="tpu_custom_call" | custom-call | flops 4400000000 | bytes 65536 | tf_op jit(solution)/shard_map/fetch/pallas_call | solution.py:344
  96.2 0.1 collective-permute-done.17.d_
  96.3 0.0 collective-permute-done.15.b
  96.3 2.7 %collective-permute-done.16.c_ = bf16[256,256]{1,0:T(8,128)(2,1)S(1)} collective-permute-done((bf16[256,256]{1,0:T(8,128)(2,1)S(1)}, bf16[256,256]{1,0:T(8,128)(2,1)S(1)}, u32[]{:S(2)}, u32[]{:S(2)}) %collective-permute-start.16) | collective-permute-done | bytes 131104 | tf_op jit(solution)/shard_map/ppermute | solution.py:39
  99.0 0.0 collective-permute-done.18.t_ref
  99.0 3.7 %feats.1 = (bf16[256,3840]{1,0:T(8,128)(2,1)}, bf16[256,2048]{1,0:T(8,128)(2,1)}) custom-call(s32[4]{0:T(128)S(1)} %pad_add_fusion.1.ix, bf16[256,256]{1,0:T(8,128)(2,1)S(1)} %get-tuple-element.41.a, bf16[256,256]{1,0:T(8,128)(2,1)S(1)} %collective-permute-done.15.b, bf16[256,256]{1,0:T(8,128)(2,1)S(1)} %collective-permute-done.16.c_, ...), custom_call_target="tpu_custom_call" | custom-call | flops 4400000000 | bytes 65536 | tf_op jit(solution)/shard_map/feats/pallas_call | solution.py:403
  (20 shorter events, 0.2 us)
Async XLA Ops:
  0.7 0.7 copy-start.2
  1.4 31.8 %copy-start.3 = (bf16[256,2048]{1,0:T(8,128)(2,1)S(1)}, bf16[256,2048]{1,0:T(8,128)(2,1)}, u32[]{:S(2)}) copy-start(bf16[256,2048]{1,0:T(8,128)(2,1)} %q.5) | copy-start | bytes 3145732
  1.4 31.8 %copy-start.4 = (bf16[256,2048]{1,0:T(8,128)(2,1)S(1)}, bf16[256,2048]{1,0:T(8,128)(2,1)}, u32[]{:S(2)}) copy-start(bf16[256,2048]{1,0:T(8,128)(2,1)} %g.5) | copy-start | bytes 3145732
  1.4 31.8 %copy-start.11 = (s32[8,8]{1,0:T(8,128)S(1)}, s32[8,8]{1,0:T(8,128)}, u32[]{:S(2)}) copy-start(s32[8,8]{1,0:T(8,128)} %se.5) | copy-start | bytes 772
  6.7 9.1 %collective-permute-start.7 = (bf16[256,128]{1,0:T(8,128)(2,1)S(1)}, bf16[256,128]{1,0:T(8,128)(2,1)S(1)}, u32[]{:S(2)}, u32[]{:S(2)}) collective-permute-start(bf16[256,128]{1,0:T(8,128)(2,1)S(1)} %get-tuple-element.27), channel_id=1, source_target_pairs={{0,4},{1,5},{2,6},{3,7},{4,0},{5,1},{6,2},{7,3},{8,12},{9,13},{10,... | collective-permute-start | bytes 196616 | tf_op jit(solution)/shard_map/ppermute | solution.py:39
  11.2 6.6 %collective-permute-start.8 = (bf16[256,128]{1,0:T(8,128)(2,1)S(1)}, bf16[256,128]{1,0:T(8,128)(2,1)S(1)}, u32[]{:S(2)}, u32[]{:S(2)}) collective-permute-start(bf16[256,128]{1,0:T(8,128)(2,1)S(1)} %get-tuple-element.28), channel_id=1, source_target_pairs={{0,12},{1,13},{2,14},{3,15},{4,8},{5,9},{6,10},{7,11},{8,4},{9,5},... | collective-permute-start | bytes 196616 | tf_op jit(solution)/shard_map/ppermute | solution.py:39
  11.8 6.0 %collective-permute-start = (bf16[272,128]{1,0:T(8,128)(2,1)S(1)}, bf16[272,128]{1,0:T(8,128)(2,1)S(1)}, u32[]{:S(2)}, u32[]{:S(2)}) collective-permute-start(bf16[272,128]{1,0:T(8,128)(2,1)S(1)} %get-tuple-element.21), channel_id=1, source_target_pairs={{0,8},{1,9},{2,10},{3,11},{4,12},{5,13},{6,14},{7,15},{8,0},{9,1},... | collective-permute-start | bytes 208904 | tf_op jit(solution)/shard_map/ppermute | solution.py:39
  12.1 8.9 %collective-permute-start.1 = (f32[256,128]{1,0:T(8,128)S(1)}, f32[256,128]{1,0:T(8,128)S(1)}, u32[]{:S(2)}, u32[]{:S(2)}) collective-permute-start(f32[256,128]{1,0:T(8,128)S(1)} %get-tuple-element.23), channel_id=1, source_target_pairs={{0,4},{1,5},{2,6},{3,7},{4,0},{5,1},{6,2},{7,3},{8,12},{9,13},{10,... | collective-permute-start | bytes 393224 | tf_op jit(solution)/shard_map/ppermute | solution.py:39
  15.0 6.4 %collective-permute-start.2 = (f32[256,128]{1,0:T(8,128)S(1)}, f32[256,128]{1,0:T(8,128)S(1)}, u32[]{:S(2)}, u32[]{:S(2)}) collective-permute-start(f32[256,128]{1,0:T(8,128)S(1)} %get-tuple-element.24), channel_id=1, source_target_pairs={{0,8},{1,9},{2,10},{3,11},{4,12},{5,13},{6,14},{7,15},{8,0},{9,1},... | collective-permute-start | bytes 393224 | tf_op jit(solution)/shard_map/ppermute | solution.py:39
  15.8 6.9 %collective-permute-start.3 = (f32[256,128]{1,0:T(8,128)S(1)}, f32[256,128]{1,0:T(8,128)S(1)}, u32[]{:S(2)}, u32[]{:S(2)}) collective-permute-start(f32[256,128]{1,0:T(8,128)S(1)} %get-tuple-element.25), channel_id=1, source_target_pairs={{0,12},{1,13},{2,14},{3,15},{4,8},{5,9},{6,10},{7,11},{8,4},{9,5},... | collective-permute-start | bytes 393224 | tf_op jit(solution)/shard_map/ppermute | solution.py:39
  17.9 23.0 %copy-start = (bf16[512,128]{1,0:T(8,128)(2,1)}, bf16[512,128]{1,0:T(8,128)(2,1)S(1)}, u32[]{:S(2)}) copy-start(bf16[512,128]{1,0:T(8,128)(2,1)S(1)} %pad_maximum_fusion.1.v0.refs_3_) | copy-start | bytes 393220
  17.9 8.4 %collective-permute-start.11 = (bf16[512,128]{1,0:T(8,128)(2,1)S(1)}, bf16[512,128]{1,0:T(8,128)(2,1)S(1)}, u32[]{:S(2)}, u32[]{:S(2)}) collective-permute-start(bf16[512,128]{1,0:T(8,128)(2,1)S(1)} %pad_maximum_fusion.1.v0.refs_3_), channel_id=1, source_target_pairs={{0,3},{1,2},{2,1},{3,0},{4,7},{5,6},{6,5},{7,4},{8,11},{9,10},{10,... | collective-permute-start | bytes 393224 | tf_op jit(solution)/shard_map/ppermute | solution.py:39
  20.7 6.1 %collective-permute-start.10 = (bf16[512,128]{1,0:T(8,128)(2,1)S(1)}, bf16[512,128]{1,0:T(8,128)(2,1)S(1)}, u32[]{:S(2)}, u32[]{:S(2)}) collective-permute-start(bf16[512,128]{1,0:T(8,128)(2,1)S(1)} %pad_maximum_fusion.1.v0.refs_3_), channel_id=1, source_target_pairs={{0,2},{1,3},{2,0},{3,1},{4,6},{5,7},{6,4},{7,5},{8,10},{9,11},{10,... | collective-permute-start | bytes 393224 | tf_op jit(solution)/shard_map/ppermute | solution.py:39
  21.1 6.5 %collective-permute-start.9 = (bf16[512,128]{1,0:T(8,128)(2,1)S(1)}, bf16[512,128]{1,0:T(8,128)(2,1)S(1)}, u32[]{:S(2)}, u32[]{:S(2)}) collective-permute-start(bf16[512,128]{1,0:T(8,128)(2,1)S(1)} %pad_maximum_fusion.1.v0.refs_3_), channel_id=1, source_target_pairs={{0,1},{1,0},{2,3},{3,2},{4,5},{5,4},{6,7},{7,6},{8,9},{9,8},{10,11... | collective-permute-start | bytes 393224 | tf_op jit(solution)/shard_map/ppermute | solution.py:39
  22.7 18.2 %copy-start.1 = (bf16[512,128]{1,0:T(8,128)(2,1)}, bf16[512,128]{1,0:T(8,128)(2,1)S(1)}, u32[]{:S(2)}) copy-start(bf16[512,128]{1,0:T(8,128)(2,1)S(1)} %pad_maximum_fusion.k0.refs_1_) | copy-start | bytes 393220
  22.8 9.1 %collective-permute-start.6 = (bf16[512,128]{1,0:T(8,128)(2,1)S(1)}, bf16[512,128]{1,0:T(8,128)(2,1)S(1)}, u32[]{:S(2)}, u32[]{:S(2)}) collective-permute-start(bf16[512,128]{1,0:T(8,128)(2,1)S(1)} %pad_maximum_fusion.k0.refs_1_), channel_id=1, source_target_pairs={{0,3},{1,2},{2,1},{3,0},{4,7},{5,6},{6,5},{7,4},{8,11},{9,10},{10,... | collective-permute-start | bytes 393224 | tf_op jit(solution)/shard_map/ppermute | solution.py:39
  25.6 7.1 %collective-permute-start.5 = (bf16[512,128]{1,0:T(8,128)(2,1)S(1)}, bf16[512,128]{1,0:T(8,128)(2,1)S(1)}, u32[]{:S(2)}, u32[]{:S(2)}) collective-permute-start(bf16[512,128]{1,0:T(8,128)(2,1)S(1)} %pad_maximum_fusion.k0.refs_1_), channel_id=1, source_target_pairs={{0,2},{1,3},{2,0},{3,1},{4,6},{5,7},{6,4},{7,5},{8,10},{9,11},{10,... | collective-permute-start | bytes 393224 | tf_op jit(solution)/shard_map/ppermute | solution.py:39
  26.2 14.7 %copy-start.5 = (bf16[512,128]{1,0:T(8,128)(2,1)}, bf16[512,128]{1,0:T(8,128)(2,1)S(1)}, u32[]{:S(2)}) copy-start(bf16[512,128]{1,0:T(8,128)(2,1)S(1)} %collective-permute-done.11.v3.refs_2_) | copy-start | bytes 393220
  26.2 6.9 %collective-permute-start.4 = (bf16[512,128]{1,0:T(8,128)(2,1)S(1)}, bf16[512,128]{1,0:T(8,128)(2,1)S(1)}, u32[]{:S(2)}, u32[]{:S(2)}) collective-permute-start(bf16[512,128]{1,0:T(8,128)(2,1)S(1)} %pad_maximum_fusion.k0.refs_1_), channel_id=1, source_target_pairs={{0,1},{1,0},{2,3},{3,2},{4,5},{5,4},{6,7},{7,6},{8,9},{9,8},{10,11... | collective-permute-start | bytes 393224 | tf_op jit(solution)/shard_map/ppermute | solution.py:39
  26.8 14.1 %copy-start.6 = (bf16[512,128]{1,0:T(8,128)(2,1)}, bf16[512,128]{1,0:T(8,128)(2,1)S(1)}, u32[]{:S(2)}) copy-start(bf16[512,128]{1,0:T(8,128)(2,1)S(1)} %collective-permute-done.10.v2.refs_2_) | copy-start | bytes 393220
  27.5 13.4 %copy-start.8 = (bf16[512,128]{1,0:T(8,128)(2,1)}, bf16[512,128]{1,0:T(8,128)(2,1)S(1)}, u32[]{:S(2)}) copy-start(bf16[512,128]{1,0:T(8,128)(2,1)S(1)} %collective-permute-done.9.v1.refs_3_) | copy-start | bytes 393220
  31.9 9.1 %copy-start.7 = (bf16[512,128]{1,0:T(8,128)(2,1)}, bf16[512,128]{1,0:T(8,128)(2,1)S(1)}, u32[]{:S(2)}) copy-start(bf16[512,128]{1,0:T(8,128)(2,1)S(1)} %collective-permute-done.6.k3.refs_0_) | copy-start | bytes 393220
  32.6 8.3 %copy-start.9 = (bf16[512,128]{1,0:T(8,128)(2,1)}, bf16[512,128]{1,0:T(8,128)(2,1)S(1)}, u32[]{:S(2)}) copy-start(bf16[512,128]{1,0:T(8,128)(2,1)S(1)} %collective-permute-done.5.k2.refs_0_) | copy-start | bytes 393220
  33.2 7.8 %copy-start.10 = (bf16[512,128]{1,0:T(8,128)(2,1)}, bf16[512,128]{1,0:T(8,128)(2,1)S(1)}, u32[]{:S(2)}) copy-start(bf16[512,128]{1,0:T(8,128)(2,1)S(1)} %collective-permute-done.4.k1.refs_1_) | copy-start | bytes 393220
  51.7 13.6 %all-to-all-start.1 = ((bf16[8,32,1024]{2,1,0:T(8,128)(2,1)}), bf16[8,32,1024]{2,1,0:T(8,128)(2,1)S(1)}, u32[]{:S(2)}, u32[]{:S(2)}) async-start(bf16[8,32,1024]{2,1,0:T(8,128)(2,1)} %get-tuple-element.30), calls=%async_computation.1 | async-start | bytes 1048576 | tf_op jit(solution)/shard_map/all_to_all | solution.py:435
  62.4 15.2 %collective-permute-start.12 = (bf16[512,256]{1,0:T(8,128)(2,1)}, bf16[512,256]{1,0:T(8,128)(2,1)}, u32[]{:S(2)}, u32[]{:S(2)}) collective-permute-start(bf16[512,256]{1,0:T(8,128)(2,1)} %get-tuple-element.32), channel_id=1, source_target_pairs={{0,2},{1,3},{2,0},{3,1},{4,6},{5,7},{6,4},{7,5},{8,10},{9,11},{10,... | collective-permute-start | bytes 786440 | tf_op jit(solution)/shard_map/ppermute | solution.py:39
  64.9 12.6 %collective-permute-start.13 = (bf16[512,256]{1,0:T(8,128)(2,1)}, bf16[512,256]{1,0:T(8,128)(2,1)}, u32[]{:S(2)}, u32[]{:S(2)}) collective-permute-start(bf16[512,256]{1,0:T(8,128)(2,1)} %get-tuple-element.33), channel_id=1, source_target_pairs={{0,1},{1,0},{2,3},{3,2},{4,5},{5,4},{6,7},{7,6},{8,9},{9,8},{10,11... | collective-permute-start | bytes 786440 | tf_op jit(solution)/shard_map/ppermute | solution.py:39
  72.2 6.6 %collective-permute-start.14 = (bf16[512,256]{1,0:T(8,128)(2,1)}, bf16[512,256]{1,0:T(8,128)(2,1)S(1)}, u32[]{:S(2)}, u32[]{:S(2)}) collective-permute-start(bf16[512,256]{1,0:T(8,128)(2,1)} %get-tuple-element.34), channel_id=1, source_target_pairs={{0,3},{1,2},{2,1},{3,0},{4,7},{5,6},{6,5},{7,4},{8,11},{9,10},{10,... | collective-permute-start | bytes 786440 | tf_op jit(solution)/shard_map/ppermute | solution.py:39
  72.6 12.5 %all-to-all-start.2 = ((bf16[8,32,1024]{2,1,0:T(8,128)(2,1)}), bf16[8,32,1024]{2,1,0:T(8,128)(2,1)S(1)}, u32[]{:S(2)}, u32[]{:S(2)}) async-start(bf16[8,32,1024]{2,1,0:T(8,128)(2,1)} %get-tuple-element.37), calls=%async_computation.2 | async-start | bytes 1048576 | tf_op jit(solution)/shard_map/all_to_all | solution.py:435
  85.1 13.8 %collective-permute-start.18 = (bf16[256,1024]{1,0:T(8,128)(2,1)S(1)}, bf16[256,1024]{1,0:T(8,128)(2,1)S(1)}, u32[]{:S(2)}, u32[]{:S(2)}) collective-permute-start(bf16[256,1024]{1,0:T(8,128)(2,1)S(1)} %bitcast.6), channel_id=1, source_target_pairs={{0,8},{1,9},{2,10},{3,11},{4,12},{5,13},{6,14},{7,15},{8,0},{9,1},... | collective-permute-start | bytes 1572872 | tf_op jit(solution)/shard_map/ppermute | solution.py:39
  89.5 6.8 %collective-permute-start.17 = (bf16[256,256]{1,0:T(8,128)(2,1)S(1)}, bf16[256,256]{1,0:T(8,128)(2,1)S(1)}, u32[]{:S(2)}, u32[]{:S(2)}) collective-permute-start(bf16[256,256]{1,0:T(8,128)(2,1)S(1)} %get-tuple-element.40), channel_id=1, source_target_pairs={{0,12},{1,13},{2,14},{3,15},{4,8},{5,9},{6,10},{7,11},{8,4},{9,5},... | collective-permute-start | bytes 393224 | tf_op jit(solution)/shard_map/ppermute | solution.py:39
  91.5 4.8 %collective-permute-start.15 = (bf16[256,256]{1,0:T(8,128)(2,1)S(1)}, bf16[256,256]{1,0:T(8,128)(2,1)S(1)}, u32[]{:S(2)}, u32[]{:S(2)}) collective-permute-start(bf16[256,256]{1,0:T(8,128)(2,1)S(1)} %get-tuple-element.40), channel_id=1, source_target_pairs={{0,8},{1,9},{2,10},{3,11},{4,12},{5,13},{6,14},{7,15},{8,0},{9,1},... | collective-permute-start | bytes 393224 | tf_op jit(solution)/shard_map/ppermute | solution.py:39
  92.0 6.9 %collective-permute-start.16 = (bf16[256,256]{1,0:T(8,128)(2,1)S(1)}, bf16[256,256]{1,0:T(8,128)(2,1)S(1)}, u32[]{:S(2)}, u32[]{:S(2)}) collective-permute-start(bf16[256,256]{1,0:T(8,128)(2,1)S(1)} %get-tuple-element.41.a), channel_id=1, source_target_pairs={{0,4},{1,5},{2,6},{3,7},{4,0},{5,1},{6,2},{7,3},{8,12},{9,13},{10,... | collective-permute-start | bytes 393224 | tf_op jit(solution)/shard_map/ppermute | solution.py:39

commit v6 on v5

--- a/solution.py
+++ b/solution.py
@@ -52,13 +52,13 @@
     return pltpu.with_memory_space_constraint(x, pltpu.HBM)
 
 
-def project(idx, tiles, feats, key_weight, value_weight):
+def project(idx, count, feats, key_weight, value_weight):
     rows, feat = feats.shape
     cols = key_weight.shape[1]
     steps = 5
     chunk = feat // steps
 
-    def body(ix, tl, x_hbm, wk_hbm, wv_hbm, k0, kc, kh, khc, v0, vc, vh, vhc, x, wk, wv, acc, sems):
+    def body(ix, x_hbm, wk_hbm, wv_hbm, k0, kc, kh, khc, v0, vc, vh, vhc, x, wk, wv, acc, sems):
         copies = []
         for s in range(steps):
             at = slice(s * chunk, (s + 1) * chunk)
@@ -94,8 +94,8 @@
                 ref[:rows, :] = piece(which, hh, cc).astype(ref.dtype)
         lane = lax.broadcasted_iota(jnp.int32, (extra, HD), 1)
         ids = jnp.zeros((extra, HD), F32)
-        for e in range(tiles.shape[0]):
-            ids = jnp.where(lane == e, tl[e].astype(F32), ids)
+        for e in range(count):
+            ids = jnp.where(lane == e, ix[4 + e].astype(F32), ids)
         vc[rows:, :] = ids.astype(BF)
 
     extra = 16
@@ -107,7 +107,7 @@
         body,
         out_shape=outs,
         grid_spec=pltpu.PrefetchScalarGridSpec(
-            num_scalar_prefetch=2,
+            num_scalar_prefetch=1,
             grid=(1,),
             in_specs=[pl.BlockSpec(memory_space=pltpu.HBM)] * 3,
             out_specs=[spec(o.shape) for o in outs],
@@ -122,7 +122,7 @@
         compiler_params=pltpu.CompilerParams(vmem_limit_bytes=24 << 20),
         name="project",
         cost_estimate=cost(4),
-    )(idx, tiles, in_hbm(feats), in_hbm(key_weight), in_hbm(value_weight))
+    )(idx, in_hbm(feats), in_hbm(key_weight), in_hbm(value_weight))
 
 
 def tile_cap(ix, tiles, sees, block, chunk, tile):
@@ -356,27 +356,25 @@
     )(in_hbm(key_weight), in_hbm(value_weight), token)
 
 
-def feature_grad(idx, own, oc, oh, ohc, key_weight, value_weight, mine, theirs):
+def feature_grad(idx, own, oc, oh, ohc, key_weight, value_weight, mine):
     rows = own.shape[0]
     feat, cols = key_weight.shape
     steps = 5
     chunk = feat // steps
     half = mine.shape[1]
 
-    def body(ix, a, b, c_, d_, wk, wv, m_ref, t_ref, out_hbm, attn, both, out, sems):
+    def body(ix, a, b, c_, d_, wk, wv, m_ref, out_hbm, attn, both, out, sems):
         h = ix[0]
         c = ix[1]
 
-        def place(src, cc, s):
-            at = pl.multiple_of(cc * half, half)
-            return pltpu.make_async_copy(src, attn.at[:, pl.ds(at, half)], sems.at[1, s])
+        mine_at = attn.at[:, pl.ds(pl.multiple_of(c * half, half), half)]
+        place = pltpu.make_async_copy(m_ref, mine_at, sems.at[1, 0])
 
         def store(s):
             at = slice(s * chunk, (s + 1) * chunk)
             return pltpu.make_async_copy(out.at[s], out_hbm.at[:, at], sems.at[0, s])
 
-        place(m_ref, c, 0).start()
-        place(t_ref, 1 - c, 1).start()
+        place.start()
 
         def put(hh, cc, x):
             at = pl.multiple_of((hh * 2 + cc) * HD, HD)
@@ -393,8 +391,7 @@
             store(s).start()
         for s in range(steps):
             store(s).wait()
-        place(m_ref, c, 0).wait()
-        place(t_ref, 1 - c, 1).wait()
+        place.wait()
 
     piece = spec((rows, 2 * HD))
     hbm = pl.BlockSpec(memory_space=pltpu.HBM)
@@ -409,7 +406,7 @@
         grid_spec=pltpu.PrefetchScalarGridSpec(
             num_scalar_prefetch=1,
             grid=(1,),
-            in_specs=[piece] * 4 + [vmem] * 2 + [anywhere] * 2,
+            in_specs=[piece] * 4 + [vmem] * 2 + [anywhere],
             out_specs=[hbm, hbm],
             scratch_shapes=[
                 pltpu.VMEM((2, rows, cols), BF),
@@ -420,7 +417,33 @@
         compiler_params=pltpu.CompilerParams(vmem_limit_bytes=8 << 20),
         name="feats",
         cost_estimate=cost(4),
-    )(idx, own, oc, oh, ohc, key_weight, value_weight, mine, theirs)
+    )(idx, own, oc, oh, ohc, key_weight, value_weight, mine)
+
+
+def add_theirs(idx, attn, theirs):
+    half = theirs.shape[1]
+
+    def body(ix, _, t_ref, out, sem):
+        at = pl.multiple_of((1 - ix[1]) * half, half)
+        copy = pltpu.make_async_copy(t_ref, out.at[:, pl.ds(at, half)], sem)
+        copy.start()
+        copy.wait()
+
+    hbm = pl.BlockSpec(memory_space=pltpu.HBM)
+    return pl.pallas_call(
+        body,
+        out_shape=jax.ShapeDtypeStruct(attn.shape, BF),
+        grid_spec=pltpu.PrefetchScalarGridSpec(
+            num_scalar_prefetch=1,
+            grid=(1,),
+            in_specs=[hbm, pl.BlockSpec(memory_space=pl.ANY)],
+            out_specs=hbm,
+            scratch_shapes=[pltpu.SemaphoreType.DMA],
+        ),
+        input_output_aliases={1: 0},
+        compiler_params=pltpu.CompilerParams(vmem_limit_bytes=1 << 20),
+        name="theirs",
+    )(idx, attn, theirs)
 
 
 def solution(mesh):
@@ -441,8 +464,9 @@
         img = lax.axis_index("img")
         core = img % 2
         idx = jnp.stack([lax.axis_index("head"), core, lax.axis_index("txt"), img // 2]).astype(jnp.int32)
+        idx = jnp.concatenate([idx, tile_image])
         own_k, c_k, h_k, hc_k, own_v, c_v, h_v, hc_v = project(
-            idx, tile_image, image_feats, key_weight, value_weight
+            idx, tile_image.shape[0], image_feats, key_weight, value_weight
         )
         h_v, hc_v, c_v = to_h(h_v), to_hc(hc_v), to_c(c_v)
         h_k, hc_k, c_k = to_h(h_k), to_hc(hc_k), to_c(c_k)
@@ -476,9 +500,14 @@
         total = total.astype(BF)
         rows = total.shape[0] // 2
         near, other = total[:rows], total[rows:]
-        pieces = near, to_c(other), to_h(near), to_hc(other)
+        side, ahead, across = to_c(other), to_h(near), to_hc(other)
         key_near, value_near = fetch_weights(key_weight, value_weight, total)
-        grad_feats, attn_out = feature_grad(idx, *pieces, key_near, value_near, mine, to_c(mine))
+        mine, side = lax.optimization_barrier((mine, side))
+        theirs = to_c(mine)
+        grad_feats, attn_out = feature_grad(
+            idx, near, side, ahead, across, key_near, value_near, mine
+        )
+        attn_out = add_theirs(idx, attn_out, theirs)
         return attn_out, grad_feats
 
     placed = (

time: 103 us -> 101 us (0.981)
  waiting for transfers between devices: 17.7 us -> 10.3 us
  starting transfers between devices: 37.5 us -> 42.6 us
  Pallas kernels: 33.8 us -> 35.2 us
  blocking collectives: 10.8 us -> 9.63 us
    all_to_all x2, waiting for transfers between devices: 5.16 us -> 0.01 us  [swap8(): return lax.all_to_all(x, 'img', 0, 0, axis_index_groups=chips, tiled=True)]
    ppermute x19, starting transfers between devices: 28.9 us -> 34 us  [moved(): return lambda x: lax.ppermute(x, AXES, pairs)]
    ppermute x19, waiting for transfers between devices: 12.6 us -> 10.3 us  [moved(): return lambda x: lax.ppermute(x, AXES, pairs)]
    pallas_call x0 -> x1, Pallas kernels: none -> 1.35 us  [add_theirs(): pl.pallas_call(body, out_shape=jax.ShapeDtypeStruct(attn.shape, BF), grid...]
    all_to_all x1, blocking collectives: 10.8 us -> 9.63 us  [swap8(): return lax.all_to_all(x, 'img', 0, 0, axis_index_groups=chips, tiled=True)]
  transfers between devices with their start and end apart: 21 -> 21, of which waited for: 11 -> 7; matrix products, arithmetic and copies ran while one was open for 1% -> 1% of each run, Pallas kernels for 17% -> 21%
where the time goes in v6:
time: 101 us
  starting transfers between devices  42.6 us (42%)
  Pallas kernels  35.2 us (35%)
  waiting for transfers between devices  10.3 us (10%)
  blocking collectives  9.63 us (10%)
  other arithmetic  1.26 us (1%)
  between operations  1.03 us (1%)
    ppermute x19, starting transfers between devices, moved(): return lambda x: lax.ppermute(x, AXES, pairs)  34 us
    pallas_call x2, Pallas kernels, backward(): pl.pallas_call(body, out_shape=out_shape, grid_spec=pltpu.PrefetchScalarG...  13.8 us
    ppermute x19, waiting for transfers between devices, moved(): return lambda x: lax.ppermute(x, AXES, pairs)  10.3 us
    all_to_all x1, blocking collectives, swap8(): return lax.all_to_all(x, 'img', 0, 0, axis_index_groups=chips, tiled=True)  9.63 us
    all_to_all x2, starting transfers between devices, swap8(): return lax.all_to_all(x, 'img', 0, 0, axis_index_groups=chips, tiled=True)  8.57 us
    pallas_call x1, Pallas kernels, forward(): pl.pallas_call(body, out_shape=(jax.ShapeDtypeStruct((8, share, width), B...  7.72 us
    pallas_call x1, Pallas kernels, project(): pl.pallas_call(body, out_shape=outs, grid_spec=pltpu.PrefetchScalarGridSp...  5.29 us
    pallas_call x1, Pallas kernels, feature_grad(): pl.pallas_call(body, out_shape=(jax.ShapeDtypeStruct((rows, feat), BF), j...  3.7 us
  transfers between devices with their start and end apart: 21, of which 7 were waited for; matrix products, arithmetic and copies ran while one was open for 1% of the time, Pallas kernels for 21%

profile of v6, /device:TPU:1, one launch (start us, length us, event | category | flops | bytes accessed | tf_op | source)
XLA Modules:
  0.0 100.9 jit_solution(5894623409914271325)
XLA Ops:
  0.6 0.7 concatenate.9.ix
  1.4 0.0 copy-start.10
  1.4 5.3 %project.1 = (f32[256,128]{1,0:T(8,128)S(1)}, f32[256,128]{1,0:T(8,128)S(1)}, f32[256,128]{1,0:T(8,128)S(1)}, f32[256,128]{1,0:T(8,128)S(1)}, f32[256,128]{1,0:T...) custom-call(s32[12]{0:T(128)S(1)} %concatenate.9.ix, ...), custom_call_target="tpu_custom_call" | custom-call | flops 4400000000 | bytes 65536 | tf_op jit(solution)/shard_map/project/pallas_call | solution.py:106
  6.7 4.5 %collective-permute-start.7 = (bf16[256,128]{1,0:T(8,128)(2,1)S(1)}, bf16[256,128]{1,0:T(8,128)(2,1)S(1)}, u32[]{:S(2)}, u32[]{:S(2)}) collective-permute-start(bf16[256,128]{1,0:T(8,128)(2,1)S(1)} %get-tuple-element.29), channel_id=1, source_target_pairs={{0,4},{1,5},{2,6},{3,7},{4,0},{5,1},{6,2},{7,3},{8,12},{9,13},{10,... | collective-permute-start | bytes 196616 | tf_op jit(solution)/shard_map/ppermute | solution.py:39
  11.2 1.0 collective-permute-start
  12.2 0.0 collective-permute-start.8
  12.2 2.9 %collective-permute-start.1 = (f32[256,128]{1,0:T(8,128)S(1)}, f32[256,128]{1,0:T(8,128)S(1)}, u32[]{:S(2)}, u32[]{:S(2)}) collective-permute-start(f32[256,128]{1,0:T(8,128)S(1)} %get-tuple-element.25), channel_id=1, source_target_pairs={{0,4},{1,5},{2,6},{3,7},{4,0},{5,1},{6,2},{7,3},{8,12},{9,13},{10,... | collective-permute-start | bytes 393224 | tf_op jit(solution)/shard_map/ppermute | solution.py:39
  15.0 0.8 collective-permute-start.2
  15.8 0.0 collective-permute-done.7
  15.8 2.3 %collective-permute-start.3 = (f32[256,128]{1,0:T(8,128)S(1)}, f32[256,128]{1,0:T(8,128)S(1)}, u32[]{:S(2)}, u32[]{:S(2)}) collective-permute-start(f32[256,128]{1,0:T(8,128)S(1)} %get-tuple-element.27), channel_id=1, source_target_pairs={{0,12},{1,13},{2,14},{3,15},{4,8},{5,9},{6,10},{7,11},{8,4},{9,5},... | collective-permute-start | bytes 393224 | tf_op jit(solution)/shard_map/ppermute | solution.py:39
  18.1 0.0 collective-permute-done.8
  18.1 0.0 collective-permute-done
  18.2 0.0 copy-start
  18.2 3.0 %collective-permute-start.10 = (bf16[512,128]{1,0:T(8,128)(2,1)S(1)}, bf16[512,128]{1,0:T(8,128)(2,1)S(1)}, u32[]{:S(2)}, u32[]{:S(2)}) collective-permute-start(bf16[512,128]{1,0:T(8,128)(2,1)S(1)} %pad_maximum_fusion.1.v0.refs_3_), channel_id=1, source_target_pairs={{0,2},{1,3},{2,0},{3,1},{4,6},{5,7},{6,4},{7,5},{8,10},{9,11},{10,... | collective-permute-start | bytes 393224 | tf_op jit(solution)/shard_map/ppermute | solution.py:39
  21.2 0.8 collective-permute-start.11
  21.9 0.0 collective-permute-done.1
  21.9 0.0 collective-permute-start.9
  22.0 0.0 collective-permute-done.2
  22.0 1.3 %collective-permute-done.3 = f32[256,128]{1,0:T(8,128)S(1)} collective-permute-done((f32[256,128]{1,0:T(8,128)S(1)}, f32[256,128]{1,0:T(8,128)S(1)}, u32[]{:S(2)}, u32[]{:S(2)}) %collective-permute-start.3) | collective-permute-done | bytes 131104 | tf_op jit(solution)/shard_map/ppermute | solution.py:39
  23.3 0.0 copy-start.1
  23.3 1.1 %collective-permute-start.4 = (bf16[512,128]{1,0:T(8,128)(2,1)S(1)}, bf16[512,128]{1,0:T(8,128)(2,1)S(1)}, u32[]{:S(2)}, u32[]{:S(2)}) collective-permute-start(bf16[512,128]{1,0:T(8,128)(2,1)S(1)} %pad_maximum_fusion.k0.refs_1_), channel_id=1, source_target_pairs={{0,1},{1,0},{2,3},{3,2},{4,5},{5,4},{6,7},{7,6},{8,9},{9,8},{10,11... | collective-permute-start | bytes 393224 | tf_op jit(solution)/shard_map/ppermute | solution.py:39
  24.4 2.9 %collective-permute-start.5 = (bf16[512,128]{1,0:T(8,128)(2,1)S(1)}, bf16[512,128]{1,0:T(8,128)(2,1)S(1)}, u32[]{:S(2)}, u32[]{:S(2)}) collective-permute-start(bf16[512,128]{1,0:T(8,128)(2,1)S(1)} %pad_maximum_fusion.k0.refs_1_), channel_id=1, source_target_pairs={{0,2},{1,3},{2,0},{3,1},{4,6},{5,7},{6,4},{7,5},{8,10},{9,11},{10,... | collective-permute-start | bytes 393224 | tf_op jit(solution)/shard_map/ppermute | solution.py:39
  27.3 0.0 collective-permute-done.10.v2.refs_2_
  27.3 0.4 collective-permute-start.6
  27.7 0.0 copy-done.11
  27.7 0.1 collective-permute-done.11.v3.refs_2_
  27.8 0.6 collective-permute-done.9.v1.refs_3_
  28.4 2.5 %collective-permute-done.4.k1.refs_1_ = bf16[512,128]{1,0:T(8,128)(2,1)S(1)} collective-permute-done((bf16[512,128]{1,0:T(8,128)(2,1)S(1)}, bf16[512,128]{1,0:T(8,128)(2,1)S(1)}, u32[]{:S(2)}, u32[]{:S(2)}) %collective-permute-start.4) | collective-permute-done | bytes 131104 | tf_op jit(solution)/shard_map/ppermute | solution.py:39
  31.0 3.3 %collective-permute-done.5.k2.refs_0_ = bf16[512,128]{1,0:T(8,128)(2,1)S(1)} collective-permute-done((bf16[512,128]{1,0:T(8,128)(2,1)S(1)}, bf16[512,128]{1,0:T(8,128)(2,1)S(1)}, u32[]{:S(2)}, u32[]{:S(2)}) %collective-permute-start.5) | collective-permute-done | bytes 131104 | tf_op jit(solution)/shard_map/ppermute | solution.py:39
  34.3 2.0 %collective-permute-done.6.k3.refs_0_ = bf16[512,128]{1,0:T(8,128)(2,1)S(1)} collective-permute-done((bf16[512,128]{1,0:T(8,128)(2,1)S(1)}, bf16[512,128]{1,0:T(8,128)(2,1)S(1)}, u32[]{:S(2)}, u32[]{:S(2)}) %collective-permute-start.6) | collective-permute-done | bytes 131104 | tf_op jit(solution)/shard_map/ppermute | solution.py:39
  36.3 0.0 copy-done.2
  36.3 0.0 copy-done.3
  36.3 0.0 copy-done.10
  36.3 0.0 copy-start.7
  36.4 7.7 %fwd.1 = (bf16[8,32,1024]{2,1,0:T(8,128)(2,1)}, f32[8,16,256]{2,1,0:T(8,128)S(1)}) custom-call(s32[12]{0:T(128)S(1)} %concatenate.9.ix, s32[2,8]{1,0:T(2,128)S(1)} %pad_add_fusion.tl, s32[8,8]{1,0:T(8,128)S(1)} %copy-done.10, bf16[256,2048]{1,0:T(8,128)(2,1)S(1)} %copy-done.2, bf16[256,2048]{1,0:T(8,128)(2,1)S(1)} %copy-done.3, ...), custom_call_target="tpu_custom_call" | custom-call | flops 7699999744 | bytes 65536 | tf_op jit(solution)/shard_map/fwd/pallas_call | solution.py:189
  44.1 0.0 copy-done
  44.1 0.0 copy-done.1
  44.1 0.0 copy-done.5
  44.1 0.0 copy-done.4
  44.1 9.6 %all_to_all.15.st = f32[8,16,256]{2,1,0:T(8,128)S(1)} all-to-all(f32[8,16,256]{2,1,0:T(8,128)S(1)} %get-tuple-element.31), channel_id=1, replica_groups={{0,16,32,48,64,80,96,112},{8,24,40,56,72,88,104,120},{1,17,33,49,65,81,..., dimensions={0} | all-to-all | bytes 262144 | tf_op jit(solution)/shard_map/all_to_all | solution.py:458
  53.8 3.7 %all-to-all-start.1 = ((bf16[8,32,1024]{2,1,0:T(8,128)(2,1)}), bf16[8,32,1024]{2,1,0:T(8,128)(2,1)S(1)}, u32[]{:S(2)}, u32[]{:S(2)}) async-start(bf16[8,32,1024]{2,1,0:T(8,128)(2,1)} %get-tuple-element.32), calls=%async_computation.1 | async-start | bytes 1048576 | tf_op jit(solution)/shard_map/all_to_all | solution.py:458
  57.4 7.0 %grads21.1 = (bf16[512,256]{1,0:T(8,128)(2,1)}, bf16[512,256]{1,0:T(8,128)(2,1)}) custom-call(s32[12]{0:T(128)S(1)} %concatenate.9.ix, s32[2,8]{1,0:T(2,128)S(1)} %pad_add_fusion.tl, s32[8,8]{1,0:T(8,128)S(1)} %copy-done.10, bf16[256,2048]{1,0:T(8,128)(2,1)S(1)} %copy-done.2, bf16[256,2048]{1,0:T(8,128)(2,1)S(1)} %copy-done.3, ...), custom_call_target="tpu_custom_call" | custom-call | flops 6600000000 | bytes 65536 | tf_op jit(solution)/shard_map/grads21/pallas_call | solution.py:310
  64.4 0.0 collective-permute-start.12
  64.4 1.1 %collective-permute-start.13 = (bf16[512,256]{1,0:T(8,128)(2,1)}, bf16[512,256]{1,0:T(8,128)(2,1)}, u32[]{:S(2)}, u32[]{:S(2)}) collective-permute-start(bf16[512,256]{1,0:T(8,128)(2,1)} %get-tuple-element.35), channel_id=1, source_target_pairs={{0,1},{1,0},{2,3},{3,2},{4,5},{5,4},{6,7},{7,6},{8,9},{9,8},{10,11... | collective-permute-start | bytes 786440 | tf_op jit(solution)/shard_map/ppermute | solution.py:39
  65.5 0.0 all-to-all-done.1.refs_4_
  65.5 6.8 %grads30.1 = (bf16[512,256]{1,0:T(8,128)(2,1)}, f32[512,256]{1,0:T(8,128)S(1)}, bf16[8,32,1024]{2,1,0:T(8,128)(2,1)}) custom-call(s32[12]{0:T(128)S(1)} %concatenate.9.ix, s32[2,8]{1,0:T(2,128)S(1)} %pad_add_fusion.tl, s32[8,8]{1,0:T(8,128)S(1)} %copy-done.10, bf16[256,2048]{1,0:T(8,128)(2,1)S(1)} %copy-done.2, bf16[256,2048]{1,0:T(8,128)(2,1)S(1)} %copy-done.3, ...), custom_call_target="tpu_custom_call" | custom-call | flops 6600000000 | bytes 65536 | tf_op jit(solution)/shard_map/grads30/pallas_call | solution.py:310
  72.3 2.2 %collective-permute-start.14 = (bf16[512,256]{1,0:T(8,128)(2,1)}, bf16[512,256]{1,0:T(8,128)(2,1)S(1)}, u32[]{:S(2)}, u32[]{:S(2)}) collective-permute-start(bf16[512,256]{1,0:T(8,128)(2,1)} %get-tuple-element.36), channel_id=1, source_target_pairs={{0,3},{1,2},{2,1},{3,0},{4,7},{5,6},{6,5},{7,4},{8,11},{9,10},{10,... | collective-permute-start | bytes 786440 | tf_op jit(solution)/shard_map/ppermute | solution.py:39
  74.5 4.9 %all-to-all-start.2 = ((bf16[8,32,1024]{2,1,0:T(8,128)(2,1)}), bf16[8,32,1024]{2,1,0:T(8,128)(2,1)S(1)}, u32[]{:S(2)}, u32[]{:S(2)}) async-start(bf16[8,32,1024]{2,1,0:T(8,128)(2,1)} %get-tuple-element.37), calls=%async_computation.2 | async-start | bytes 1048576 | tf_op jit(solution)/shard_map/all_to_all | solution.py:458
  79.4 0.0 collective-permute-done.12
  79.4 0.0 collective-permute-done.13
  79.4 0.0 collective-permute-done.14
  79.5 1.2 %add_convert_fusion._ = bf16[512,256]{1,0:T(8,128)(2,1)S(1)} fusion(bf16[512,256]{1,0:T(8,128)(2,1)S(1)} %collective-permute-done.14, bf16[512,256]{1,0:T(8,128)(2,1)} %collective-permute-done.13, f32[512,256]{1,0:T(8,128)S(1)} %get-tuple-element.33, bf16[512,256]{1,0:T(8,128)(2,1)} %collective-permute-done.12), kind=kLoop, calls=%fused_computation | loop fusion | flops 917504 | bytes 1572864 | tf_op jit(solution)/shard_map/convert_element_type | solution.py:500
  80.7 3.9 %collective-permute-start.15 = (bf16[256,256]{1,0:T(8,128)(2,1)S(1)}, bf16[256,256]{1,0:T(8,128)(2,1)S(1)}, u32[]{:S(2)}, u32[]{:S(2)}) collective-permute-start(bf16[256,256]{1,0:T(8,128)(2,1)S(1)} %get-tuple-element.44), channel_id=1, source_target_pairs={{0,8},{1,9},{2,10},{3,11},{4,12},{5,13},{6,14},{7,15},{8,0},{9,1},... | collective-permute-start | bytes 393224 | tf_op jit(solution)/shard_map/ppermute | solution.py:39
  84.5 1.2 %collective-permute-start.17 = (bf16[256,256]{1,0:T(8,128)(2,1)S(1)}, bf16[256,256]{1,0:T(8,128)(2,1)S(1)}, u32[]{:S(2)}, u32[]{:S(2)}) collective-permute-start(bf16[256,256]{1,0:T(8,128)(2,1)S(1)} %get-tuple-element.44), channel_id=1, source_target_pairs={{0,12},{1,13},{2,14},{3,15},{4,8},{5,9},{6,10},{7,11},{8,4},{9,5},... | collective-permute-start | bytes 393224 | tf_op jit(solution)/shard_map/ppermute | solution.py:39
  85.7 1.7 %collective-permute-start.16 = (bf16[256,256]{1,0:T(8,128)(2,1)S(1)}, bf16[256,256]{1,0:T(8,128)(2,1)S(1)}, u32[]{:S(2)}, u32[]{:S(2)}) collective-permute-start(bf16[256,256]{1,0:T(8,128)(2,1)S(1)} %get-tuple-element.45.a), channel_id=1, source_target_pairs={{0,4},{1,5},{2,6},{3,7},{4,0},{5,1},{6,2},{7,3},{8,12},{9,13},{10,... | collective-permute-start | bytes 393224 | tf_op jit(solution)/shard_map/ppermute | solution.py:39
  87.5 0.0 collective-permute-done.15.b
  87.5 0.0 all-to-all-done.2
  87.5 4.4 %collective-permute-start.18 = (bf16[256,1024]{1,0:T(8,128)(2,1)S(1)}, bf16[256,1024]{1,0:T(8,128)(2,1)S(1)}, u32[]{:S(2)}, u32[]{:S(2)}) collective-permute-start(bf16[256,1024]{1,0:T(8,128)(2,1)S(1)} %bitcast.6), channel_id=1, source_target_pairs={{0,8},{1,9},{2,10},{3,11},{4,12},{5,13},{6,14},{7,15},{8,0},{9,1},... | collective-permute-start | bytes 1572872 | tf_op jit(solution)/shard_map/ppermute | solution.py:39
  91.9 3.3 %fetch.1 = (bf16[3840,512]{1,0:T(8,128)(2,1)S(1)}, bf16[3840,512]{1,0:T(8,128)(2,1)S(1)}) custom-call(bf16[3840,512]{1,0:T(8,128)(2,1)} %k_hbm.1, bf16[3840,512]{1,0:T(8,128)(2,1)} %v_hbm.1, bf16[512,256]{1,0:T(8,128)(2,1)S(1)} %add_convert_fusion._), custom_call_target="tpu_custom_call" | custom-call | flops 4400000000 | bytes 65536 | tf_op jit(solution)/shard_map/fetch/pallas_call | solution.py:344
  95.3 0.4 collective-permute-done.16.c_
  95.7 0.0 collective-permute-done.17.d_
  95.7 3.7 %feats.1 = (bf16[256,3840]{1,0:T(8,128)(2,1)}, bf16[256,2048]{1,0:T(8,128)(2,1)}) custom-call(s32[12]{0:T(128)S(1)} %concatenate.9.ix, bf16[256,256]{1,0:T(8,128)(2,1)S(1)} %get-tuple-element.45.a, bf16[256,256]{1,0:T(8,128)(2,1)S(1)} %collective-permute-done.15.b, bf16[256,256]{1,0:T(8,128)(2,1)S(1)} %collective-permute-done.16.c_, ...), custom_call_target="tpu_custom_call" | custom-call | flops 4400000000 | bytes 65536 | tf_op jit(solution)/shard_map/feats/pallas_call | solution.py:400
  99.4 0.0 collective-permute-done.18.t_ref
  99.4 1.4 %theirs.1 = bf16[256,2048]{1,0:T(8,128)(2,1)} custom-call(s32[12]{0:T(128)S(1)} %concatenate.9.ix, bf16[256,2048]{1,0:T(8,128)(2,1)} %get-tuple-element.42._, bf16[256,1024]{1,0:T(8,128)(2,1)S(1)} %collective-permute-done.18.t_ref), custom_call_target="tpu_custom_call", output_to_operand_aliasing={{}: (1, {})} | custom-call | tf_op jit(solution)/shard_map/theirs/pallas_call | solution.py:433
  (21 shorter events, 0.1 us)
Async XLA Ops:
  1.4 26.4 %copy-start.11 = (s32[8]{0:T(128)S(1)}, s32[8]{0:T(128)}, u32[]{:S(2)}) copy-start(s32[8]{0:T(128)} %param.12) | copy-start | bytes 100
  1.4 35.0 %copy-start.2 = (bf16[256,2048]{1,0:T(8,128)(2,1)S(1)}, bf16[256,2048]{1,0:T(8,128)(2,1)}, u32[]{:S(2)}) copy-start(bf16[256,2048]{1,0:T(8,128)(2,1)} %q.5) | copy-start | bytes 3145732
  1.4 35.0 %copy-start.3 = (bf16[256,2048]{1,0:T(8,128)(2,1)S(1)}, bf16[256,2048]{1,0:T(8,128)(2,1)}, u32[]{:S(2)}) copy-start(bf16[256,2048]{1,0:T(8,128)(2,1)} %g.5) | copy-start | bytes 3145732
  1.4 35.0 %copy-start.10 = (s32[8,8]{1,0:T(8,128)S(1)}, s32[8,8]{1,0:T(8,128)}, u32[]{:S(2)}) copy-start(s32[8,8]{1,0:T(8,128)} %se.5) | copy-start | bytes 772
  6.7 9.1 %collective-permute-start.7 = (bf16[256,128]{1,0:T(8,128)(2,1)S(1)}, bf16[256,128]{1,0:T(8,128)(2,1)S(1)}, u32[]{:S(2)}, u32[]{:S(2)}) collective-permute-start(bf16[256,128]{1,0:T(8,128)(2,1)S(1)} %get-tuple-element.29), channel_id=1, source_target_pairs={{0,4},{1,5},{2,6},{3,7},{4,0},{5,1},{6,2},{7,3},{8,12},{9,13},{10,... | collective-permute-start | bytes 196616 | tf_op jit(solution)/shard_map/ppermute | solution.py:39
  11.2 6.9 %collective-permute-start = (bf16[272,128]{1,0:T(8,128)(2,1)S(1)}, bf16[272,128]{1,0:T(8,128)(2,1)S(1)}, u32[]{:S(2)}, u32[]{:S(2)}) collective-permute-start(bf16[272,128]{1,0:T(8,128)(2,1)S(1)} %get-tuple-element.23), channel_id=1, source_target_pairs={{0,8},{1,9},{2,10},{3,11},{4,12},{5,13},{6,14},{7,15},{8,0},{9,1},... | collective-permute-start | bytes 208904 | tf_op jit(solution)/shard_map/ppermute | solution.py:39
  12.2 5.9 %collective-permute-start.8 = (bf16[256,128]{1,0:T(8,128)(2,1)S(1)}, bf16[256,128]{1,0:T(8,128)(2,1)S(1)}, u32[]{:S(2)}, u32[]{:S(2)}) collective-permute-start(bf16[256,128]{1,0:T(8,128)(2,1)S(1)} %get-tuple-element.30), channel_id=1, source_target_pairs={{0,12},{1,13},{2,14},{3,15},{4,8},{5,9},{6,10},{7,11},{8,4},{9,5},... | collective-permute-start | bytes 196616 | tf_op jit(solution)/shard_map/ppermute | solution.py:39
  12.2 9.8 %collective-permute-start.1 = (f32[256,128]{1,0:T(8,128)S(1)}, f32[256,128]{1,0:T(8,128)S(1)}, u32[]{:S(2)}, u32[]{:S(2)}) collective-permute-start(f32[256,128]{1,0:T(8,128)S(1)} %get-tuple-element.25), channel_id=1, source_target_pairs={{0,4},{1,5},{2,6},{3,7},{4,0},{5,1},{6,2},{7,3},{8,12},{9,13},{10,... | collective-permute-start | bytes 393224 | tf_op jit(solution)/shard_map/ppermute | solution.py:39
  15.0 6.9 %collective-permute-start.2 = (f32[256,128]{1,0:T(8,128)S(1)}, f32[256,128]{1,0:T(8,128)S(1)}, u32[]{:S(2)}, u32[]{:S(2)}) collective-permute-start(f32[256,128]{1,0:T(8,128)S(1)} %get-tuple-element.26), channel_id=1, source_target_pairs={{0,8},{1,9},{2,10},{3,11},{4,12},{5,13},{6,14},{7,15},{8,0},{9,1},... | collective-permute-start | bytes 393224 | tf_op jit(solution)/shard_map/ppermute | solution.py:39
  15.8 7.5 %collective-permute-start.3 = (f32[256,128]{1,0:T(8,128)S(1)}, f32[256,128]{1,0:T(8,128)S(1)}, u32[]{:S(2)}, u32[]{:S(2)}) collective-permute-start(f32[256,128]{1,0:T(8,128)S(1)} %get-tuple-element.27), channel_id=1, source_target_pairs={{0,12},{1,13},{2,14},{3,15},{4,8},{5,9},{6,10},{7,11},{8,4},{9,5},... | collective-permute-start | bytes 393224 | tf_op jit(solution)/shard_map/ppermute | solution.py:39
  18.2 25.9 %copy-start = (bf16[512,128]{1,0:T(8,128)(2,1)}, bf16[512,128]{1,0:T(8,128)(2,1)S(1)}, u32[]{:S(2)}) copy-start(bf16[512,128]{1,0:T(8,128)(2,1)S(1)} %pad_maximum_fusion.1.v0.refs_3_) | copy-start | bytes 393220
  18.2 9.2 %collective-permute-start.10 = (bf16[512,128]{1,0:T(8,128)(2,1)S(1)}, bf16[512,128]{1,0:T(8,128)(2,1)S(1)}, u32[]{:S(2)}, u32[]{:S(2)}) collective-permute-start(bf16[512,128]{1,0:T(8,128)(2,1)S(1)} %pad_maximum_fusion.1.v0.refs_3_), channel_id=1, source_target_pairs={{0,2},{1,3},{2,0},{3,1},{4,6},{5,7},{6,4},{7,5},{8,10},{9,11},{10,... | collective-permute-start | bytes 393224 | tf_op jit(solution)/shard_map/ppermute | solution.py:39
  21.2 6.7 %collective-permute-start.11 = (bf16[512,128]{1,0:T(8,128)(2,1)S(1)}, bf16[512,128]{1,0:T(8,128)(2,1)S(1)}, u32[]{:S(2)}, u32[]{:S(2)}) collective-permute-start(bf16[512,128]{1,0:T(8,128)(2,1)S(1)} %pad_maximum_fusion.1.v0.refs_3_), channel_id=1, source_target_pairs={{0,3},{1,2},{2,1},{3,0},{4,7},{5,6},{6,5},{7,4},{8,11},{9,10},{10,... | collective-permute-start | bytes 393224 | tf_op jit(solution)/shard_map/ppermute | solution.py:39
  21.9 6.5 %collective-permute-start.9 = (bf16[512,128]{1,0:T(8,128)(2,1)S(1)}, bf16[512,128]{1,0:T(8,128)(2,1)S(1)}, u32[]{:S(2)}, u32[]{:S(2)}) collective-permute-start(bf16[512,128]{1,0:T(8,128)(2,1)S(1)} %pad_maximum_fusion.1.v0.refs_3_), channel_id=1, source_target_pairs={{0,1},{1,0},{2,3},{3,2},{4,5},{5,4},{6,7},{7,6},{8,9},{9,8},{10,11... | collective-permute-start | bytes 393224 | tf_op jit(solution)/shard_map/ppermute | solution.py:39
  23.3 20.8 %copy-start.1 = (bf16[512,128]{1,0:T(8,128)(2,1)}, bf16[512,128]{1,0:T(8,128)(2,1)S(1)}, u32[]{:S(2)}) copy-start(bf16[512,128]{1,0:T(8,128)(2,1)S(1)} %pad_maximum_fusion.k0.refs_1_) | copy-start | bytes 393220
  23.3 7.6 %collective-permute-start.4 = (bf16[512,128]{1,0:T(8,128)(2,1)S(1)}, bf16[512,128]{1,0:T(8,128)(2,1)S(1)}, u32[]{:S(2)}, u32[]{:S(2)}) collective-permute-start(bf16[512,128]{1,0:T(8,128)(2,1)S(1)} %pad_maximum_fusion.k0.refs_1_), channel_id=1, source_target_pairs={{0,1},{1,0},{2,3},{3,2},{4,5},{5,4},{6,7},{7,6},{8,9},{9,8},{10,11... | collective-permute-start | bytes 393224 | tf_op jit(solution)/shard_map/ppermute | solution.py:39
  24.4 9.9 %collective-permute-start.5 = (bf16[512,128]{1,0:T(8,128)(2,1)S(1)}, bf16[512,128]{1,0:T(8,128)(2,1)S(1)}, u32[]{:S(2)}, u32[]{:S(2)}) collective-permute-start(bf16[512,128]{1,0:T(8,128)(2,1)S(1)} %pad_maximum_fusion.k0.refs_1_), channel_id=1, source_target_pairs={{0,2},{1,3},{2,0},{3,1},{4,6},{5,7},{6,4},{7,5},{8,10},{9,11},{10,... | collective-permute-start | bytes 393224 | tf_op jit(solution)/shard_map/ppermute | solution.py:39
  27.3 16.8 %copy-start.5 = (bf16[512,128]{1,0:T(8,128)(2,1)}, bf16[512,128]{1,0:T(8,128)(2,1)S(1)}, u32[]{:S(2)}) copy-start(bf16[512,128]{1,0:T(8,128)(2,1)S(1)} %collective-permute-done.10.v2.refs_2_) | copy-start | bytes 393220
  27.3 9.0 %collective-permute-start.6 = (bf16[512,128]{1,0:T(8,128)(2,1)S(1)}, bf16[512,128]{1,0:T(8,128)(2,1)S(1)}, u32[]{:S(2)}, u32[]{:S(2)}) collective-permute-start(bf16[512,128]{1,0:T(8,128)(2,1)S(1)} %pad_maximum_fusion.k0.refs_1_), channel_id=1, source_target_pairs={{0,3},{1,2},{2,1},{3,0},{4,7},{5,6},{6,5},{7,4},{8,11},{9,10},{10,... | collective-permute-start | bytes 393224 | tf_op jit(solution)/shard_map/ppermute | solution.py:39
  27.8 16.3 %copy-start.4 = (bf16[512,128]{1,0:T(8,128)(2,1)}, bf16[512,128]{1,0:T(8,128)(2,1)S(1)}, u32[]{:S(2)}) copy-start(bf16[512,128]{1,0:T(8,128)(2,1)S(1)} %collective-permute-done.11.v3.refs_2_) | copy-start | bytes 393220
  28.4 15.7 %copy-start.6 = (bf16[512,128]{1,0:T(8,128)(2,1)}, bf16[512,128]{1,0:T(8,128)(2,1)S(1)}, u32[]{:S(2)}) copy-start(bf16[512,128]{1,0:T(8,128)(2,1)S(1)} %collective-permute-done.9.v1.refs_3_) | copy-start | bytes 393220
  30.9 13.2 %copy-start.8 = (bf16[512,128]{1,0:T(8,128)(2,1)}, bf16[512,128]{1,0:T(8,128)(2,1)S(1)}, u32[]{:S(2)}) copy-start(bf16[512,128]{1,0:T(8,128)(2,1)S(1)} %collective-permute-done.4.k1.refs_1_) | copy-start | bytes 393220
  34.3 9.8 %copy-start.9 = (bf16[512,128]{1,0:T(8,128)(2,1)}, bf16[512,128]{1,0:T(8,128)(2,1)S(1)}, u32[]{:S(2)}) copy-start(bf16[512,128]{1,0:T(8,128)(2,1)S(1)} %collective-permute-done.5.k2.refs_0_) | copy-start | bytes 393220
  36.3 7.8 %copy-start.7 = (bf16[512,128]{1,0:T(8,128)(2,1)}, bf16[512,128]{1,0:T(8,128)(2,1)S(1)}, u32[]{:S(2)}) copy-start(bf16[512,128]{1,0:T(8,128)(2,1)S(1)} %collective-permute-done.6.k3.refs_0_) | copy-start | bytes 393220
  53.8 11.7 %all-to-all-start.1 = ((bf16[8,32,1024]{2,1,0:T(8,128)(2,1)}), bf16[8,32,1024]{2,1,0:T(8,128)(2,1)S(1)}, u32[]{:S(2)}, u32[]{:S(2)}) async-start(bf16[8,32,1024]{2,1,0:T(8,128)(2,1)} %get-tuple-element.32), calls=%async_computation.1 | async-start | bytes 1048576 | tf_op jit(solution)/shard_map/all_to_all | solution.py:458
  64.4 15.0 %collective-permute-start.12 = (bf16[512,256]{1,0:T(8,128)(2,1)}, bf16[512,256]{1,0:T(8,128)(2,1)}, u32[]{:S(2)}, u32[]{:S(2)}) collective-permute-start(bf16[512,256]{1,0:T(8,128)(2,1)} %get-tuple-element.34), channel_id=1, source_target_pairs={{0,2},{1,3},{2,0},{3,1},{4,6},{5,7},{6,4},{7,5},{8,10},{9,11},{10,... | collective-permute-start | bytes 786440 | tf_op jit(solution)/shard_map/ppermute | solution.py:39
  64.4 15.0 %collective-permute-start.13 = (bf16[512,256]{1,0:T(8,128)(2,1)}, bf16[512,256]{1,0:T(8,128)(2,1)}, u32[]{:S(2)}, u32[]{:S(2)}) collective-permute-start(bf16[512,256]{1,0:T(8,128)(2,1)} %get-tuple-element.35), channel_id=1, source_target_pairs={{0,1},{1,0},{2,3},{3,2},{4,5},{5,4},{6,7},{7,6},{8,9},{9,8},{10,11... | collective-permute-start | bytes 786440 | tf_op jit(solution)/shard_map/ppermute | solution.py:39
  72.3 7.1 %collective-permute-start.14 = (bf16[512,256]{1,0:T(8,128)(2,1)}, bf16[512,256]{1,0:T(8,128)(2,1)S(1)}, u32[]{:S(2)}, u32[]{:S(2)}) collective-permute-start(bf16[512,256]{1,0:T(8,128)(2,1)} %get-tuple-element.36), channel_id=1, source_target_pairs={{0,3},{1,2},{2,1},{3,0},{4,7},{5,6},{6,5},{7,4},{8,11},{9,10},{10,... | collective-permute-start | bytes 786440 | tf_op jit(solution)/shard_map/ppermute | solution.py:39
  74.5 13.0 %all-to-all-start.2 = ((bf16[8,32,1024]{2,1,0:T(8,128)(2,1)}), bf16[8,32,1024]{2,1,0:T(8,128)(2,1)S(1)}, u32[]{:S(2)}, u32[]{:S(2)}) async-start(bf16[8,32,1024]{2,1,0:T(8,128)(2,1)} %get-tuple-element.37), calls=%async_computation.2 | async-start | bytes 1048576 | tf_op jit(solution)/shard_map/all_to_all | solution.py:458
  80.7 6.8 %collective-permute-start.15 = (bf16[256,256]{1,0:T(8,128)(2,1)S(1)}, bf16[256,256]{1,0:T(8,128)(2,1)S(1)}, u32[]{:S(2)}, u32[]{:S(2)}) collective-permute-start(bf16[256,256]{1,0:T(8,128)(2,1)S(1)} %get-tuple-element.44), channel_id=1, source_target_pairs={{0,8},{1,9},{2,10},{3,11},{4,12},{5,13},{6,14},{7,15},{8,0},{9,1},... | collective-permute-start | bytes 393224 | tf_op jit(solution)/shard_map/ppermute | solution.py:39
  84.5 11.1 %collective-permute-start.17 = (bf16[256,256]{1,0:T(8,128)(2,1)S(1)}, bf16[256,256]{1,0:T(8,128)(2,1)S(1)}, u32[]{:S(2)}, u32[]{:S(2)}) collective-permute-start(bf16[256,256]{1,0:T(8,128)(2,1)S(1)} %get-tuple-element.44), channel_id=1, source_target_pairs={{0,12},{1,13},{2,14},{3,15},{4,8},{5,9},{6,10},{7,11},{8,4},{9,5},... | collective-permute-start | bytes 393224 | tf_op jit(solution)/shard_map/ppermute | solution.py:39
  85.7 9.9 %collective-permute-start.16 = (bf16[256,256]{1,0:T(8,128)(2,1)S(1)}, bf16[256,256]{1,0:T(8,128)(2,1)S(1)}, u32[]{:S(2)}, u32[]{:S(2)}) collective-permute-start(bf16[256,256]{1,0:T(8,128)(2,1)S(1)} %get-tuple-element.45.a), channel_id=1, source_target_pairs={{0,4},{1,5},{2,6},{3,7},{4,0},{5,1},{6,2},{7,3},{8,12},{9,13},{10,... | collective-permute-start | bytes 393224 | tf_op jit(solution)/shard_map/ppermute | solution.py:39
  87.5 11.9 %collective-permute-start.18 = (bf16[256,1024]{1,0:T(8,128)(2,1)S(1)}, bf16[256,1024]{1,0:T(8,128)(2,1)S(1)}, u32[]{:S(2)}, u32[]{:S(2)}) collective-permute-start(bf16[256,1024]{1,0:T(8,128)(2,1)S(1)} %bitcast.6), channel_id=1, source_target_pairs={{0,8},{1,9},{2,10},{3,11},{4,12},{5,13},{6,14},{7,15},{8,0},{9,1},... | collective-permute-start | bytes 1572872 | tf_op jit(solution)/shard_map/ppermute | solution.py:39

commit v7 on v6

--- a/solution.py
+++ b/solution.py
@@ -155,18 +155,18 @@
         ]
         lane = lax.broadcasted_iota(jnp.int32, (rows, HD), 1)
         st = jnp.zeros((rows, HD), F32)
-        for h in range(heads):
-            cols = slice(h * HD, (h + 1) * HD)
-            slot = h % 2
-            qh = q[:, cols]
-            best = [None, None]
+        group = 2
+        for h0 in range(0, heads, group):
+            qh = jnp.concatenate([q[:, h * HD : (h + 1) * HD] for h in range(h0, h0 + group)], axis=0)
+            best = [None] * (2 * group)
+            slot = (h0 // group) % 2
             for j in range(n):
                 s = dot_nt(qh, ks[j][...]) * C2
-                for b in range(2):
+                for b in range(2 * group):
                     for e in range(per):
                         y = jnp.minimum(
                             s[b * TBLK : (b + 1) * TBLK, e * TILE : (e + 1) * TILE],
-                            caps[b][j * per + e],
+                            caps[b % 2][j * per + e],
                         )
                         at = j * span + e * TILE
                         y_scr[slot, b * TBLK : (b + 1) * TBLK, at : at + TILE] = y
@@ -174,13 +174,17 @@
             m = jnp.max(jnp.concatenate(best, axis=0), axis=1, keepdims=True)
             p = jnp.exp2(y_scr[slot] - m).astype(BF)
             r = dot_nn(p, va[...])
-            den = r[:, HD:]
-            o = r[:, :HD] / den
-            out[:, :, cols] = o.astype(BF).reshape(8, share, HD)
-            lse = m + jnp.log2(den)
-            delta = jnp.sum(o * g[:, cols].astype(F32), axis=1, keepdims=True)
-            st = jnp.where(lane == h, lse, st)
-            st = jnp.where(lane == heads + h, delta, st)
+            for k in range(group):
+                h = h0 + k
+                cols = slice(h * HD, (h + 1) * HD)
+                mine = slice(k * rows, (k + 1) * rows)
+                den = r[mine, HD:]
+                o = r[mine, :HD] / den
+                out[:, :, cols] = o.astype(BF).reshape(8, share, HD)
+                lse = m[mine] + jnp.log2(den)
+                delta = jnp.sum(o * g[:, cols].astype(F32), axis=1, keepdims=True)
+                st = jnp.where(lane == h, lse, st)
+                st = jnp.where(lane == heads + h, delta, st)
         flat = st.T[: 2 * heads, :]
         for i in range(8):
             st_out[i] = flat
@@ -198,11 +202,11 @@
             in_specs=[pl.BlockSpec((rows, width), own)] * 2 + [spec((span, HD))] * 8,
             out_specs=[spec((8, share, width)), spec((8, 2 * heads, rows))],
             scratch_shapes=[
-                pltpu.VMEM((2, rows, total), F32),
+                pltpu.VMEM((2, 2 * rows, total), F32),
                 pltpu.VMEM((total, 2 * HD), BF),
             ],
         ),
-        compiler_params=pltpu.CompilerParams(vmem_limit_bytes=24 << 20),
+        compiler_params=pltpu.CompilerParams(vmem_limit_bytes=40 << 20),
         name="fwd",
         cost_estimate=cost(7),
     )(idx, tiles, sees, queries, grad_out, *keys, *values)
@@ -267,24 +271,25 @@
             ]
             kk = k_ref[...]
             vv = v_ref[...]
-            for h in range(heads):
-                cols = slice(h * HD, (h + 1) * HD)
-                qh = q[:, cols]
-                gh = g[:, cols]
+            group = 2
+            for h0 in range(0, heads, group):
+                hs = range(h0, h0 + group)
+                qh = jnp.concatenate([q[:, h * HD : (h + 1) * HD] for h in hs], axis=0)
+                gh = jnp.concatenate([g[:, h * HD : (h + 1) * HD] for h in hs], axis=0)
                 s = dot_nt(kk, qh) * C2
                 d = dot_nt(vv, gh)
-                lh = lse[h : h + 1, :]
-                dh = delta[h : h + 1, :]
+                dh = jnp.concatenate([delta[h : h + 1, :] for h in hs], axis=1)
                 ps = []
                 ds = []
                 for e in range(per):
                     at = slice(e * TILE, (e + 1) * TILE)
-                    p = jnp.exp2(jnp.minimum(s[at, :], caps[e]) - lh)
+                    lh = jnp.concatenate([jnp.where(caps[e] > 0, lse[h : h + 1, :], -NEG) for h in hs], axis=1)
+                    p = jnp.exp2(s[at, :] - lh)
                     ps.append(p.astype(BF))
                     ds.append((p * (d[at, :] - dh) * SCALE).astype(BF))
                 pv = dot_nn(jnp.concatenate(ps, axis=0), gh)
                 pk = dot_nn(jnp.concatenate(ds, axis=0), qh)
-                if h == 0:
+                if h0 == 0:
                     dv[...] = pv
                     dk[...] = pk
                 else:
@@ -317,7 +322,7 @@
             out_specs=out_specs,
             scratch_shapes=scratch,
         ),
-        compiler_params=pltpu.CompilerParams(vmem_limit_bytes=20 << 20),
+        compiler_params=pltpu.CompilerParams(vmem_limit_bytes=32 << 20),
         name="grads" + "".join(map(str, chunks)),
         cost_estimate=cost(3 * n),
     )(idx, tiles, sees, queries, grad_out, stats, *[keys[k] for k in chunks], *[values[k] for k in chunks], *more)

time: 101 us -> 102 us (level)
  transfers between devices with their start and end apart: 21 -> 21, of which waited for: 7 -> 7; matrix products, arithmetic and copies ran while one was open for 1% -> 1% of each run, Pallas kernels for 21% -> 20%
where the time goes in v7:
time: 102 us; the launch traced here: 101 us
  starting transfers between devices  42.6 us (42%)
  Pallas kernels  35.6 us (35%)
  waiting for transfers between devices  10.3 us (10%)
  blocking collectives  9.63 us (9%)
  other arithmetic  1.26 us (1%)
  between operations  1.06 us (1%)
    ppermute x19, starting transfers between devices, moved(): return lambda x: lax.ppermute(x, AXES, pairs)  34.1 us
    pallas_call x2, Pallas kernels, backward(): pl.pallas_call(body, out_shape=out_shape, grid_spec=pltpu.PrefetchScalarG...  13.7 us
    ppermute x19, waiting for transfers between devices, moved(): return lambda x: lax.ppermute(x, AXES, pairs)  10.3 us
    all_to_all x1, blocking collectives, swap8(): return lax.all_to_all(x, 'img', 0, 0, axis_index_groups=chips, tiled=True)  9.63 us
    all_to_all x2, starting transfers between devices, swap8(): return lax.all_to_all(x, 'img', 0, 0, axis_index_groups=chips, tiled=True)  8.55 us
    pallas_call x1, Pallas kernels, forward(): pl.pallas_call(body, out_shape=(jax.ShapeDtypeStruct((8, share, width), B...  8.21 us
    pallas_call x1, Pallas kernels, project(): pl.pallas_call(body, out_shape=outs, grid_spec=pltpu.PrefetchScalarGridSp...  5.29 us
    pallas_call x1, Pallas kernels, feature_grad(): pl.pallas_call(body, out_shape=(jax.ShapeDtypeStruct((rows, feat), BF), j...  3.7 us
  transfers between devices with their start and end apart: 21, of which 7 were waited for; matrix products, arithmetic and copies ran while one was open for 1% of the time, Pallas kernels for 20%

profile of v7, /device:TPU:1, one launch (start us, length us, event | category | flops | bytes accessed | tf_op | source)
XLA Modules:
  0.0 101.3 jit_solution(17233306809861764759)
XLA Ops:
  0.6 0.7 concatenate.9.ix
  1.4 0.0 copy-start.10
  1.4 5.3 %project.1 = (f32[256,128]{1,0:T(8,128)S(1)}, f32[256,128]{1,0:T(8,128)S(1)}, f32[256,128]{1,0:T(8,128)S(1)}, f32[256,128]{1,0:T(8,128)S(1)}, f32[256,128]{1,0:T...) custom-call(s32[12]{0:T(128)S(1)} %concatenate.9.ix, ...), custom_call_target="tpu_custom_call" | custom-call | flops 4400000000 | bytes 65536 | tf_op jit(solution)/shard_map/project/pallas_call | solution.py:106
  6.7 4.5 %collective-permute-start.7 = (bf16[256,128]{1,0:T(8,128)(2,1)S(1)}, bf16[256,128]{1,0:T(8,128)(2,1)S(1)}, u32[]{:S(2)}, u32[]{:S(2)}) collective-permute-start(bf16[256,128]{1,0:T(8,128)(2,1)S(1)} %get-tuple-element.29), channel_id=1, source_target_pairs={{0,4},{1,5},{2,6},{3,7},{4,0},{5,1},{6,2},{7,3},{8,12},{9,13},{10,... | collective-permute-start | bytes 196616 | tf_op jit(solution)/shard_map/ppermute | solution.py:39
  11.2 1.0 collective-permute-start
  12.2 0.0 collective-permute-start.8
  12.2 2.9 %collective-permute-start.1 = (f32[256,128]{1,0:T(8,128)S(1)}, f32[256,128]{1,0:T(8,128)S(1)}, u32[]{:S(2)}, u32[]{:S(2)}) collective-permute-start(f32[256,128]{1,0:T(8,128)S(1)} %get-tuple-element.25), channel_id=1, source_target_pairs={{0,4},{1,5},{2,6},{3,7},{4,0},{5,1},{6,2},{7,3},{8,12},{9,13},{10,... | collective-permute-start | bytes 393224 | tf_op jit(solution)/shard_map/ppermute | solution.py:39
  15.0 0.8 collective-permute-start.2
  15.8 0.0 collective-permute-done.7
  15.8 2.3 %collective-permute-start.3 = (f32[256,128]{1,0:T(8,128)S(1)}, f32[256,128]{1,0:T(8,128)S(1)}, u32[]{:S(2)}, u32[]{:S(2)}) collective-permute-start(f32[256,128]{1,0:T(8,128)S(1)} %get-tuple-element.27), channel_id=1, source_target_pairs={{0,12},{1,13},{2,14},{3,15},{4,8},{5,9},{6,10},{7,11},{8,4},{9,5},... | collective-permute-start | bytes 393224 | tf_op jit(solution)/shard_map/ppermute | solution.py:39
  18.1 0.0 collective-permute-done.8
  18.1 0.0 collective-permute-done
  18.2 0.0 copy-start
  18.2 3.0 %collective-permute-start.10 = (bf16[512,128]{1,0:T(8,128)(2,1)S(1)}, bf16[512,128]{1,0:T(8,128)(2,1)S(1)}, u32[]{:S(2)}, u32[]{:S(2)}) collective-permute-start(bf16[512,128]{1,0:T(8,128)(2,1)S(1)} %pad_maximum_fusion.1.v0.refs_3_), channel_id=1, source_target_pairs={{0,2},{1,3},{2,0},{3,1},{4,6},{5,7},{6,4},{7,5},{8,10},{9,11},{10,... | collective-permute-start | bytes 393224 | tf_op jit(solution)/shard_map/ppermute | solution.py:39
  21.2 0.8 collective-permute-start.11
  21.9 0.0 collective-permute-done.1
  21.9 0.0 collective-permute-start.9
  22.0 0.0 collective-permute-done.2
  22.0 1.3 %collective-permute-done.3 = f32[256,128]{1,0:T(8,128)S(1)} collective-permute-done((f32[256,128]{1,0:T(8,128)S(1)}, f32[256,128]{1,0:T(8,128)S(1)}, u32[]{:S(2)}, u32[]{:S(2)}) %collective-permute-start.3) | collective-permute-done | bytes 131104 | tf_op jit(solution)/shard_map/ppermute | solution.py:39
  23.3 0.0 copy-start.1
  23.3 1.1 %collective-permute-start.4 = (bf16[512,128]{1,0:T(8,128)(2,1)S(1)}, bf16[512,128]{1,0:T(8,128)(2,1)S(1)}, u32[]{:S(2)}, u32[]{:S(2)}) collective-permute-start(bf16[512,128]{1,0:T(8,128)(2,1)S(1)} %pad_maximum_fusion.k0.refs_1_), channel_id=1, source_target_pairs={{0,1},{1,0},{2,3},{3,2},{4,5},{5,4},{6,7},{7,6},{8,9},{9,8},{10,11... | collective-permute-start | bytes 393224 | tf_op jit(solution)/shard_map/ppermute | solution.py:39
  24.4 2.9 %collective-permute-start.5 = (bf16[512,128]{1,0:T(8,128)(2,1)S(1)}, bf16[512,128]{1,0:T(8,128)(2,1)S(1)}, u32[]{:S(2)}, u32[]{:S(2)}) collective-permute-start(bf16[512,128]{1,0:T(8,128)(2,1)S(1)} %pad_maximum_fusion.k0.refs_1_), channel_id=1, source_target_pairs={{0,2},{1,3},{2,0},{3,1},{4,6},{5,7},{6,4},{7,5},{8,10},{9,11},{10,... | collective-permute-start | bytes 393224 | tf_op jit(solution)/shard_map/ppermute | solution.py:39
  27.3 0.0 collective-permute-done.10.v2.refs_2_
  27.3 0.4 collective-permute-start.6
  27.7 0.0 copy-done.11
  27.7 0.1 collective-permute-done.11.v3.refs_2_
  27.8 0.6 collective-permute-done.9.v1.refs_3_
  28.4 2.5 %collective-permute-done.4.k1.refs_1_ = bf16[512,128]{1,0:T(8,128)(2,1)S(1)} collective-permute-done((bf16[512,128]{1,0:T(8,128)(2,1)S(1)}, bf16[512,128]{1,0:T(8,128)(2,1)S(1)}, u32[]{:S(2)}, u32[]{:S(2)}) %collective-permute-start.4) | collective-permute-done | bytes 131104 | tf_op jit(solution)/shard_map/ppermute | solution.py:39
  31.0 3.3 %collective-permute-done.5.k2.refs_0_ = bf16[512,128]{1,0:T(8,128)(2,1)S(1)} collective-permute-done((bf16[512,128]{1,0:T(8,128)(2,1)S(1)}, bf16[512,128]{1,0:T(8,128)(2,1)S(1)}, u32[]{:S(2)}, u32[]{:S(2)}) %collective-permute-start.5) | collective-permute-done | bytes 131104 | tf_op jit(solution)/shard_map/ppermute | solution.py:39
  34.3 2.0 %collective-permute-done.6.k3.refs_0_ = bf16[512,128]{1,0:T(8,128)(2,1)S(1)} collective-permute-done((bf16[512,128]{1,0:T(8,128)(2,1)S(1)}, bf16[512,128]{1,0:T(8,128)(2,1)S(1)}, u32[]{:S(2)}, u32[]{:S(2)}) %collective-permute-start.6) | collective-permute-done | bytes 131104 | tf_op jit(solution)/shard_map/ppermute | solution.py:39
  36.3 0.0 copy-done.2
  36.3 0.0 copy-done.3
  36.3 0.0 copy-done.10
  36.3 0.0 copy-start.7
  36.4 8.2 %fwd.1 = (bf16[8,32,1024]{2,1,0:T(8,128)(2,1)}, f32[8,16,256]{2,1,0:T(8,128)S(1)}) custom-call(s32[12]{0:T(128)S(1)} %concatenate.9.ix, s32[2,8]{1,0:T(2,128)S(1)} %pad_add_fusion.tl, s32[8,8]{1,0:T(8,128)S(1)} %copy-done.10, bf16[256,2048]{1,0:T(8,128)(2,1)S(1)} %copy-done.2, bf16[256,2048]{1,0:T(8,128)(2,1)S(1)} %copy-done.3, ...), custom_call_target="tpu_custom_call" | custom-call | flops 7699999744 | bytes 65536 | tf_op jit(solution)/shard_map/fwd/pallas_call | solution.py:193
  44.6 0.0 copy-done
  44.6 0.0 copy-done.1
  44.6 0.0 copy-done.5
  44.6 0.0 copy-done.4
  44.6 9.6 %all_to_all.15.st = f32[8,16,256]{2,1,0:T(8,128)S(1)} all-to-all(f32[8,16,256]{2,1,0:T(8,128)S(1)} %get-tuple-element.31), channel_id=1, replica_groups={{0,16,32,48,64,80,96,112},{8,24,40,56,72,88,104,120},{1,17,33,49,65,81,..., dimensions={0} | all-to-all | bytes 262144 | tf_op jit(solution)/shard_map/all_to_all | solution.py:463
  54.3 3.5 %all-to-all-start.1 = ((bf16[8,32,1024]{2,1,0:T(8,128)(2,1)}), bf16[8,32,1024]{2,1,0:T(8,128)(2,1)S(1)}, u32[]{:S(2)}, u32[]{:S(2)}) async-start(bf16[8,32,1024]{2,1,0:T(8,128)(2,1)} %get-tuple-element.32), calls=%async_computation.1 | async-start | bytes 1048576 | tf_op jit(solution)/shard_map/all_to_all | solution.py:463
  57.8 7.0 %grads21.1 = (bf16[512,256]{1,0:T(8,128)(2,1)}, bf16[512,256]{1,0:T(8,128)(2,1)}) custom-call(s32[12]{0:T(128)S(1)} %concatenate.9.ix, s32[2,8]{1,0:T(2,128)S(1)} %pad_add_fusion.tl, s32[8,8]{1,0:T(8,128)S(1)} %copy-done.10, bf16[256,2048]{1,0:T(8,128)(2,1)S(1)} %copy-done.2, bf16[256,2048]{1,0:T(8,128)(2,1)S(1)} %copy-done.3, ...), custom_call_target="tpu_custom_call" | custom-call | flops 6600000000 | bytes 65536 | tf_op jit(solution)/shard_map/grads21/pallas_call | solution.py:315
  64.7 0.0 collective-permute-start.12
  64.7 1.1 %collective-permute-start.13 = (bf16[512,256]{1,0:T(8,128)(2,1)}, bf16[512,256]{1,0:T(8,128)(2,1)}, u32[]{:S(2)}, u32[]{:S(2)}) collective-permute-start(bf16[512,256]{1,0:T(8,128)(2,1)} %get-tuple-element.35), channel_id=1, source_target_pairs={{0,1},{1,0},{2,3},{3,2},{4,5},{5,4},{6,7},{7,6},{8,9},{9,8},{10,11... | collective-permute-start | bytes 786440 | tf_op jit(solution)/shard_map/ppermute | solution.py:39
  65.8 0.0 all-to-all-done.1.refs_4_
  65.8 6.8 %grads30.1 = (bf16[512,256]{1,0:T(8,128)(2,1)}, f32[512,256]{1,0:T(8,128)S(1)}, bf16[8,32,1024]{2,1,0:T(8,128)(2,1)}) custom-call(s32[12]{0:T(128)S(1)} %concatenate.9.ix, s32[2,8]{1,0:T(2,128)S(1)} %pad_add_fusion.tl, s32[8,8]{1,0:T(8,128)S(1)} %copy-done.10, bf16[256,2048]{1,0:T(8,128)(2,1)S(1)} %copy-done.2, bf16[256,2048]{1,0:T(8,128)(2,1)S(1)} %copy-done.3, ...), custom_call_target="tpu_custom_call" | custom-call | flops 6600000000 | bytes 65536 | tf_op jit(solution)/shard_map/grads30/pallas_call | solution.py:315
  72.5 2.2 %collective-permute-start.14 = (bf16[512,256]{1,0:T(8,128)(2,1)}, bf16[512,256]{1,0:T(8,128)(2,1)S(1)}, u32[]{:S(2)}, u32[]{:S(2)}) collective-permute-start(bf16[512,256]{1,0:T(8,128)(2,1)} %get-tuple-element.36), channel_id=1, source_target_pairs={{0,3},{1,2},{2,1},{3,0},{4,7},{5,6},{6,5},{7,4},{8,11},{9,10},{10,... | collective-permute-start | bytes 786440 | tf_op jit(solution)/shard_map/ppermute | solution.py:39
  74.7 5.1 %all-to-all-start.2 = ((bf16[8,32,1024]{2,1,0:T(8,128)(2,1)}), bf16[8,32,1024]{2,1,0:T(8,128)(2,1)S(1)}, u32[]{:S(2)}, u32[]{:S(2)}) async-start(bf16[8,32,1024]{2,1,0:T(8,128)(2,1)} %get-tuple-element.37), calls=%async_computation.2 | async-start | bytes 1048576 | tf_op jit(solution)/shard_map/all_to_all | solution.py:463
  79.8 0.0 collective-permute-done.12
  79.8 0.0 collective-permute-done.13
  79.8 0.0 collective-permute-done.14
  79.8 1.2 %add_convert_fusion._ = bf16[512,256]{1,0:T(8,128)(2,1)S(1)} fusion(bf16[512,256]{1,0:T(8,128)(2,1)S(1)} %collective-permute-done.14, bf16[512,256]{1,0:T(8,128)(2,1)} %collective-permute-done.13, f32[512,256]{1,0:T(8,128)S(1)} %get-tuple-element.33, bf16[512,256]{1,0:T(8,128)(2,1)} %collective-permute-done.12), kind=kLoop, calls=%fused_computation | loop fusion | flops 917504 | bytes 1572864 | tf_op jit(solution)/shard_map/convert_element_type | solution.py:505
  81.0 3.9 %collective-permute-start.15 = (bf16[256,256]{1,0:T(8,128)(2,1)S(1)}, bf16[256,256]{1,0:T(8,128)(2,1)S(1)}, u32[]{:S(2)}, u32[]{:S(2)}) collective-permute-start(bf16[256,256]{1,0:T(8,128)(2,1)S(1)} %get-tuple-element.44), channel_id=1, source_target_pairs={{0,8},{1,9},{2,10},{3,11},{4,12},{5,13},{6,14},{7,15},{8,0},{9,1},... | collective-permute-start | bytes 393224 | tf_op jit(solution)/shard_map/ppermute | solution.py:39
  84.9 1.2 %collective-permute-start.17 = (bf16[256,256]{1,0:T(8,128)(2,1)S(1)}, bf16[256,256]{1,0:T(8,128)(2,1)S(1)}, u32[]{:S(2)}, u32[]{:S(2)}) collective-permute-start(bf16[256,256]{1,0:T(8,128)(2,1)S(1)} %get-tuple-element.44), channel_id=1, source_target_pairs={{0,12},{1,13},{2,14},{3,15},{4,8},{5,9},{6,10},{7,11},{8,4},{9,5},... | collective-permute-start | bytes 393224 | tf_op jit(solution)/shard_map/ppermute | solution.py:39
  86.1 1.8 %collective-permute-start.16 = (bf16[256,256]{1,0:T(8,128)(2,1)S(1)}, bf16[256,256]{1,0:T(8,128)(2,1)S(1)}, u32[]{:S(2)}, u32[]{:S(2)}) collective-permute-start(bf16[256,256]{1,0:T(8,128)(2,1)S(1)} %get-tuple-element.45.a), channel_id=1, source_target_pairs={{0,4},{1,5},{2,6},{3,7},{4,0},{5,1},{6,2},{7,3},{8,12},{9,13},{10,... | collective-permute-start | bytes 393224 | tf_op jit(solution)/shard_map/ppermute | solution.py:39
  87.9 0.0 collective-permute-done.15.b
  87.9 0.0 all-to-all-done.2
  87.9 4.4 %collective-permute-start.18 = (bf16[256,1024]{1,0:T(8,128)(2,1)S(1)}, bf16[256,1024]{1,0:T(8,128)(2,1)S(1)}, u32[]{:S(2)}, u32[]{:S(2)}) collective-permute-start(bf16[256,1024]{1,0:T(8,128)(2,1)S(1)} %bitcast.6), channel_id=1, source_target_pairs={{0,8},{1,9},{2,10},{3,11},{4,12},{5,13},{6,14},{7,15},{8,0},{9,1},... | collective-permute-start | bytes 1572872 | tf_op jit(solution)/shard_map/ppermute | solution.py:39
  92.3 3.3 %fetch.1 = (bf16[3840,512]{1,0:T(8,128)(2,1)S(1)}, bf16[3840,512]{1,0:T(8,128)(2,1)S(1)}) custom-call(bf16[3840,512]{1,0:T(8,128)(2,1)} %k_hbm.1, bf16[3840,512]{1,0:T(8,128)(2,1)} %v_hbm.1, bf16[512,256]{1,0:T(8,128)(2,1)S(1)} %add_convert_fusion._), custom_call_target="tpu_custom_call" | custom-call | flops 4400000000 | bytes 65536 | tf_op jit(solution)/shard_map/fetch/pallas_call | solution.py:349
  95.7 0.4 collective-permute-done.16.c_
  96.0 0.0 collective-permute-done.17.d_
  96.0 3.7 %feats.1 = (bf16[256,3840]{1,0:T(8,128)(2,1)}, bf16[256,2048]{1,0:T(8,128)(2,1)}) custom-call(s32[12]{0:T(128)S(1)} %concatenate.9.ix, bf16[256,256]{1,0:T(8,128)(2,1)S(1)} %get-tuple-element.45.a, bf16[256,256]{1,0:T(8,128)(2,1)S(1)} %collective-permute-done.15.b, bf16[256,256]{1,0:T(8,128)(2,1)S(1)} %collective-permute-done.16.c_, ...), custom_call_target="tpu_custom_call" | custom-call | flops 4400000000 | bytes 65536 | tf_op jit(solution)/shard_map/feats/pallas_call | solution.py:405
  99.7 0.0 collective-permute-done.18.t_ref
  99.7 1.4 %theirs.1 = bf16[256,2048]{1,0:T(8,128)(2,1)} custom-call(s32[12]{0:T(128)S(1)} %concatenate.9.ix, bf16[256,2048]{1,0:T(8,128)(2,1)} %get-tuple-element.42._, bf16[256,1024]{1,0:T(8,128)(2,1)S(1)} %collective-permute-done.18.t_ref), custom_call_target="tpu_custom_call", output_to_operand_aliasing={{}: (1, {})} | custom-call | tf_op jit(solution)/shard_map/theirs/pallas_call | solution.py:438
  (21 shorter events, 0.1 us)
Async XLA Ops:
  1.4 26.4 %copy-start.11 = (s32[8]{0:T(128)S(1)}, s32[8]{0:T(128)}, u32[]{:S(2)}) copy-start(s32[8]{0:T(128)} %param.12) | copy-start | bytes 100
  1.4 35.0 %copy-start.2 = (bf16[256,2048]{1,0:T(8,128)(2,1)S(1)}, bf16[256,2048]{1,0:T(8,128)(2,1)}, u32[]{:S(2)}) copy-start(bf16[256,2048]{1,0:T(8,128)(2,1)} %q.5) | copy-start | bytes 3145732
  1.4 35.0 %copy-start.3 = (bf16[256,2048]{1,0:T(8,128)(2,1)S(1)}, bf16[256,2048]{1,0:T(8,128)(2,1)}, u32[]{:S(2)}) copy-start(bf16[256,2048]{1,0:T(8,128)(2,1)} %g.5) | copy-start | bytes 3145732
  1.4 35.0 %copy-start.10 = (s32[8,8]{1,0:T(8,128)S(1)}, s32[8,8]{1,0:T(8,128)}, u32[]{:S(2)}) copy-start(s32[8,8]{1,0:T(8,128)} %se.5) | copy-start | bytes 772
  6.7 9.1 %collective-permute-start.7 = (bf16[256,128]{1,0:T(8,128)(2,1)S(1)}, bf16[256,128]{1,0:T(8,128)(2,1)S(1)}, u32[]{:S(2)}, u32[]{:S(2)}) collective-permute-start(bf16[256,128]{1,0:T(8,128)(2,1)S(1)} %get-tuple-element.29), channel_id=1, source_target_pairs={{0,4},{1,5},{2,6},{3,7},{4,0},{5,1},{6,2},{7,3},{8,12},{9,13},{10,... | collective-permute-start | bytes 196616 | tf_op jit(solution)/shard_map/ppermute | solution.py:39
  11.2 6.9 %collective-permute-start = (bf16[272,128]{1,0:T(8,128)(2,1)S(1)}, bf16[272,128]{1,0:T(8,128)(2,1)S(1)}, u32[]{:S(2)}, u32[]{:S(2)}) collective-permute-start(bf16[272,128]{1,0:T(8,128)(2,1)S(1)} %get-tuple-element.23), channel_id=1, source_target_pairs={{0,8},{1,9},{2,10},{3,11},{4,12},{5,13},{6,14},{7,15},{8,0},{9,1},... | collective-permute-start | bytes 208904 | tf_op jit(solution)/shard_map/ppermute | solution.py:39
  12.2 5.9 %collective-permute-start.8 = (bf16[256,128]{1,0:T(8,128)(2,1)S(1)}, bf16[256,128]{1,0:T(8,128)(2,1)S(1)}, u32[]{:S(2)}, u32[]{:S(2)}) collective-permute-start(bf16[256,128]{1,0:T(8,128)(2,1)S(1)} %get-tuple-element.30), channel_id=1, source_target_pairs={{0,12},{1,13},{2,14},{3,15},{4,8},{5,9},{6,10},{7,11},{8,4},{9,5},... | collective-permute-start | bytes 196616 | tf_op jit(solution)/shard_map/ppermute | solution.py:39
  12.2 9.8 %collective-permute-start.1 = (f32[256,128]{1,0:T(8,128)S(1)}, f32[256,128]{1,0:T(8,128)S(1)}, u32[]{:S(2)}, u32[]{:S(2)}) collective-permute-start(f32[256,128]{1,0:T(8,128)S(1)} %get-tuple-element.25), channel_id=1, source_target_pairs={{0,4},{1,5},{2,6},{3,7},{4,0},{5,1},{6,2},{7,3},{8,12},{9,13},{10,... | collective-permute-start | bytes 393224 | tf_op jit(solution)/shard_map/ppermute | solution.py:39
  15.0 6.9 %collective-permute-start.2 = (f32[256,128]{1,0:T(8,128)S(1)}, f32[256,128]{1,0:T(8,128)S(1)}, u32[]{:S(2)}, u32[]{:S(2)}) collective-permute-start(f32[256,128]{1,0:T(8,128)S(1)} %get-tuple-element.26), channel_id=1, source_target_pairs={{0,8},{1,9},{2,10},{3,11},{4,12},{5,13},{6,14},{7,15},{8,0},{9,1},... | collective-permute-start | bytes 393224 | tf_op jit(solution)/shard_map/ppermute | solution.py:39
  15.8 7.5 %collective-permute-start.3 = (f32[256,128]{1,0:T(8,128)S(1)}, f32[256,128]{1,0:T(8,128)S(1)}, u32[]{:S(2)}, u32[]{:S(2)}) collective-permute-start(f32[256,128]{1,0:T(8,128)S(1)} %get-tuple-element.27), channel_id=1, source_target_pairs={{0,12},{1,13},{2,14},{3,15},{4,8},{5,9},{6,10},{7,11},{8,4},{9,5},... | collective-permute-start | bytes 393224 | tf_op jit(solution)/shard_map/ppermute | solution.py:39
  18.2 26.4 %copy-start = (bf16[512,128]{1,0:T(8,128)(2,1)}, bf16[512,128]{1,0:T(8,128)(2,1)S(1)}, u32[]{:S(2)}) copy-start(bf16[512,128]{1,0:T(8,128)(2,1)S(1)} %pad_maximum_fusion.1.v0.refs_3_) | copy-start | bytes 393220
  18.2 9.2 %collective-permute-start.10 = (bf16[512,128]{1,0:T(8,128)(2,1)S(1)}, bf16[512,128]{1,0:T(8,128)(2,1)S(1)}, u32[]{:S(2)}, u32[]{:S(2)}) collective-permute-start(bf16[512,128]{1,0:T(8,128)(2,1)S(1)} %pad_maximum_fusion.1.v0.refs_3_), channel_id=1, source_target_pairs={{0,2},{1,3},{2,0},{3,1},{4,6},{5,7},{6,4},{7,5},{8,10},{9,11},{10,... | collective-permute-start | bytes 393224 | tf_op jit(solution)/shard_map/ppermute | solution.py:39
  21.2 6.7 %collective-permute-start.11 = (bf16[512,128]{1,0:T(8,128)(2,1)S(1)}, bf16[512,128]{1,0:T(8,128)(2,1)S(1)}, u32[]{:S(2)}, u32[]{:S(2)}) collective-permute-start(bf16[512,128]{1,0:T(8,128)(2,1)S(1)} %pad_maximum_fusion.1.v0.refs_3_), channel_id=1, source_target_pairs={{0,3},{1,2},{2,1},{3,0},{4,7},{5,6},{6,5},{7,4},{8,11},{9,10},{10,... | collective-permute-start | bytes 393224 | tf_op jit(solution)/shard_map/ppermute | solution.py:39
  21.9 6.5 %collective-permute-start.9 = (bf16[512,128]{1,0:T(8,128)(2,1)S(1)}, bf16[512,128]{1,0:T(8,128)(2,1)S(1)}, u32[]{:S(2)}, u32[]{:S(2)}) collective-permute-start(bf16[512,128]{1,0:T(8,128)(2,1)S(1)} %pad_maximum_fusion.1.v0.refs_3_), channel_id=1, source_target_pairs={{0,1},{1,0},{2,3},{3,2},{4,5},{5,4},{6,7},{7,6},{8,9},{9,8},{10,11... | collective-permute-start | bytes 393224 | tf_op jit(solution)/shard_map/ppermute | solution.py:39
  23.3 21.3 %copy-start.1 = (bf16[512,128]{1,0:T(8,128)(2,1)}, bf16[512,128]{1,0:T(8,128)(2,1)S(1)}, u32[]{:S(2)}) copy-start(bf16[512,128]{1,0:T(8,128)(2,1)S(1)} %pad_maximum_fusion.k0.refs_1_) | copy-start | bytes 393220
  23.3 7.6 %collective-permute-start.4 = (bf16[512,128]{1,0:T(8,128)(2,1)S(1)}, bf16[512,128]{1,0:T(8,128)(2,1)S(1)}, u32[]{:S(2)}, u32[]{:S(2)}) collective-permute-start(bf16[512,128]{1,0:T(8,128)(2,1)S(1)} %pad_maximum_fusion.k0.refs_1_), channel_id=1, source_target_pairs={{0,1},{1,0},{2,3},{3,2},{4,5},{5,4},{6,7},{7,6},{8,9},{9,8},{10,11... | collective-permute-start | bytes 393224 | tf_op jit(solution)/shard_map/ppermute | solution.py:39
  24.4 9.9 %collective-permute-start.5 = (bf16[512,128]{1,0:T(8,128)(2,1)S(1)}, bf16[512,128]{1,0:T(8,128)(2,1)S(1)}, u32[]{:S(2)}, u32[]{:S(2)}) collective-permute-start(bf16[512,128]{1,0:T(8,128)(2,1)S(1)} %pad_maximum_fusion.k0.refs_1_), channel_id=1, source_target_pairs={{0,2},{1,3},{2,0},{3,1},{4,6},{5,7},{6,4},{7,5},{8,10},{9,11},{10,... | collective-permute-start | bytes 393224 | tf_op jit(solution)/shard_map/ppermute | solution.py:39
  27.3 17.2 %copy-start.5 = (bf16[512,128]{1,0:T(8,128)(2,1)}, bf16[512,128]{1,0:T(8,128)(2,1)S(1)}, u32[]{:S(2)}) copy-start(bf16[512,128]{1,0:T(8,128)(2,1)S(1)} %collective-permute-done.10.v2.refs_2_) | copy-start | bytes 393220
  27.3 9.0 %collective-permute-start.6 = (bf16[512,128]{1,0:T(8,128)(2,1)S(1)}, bf16[512,128]{1,0:T(8,128)(2,1)S(1)}, u32[]{:S(2)}, u32[]{:S(2)}) collective-permute-start(bf16[512,128]{1,0:T(8,128)(2,1)S(1)} %pad_maximum_fusion.k0.refs_1_), channel_id=1, source_target_pairs={{0,3},{1,2},{2,1},{3,0},{4,7},{5,6},{6,5},{7,4},{8,11},{9,10},{10,... | collective-permute-start | bytes 393224 | tf_op jit(solution)/shard_map/ppermute | solution.py:39
  27.8 16.7 %copy-start.4 = (bf16[512,128]{1,0:T(8,128)(2,1)}, bf16[512,128]{1,0:T(8,128)(2,1)S(1)}, u32[]{:S(2)}) copy-start(bf16[512,128]{1,0:T(8,128)(2,1)S(1)} %collective-permute-done.11.v3.refs_2_) | copy-start | bytes 393220
  28.4 16.2 %copy-start.6 = (bf16[512,128]{1,0:T(8,128)(2,1)}, bf16[512,128]{1,0:T(8,128)(2,1)S(1)}, u32[]{:S(2)}) copy-start(bf16[512,128]{1,0:T(8,128)(2,1)S(1)} %collective-permute-done.9.v1.refs_3_) | copy-start | bytes 393220
  30.9 13.6 %copy-start.8 = (bf16[512,128]{1,0:T(8,128)(2,1)}, bf16[512,128]{1,0:T(8,128)(2,1)S(1)}, u32[]{:S(2)}) copy-start(bf16[512,128]{1,0:T(8,128)(2,1)S(1)} %collective-permute-done.4.k1.refs_1_) | copy-start | bytes 393220
  34.3 10.3 %copy-start.9 = (bf16[512,128]{1,0:T(8,128)(2,1)}, bf16[512,128]{1,0:T(8,128)(2,1)S(1)}, u32[]{:S(2)}) copy-start(bf16[512,128]{1,0:T(8,128)(2,1)S(1)} %collective-permute-done.5.k2.refs_0_) | copy-start | bytes 393220
  36.3 8.3 %copy-start.7 = (bf16[512,128]{1,0:T(8,128)(2,1)}, bf16[512,128]{1,0:T(8,128)(2,1)S(1)}, u32[]{:S(2)}) copy-start(bf16[512,128]{1,0:T(8,128)(2,1)S(1)} %collective-permute-done.6.k3.refs_0_) | copy-start | bytes 393220
  54.3 11.5 %all-to-all-start.1 = ((bf16[8,32,1024]{2,1,0:T(8,128)(2,1)}), bf16[8,32,1024]{2,1,0:T(8,128)(2,1)S(1)}, u32[]{:S(2)}, u32[]{:S(2)}) async-start(bf16[8,32,1024]{2,1,0:T(8,128)(2,1)} %get-tuple-element.32), calls=%async_computation.1 | async-start | bytes 1048576 | tf_op jit(solution)/shard_map/all_to_all | solution.py:463
  64.7 15.1 %collective-permute-start.12 = (bf16[512,256]{1,0:T(8,128)(2,1)}, bf16[512,256]{1,0:T(8,128)(2,1)}, u32[]{:S(2)}, u32[]{:S(2)}) collective-permute-start(bf16[512,256]{1,0:T(8,128)(2,1)} %get-tuple-element.34), channel_id=1, source_target_pairs={{0,2},{1,3},{2,0},{3,1},{4,6},{5,7},{6,4},{7,5},{8,10},{9,11},{10,... | collective-permute-start | bytes 786440 | tf_op jit(solution)/shard_map/ppermute | solution.py:39
  64.7 15.1 %collective-permute-start.13 = (bf16[512,256]{1,0:T(8,128)(2,1)}, bf16[512,256]{1,0:T(8,128)(2,1)}, u32[]{:S(2)}, u32[]{:S(2)}) collective-permute-start(bf16[512,256]{1,0:T(8,128)(2,1)} %get-tuple-element.35), channel_id=1, source_target_pairs={{0,1},{1,0},{2,3},{3,2},{4,5},{5,4},{6,7},{7,6},{8,9},{9,8},{10,11... | collective-permute-start | bytes 786440 | tf_op jit(solution)/shard_map/ppermute | solution.py:39
  72.5 7.3 %collective-permute-start.14 = (bf16[512,256]{1,0:T(8,128)(2,1)}, bf16[512,256]{1,0:T(8,128)(2,1)S(1)}, u32[]{:S(2)}, u32[]{:S(2)}) collective-permute-start(bf16[512,256]{1,0:T(8,128)(2,1)} %get-tuple-element.36), channel_id=1, source_target_pairs={{0,3},{1,2},{2,1},{3,0},{4,7},{5,6},{6,5},{7,4},{8,11},{9,10},{10,... | collective-permute-start | bytes 786440 | tf_op jit(solution)/shard_map/ppermute | solution.py:39
  74.7 13.1 %all-to-all-start.2 = ((bf16[8,32,1024]{2,1,0:T(8,128)(2,1)}), bf16[8,32,1024]{2,1,0:T(8,128)(2,1)S(1)}, u32[]{:S(2)}, u32[]{:S(2)}) async-start(bf16[8,32,1024]{2,1,0:T(8,128)(2,1)} %get-tuple-element.37), calls=%async_computation.2 | async-start | bytes 1048576 | tf_op jit(solution)/shard_map/all_to_all | solution.py:463
  81.0 6.9 %collective-permute-start.15 = (bf16[256,256]{1,0:T(8,128)(2,1)S(1)}, bf16[256,256]{1,0:T(8,128)(2,1)S(1)}, u32[]{:S(2)}, u32[]{:S(2)}) collective-permute-start(bf16[256,256]{1,0:T(8,128)(2,1)S(1)} %get-tuple-element.44), channel_id=1, source_target_pairs={{0,8},{1,9},{2,10},{3,11},{4,12},{5,13},{6,14},{7,15},{8,0},{9,1},... | collective-permute-start | bytes 393224 | tf_op jit(solution)/shard_map/ppermute | solution.py:39
  84.9 11.1 %collective-permute-start.17 = (bf16[256,256]{1,0:T(8,128)(2,1)S(1)}, bf16[256,256]{1,0:T(8,128)(2,1)S(1)}, u32[]{:S(2)}, u32[]{:S(2)}) collective-permute-start(bf16[256,256]{1,0:T(8,128)(2,1)S(1)} %get-tuple-element.44), channel_id=1, source_target_pairs={{0,12},{1,13},{2,14},{3,15},{4,8},{5,9},{6,10},{7,11},{8,4},{9,5},... | collective-permute-start | bytes 393224 | tf_op jit(solution)/shard_map/ppermute | solution.py:39
  86.1 9.9 %collective-permute-start.16 = (bf16[256,256]{1,0:T(8,128)(2,1)S(1)}, bf16[256,256]{1,0:T(8,128)(2,1)S(1)}, u32[]{:S(2)}, u32[]{:S(2)}) collective-permute-start(bf16[256,256]{1,0:T(8,128)(2,1)S(1)} %get-tuple-element.45.a), channel_id=1, source_target_pairs={{0,4},{1,5},{2,6},{3,7},{4,0},{5,1},{6,2},{7,3},{8,12},{9,13},{10,... | collective-permute-start | bytes 393224 | tf_op jit(solution)/shard_map/ppermute | solution.py:39
  87.9 11.9 %collective-permute-start.18 = (bf16[256,1024]{1,0:T(8,128)(2,1)S(1)}, bf16[256,1024]{1,0:T(8,128)(2,1)S(1)}, u32[]{:S(2)}, u32[]{:S(2)}) collective-permute-start(bf16[256,1024]{1,0:T(8,128)(2,1)S(1)} %bitcast.6), channel_id=1, source_target_pairs={{0,8},{1,9},{2,10},{3,11},{4,12},{5,13},{6,14},{7,15},{8,0},{9,1},... | collective-permute-start | bytes 1572872 | tf_op jit(solution)/shard_map/ppermute | solution.py:39

commit v8 on v6

--- a/solution.py
+++ b/solution.py
@@ -143,7 +143,7 @@
     share = rows // 8
     per = span // TILE
 
-    def body(ix, tl, se, q, g, k0, k1, k2, k3, v0, v1, v2, v3, out, st_out, y_scr, va):
+    def body(ix, tl, se, q, g, k3, k2, k1, k0, v3, v2, v1, v0, out, st_out, y_scr, va):
         ks = (k0, k1, k2, k3)
         vs = (v0, v1, v2, v3)
         for j in range(n):
@@ -205,7 +205,7 @@
         compiler_params=pltpu.CompilerParams(vmem_limit_bytes=24 << 20),
         name="fwd",
         cost_estimate=cost(7),
-    )(idx, tiles, sees, queries, grad_out, *keys, *values)
+    )(idx, tiles, sees, queries, grad_out, *keys[::-1], *values[::-1])
 
 
 def merge_weights(st, heads):

time: 101 us -> 99.6 us (0.986)
  waiting for transfers between devices: 10.3 us -> 9.01 us
    ppermute x19, waiting for transfers between devices: 10.3 us -> 9 us  [moved(): return lambda x: lax.ppermute(x, AXES, pairs)]
  transfers between devices with their start and end apart: 21 -> 21, of which waited for: 7 -> 6; matrix products, arithmetic and copies ran while one was open for 1% -> 1% of each run, Pallas kernels for 21% -> 21%
where the time goes in v8:
time: 99.6 us; the launch traced here: 99.2 us
  starting transfers between devices  41.6 us (42%)
  Pallas kernels  35.2 us (35%)
  blocking collectives  10.3 us (10%)
  waiting for transfers between devices  9.01 us (9%)
  other arithmetic  1.26 us (1%)
  between operations  1.04 us (1%)
    ppermute x19, starting transfers between devices, moved(): return lambda x: lax.ppermute(x, AXES, pairs)  33.1 us
    pallas_call x2, Pallas kernels, backward(): pl.pallas_call(body, out_shape=out_shape, grid_spec=pltpu.PrefetchScalarG...  13.8 us
    all_to_all x1, blocking collectives, swap8(): return lax.all_to_all(x, 'img', 0, 0, axis_index_groups=chips, tiled=True)  10.3 us
    ppermute x19, waiting for transfers between devices, moved(): return lambda x: lax.ppermute(x, AXES, pairs)  9 us
    all_to_all x2, starting transfers between devices, swap8(): return lax.all_to_all(x, 'img', 0, 0, axis_index_groups=chips, tiled=True)  8.57 us
    pallas_call x1, Pallas kernels, forward(): pl.pallas_call(body, out_shape=(jax.ShapeDtypeStruct((8, share, width), B...  7.72 us
    pallas_call x1, Pallas kernels, project(): pl.pallas_call(body, out_shape=outs, grid_spec=pltpu.PrefetchScalarGridSp...  5.29 us
    pallas_call x1, Pallas kernels, feature_grad(): pl.pallas_call(body, out_shape=(jax.ShapeDtypeStruct((rows, feat), BF), j...  3.7 us
  transfers between devices with their start and end apart: 21, of which 6 were waited for; matrix products, arithmetic and copies ran while one was open for 1% of the time, Pallas kernels for 21%

profile of v8, /device:TPU:1, one launch (start us, length us, event | category | flops | bytes accessed | tf_op | source)
XLA Modules:
  0.0 99.2 jit_solution(12450977328598063165)
XLA Ops:
  0.6 0.7 concatenate.9.ix
  1.4 0.0 copy-start.10
  1.4 5.3 %project.1 = (f32[256,128]{1,0:T(8,128)S(1)}, f32[256,128]{1,0:T(8,128)S(1)}, f32[256,128]{1,0:T(8,128)S(1)}, f32[256,128]{1,0:T(8,128)S(1)}, f32[256,128]{1,0:T...) custom-call(s32[12]{0:T(128)S(1)} %concatenate.9.ix, ...), custom_call_target="tpu_custom_call" | custom-call | flops 4400000000 | bytes 65536 | tf_op jit(solution)/shard_map/project/pallas_call | solution.py:106
  6.7 4.5 %collective-permute-start.7 = (bf16[256,128]{1,0:T(8,128)(2,1)S(1)}, bf16[256,128]{1,0:T(8,128)(2,1)S(1)}, u32[]{:S(2)}, u32[]{:S(2)}) collective-permute-start(bf16[256,128]{1,0:T(8,128)(2,1)S(1)} %get-tuple-element.29), channel_id=1, source_target_pairs={{0,4},{1,5},{2,6},{3,7},{4,0},{5,1},{6,2},{7,3},{8,12},{9,13},{10,... | collective-permute-start | bytes 196616 | tf_op jit(solution)/shard_map/ppermute | solution.py:39
  11.2 1.0 collective-permute-start
  12.2 0.0 collective-permute-start.8
  12.2 2.9 %collective-permute-start.1 = (f32[256,128]{1,0:T(8,128)S(1)}, f32[256,128]{1,0:T(8,128)S(1)}, u32[]{:S(2)}, u32[]{:S(2)}) collective-permute-start(f32[256,128]{1,0:T(8,128)S(1)} %get-tuple-element.25), channel_id=1, source_target_pairs={{0,4},{1,5},{2,6},{3,7},{4,0},{5,1},{6,2},{7,3},{8,12},{9,13},{10,... | collective-permute-start | bytes 393224 | tf_op jit(solution)/shard_map/ppermute | solution.py:39
  15.0 0.8 collective-permute-start.2
  15.8 0.0 collective-permute-done.7
  15.8 2.3 %collective-permute-start.3 = (f32[256,128]{1,0:T(8,128)S(1)}, f32[256,128]{1,0:T(8,128)S(1)}, u32[]{:S(2)}, u32[]{:S(2)}) collective-permute-start(f32[256,128]{1,0:T(8,128)S(1)} %get-tuple-element.27), channel_id=1, source_target_pairs={{0,12},{1,13},{2,14},{3,15},{4,8},{5,9},{6,10},{7,11},{8,4},{9,5},... | collective-permute-start | bytes 393224 | tf_op jit(solution)/shard_map/ppermute | solution.py:39
  18.1 0.0 collective-permute-done.8
  18.1 0.0 collective-permute-done
  18.2 0.0 copy-start
  18.2 3.0 %collective-permute-start.10 = (bf16[512,128]{1,0:T(8,128)(2,1)S(1)}, bf16[512,128]{1,0:T(8,128)(2,1)S(1)}, u32[]{:S(2)}, u32[]{:S(2)}) collective-permute-start(bf16[512,128]{1,0:T(8,128)(2,1)S(1)} %pad_maximum_fusion.1.v0.refs_3_), channel_id=1, source_target_pairs={{0,2},{1,3},{2,0},{3,1},{4,6},{5,7},{6,4},{7,5},{8,10},{9,11},{10,... | collective-permute-start | bytes 393224 | tf_op jit(solution)/shard_map/ppermute | solution.py:39
  21.2 0.4 collective-permute-start.11
  21.6 0.0 collective-permute-done.1
  21.6 1.0 %collective-permute-start.9 = (bf16[512,128]{1,0:T(8,128)(2,1)S(1)}, bf16[512,128]{1,0:T(8,128)(2,1)S(1)}, u32[]{:S(2)}, u32[]{:S(2)}) collective-permute-start(bf16[512,128]{1,0:T(8,128)(2,1)S(1)} %pad_maximum_fusion.1.v0.refs_3_), channel_id=1, source_target_pairs={{0,3},{1,2},{2,1},{3,0},{4,7},{5,6},{6,5},{7,4},{8,11},{9,10},{10,... | collective-permute-start | bytes 393224 | tf_op jit(solution)/shard_map/ppermute | solution.py:39
  22.6 0.0 collective-permute-done.2
  22.6 0.7 collective-permute-done.3
  23.3 0.0 copy-start.1
  23.3 2.8 %collective-permute-start.4 = (bf16[512,128]{1,0:T(8,128)(2,1)S(1)}, bf16[512,128]{1,0:T(8,128)(2,1)S(1)}, u32[]{:S(2)}, u32[]{:S(2)}) collective-permute-start(bf16[512,128]{1,0:T(8,128)(2,1)S(1)} %pad_maximum_fusion.k0.refs_1_), channel_id=1, source_target_pairs={{0,3},{1,2},{2,1},{3,0},{4,7},{5,6},{6,5},{7,4},{8,11},{9,10},{10,... | collective-permute-start | bytes 393224 | tf_op jit(solution)/shard_map/ppermute | solution.py:39
  26.1 0.1 collective-permute-start.5
  26.2 0.0 collective-permute-done.10.v2.refs_2_
  26.2 0.6 collective-permute-start.6
  26.8 0.0 copy-done.11
  26.8 1.3 %collective-permute-done.11.v1.refs_3_ = bf16[512,128]{1,0:T(8,128)(2,1)S(1)} collective-permute-done((bf16[512,128]{1,0:T(8,128)(2,1)S(1)}, bf16[512,128]{1,0:T(8,128)(2,1)S(1)}, u32[]{:S(2)}, u32[]{:S(2)}) %collective-permute-start.11) | collective-permute-done | bytes 131104 | tf_op jit(solution)/shard_map/ppermute | solution.py:39
  28.2 0.0 collective-permute-done.9.v3.refs_2_
  28.2 4.0 %collective-permute-done.4.k3.refs_0_ = bf16[512,128]{1,0:T(8,128)(2,1)S(1)} collective-permute-done((bf16[512,128]{1,0:T(8,128)(2,1)S(1)}, bf16[512,128]{1,0:T(8,128)(2,1)S(1)}, u32[]{:S(2)}, u32[]{:S(2)}) %collective-permute-start.4) | collective-permute-done | bytes 131104 | tf_op jit(solution)/shard_map/ppermute | solution.py:39
  32.2 0.4 collective-permute-done.5.k2.refs_0_
  32.6 0.0 collective-permute-done.6.k1.refs_1_
  32.6 0.0 copy-done.2
  32.6 0.0 copy-done.3
  32.7 0.0 copy-done.10
  32.7 0.0 copy-start.9
  32.7 7.7 %fwd.1 = (bf16[8,32,1024]{2,1,0:T(8,128)(2,1)}, f32[8,16,256]{2,1,0:T(8,128)S(1)}) custom-call(s32[12]{0:T(128)S(1)} %concatenate.9.ix, s32[2,8]{1,0:T(2,128)S(1)} %pad_add_fusion.tl, s32[8,8]{1,0:T(8,128)S(1)} %copy-done.10, bf16[256,2048]{1,0:T(8,128)(2,1)S(1)} %copy-done.2, bf16[256,2048]{1,0:T(8,128)(2,1)S(1)} %copy-done.3, ...), custom_call_target="tpu_custom_call" | custom-call | flops 7699999744 | bytes 65536 | tf_op jit(solution)/shard_map/fwd/pallas_call | solution.py:189
  40.4 0.0 copy-done
  40.4 0.0 copy-done.1
  40.4 0.0 copy-done.5
  40.4 0.0 copy-done.6
  40.5 10.3 %all_to_all.15.st = f32[8,16,256]{2,1,0:T(8,128)S(1)} all-to-all(f32[8,16,256]{2,1,0:T(8,128)S(1)} %get-tuple-element.31), channel_id=1, replica_groups={{0,16,32,48,64,80,96,112},{8,24,40,56,72,88,104,120},{1,17,33,49,65,81,..., dimensions={0} | all-to-all | bytes 262144 | tf_op jit(solution)/shard_map/all_to_all | solution.py:458
  50.8 3.7 %all-to-all-start.1 = ((bf16[8,32,1024]{2,1,0:T(8,128)(2,1)}), bf16[8,32,1024]{2,1,0:T(8,128)(2,1)S(1)}, u32[]{:S(2)}, u32[]{:S(2)}) async-start(bf16[8,32,1024]{2,1,0:T(8,128)(2,1)} %get-tuple-element.32), calls=%async_computation.1 | async-start | bytes 1048576 | tf_op jit(solution)/shard_map/all_to_all | solution.py:458
  54.4 7.0 %grads21.1 = (bf16[512,256]{1,0:T(8,128)(2,1)}, bf16[512,256]{1,0:T(8,128)(2,1)}) custom-call(s32[12]{0:T(128)S(1)} %concatenate.9.ix, s32[2,8]{1,0:T(2,128)S(1)} %pad_add_fusion.tl, s32[8,8]{1,0:T(8,128)S(1)} %copy-done.10, bf16[256,2048]{1,0:T(8,128)(2,1)S(1)} %copy-done.2, bf16[256,2048]{1,0:T(8,128)(2,1)S(1)} %copy-done.3, ...), custom_call_target="tpu_custom_call" | custom-call | flops 6600000000 | bytes 65536 | tf_op jit(solution)/shard_map/grads21/pallas_call | solution.py:310
  61.4 3.1 %collective-permute-start.12 = (bf16[512,256]{1,0:T(8,128)(2,1)}, bf16[512,256]{1,0:T(8,128)(2,1)}, u32[]{:S(2)}, u32[]{:S(2)}) collective-permute-start(bf16[512,256]{1,0:T(8,128)(2,1)} %get-tuple-element.34), channel_id=1, source_target_pairs={{0,2},{1,3},{2,0},{3,1},{4,6},{5,7},{6,4},{7,5},{8,10},{9,11},{10,... | collective-permute-start | bytes 786440 | tf_op jit(solution)/shard_map/ppermute | solution.py:39
  64.5 0.1 collective-permute-start.13
  64.6 0.0 all-to-all-done.1.refs_4_
  64.6 6.8 %grads30.1 = (bf16[512,256]{1,0:T(8,128)(2,1)}, f32[512,256]{1,0:T(8,128)S(1)}, bf16[8,32,1024]{2,1,0:T(8,128)(2,1)}) custom-call(s32[12]{0:T(128)S(1)} %concatenate.9.ix, s32[2,8]{1,0:T(2,128)S(1)} %pad_add_fusion.tl, s32[8,8]{1,0:T(8,128)S(1)} %copy-done.10, bf16[256,2048]{1,0:T(8,128)(2,1)S(1)} %copy-done.2, bf16[256,2048]{1,0:T(8,128)(2,1)S(1)} %copy-done.3, ...), custom_call_target="tpu_custom_call" | custom-call | flops 6600000000 | bytes 65536 | tf_op jit(solution)/shard_map/grads30/pallas_call | solution.py:310
  71.4 0.7 collective-permute-start.14
  72.2 4.9 %all-to-all-start.2 = ((bf16[8,32,1024]{2,1,0:T(8,128)(2,1)}), bf16[8,32,1024]{2,1,0:T(8,128)(2,1)S(1)}, u32[]{:S(2)}, u32[]{:S(2)}) async-start(bf16[8,32,1024]{2,1,0:T(8,128)(2,1)} %get-tuple-element.37), calls=%async_computation.2 | async-start | bytes 1048576 | tf_op jit(solution)/shard_map/all_to_all | solution.py:458
  77.1 0.0 collective-permute-done.12
  77.1 0.0 collective-permute-done.13
  77.1 1.0 collective-permute-done.14
  78.1 1.2 %add_convert_fusion._ = bf16[512,256]{1,0:T(8,128)(2,1)S(1)} fusion(bf16[512,256]{1,0:T(8,128)(2,1)S(1)} %collective-permute-done.14, bf16[512,256]{1,0:T(8,128)(2,1)} %collective-permute-done.13, f32[512,256]{1,0:T(8,128)S(1)} %get-tuple-element.33, bf16[512,256]{1,0:T(8,128)(2,1)} %collective-permute-done.12), kind=kLoop, calls=%fused_computation | loop fusion | flops 917504 | bytes 1572864 | tf_op jit(solution)/shard_map/convert_element_type | solution.py:500
  79.2 4.1 %collective-permute-start.15 = (bf16[256,256]{1,0:T(8,128)(2,1)S(1)}, bf16[256,256]{1,0:T(8,128)(2,1)S(1)}, u32[]{:S(2)}, u32[]{:S(2)}) collective-permute-start(bf16[256,256]{1,0:T(8,128)(2,1)S(1)} %get-tuple-element.44), channel_id=1, source_target_pairs={{0,8},{1,9},{2,10},{3,11},{4,12},{5,13},{6,14},{7,15},{8,0},{9,1},... | collective-permute-start | bytes 393224 | tf_op jit(solution)/shard_map/ppermute | solution.py:39
  83.3 1.7 %collective-permute-start.17 = (bf16[256,256]{1,0:T(8,128)(2,1)S(1)}, bf16[256,256]{1,0:T(8,128)(2,1)S(1)}, u32[]{:S(2)}, u32[]{:S(2)}) collective-permute-start(bf16[256,256]{1,0:T(8,128)(2,1)S(1)} %get-tuple-element.44), channel_id=1, source_target_pairs={{0,12},{1,13},{2,14},{3,15},{4,8},{5,9},{6,10},{7,11},{8,4},{9,5},... | collective-permute-start | bytes 393224 | tf_op jit(solution)/shard_map/ppermute | solution.py:39
  85.0 1.3 %collective-permute-start.16 = (bf16[256,256]{1,0:T(8,128)(2,1)S(1)}, bf16[256,256]{1,0:T(8,128)(2,1)S(1)}, u32[]{:S(2)}, u32[]{:S(2)}) collective-permute-start(bf16[256,256]{1,0:T(8,128)(2,1)S(1)} %get-tuple-element.45.a), channel_id=1, source_target_pairs={{0,4},{1,5},{2,6},{3,7},{4,0},{5,1},{6,2},{7,3},{8,12},{9,13},{10,... | collective-permute-start | bytes 393224 | tf_op jit(solution)/shard_map/ppermute | solution.py:39
  86.3 0.0 collective-permute-done.15.b
  86.3 0.0 all-to-all-done.2
  86.3 2.9 %collective-permute-start.18 = (bf16[256,1024]{1,0:T(8,128)(2,1)S(1)}, bf16[256,1024]{1,0:T(8,128)(2,1)S(1)}, u32[]{:S(2)}, u32[]{:S(2)}) collective-permute-start(bf16[256,1024]{1,0:T(8,128)(2,1)S(1)} %bitcast.6), channel_id=1, source_target_pairs={{0,8},{1,9},{2,10},{3,11},{4,12},{5,13},{6,14},{7,15},{8,0},{9,1},... | collective-permute-start | bytes 1572872 | tf_op jit(solution)/shard_map/ppermute | solution.py:39
  89.2 3.3 %fetch.1 = (bf16[3840,512]{1,0:T(8,128)(2,1)S(1)}, bf16[3840,512]{1,0:T(8,128)(2,1)S(1)}) custom-call(bf16[3840,512]{1,0:T(8,128)(2,1)} %k_hbm.1, bf16[3840,512]{1,0:T(8,128)(2,1)} %v_hbm.1, bf16[512,256]{1,0:T(8,128)(2,1)S(1)} %add_convert_fusion._), custom_call_target="tpu_custom_call" | custom-call | flops 4400000000 | bytes 65536 | tf_op jit(solution)/shard_map/fetch/pallas_call | solution.py:344
  92.5 1.5 %collective-permute-done.16.c_ = bf16[256,256]{1,0:T(8,128)(2,1)S(1)} collective-permute-done((bf16[256,256]{1,0:T(8,128)(2,1)S(1)}, bf16[256,256]{1,0:T(8,128)(2,1)S(1)}, u32[]{:S(2)}, u32[]{:S(2)}) %collective-permute-start.16) | collective-permute-done | bytes 131104 | tf_op jit(solution)/shard_map/ppermute | solution.py:39
  94.0 0.0 collective-permute-done.17.d_
  94.0 3.7 %feats.1 = (bf16[256,3840]{1,0:T(8,128)(2,1)}, bf16[256,2048]{1,0:T(8,128)(2,1)}) custom-call(s32[12]{0:T(128)S(1)} %concatenate.9.ix, bf16[256,256]{1,0:T(8,128)(2,1)S(1)} %get-tuple-element.45.a, bf16[256,256]{1,0:T(8,128)(2,1)S(1)} %collective-permute-done.15.b, bf16[256,256]{1,0:T(8,128)(2,1)S(1)} %collective-permute-done.16.c_, ...), custom_call_target="tpu_custom_call" | custom-call | flops 4400000000 | bytes 65536 | tf_op jit(solution)/shard_map/feats/pallas_call | solution.py:400
  97.7 0.0 collective-permute-done.18.t_ref
  97.7 1.4 %theirs.1 = bf16[256,2048]{1,0:T(8,128)(2,1)} custom-call(s32[12]{0:T(128)S(1)} %concatenate.9.ix, bf16[256,2048]{1,0:T(8,128)(2,1)} %get-tuple-element.42._, bf16[256,1024]{1,0:T(8,128)(2,1)S(1)} %collective-permute-done.18.t_ref), custom_call_target="tpu_custom_call", output_to_operand_aliasing={{}: (1, {})} | custom-call | tf_op jit(solution)/shard_map/theirs/pallas_call | solution.py:433
  (21 shorter events, 0.1 us)
Async XLA Ops:
  1.4 25.4 %copy-start.11 = (s32[8]{0:T(128)S(1)}, s32[8]{0:T(128)}, u32[]{:S(2)}) copy-start(s32[8]{0:T(128)} %param.12) | copy-start | bytes 100
  1.4 31.3 %copy-start.2 = (bf16[256,2048]{1,0:T(8,128)(2,1)S(1)}, bf16[256,2048]{1,0:T(8,128)(2,1)}, u32[]{:S(2)}) copy-start(bf16[256,2048]{1,0:T(8,128)(2,1)} %q.5) | copy-start | bytes 3145732
  1.4 31.3 %copy-start.3 = (bf16[256,2048]{1,0:T(8,128)(2,1)S(1)}, bf16[256,2048]{1,0:T(8,128)(2,1)}, u32[]{:S(2)}) copy-start(bf16[256,2048]{1,0:T(8,128)(2,1)} %g.5) | copy-start | bytes 3145732
  1.4 31.3 %copy-start.10 = (s32[8,8]{1,0:T(8,128)S(1)}, s32[8,8]{1,0:T(8,128)}, u32[]{:S(2)}) copy-start(s32[8,8]{1,0:T(8,128)} %se.5) | copy-start | bytes 772
  6.7 9.1 %collective-permute-start.7 = (bf16[256,128]{1,0:T(8,128)(2,1)S(1)}, bf16[256,128]{1,0:T(8,128)(2,1)S(1)}, u32[]{:S(2)}, u32[]{:S(2)}) collective-permute-start(bf16[256,128]{1,0:T(8,128)(2,1)S(1)} %get-tuple-element.29), channel_id=1, source_target_pairs={{0,4},{1,5},{2,6},{3,7},{4,0},{5,1},{6,2},{7,3},{8,12},{9,13},{10,... | collective-permute-start | bytes 196616 | tf_op jit(solution)/shard_map/ppermute | solution.py:39
  11.2 6.9 %collective-permute-start = (bf16[272,128]{1,0:T(8,128)(2,1)S(1)}, bf16[272,128]{1,0:T(8,128)(2,1)S(1)}, u32[]{:S(2)}, u32[]{:S(2)}) collective-permute-start(bf16[272,128]{1,0:T(8,128)(2,1)S(1)} %get-tuple-element.23), channel_id=1, source_target_pairs={{0,8},{1,9},{2,10},{3,11},{4,12},{5,13},{6,14},{7,15},{8,0},{9,1},... | collective-permute-start | bytes 208904 | tf_op jit(solution)/shard_map/ppermute | solution.py:39
  12.2 5.9 %collective-permute-start.8 = (bf16[256,128]{1,0:T(8,128)(2,1)S(1)}, bf16[256,128]{1,0:T(8,128)(2,1)S(1)}, u32[]{:S(2)}, u32[]{:S(2)}) collective-permute-start(bf16[256,128]{1,0:T(8,128)(2,1)S(1)} %get-tuple-element.30), channel_id=1, source_target_pairs={{0,12},{1,13},{2,14},{3,15},{4,8},{5,9},{6,10},{7,11},{8,4},{9,5},... | collective-permute-start | bytes 196616 | tf_op jit(solution)/shard_map/ppermute | solution.py:39
  12.2 9.4 %collective-permute-start.1 = (f32[256,128]{1,0:T(8,128)S(1)}, f32[256,128]{1,0:T(8,128)S(1)}, u32[]{:S(2)}, u32[]{:S(2)}) collective-permute-start(f32[256,128]{1,0:T(8,128)S(1)} %get-tuple-element.25), channel_id=1, source_target_pairs={{0,4},{1,5},{2,6},{3,7},{4,0},{5,1},{6,2},{7,3},{8,12},{9,13},{10,... | collective-permute-start | bytes 393224 | tf_op jit(solution)/shard_map/ppermute | solution.py:39
  15.0 7.6 %collective-permute-start.2 = (f32[256,128]{1,0:T(8,128)S(1)}, f32[256,128]{1,0:T(8,128)S(1)}, u32[]{:S(2)}, u32[]{:S(2)}) collective-permute-start(f32[256,128]{1,0:T(8,128)S(1)} %get-tuple-element.26), channel_id=1, source_target_pairs={{0,8},{1,9},{2,10},{3,11},{4,12},{5,13},{6,14},{7,15},{8,0},{9,1},... | collective-permute-start | bytes 393224 | tf_op jit(solution)/shard_map/ppermute | solution.py:39
  15.8 7.5 %collective-permute-start.3 = (f32[256,128]{1,0:T(8,128)S(1)}, f32[256,128]{1,0:T(8,128)S(1)}, u32[]{:S(2)}, u32[]{:S(2)}) collective-permute-start(f32[256,128]{1,0:T(8,128)S(1)} %get-tuple-element.27), channel_id=1, source_target_pairs={{0,12},{1,13},{2,14},{3,15},{4,8},{5,9},{6,10},{7,11},{8,4},{9,5},... | collective-permute-start | bytes 393224 | tf_op jit(solution)/shard_map/ppermute | solution.py:39
  18.2 22.2 %copy-start = (bf16[512,128]{1,0:T(8,128)(2,1)}, bf16[512,128]{1,0:T(8,128)(2,1)S(1)}, u32[]{:S(2)}) copy-start(bf16[512,128]{1,0:T(8,128)(2,1)S(1)} %pad_maximum_fusion.1.v0.refs_3_) | copy-start | bytes 393220
  18.2 8.0 %collective-permute-start.10 = (bf16[512,128]{1,0:T(8,128)(2,1)S(1)}, bf16[512,128]{1,0:T(8,128)(2,1)S(1)}, u32[]{:S(2)}, u32[]{:S(2)}) collective-permute-start(bf16[512,128]{1,0:T(8,128)(2,1)S(1)} %pad_maximum_fusion.1.v0.refs_3_), channel_id=1, source_target_pairs={{0,2},{1,3},{2,0},{3,1},{4,6},{5,7},{6,4},{7,5},{8,10},{9,11},{10,... | collective-permute-start | bytes 393224 | tf_op jit(solution)/shard_map/ppermute | solution.py:39
  21.2 7.0 %collective-permute-start.11 = (bf16[512,128]{1,0:T(8,128)(2,1)S(1)}, bf16[512,128]{1,0:T(8,128)(2,1)S(1)}, u32[]{:S(2)}, u32[]{:S(2)}) collective-permute-start(bf16[512,128]{1,0:T(8,128)(2,1)S(1)} %pad_maximum_fusion.1.v0.refs_3_), channel_id=1, source_target_pairs={{0,1},{1,0},{2,3},{3,2},{4,5},{5,4},{6,7},{7,6},{8,9},{9,8},{10,11... | collective-permute-start | bytes 393224 | tf_op jit(solution)/shard_map/ppermute | solution.py:39
  21.6 6.6 %collective-permute-start.9 = (bf16[512,128]{1,0:T(8,128)(2,1)S(1)}, bf16[512,128]{1,0:T(8,128)(2,1)S(1)}, u32[]{:S(2)}, u32[]{:S(2)}) collective-permute-start(bf16[512,128]{1,0:T(8,128)(2,1)S(1)} %pad_maximum_fusion.1.v0.refs_3_), channel_id=1, source_target_pairs={{0,3},{1,2},{2,1},{3,0},{4,7},{5,6},{6,5},{7,4},{8,11},{9,10},{10,... | collective-permute-start | bytes 393224 | tf_op jit(solution)/shard_map/ppermute | solution.py:39
  23.3 17.1 %copy-start.1 = (bf16[512,128]{1,0:T(8,128)(2,1)}, bf16[512,128]{1,0:T(8,128)(2,1)S(1)}, u32[]{:S(2)}) copy-start(bf16[512,128]{1,0:T(8,128)(2,1)S(1)} %pad_maximum_fusion.k0.refs_1_) | copy-start | bytes 393220
  23.3 8.9 %collective-permute-start.4 = (bf16[512,128]{1,0:T(8,128)(2,1)S(1)}, bf16[512,128]{1,0:T(8,128)(2,1)S(1)}, u32[]{:S(2)}, u32[]{:S(2)}) collective-permute-start(bf16[512,128]{1,0:T(8,128)(2,1)S(1)} %pad_maximum_fusion.k0.refs_1_), channel_id=1, source_target_pairs={{0,3},{1,2},{2,1},{3,0},{4,7},{5,6},{6,5},{7,4},{8,11},{9,10},{10,... | collective-permute-start | bytes 393224 | tf_op jit(solution)/shard_map/ppermute | solution.py:39
  26.1 6.5 %collective-permute-start.5 = (bf16[512,128]{1,0:T(8,128)(2,1)S(1)}, bf16[512,128]{1,0:T(8,128)(2,1)S(1)}, u32[]{:S(2)}, u32[]{:S(2)}) collective-permute-start(bf16[512,128]{1,0:T(8,128)(2,1)S(1)} %pad_maximum_fusion.k0.refs_1_), channel_id=1, source_target_pairs={{0,2},{1,3},{2,0},{3,1},{4,6},{5,7},{6,4},{7,5},{8,10},{9,11},{10,... | collective-permute-start | bytes 393224 | tf_op jit(solution)/shard_map/ppermute | solution.py:39
  26.2 14.2 %copy-start.5 = (bf16[512,128]{1,0:T(8,128)(2,1)}, bf16[512,128]{1,0:T(8,128)(2,1)S(1)}, u32[]{:S(2)}) copy-start(bf16[512,128]{1,0:T(8,128)(2,1)S(1)} %collective-permute-done.10.v2.refs_2_) | copy-start | bytes 393220
  26.2 6.4 %collective-permute-start.6 = (bf16[512,128]{1,0:T(8,128)(2,1)S(1)}, bf16[512,128]{1,0:T(8,128)(2,1)S(1)}, u32[]{:S(2)}, u32[]{:S(2)}) collective-permute-start(bf16[512,128]{1,0:T(8,128)(2,1)S(1)} %pad_maximum_fusion.k0.refs_1_), channel_id=1, source_target_pairs={{0,1},{1,0},{2,3},{3,2},{4,5},{5,4},{6,7},{7,6},{8,9},{9,8},{10,11... | collective-permute-start | bytes 393224 | tf_op jit(solution)/shard_map/ppermute | solution.py:39
  28.2 12.2 %copy-start.6 = (bf16[512,128]{1,0:T(8,128)(2,1)}, bf16[512,128]{1,0:T(8,128)(2,1)S(1)}, u32[]{:S(2)}) copy-start(bf16[512,128]{1,0:T(8,128)(2,1)S(1)} %collective-permute-done.11.v1.refs_3_) | copy-start | bytes 393220
  28.2 12.2 %copy-start.4 = (bf16[512,128]{1,0:T(8,128)(2,1)}, bf16[512,128]{1,0:T(8,128)(2,1)S(1)}, u32[]{:S(2)}) copy-start(bf16[512,128]{1,0:T(8,128)(2,1)S(1)} %collective-permute-done.9.v3.refs_2_) | copy-start | bytes 393220
  32.2 8.2 %copy-start.7 = (bf16[512,128]{1,0:T(8,128)(2,1)}, bf16[512,128]{1,0:T(8,128)(2,1)S(1)}, u32[]{:S(2)}) copy-start(bf16[512,128]{1,0:T(8,128)(2,1)S(1)} %collective-permute-done.4.k3.refs_0_) | copy-start | bytes 393220
  32.6 7.8 %copy-start.8 = (bf16[512,128]{1,0:T(8,128)(2,1)}, bf16[512,128]{1,0:T(8,128)(2,1)S(1)}, u32[]{:S(2)}) copy-start(bf16[512,128]{1,0:T(8,128)(2,1)S(1)} %collective-permute-done.5.k2.refs_0_) | copy-start | bytes 393220
  32.7 7.8 %copy-start.9 = (bf16[512,128]{1,0:T(8,128)(2,1)}, bf16[512,128]{1,0:T(8,128)(2,1)S(1)}, u32[]{:S(2)}) copy-start(bf16[512,128]{1,0:T(8,128)(2,1)S(1)} %collective-permute-done.6.k1.refs_1_) | copy-start | bytes 393220
  50.8 13.8 %all-to-all-start.1 = ((bf16[8,32,1024]{2,1,0:T(8,128)(2,1)}), bf16[8,32,1024]{2,1,0:T(8,128)(2,1)S(1)}, u32[]{:S(2)}, u32[]{:S(2)}) async-start(bf16[8,32,1024]{2,1,0:T(8,128)(2,1)} %get-tuple-element.32), calls=%async_computation.1 | async-start | bytes 1048576 | tf_op jit(solution)/shard_map/all_to_all | solution.py:458
  61.4 15.6 %collective-permute-start.12 = (bf16[512,256]{1,0:T(8,128)(2,1)}, bf16[512,256]{1,0:T(8,128)(2,1)}, u32[]{:S(2)}, u32[]{:S(2)}) collective-permute-start(bf16[512,256]{1,0:T(8,128)(2,1)} %get-tuple-element.34), channel_id=1, source_target_pairs={{0,2},{1,3},{2,0},{3,1},{4,6},{5,7},{6,4},{7,5},{8,10},{9,11},{10,... | collective-permute-start | bytes 786440 | tf_op jit(solution)/shard_map/ppermute | solution.py:39
  64.5 12.6 %collective-permute-start.13 = (bf16[512,256]{1,0:T(8,128)(2,1)}, bf16[512,256]{1,0:T(8,128)(2,1)}, u32[]{:S(2)}, u32[]{:S(2)}) collective-permute-start(bf16[512,256]{1,0:T(8,128)(2,1)} %get-tuple-element.35), channel_id=1, source_target_pairs={{0,1},{1,0},{2,3},{3,2},{4,5},{5,4},{6,7},{7,6},{8,9},{9,8},{10,11... | collective-permute-start | bytes 786440 | tf_op jit(solution)/shard_map/ppermute | solution.py:39
  71.4 6.6 %collective-permute-start.14 = (bf16[512,256]{1,0:T(8,128)(2,1)}, bf16[512,256]{1,0:T(8,128)(2,1)S(1)}, u32[]{:S(2)}, u32[]{:S(2)}) collective-permute-start(bf16[512,256]{1,0:T(8,128)(2,1)} %get-tuple-element.36), channel_id=1, source_target_pairs={{0,3},{1,2},{2,1},{3,0},{4,7},{5,6},{6,5},{7,4},{8,11},{9,10},{10,... | collective-permute-start | bytes 786440 | tf_op jit(solution)/shard_map/ppermute | solution.py:39
  72.2 14.1 %all-to-all-start.2 = ((bf16[8,32,1024]{2,1,0:T(8,128)(2,1)}), bf16[8,32,1024]{2,1,0:T(8,128)(2,1)S(1)}, u32[]{:S(2)}, u32[]{:S(2)}) async-start(bf16[8,32,1024]{2,1,0:T(8,128)(2,1)} %get-tuple-element.37), calls=%async_computation.2 | async-start | bytes 1048576 | tf_op jit(solution)/shard_map/all_to_all | solution.py:458
  79.2 7.1 %collective-permute-start.15 = (bf16[256,256]{1,0:T(8,128)(2,1)S(1)}, bf16[256,256]{1,0:T(8,128)(2,1)S(1)}, u32[]{:S(2)}, u32[]{:S(2)}) collective-permute-start(bf16[256,256]{1,0:T(8,128)(2,1)S(1)} %get-tuple-element.44), channel_id=1, source_target_pairs={{0,8},{1,9},{2,10},{3,11},{4,12},{5,13},{6,14},{7,15},{8,0},{9,1},... | collective-permute-start | bytes 393224 | tf_op jit(solution)/shard_map/ppermute | solution.py:39
  83.3 10.7 %collective-permute-start.17 = (bf16[256,256]{1,0:T(8,128)(2,1)S(1)}, bf16[256,256]{1,0:T(8,128)(2,1)S(1)}, u32[]{:S(2)}, u32[]{:S(2)}) collective-permute-start(bf16[256,256]{1,0:T(8,128)(2,1)S(1)} %get-tuple-element.44), channel_id=1, source_target_pairs={{0,12},{1,13},{2,14},{3,15},{4,8},{5,9},{6,10},{7,11},{8,4},{9,5},... | collective-permute-start | bytes 393224 | tf_op jit(solution)/shard_map/ppermute | solution.py:39
  85.0 9.0 %collective-permute-start.16 = (bf16[256,256]{1,0:T(8,128)(2,1)S(1)}, bf16[256,256]{1,0:T(8,128)(2,1)S(1)}, u32[]{:S(2)}, u32[]{:S(2)}) collective-permute-start(bf16[256,256]{1,0:T(8,128)(2,1)S(1)} %get-tuple-element.45.a), channel_id=1, source_target_pairs={{0,4},{1,5},{2,6},{3,7},{4,0},{5,1},{6,2},{7,3},{8,12},{9,13},{10,... | collective-permute-start | bytes 393224 | tf_op jit(solution)/shard_map/ppermute | solution.py:39
  86.3 11.4 %collective-permute-start.18 = (bf16[256,1024]{1,0:T(8,128)(2,1)S(1)}, bf16[256,1024]{1,0:T(8,128)(2,1)S(1)}, u32[]{:S(2)}, u32[]{:S(2)}) collective-permute-start(bf16[256,1024]{1,0:T(8,128)(2,1)S(1)} %bitcast.6), channel_id=1, source_target_pairs={{0,8},{1,9},{2,10},{3,11},{4,12},{5,13},{6,14},{7,15},{8,0},{9,1},... | collective-permute-start | bytes 1572872 | tf_op jit(solution)/shard_map/ppermute | solution.py:39

commit v9 on v8

--- a/solution.py
+++ b/solution.py
@@ -240,7 +240,7 @@
             out[i, :, cols] = v
 
 
-def backward(idx, tiles, sees, queries, grad_out, keys, values, stats, chunks, parts=None):
+def backward(idx, tiles, sees, queries, grad_out, keys, values, stats, chunks, parts=None, after=None):
     rows = queries.shape[0]
     heads = 8
     width = heads * HD
@@ -254,7 +254,7 @@
         if parts is None:
             outs, (dk, dv) = refs[:n], refs[n:]
         else:
-            x, outs, (merged, dk, dv, w_scr) = refs[0], refs[1 : n + 1], refs[n + 1 :]
+            x, outs, (merged, dk, dv, w_scr) = refs[0], refs[2 : n + 2], refs[n + 2 :]
         lane = lax.broadcasted_iota(jnp.int32, (1, rows), 1)
         for chunk, k_ref, v_ref, out in zip(chunks, k_refs, v_refs, outs):
             caps = [
@@ -302,8 +302,8 @@
     scratch = [pltpu.VMEM((span, HD), F32)] * 2
     more = []
     if parts is not None:
-        more.append(parts)
-        in_specs.append(spec(parts.shape))
+        more += [parts, after]
+        in_specs += [spec(parts.shape), pl.BlockSpec(memory_space=pl.ANY)]
         out_shape.append(jax.ShapeDtypeStruct(parts.shape, BF))
         out_specs.append(spec(parts.shape))
         scratch.append(pltpu.VMEM((rows, HD), F32))
@@ -492,7 +492,8 @@
             return backward(idx, tiles, text_sees, queries, grad_out, keys, values, stats, chunks, *more)
 
         second, first = grads((2, 1))
-        third, total, merged = grads((3, 0), parts)
+        (third,) = grads((3,))
+        total, merged = grads((0,), parts, third)
         far = [to_t[2](second), to_t[1](first), to_t[3](third)]
         mine = swap8(merged).reshape(queries.shape[0], -1)
         for x in far:

time: 99.6 us -> 101 us (1.014)
  Pallas kernels: 35.2 us -> 37.6 us
  waiting for transfers between devices: 9.01 us -> 7.25 us
    pallas_call x2 -> x3, Pallas kernels: 13.8 us -> 16.2 us  [backward(): pl.pallas_call(body, out_shape=out_shape, grid_spec=pltpu.PrefetchScalarG...]
    ppermute x19, waiting for transfers between devices: 9 us -> 7.24 us  [moved(): return lambda x: lax.ppermute(x, AXES, pairs)]
  transfers between devices with their start and end apart: 21 -> 21, of which waited for: 6 -> 5; matrix products, arithmetic and copies ran while one was open for 1% -> 1% of each run, Pallas kernels for 21% -> 23%
where the time goes in v9:
time: 101 us
  starting transfers between devices  42.5 us (42%)
  Pallas kernels  37.6 us (37%)
  blocking collectives  10.3 us (10%)
  waiting for transfers between devices  7.25 us (7%)
  other arithmetic  1.33 us (1%)
  between operations  1.05 us (1%)
    ppermute x19, starting transfers between devices, moved(): return lambda x: lax.ppermute(x, AXES, pairs)  34 us
    pallas_call x3, Pallas kernels, backward(): pl.pallas_call(body, out_shape=out_shape, grid_spec=pltpu.PrefetchScalarG...  16.2 us
    all_to_all x1, blocking collectives, swap8(): return lax.all_to_all(x, 'img', 0, 0, axis_index_groups=chips, tiled=True)  10.3 us
    all_to_all x2, starting transfers between devices, swap8(): return lax.all_to_all(x, 'img', 0, 0, axis_index_groups=chips, tiled=True)  8.56 us
    pallas_call x1, Pallas kernels, forward(): pl.pallas_call(body, out_shape=(jax.ShapeDtypeStruct((8, share, width), B...  7.73 us
    ppermute x19, waiting for transfers between devices, moved(): return lambda x: lax.ppermute(x, AXES, pairs)  7.24 us
    pallas_call x1, Pallas kernels, project(): pl.pallas_call(body, out_shape=outs, grid_spec=pltpu.PrefetchScalarGridSp...  5.29 us
    pallas_call x1, Pallas kernels, feature_grad(): pl.pallas_call(body, out_shape=(jax.ShapeDtypeStruct((rows, feat), BF), j...  3.7 us
  transfers between devices with their start and end apart: 21, of which 5 were waited for; matrix products, arithmetic and copies ran while one was open for 1% of the time, Pallas kernels for 23%

profile of v9, /device:TPU:1, one launch (start us, length us, event | category | flops | bytes accessed | tf_op | source)
XLA Modules:
  0.0 100.8 jit_solution(3640394072597428288)
XLA Ops:
  0.6 0.7 concatenate.9.ix
  1.4 0.0 copy-start.10
  1.4 5.3 %project.1 = (f32[256,128]{1,0:T(8,128)S(1)}, f32[256,128]{1,0:T(8,128)S(1)}, f32[256,128]{1,0:T(8,128)S(1)}, f32[256,128]{1,0:T(8,128)S(1)}, f32[256,128]{1,0:T...) custom-call(s32[12]{0:T(128)S(1)} %concatenate.9.ix, ...), custom_call_target="tpu_custom_call" | custom-call | flops 4400000000 | bytes 65536 | tf_op jit(solution)/shard_map/project/pallas_call | solution.py:106
  6.7 4.5 %collective-permute-start.7 = (bf16[256,128]{1,0:T(8,128)(2,1)S(1)}, bf16[256,128]{1,0:T(8,128)(2,1)S(1)}, u32[]{:S(2)}, u32[]{:S(2)}) collective-permute-start(bf16[256,128]{1,0:T(8,128)(2,1)S(1)} %get-tuple-element.28), channel_id=1, source_target_pairs={{0,4},{1,5},{2,6},{3,7},{4,0},{5,1},{6,2},{7,3},{8,12},{9,13},{10,... | collective-permute-start | bytes 196616 | tf_op jit(solution)/shard_map/ppermute | solution.py:39
  11.2 1.0 collective-permute-start
  12.2 0.0 collective-permute-start.8
  12.2 2.9 %collective-permute-start.1 = (f32[256,128]{1,0:T(8,128)S(1)}, f32[256,128]{1,0:T(8,128)S(1)}, u32[]{:S(2)}, u32[]{:S(2)}) collective-permute-start(f32[256,128]{1,0:T(8,128)S(1)} %get-tuple-element.24), channel_id=1, source_target_pairs={{0,4},{1,5},{2,6},{3,7},{4,0},{5,1},{6,2},{7,3},{8,12},{9,13},{10,... | collective-permute-start | bytes 393224 | tf_op jit(solution)/shard_map/ppermute | solution.py:39
  15.0 0.8 collective-permute-start.2
  15.8 0.0 collective-permute-done.7
  15.8 2.3 %collective-permute-start.3 = (f32[256,128]{1,0:T(8,128)S(1)}, f32[256,128]{1,0:T(8,128)S(1)}, u32[]{:S(2)}, u32[]{:S(2)}) collective-permute-start(f32[256,128]{1,0:T(8,128)S(1)} %get-tuple-element.26), channel_id=1, source_target_pairs={{0,12},{1,13},{2,14},{3,15},{4,8},{5,9},{6,10},{7,11},{8,4},{9,5},... | collective-permute-start | bytes 393224 | tf_op jit(solution)/shard_map/ppermute | solution.py:39
  18.1 0.0 collective-permute-done.8
  18.1 0.0 collective-permute-done
  18.2 0.0 copy-start
  18.2 3.0 %collective-permute-start.10 = (bf16[512,128]{1,0:T(8,128)(2,1)S(1)}, bf16[512,128]{1,0:T(8,128)(2,1)S(1)}, u32[]{:S(2)}, u32[]{:S(2)}) collective-permute-start(bf16[512,128]{1,0:T(8,128)(2,1)S(1)} %pad_maximum_fusion.1.v0.refs_1_), channel_id=1, source_target_pairs={{0,2},{1,3},{2,0},{3,1},{4,6},{5,7},{6,4},{7,5},{8,10},{9,11},{10,... | collective-permute-start | bytes 393224 | tf_op jit(solution)/shard_map/ppermute | solution.py:39
  21.2 0.4 collective-permute-start.11
  21.6 0.0 collective-permute-done.1
  21.6 1.0 collective-permute-start.9
  22.6 0.0 collective-permute-done.2
  22.6 0.7 collective-permute-done.3
  23.3 0.0 copy-start.1
  23.3 2.8 %collective-permute-start.4 = (bf16[512,128]{1,0:T(8,128)(2,1)S(1)}, bf16[512,128]{1,0:T(8,128)(2,1)S(1)}, u32[]{:S(2)}, u32[]{:S(2)}) collective-permute-start(bf16[512,128]{1,0:T(8,128)(2,1)S(1)} %pad_maximum_fusion.k0.refs_0_), channel_id=1, source_target_pairs={{0,3},{1,2},{2,1},{3,0},{4,7},{5,6},{6,5},{7,4},{8,11},{9,10},{10,... | collective-permute-start | bytes 393224 | tf_op jit(solution)/shard_map/ppermute | solution.py:39
  26.1 0.1 collective-permute-start.5
  26.2 0.0 collective-permute-done.10.v2.refs_2_
  26.2 0.6 collective-permute-start.6
  26.8 0.0 copy-done.11
  26.8 1.3 %collective-permute-done.11.v1.refs_3_ = bf16[512,128]{1,0:T(8,128)(2,1)S(1)} collective-permute-done((bf16[512,128]{1,0:T(8,128)(2,1)S(1)}, bf16[512,128]{1,0:T(8,128)(2,1)S(1)}, u32[]{:S(2)}, u32[]{:S(2)}) %collective-permute-start.11) | collective-permute-done | bytes 131104 | tf_op jit(solution)/shard_map/ppermute | solution.py:39
  28.2 0.0 collective-permute-done.9.v3.refs_1_
  28.2 4.0 %collective-permute-done.4.k3.refs_0_ = bf16[512,128]{1,0:T(8,128)(2,1)S(1)} collective-permute-done((bf16[512,128]{1,0:T(8,128)(2,1)S(1)}, bf16[512,128]{1,0:T(8,128)(2,1)S(1)}, u32[]{:S(2)}, u32[]{:S(2)}) %collective-permute-start.4) | collective-permute-done | bytes 131104 | tf_op jit(solution)/shard_map/ppermute | solution.py:39
  32.2 0.4 collective-permute-done.5.k2.refs_0_
  32.6 0.0 collective-permute-done.6.k1.refs_1_
  32.6 0.0 copy-done.2
  32.6 0.0 copy-done.3
  32.7 0.0 copy-done.10
  32.7 0.0 copy-start.9
  32.7 7.7 %fwd.1 = (bf16[8,32,1024]{2,1,0:T(8,128)(2,1)}, f32[8,16,256]{2,1,0:T(8,128)S(1)}) custom-call(s32[12]{0:T(128)S(1)} %concatenate.9.ix, s32[2,8]{1,0:T(2,128)S(1)} %pad_add_fusion.tl, s32[8,8]{1,0:T(8,128)S(1)} %copy-done.10, bf16[256,2048]{1,0:T(8,128)(2,1)S(1)} %copy-done.2, bf16[256,2048]{1,0:T(8,128)(2,1)S(1)} %copy-done.3, ...), custom_call_target="tpu_custom_call" | custom-call | flops 7699999744 | bytes 65536 | tf_op jit(solution)/shard_map/fwd/pallas_call | solution.py:189
  40.4 0.0 copy-done
  40.4 0.0 copy-done.1
  40.4 0.0 copy-done.5
  40.5 10.3 %all_to_all.15.st = f32[8,16,256]{2,1,0:T(8,128)S(1)} all-to-all(f32[8,16,256]{2,1,0:T(8,128)S(1)} %get-tuple-element.30), channel_id=1, replica_groups={{0,16,32,48,64,80,96,112},{8,24,40,56,72,88,104,120},{1,17,33,49,65,81,..., dimensions={0} | all-to-all | bytes 262144 | tf_op jit(solution)/shard_map/all_to_all | solution.py:458
  50.8 3.7 %all-to-all-start.1 = ((bf16[8,32,1024]{2,1,0:T(8,128)(2,1)}), bf16[8,32,1024]{2,1,0:T(8,128)(2,1)S(1)}, u32[]{:S(2)}, u32[]{:S(2)}) async-start(bf16[8,32,1024]{2,1,0:T(8,128)(2,1)} %get-tuple-element.31), calls=%async_computation.1 | async-start | bytes 1048576 | tf_op jit(solution)/shard_map/all_to_all | solution.py:458
  54.4 7.0 %grads21.1 = (bf16[512,256]{1,0:T(8,128)(2,1)}, bf16[512,256]{1,0:T(8,128)(2,1)}) custom-call(s32[12]{0:T(128)S(1)} %concatenate.9.ix, s32[2,8]{1,0:T(2,128)S(1)} %pad_add_fusion.tl, s32[8,8]{1,0:T(8,128)S(1)} %copy-done.10, bf16[256,2048]{1,0:T(8,128)(2,1)S(1)} %copy-done.2, bf16[256,2048]{1,0:T(8,128)(2,1)S(1)} %copy-done.3, ...), custom_call_target="tpu_custom_call" | custom-call | flops 6600000000 | bytes 65536 | tf_op jit(solution)/shard_map/grads21/pallas_call | solution.py:310
  61.4 3.1 %collective-permute-start.12 = (bf16[512,256]{1,0:T(8,128)(2,1)}, bf16[512,256]{1,0:T(8,128)(2,1)}, u32[]{:S(2)}, u32[]{:S(2)}) collective-permute-start(bf16[512,256]{1,0:T(8,128)(2,1)} %get-tuple-element.33), channel_id=1, source_target_pairs={{0,2},{1,3},{2,0},{3,1},{4,6},{5,7},{6,4},{7,5},{8,10},{9,11},{10,... | collective-permute-start | bytes 786440 | tf_op jit(solution)/shard_map/ppermute | solution.py:39
  64.5 0.1 collective-permute-start.13
  64.6 4.7 %grads3.1.refs_3_ = bf16[512,256]{1,0:T(8,128)(2,1)} custom-call(s32[12]{0:T(128)S(1)} %concatenate.9.ix, s32[2,8]{1,0:T(2,128)S(1)} %pad_add_fusion.tl, s32[8,8]{1,0:T(8,128)S(1)} %copy-done.10, bf16[256,2048]{1,0:T(8,128)(2,1)S(1)} %copy-done.2, bf16[256,2048]{1,0:T(8,128)(2,1)S(1)} %copy-done.3, f32[8,16,256]{2,1,0:T(8,128)S(1)} %all_to_all.15.st, ...), custom_call_target="tpu_custom_call" | custom-call | flops 3300000000 | bytes 65536 | tf_op jit(solution)/shard_map/grads3/pallas_call | solution.py:310
  69.3 0.7 collective-permute-start.14
  70.0 0.0 all-to-all-done.1.refs_2_
  70.0 4.5 %grads0.1 = (f32[512,256]{1,0:T(8,128)S(1)}, bf16[8,32,1024]{2,1,0:T(8,128)(2,1)}) custom-call(s32[12]{0:T(128)S(1)} %concatenate.9.ix, s32[2,8]{1,0:T(2,128)S(1)} %pad_add_fusion.tl, s32[8,8]{1,0:T(8,128)S(1)} %copy-done.10, bf16[256,2048]{1,0:T(8,128)(2,1)S(1)} %copy-done.2, bf16[256,2048]{1,0:T(8,128)(2,1)S(1)} %copy-done.3, ...), custom_call_target="tpu_custom_call" | custom-call | flops 3300000000 | bytes 65536 | tf_op jit(solution)/shard_map/grads0/pallas_call | solution.py:310
  74.5 4.9 %all-to-all-start.2 = ((bf16[8,32,1024]{2,1,0:T(8,128)(2,1)}), bf16[8,32,1024]{2,1,0:T(8,128)(2,1)S(1)}, u32[]{:S(2)}, u32[]{:S(2)}) async-start(bf16[8,32,1024]{2,1,0:T(8,128)(2,1)} %get-tuple-element.35), calls=%async_computation.2 | async-start | bytes 1048576 | tf_op jit(solution)/shard_map/all_to_all | solution.py:458
  79.4 0.0 collective-permute-done.12
  79.4 0.0 collective-permute-done.13
  79.4 0.0 collective-permute-done.14
  79.4 1.2 %add_convert_fusion._ = bf16[512,256]{1,0:T(8,128)(2,1)S(1)} fusion(bf16[512,256]{1,0:T(8,128)(2,1)} %collective-permute-done.14, bf16[512,256]{1,0:T(8,128)(2,1)} %collective-permute-done.13, f32[512,256]{1,0:T(8,128)S(1)} %get-tuple-element.32, bf16[512,256]{1,0:T(8,128)(2,1)} %collective-permute-done.12), kind=kLoop, calls=%fused_computation | loop fusion | flops 917504 | bytes 1572864 | tf_op jit(solution)/shard_map/convert_element_type | solution.py:501
  80.7 3.5 %collective-permute-start.15 = (bf16[256,256]{1,0:T(8,128)(2,1)S(1)}, bf16[256,256]{1,0:T(8,128)(2,1)S(1)}, u32[]{:S(2)}, u32[]{:S(2)}) collective-permute-start(bf16[256,256]{1,0:T(8,128)(2,1)S(1)} %get-tuple-element.42), channel_id=1, source_target_pairs={{0,8},{1,9},{2,10},{3,11},{4,12},{5,13},{6,14},{7,15},{8,0},{9,1},... | collective-permute-start | bytes 393224 | tf_op jit(solution)/shard_map/ppermute | solution.py:39
  84.2 2.2 %collective-permute-start.17 = (bf16[256,256]{1,0:T(8,128)(2,1)S(1)}, bf16[256,256]{1,0:T(8,128)(2,1)S(1)}, u32[]{:S(2)}, u32[]{:S(2)}) collective-permute-start(bf16[256,256]{1,0:T(8,128)(2,1)S(1)} %get-tuple-element.42), channel_id=1, source_target_pairs={{0,12},{1,13},{2,14},{3,15},{4,8},{5,9},{6,10},{7,11},{8,4},{9,5},... | collective-permute-start | bytes 393224 | tf_op jit(solution)/shard_map/ppermute | solution.py:39
  86.4 0.7 collective-permute-start.16
  87.2 0.0 collective-permute-done.15.b
  87.2 0.0 all-to-all-done.2
  87.2 4.4 %collective-permute-start.18 = (bf16[256,1024]{1,0:T(8,128)(2,1)S(1)}, bf16[256,1024]{1,0:T(8,128)(2,1)S(1)}, u32[]{:S(2)}, u32[]{:S(2)}) collective-permute-start(bf16[256,1024]{1,0:T(8,128)(2,1)S(1)} %bitcast.6), channel_id=1, source_target_pairs={{0,8},{1,9},{2,10},{3,11},{4,12},{5,13},{6,14},{7,15},{8,0},{9,1},... | collective-permute-start | bytes 1572872 | tf_op jit(solution)/shard_map/ppermute | solution.py:39
  91.5 3.3 %fetch.1 = (bf16[3840,512]{1,0:T(8,128)(2,1)S(1)}, bf16[3840,512]{1,0:T(8,128)(2,1)S(1)}) custom-call(bf16[3840,512]{1,0:T(8,128)(2,1)} %k_hbm.1, bf16[3840,512]{1,0:T(8,128)(2,1)} %v_hbm.1, bf16[512,256]{1,0:T(8,128)(2,1)S(1)} %add_convert_fusion._), custom_call_target="tpu_custom_call" | custom-call | flops 4400000000 | bytes 65536 | tf_op jit(solution)/shard_map/fetch/pallas_call | solution.py:344
  94.9 0.7 collective-permute-done.16.c_
  95.6 0.0 collective-permute-done.17.d_
  95.6 3.7 %feats.1 = (bf16[256,3840]{1,0:T(8,128)(2,1)}, bf16[256,2048]{1,0:T(8,128)(2,1)}) custom-call(s32[12]{0:T(128)S(1)} %concatenate.9.ix, bf16[256,256]{1,0:T(8,128)(2,1)S(1)} %get-tuple-element.43.a, bf16[256,256]{1,0:T(8,128)(2,1)S(1)} %collective-permute-done.15.b, bf16[256,256]{1,0:T(8,128)(2,1)S(1)} %collective-permute-done.16.c_, ...), custom_call_target="tpu_custom_call" | custom-call | flops 4400000000 | bytes 65536 | tf_op jit(solution)/shard_map/feats/pallas_call | solution.py:400
  99.3 0.0 collective-permute-done.18.t_ref
  99.3 1.4 %theirs.1 = bf16[256,2048]{1,0:T(8,128)(2,1)} custom-call(s32[12]{0:T(128)S(1)} %concatenate.9.ix, bf16[256,2048]{1,0:T(8,128)(2,1)} %get-tuple-element.40._, bf16[256,1024]{1,0:T(8,128)(2,1)S(1)} %collective-permute-done.18.t_ref), custom_call_target="tpu_custom_call", output_to_operand_aliasing={{}: (1, {})} | custom-call | tf_op jit(solution)/shard_map/theirs/pallas_call | solution.py:433
  (22 shorter events, 0.2 us)
Async XLA Ops:
  1.4 25.4 %copy-start.11 = (s32[8]{0:T(128)S(1)}, s32[8]{0:T(128)}, u32[]{:S(2)}) copy-start(s32[8]{0:T(128)} %param.12) | copy-start | bytes 100
  1.4 31.3 %copy-start.2 = (bf16[256,2048]{1,0:T(8,128)(2,1)S(1)}, bf16[256,2048]{1,0:T(8,128)(2,1)}, u32[]{:S(2)}) copy-start(bf16[256,2048]{1,0:T(8,128)(2,1)} %q.7) | copy-start | bytes 3145732
  1.4 31.3 %copy-start.3 = (bf16[256,2048]{1,0:T(8,128)(2,1)S(1)}, bf16[256,2048]{1,0:T(8,128)(2,1)}, u32[]{:S(2)}) copy-start(bf16[256,2048]{1,0:T(8,128)(2,1)} %g.7) | copy-start | bytes 3145732
  1.4 31.3 %copy-start.10 = (s32[8,8]{1,0:T(8,128)S(1)}, s32[8,8]{1,0:T(8,128)}, u32[]{:S(2)}) copy-start(s32[8,8]{1,0:T(8,128)} %se.7) | copy-start | bytes 772
  6.7 9.1 %collective-permute-start.7 = (bf16[256,128]{1,0:T(8,128)(2,1)S(1)}, bf16[256,128]{1,0:T(8,128)(2,1)S(1)}, u32[]{:S(2)}, u32[]{:S(2)}) collective-permute-start(bf16[256,128]{1,0:T(8,128)(2,1)S(1)} %get-tuple-element.28), channel_id=1, source_target_pairs={{0,4},{1,5},{2,6},{3,7},{4,0},{5,1},{6,2},{7,3},{8,12},{9,13},{10,... | collective-permute-start | bytes 196616 | tf_op jit(solution)/shard_map/ppermute | solution.py:39
  11.2 6.9 %collective-permute-start = (bf16[272,128]{1,0:T(8,128)(2,1)S(1)}, bf16[272,128]{1,0:T(8,128)(2,1)S(1)}, u32[]{:S(2)}, u32[]{:S(2)}) collective-permute-start(bf16[272,128]{1,0:T(8,128)(2,1)S(1)} %get-tuple-element.22), channel_id=1, source_target_pairs={{0,8},{1,9},{2,10},{3,11},{4,12},{5,13},{6,14},{7,15},{8,0},{9,1},... | collective-permute-start | bytes 208904 | tf_op jit(solution)/shard_map/ppermute | solution.py:39
  12.2 5.9 %collective-permute-start.8 = (bf16[256,128]{1,0:T(8,128)(2,1)S(1)}, bf16[256,128]{1,0:T(8,128)(2,1)S(1)}, u32[]{:S(2)}, u32[]{:S(2)}) collective-permute-start(bf16[256,128]{1,0:T(8,128)(2,1)S(1)} %get-tuple-element.29), channel_id=1, source_target_pairs={{0,12},{1,13},{2,14},{3,15},{4,8},{5,9},{6,10},{7,11},{8,4},{9,5},... | collective-permute-start | bytes 196616 | tf_op jit(solution)/shard_map/ppermute | solution.py:39
  12.2 9.4 %collective-permute-start.1 = (f32[256,128]{1,0:T(8,128)S(1)}, f32[256,128]{1,0:T(8,128)S(1)}, u32[]{:S(2)}, u32[]{:S(2)}) collective-permute-start(f32[256,128]{1,0:T(8,128)S(1)} %get-tuple-element.24), channel_id=1, source_target_pairs={{0,4},{1,5},{2,6},{3,7},{4,0},{5,1},{6,2},{7,3},{8,12},{9,13},{10,... | collective-permute-start | bytes 393224 | tf_op jit(solution)/shard_map/ppermute | solution.py:39
  15.0 7.6 %collective-permute-start.2 = (f32[256,128]{1,0:T(8,128)S(1)}, f32[256,128]{1,0:T(8,128)S(1)}, u32[]{:S(2)}, u32[]{:S(2)}) collective-permute-start(f32[256,128]{1,0:T(8,128)S(1)} %get-tuple-element.25), channel_id=1, source_target_pairs={{0,8},{1,9},{2,10},{3,11},{4,12},{5,13},{6,14},{7,15},{8,0},{9,1},... | collective-permute-start | bytes 393224 | tf_op jit(solution)/shard_map/ppermute | solution.py:39
  15.8 7.5 %collective-permute-start.3 = (f32[256,128]{1,0:T(8,128)S(1)}, f32[256,128]{1,0:T(8,128)S(1)}, u32[]{:S(2)}, u32[]{:S(2)}) collective-permute-start(f32[256,128]{1,0:T(8,128)S(1)} %get-tuple-element.26), channel_id=1, source_target_pairs={{0,12},{1,13},{2,14},{3,15},{4,8},{5,9},{6,10},{7,11},{8,4},{9,5},... | collective-permute-start | bytes 393224 | tf_op jit(solution)/shard_map/ppermute | solution.py:39
  18.2 22.3 %copy-start = (bf16[512,128]{1,0:T(8,128)(2,1)}, bf16[512,128]{1,0:T(8,128)(2,1)S(1)}, u32[]{:S(2)}) copy-start(bf16[512,128]{1,0:T(8,128)(2,1)S(1)} %pad_maximum_fusion.1.v0.refs_1_) | copy-start | bytes 393220
  18.2 8.0 %collective-permute-start.10 = (bf16[512,128]{1,0:T(8,128)(2,1)S(1)}, bf16[512,128]{1,0:T(8,128)(2,1)S(1)}, u32[]{:S(2)}, u32[]{:S(2)}) collective-permute-start(bf16[512,128]{1,0:T(8,128)(2,1)S(1)} %pad_maximum_fusion.1.v0.refs_1_), channel_id=1, source_target_pairs={{0,2},{1,3},{2,0},{3,1},{4,6},{5,7},{6,4},{7,5},{8,10},{9,11},{10,... | collective-permute-start | bytes 393224 | tf_op jit(solution)/shard_map/ppermute | solution.py:39
  21.2 7.0 %collective-permute-start.11 = (bf16[512,128]{1,0:T(8,128)(2,1)S(1)}, bf16[512,128]{1,0:T(8,128)(2,1)S(1)}, u32[]{:S(2)}, u32[]{:S(2)}) collective-permute-start(bf16[512,128]{1,0:T(8,128)(2,1)S(1)} %pad_maximum_fusion.1.v0.refs_1_), channel_id=1, source_target_pairs={{0,1},{1,0},{2,3},{3,2},{4,5},{5,4},{6,7},{7,6},{8,9},{9,8},{10,11... | collective-permute-start | bytes 393224 | tf_op jit(solution)/shard_map/ppermute | solution.py:39
  21.6 6.6 %collective-permute-start.9 = (bf16[512,128]{1,0:T(8,128)(2,1)S(1)}, bf16[512,128]{1,0:T(8,128)(2,1)S(1)}, u32[]{:S(2)}, u32[]{:S(2)}) collective-permute-start(bf16[512,128]{1,0:T(8,128)(2,1)S(1)} %pad_maximum_fusion.1.v0.refs_1_), channel_id=1, source_target_pairs={{0,3},{1,2},{2,1},{3,0},{4,7},{5,6},{6,5},{7,4},{8,11},{9,10},{10,... | collective-permute-start | bytes 393224 | tf_op jit(solution)/shard_map/ppermute | solution.py:39
  23.3 17.1 %copy-start.1 = (bf16[512,128]{1,0:T(8,128)(2,1)}, bf16[512,128]{1,0:T(8,128)(2,1)S(1)}, u32[]{:S(2)}) copy-start(bf16[512,128]{1,0:T(8,128)(2,1)S(1)} %pad_maximum_fusion.k0.refs_0_) | copy-start | bytes 393220
  23.3 8.9 %collective-permute-start.4 = (bf16[512,128]{1,0:T(8,128)(2,1)S(1)}, bf16[512,128]{1,0:T(8,128)(2,1)S(1)}, u32[]{:S(2)}, u32[]{:S(2)}) collective-permute-start(bf16[512,128]{1,0:T(8,128)(2,1)S(1)} %pad_maximum_fusion.k0.refs_0_), channel_id=1, source_target_pairs={{0,3},{1,2},{2,1},{3,0},{4,7},{5,6},{6,5},{7,4},{8,11},{9,10},{10,... | collective-permute-start | bytes 393224 | tf_op jit(solution)/shard_map/ppermute | solution.py:39
  26.1 6.5 %collective-permute-start.5 = (bf16[512,128]{1,0:T(8,128)(2,1)S(1)}, bf16[512,128]{1,0:T(8,128)(2,1)S(1)}, u32[]{:S(2)}, u32[]{:S(2)}) collective-permute-start(bf16[512,128]{1,0:T(8,128)(2,1)S(1)} %pad_maximum_fusion.k0.refs_0_), channel_id=1, source_target_pairs={{0,2},{1,3},{2,0},{3,1},{4,6},{5,7},{6,4},{7,5},{8,10},{9,11},{10,... | collective-permute-start | bytes 393224 | tf_op jit(solution)/shard_map/ppermute | solution.py:39
  26.2 14.2 %copy-start.5 = (bf16[512,128]{1,0:T(8,128)(2,1)}, bf16[512,128]{1,0:T(8,128)(2,1)S(1)}, u32[]{:S(2)}) copy-start(bf16[512,128]{1,0:T(8,128)(2,1)S(1)} %collective-permute-done.10.v2.refs_2_) | copy-start | bytes 393220
  26.2 6.4 %collective-permute-start.6 = (bf16[512,128]{1,0:T(8,128)(2,1)S(1)}, bf16[512,128]{1,0:T(8,128)(2,1)S(1)}, u32[]{:S(2)}, u32[]{:S(2)}) collective-permute-start(bf16[512,128]{1,0:T(8,128)(2,1)S(1)} %pad_maximum_fusion.k0.refs_0_), channel_id=1, source_target_pairs={{0,1},{1,0},{2,3},{3,2},{4,5},{5,4},{6,7},{7,6},{8,9},{9,8},{10,11... | collective-permute-start | bytes 393224 | tf_op jit(solution)/shard_map/ppermute | solution.py:39
  28.2 12.2 %copy-start.6 = (bf16[512,128]{1,0:T(8,128)(2,1)}, bf16[512,128]{1,0:T(8,128)(2,1)S(1)}, u32[]{:S(2)}) copy-start(bf16[512,128]{1,0:T(8,128)(2,1)S(1)} %collective-permute-done.11.v1.refs_3_) | copy-start | bytes 393220
  28.2 12.2 %copy-start.4 = (bf16[512,128]{1,0:T(8,128)(2,1)}, bf16[512,128]{1,0:T(8,128)(2,1)S(1)}, u32[]{:S(2)}) copy-start(bf16[512,128]{1,0:T(8,128)(2,1)S(1)} %collective-permute-done.9.v3.refs_1_) | copy-start | bytes 393220
  32.2 8.2 %copy-start.7 = (bf16[512,128]{1,0:T(8,128)(2,1)}, bf16[512,128]{1,0:T(8,128)(2,1)S(1)}, u32[]{:S(2)}) copy-start(bf16[512,128]{1,0:T(8,128)(2,1)S(1)} %collective-permute-done.4.k3.refs_0_) | copy-start | bytes 393220
  32.6 7.8 %copy-start.8 = (bf16[512,128]{1,0:T(8,128)(2,1)}, bf16[512,128]{1,0:T(8,128)(2,1)S(1)}, u32[]{:S(2)}) copy-start(bf16[512,128]{1,0:T(8,128)(2,1)S(1)} %collective-permute-done.5.k2.refs_0_) | copy-start | bytes 393220
  32.7 7.8 %copy-start.9 = (bf16[512,128]{1,0:T(8,128)(2,1)}, bf16[512,128]{1,0:T(8,128)(2,1)S(1)}, u32[]{:S(2)}) copy-start(bf16[512,128]{1,0:T(8,128)(2,1)S(1)} %collective-permute-done.6.k1.refs_1_) | copy-start | bytes 393220
  50.8 19.3 %all-to-all-start.1 = ((bf16[8,32,1024]{2,1,0:T(8,128)(2,1)}), bf16[8,32,1024]{2,1,0:T(8,128)(2,1)S(1)}, u32[]{:S(2)}, u32[]{:S(2)}) async-start(bf16[8,32,1024]{2,1,0:T(8,128)(2,1)} %get-tuple-element.31), calls=%async_computation.1 | async-start | bytes 1048576 | tf_op jit(solution)/shard_map/all_to_all | solution.py:458
  61.4 18.0 %collective-permute-start.12 = (bf16[512,256]{1,0:T(8,128)(2,1)}, bf16[512,256]{1,0:T(8,128)(2,1)}, u32[]{:S(2)}, u32[]{:S(2)}) collective-permute-start(bf16[512,256]{1,0:T(8,128)(2,1)} %get-tuple-element.33), channel_id=1, source_target_pairs={{0,2},{1,3},{2,0},{3,1},{4,6},{5,7},{6,4},{7,5},{8,10},{9,11},{10,... | collective-permute-start | bytes 786440 | tf_op jit(solution)/shard_map/ppermute | solution.py:39
  64.5 14.9 %collective-permute-start.13 = (bf16[512,256]{1,0:T(8,128)(2,1)}, bf16[512,256]{1,0:T(8,128)(2,1)}, u32[]{:S(2)}, u32[]{:S(2)}) collective-permute-start(bf16[512,256]{1,0:T(8,128)(2,1)} %get-tuple-element.34), channel_id=1, source_target_pairs={{0,1},{1,0},{2,3},{3,2},{4,5},{5,4},{6,7},{7,6},{8,9},{9,8},{10,11... | collective-permute-start | bytes 786440 | tf_op jit(solution)/shard_map/ppermute | solution.py:39
  69.3 10.2 %collective-permute-start.14 = (bf16[512,256]{1,0:T(8,128)(2,1)}, bf16[512,256]{1,0:T(8,128)(2,1)}, u32[]{:S(2)}, u32[]{:S(2)}) collective-permute-start(bf16[512,256]{1,0:T(8,128)(2,1)} %grads3.1.refs_3_), channel_id=1, source_target_pairs={{0,3},{1,2},{2,1},{3,0},{4,7},{5,6},{6,5},{7,4},{8,11},{9,10},{10,... | collective-permute-start | bytes 786440 | tf_op jit(solution)/shard_map/ppermute | solution.py:39
  74.5 12.6 %all-to-all-start.2 = ((bf16[8,32,1024]{2,1,0:T(8,128)(2,1)}), bf16[8,32,1024]{2,1,0:T(8,128)(2,1)S(1)}, u32[]{:S(2)}, u32[]{:S(2)}) async-start(bf16[8,32,1024]{2,1,0:T(8,128)(2,1)} %get-tuple-element.35), calls=%async_computation.2 | async-start | bytes 1048576 | tf_op jit(solution)/shard_map/all_to_all | solution.py:458
  80.7 6.5 %collective-permute-start.15 = (bf16[256,256]{1,0:T(8,128)(2,1)S(1)}, bf16[256,256]{1,0:T(8,128)(2,1)S(1)}, u32[]{:S(2)}, u32[]{:S(2)}) collective-permute-start(bf16[256,256]{1,0:T(8,128)(2,1)S(1)} %get-tuple-element.42), channel_id=1, source_target_pairs={{0,8},{1,9},{2,10},{3,11},{4,12},{5,13},{6,14},{7,15},{8,0},{9,1},... | collective-permute-start | bytes 393224 | tf_op jit(solution)/shard_map/ppermute | solution.py:39
  84.2 11.4 %collective-permute-start.17 = (bf16[256,256]{1,0:T(8,128)(2,1)S(1)}, bf16[256,256]{1,0:T(8,128)(2,1)S(1)}, u32[]{:S(2)}, u32[]{:S(2)}) collective-permute-start(bf16[256,256]{1,0:T(8,128)(2,1)S(1)} %get-tuple-element.42), channel_id=1, source_target_pairs={{0,12},{1,13},{2,14},{3,15},{4,8},{5,9},{6,10},{7,11},{8,4},{9,5},... | collective-permute-start | bytes 393224 | tf_op jit(solution)/shard_map/ppermute | solution.py:39
  86.4 9.2 %collective-permute-start.16 = (bf16[256,256]{1,0:T(8,128)(2,1)S(1)}, bf16[256,256]{1,0:T(8,128)(2,1)S(1)}, u32[]{:S(2)}, u32[]{:S(2)}) collective-permute-start(bf16[256,256]{1,0:T(8,128)(2,1)S(1)} %get-tuple-element.43.a), channel_id=1, source_target_pairs={{0,4},{1,5},{2,6},{3,7},{4,0},{5,1},{6,2},{7,3},{8,12},{9,13},{10,... | collective-permute-start | bytes 393224 | tf_op jit(solution)/shard_map/ppermute | solution.py:39
  87.2 12.1 %collective-permute-start.18 = (bf16[256,1024]{1,0:T(8,128)(2,1)S(1)}, bf16[256,1024]{1,0:T(8,128)(2,1)S(1)}, u32[]{:S(2)}, u32[]{:S(2)}) collective-permute-start(bf16[256,1024]{1,0:T(8,128)(2,1)S(1)} %bitcast.6), channel_id=1, source_target_pairs={{0,8},{1,9},{2,10},{3,11},{4,12},{5,13},{6,14},{7,15},{8,0},{9,1},... | collective-permute-start | bytes 1572872 | tf_op jit(solution)/shard_map/ppermute | solution.py:39

commit v10 on v8

--- a/solution.py
+++ b/solution.py
@@ -279,7 +279,7 @@
                 ds = []
                 for e in range(per):
                     at = slice(e * TILE, (e + 1) * TILE)
-                    p = jnp.exp2(jnp.minimum(s[at, :], caps[e]) - lh)
+                    p = jnp.exp2(s[at, :] - jnp.where(caps[e] > 0, lh, -NEG))
                     ps.append(p.astype(BF))
                     ds.append((p * (d[at, :] - dh) * SCALE).astype(BF))
                 pv = dot_nn(jnp.concatenate(ps, axis=0), gh)
@@ -423,11 +423,19 @@
 def add_theirs(idx, attn, theirs):
     half = theirs.shape[1]
 
-    def body(ix, _, t_ref, out, sem):
-        at = pl.multiple_of((1 - ix[1]) * half, half)
-        copy = pltpu.make_async_copy(t_ref, out.at[:, pl.ds(at, half)], sem)
-        copy.start()
-        copy.wait()
+    rows = theirs.shape[0]
+    parts = 4
+
+    def body(ix, _, t_ref, out, sems):
+        at = pl.ds(pl.multiple_of((1 - ix[1]) * half, half), half)
+        copies = []
+        for k in range(parts):
+            some = slice(k * rows // parts, (k + 1) * rows // parts)
+            copies.append(pltpu.make_async_copy(t_ref.at[some, :], out.at[some, at], sems.at[k]))
+        for copy in copies:
+            copy.start()
+        for copy in copies:
+            copy.wait()
 
     hbm = pl.BlockSpec(memory_space=pltpu.HBM)
     return pl.pallas_call(
@@ -438,7 +446,7 @@
             grid=(1,),
             in_specs=[hbm, pl.BlockSpec(memory_space=pl.ANY)],
             out_specs=hbm,
-            scratch_shapes=[pltpu.SemaphoreType.DMA],
+            scratch_shapes=[pltpu.SemaphoreType.DMA((parts,))],
         ),
         input_output_aliases={1: 0},
         compiler_params=pltpu.CompilerParams(vmem_limit_bytes=1 << 20),

time: 99.6 us -> 99.6 us (level)
  no operation moved by 1% of the time
where the time goes in v10:
time: 99.6 us; the launch traced here: 99.2 us
  starting transfers between devices  41.6 us (42%)
  Pallas kernels  35.1 us (35%)
  blocking collectives  10.3 us (10%)
  waiting for transfers between devices  9.01 us (9%)
  other arithmetic  1.26 us (1%)
  between operations  1.04 us (1%)
    ppermute x19, starting transfers between devices, moved(): return lambda x: lax.ppermute(x, AXES, pairs)  33.1 us
    pallas_call x2, Pallas kernels, backward(): pl.pallas_call(body, out_shape=out_shape, grid_spec=pltpu.PrefetchScalarG...  13.7 us
    all_to_all x1, blocking collectives, swap8(): return lax.all_to_all(x, 'img', 0, 0, axis_index_groups=chips, tiled=True)  10.3 us
    ppermute x19, waiting for transfers between devices, moved(): return lambda x: lax.ppermute(x, AXES, pairs)  9 us
    all_to_all x2, starting transfers between devices, swap8(): return lax.all_to_all(x, 'img', 0, 0, axis_index_groups=chips, tiled=True)  8.57 us
    pallas_call x1, Pallas kernels, forward(): pl.pallas_call(body, out_shape=(jax.ShapeDtypeStruct((8, share, width), B...  7.72 us
    pallas_call x1, Pallas kernels, project(): pl.pallas_call(body, out_shape=outs, grid_spec=pltpu.PrefetchScalarGridSp...  5.29 us
    pallas_call x1, Pallas kernels, feature_grad(): pl.pallas_call(body, out_shape=(jax.ShapeDtypeStruct((rows, feat), BF), j...  3.71 us
  transfers between devices with their start and end apart: 21, of which 6 were waited for; matrix products, arithmetic and copies ran while one was open for 1% of the time, Pallas kernels for 21%

profile of v10, /device:TPU:1, one launch (start us, length us, event | category | flops | bytes accessed | tf_op | source)
XLA Modules:
  0.0 99.2 jit_solution(2930541505450105516)
XLA Ops:
  0.6 0.7 concatenate.9.ix
  1.4 0.0 copy-start.10
  1.4 5.3 %project.1 = (f32[256,128]{1,0:T(8,128)S(1)}, f32[256,128]{1,0:T(8,128)S(1)}, f32[256,128]{1,0:T(8,128)S(1)}, f32[256,128]{1,0:T(8,128)S(1)}, f32[256,128]{1,0:T...) custom-call(s32[12]{0:T(128)S(1)} %concatenate.9.ix, ...), custom_call_target="tpu_custom_call" | custom-call | flops 4400000000 | bytes 65536 | tf_op jit(solution)/shard_map/project/pallas_call | solution.py:106
  6.7 4.5 %collective-permute-start.7 = (bf16[256,128]{1,0:T(8,128)(2,1)S(1)}, bf16[256,128]{1,0:T(8,128)(2,1)S(1)}, u32[]{:S(2)}, u32[]{:S(2)}) collective-permute-start(bf16[256,128]{1,0:T(8,128)(2,1)S(1)} %get-tuple-element.29), channel_id=1, source_target_pairs={{0,4},{1,5},{2,6},{3,7},{4,0},{5,1},{6,2},{7,3},{8,12},{9,13},{10,... | collective-permute-start | bytes 196616 | tf_op jit(solution)/shard_map/ppermute | solution.py:39
  11.2 1.0 collective-permute-start
  12.2 0.0 collective-permute-start.8
  12.2 2.9 %collective-permute-start.1 = (f32[256,128]{1,0:T(8,128)S(1)}, f32[256,128]{1,0:T(8,128)S(1)}, u32[]{:S(2)}, u32[]{:S(2)}) collective-permute-start(f32[256,128]{1,0:T(8,128)S(1)} %get-tuple-element.25), channel_id=1, source_target_pairs={{0,4},{1,5},{2,6},{3,7},{4,0},{5,1},{6,2},{7,3},{8,12},{9,13},{10,... | collective-permute-start | bytes 393224 | tf_op jit(solution)/shard_map/ppermute | solution.py:39
  15.0 0.8 collective-permute-start.2
  15.8 0.0 collective-permute-done.7
  15.8 2.3 %collective-permute-start.3 = (f32[256,128]{1,0:T(8,128)S(1)}, f32[256,128]{1,0:T(8,128)S(1)}, u32[]{:S(2)}, u32[]{:S(2)}) collective-permute-start(f32[256,128]{1,0:T(8,128)S(1)} %get-tuple-element.27), channel_id=1, source_target_pairs={{0,12},{1,13},{2,14},{3,15},{4,8},{5,9},{6,10},{7,11},{8,4},{9,5},... | collective-permute-start | bytes 393224 | tf_op jit(solution)/shard_map/ppermute | solution.py:39
  18.1 0.0 collective-permute-done.8
  18.1 0.0 collective-permute-done
  18.2 0.0 copy-start
  18.2 3.0 %collective-permute-start.10 = (bf16[512,128]{1,0:T(8,128)(2,1)S(1)}, bf16[512,128]{1,0:T(8,128)(2,1)S(1)}, u32[]{:S(2)}, u32[]{:S(2)}) collective-permute-start(bf16[512,128]{1,0:T(8,128)(2,1)S(1)} %pad_maximum_fusion.1.v0.refs_3_), channel_id=1, source_target_pairs={{0,2},{1,3},{2,0},{3,1},{4,6},{5,7},{6,4},{7,5},{8,10},{9,11},{10,... | collective-permute-start | bytes 393224 | tf_op jit(solution)/shard_map/ppermute | solution.py:39
  21.2 0.4 collective-permute-start.11
  21.6 0.0 collective-permute-done.1
  21.6 1.0 %collective-permute-start.9 = (bf16[512,128]{1,0:T(8,128)(2,1)S(1)}, bf16[512,128]{1,0:T(8,128)(2,1)S(1)}, u32[]{:S(2)}, u32[]{:S(2)}) collective-permute-start(bf16[512,128]{1,0:T(8,128)(2,1)S(1)} %pad_maximum_fusion.1.v0.refs_3_), channel_id=1, source_target_pairs={{0,3},{1,2},{2,1},{3,0},{4,7},{5,6},{6,5},{7,4},{8,11},{9,10},{10,... | collective-permute-start | bytes 393224 | tf_op jit(solution)/shard_map/ppermute | solution.py:39
  22.6 0.0 collective-permute-done.2
  22.6 0.7 collective-permute-done.3
  23.3 0.0 copy-start.1
  23.3 2.8 %collective-permute-start.4 = (bf16[512,128]{1,0:T(8,128)(2,1)S(1)}, bf16[512,128]{1,0:T(8,128)(2,1)S(1)}, u32[]{:S(2)}, u32[]{:S(2)}) collective-permute-start(bf16[512,128]{1,0:T(8,128)(2,1)S(1)} %pad_maximum_fusion.k0.refs_1_), channel_id=1, source_target_pairs={{0,3},{1,2},{2,1},{3,0},{4,7},{5,6},{6,5},{7,4},{8,11},{9,10},{10,... | collective-permute-start | bytes 393224 | tf_op jit(solution)/shard_map/ppermute | solution.py:39
  26.1 0.1 collective-permute-start.5
  26.2 0.0 collective-permute-done.10.v2.refs_2_
  26.2 0.6 collective-permute-start.6
  26.8 0.0 copy-done.11
  26.8 1.3 %collective-permute-done.11.v1.refs_3_ = bf16[512,128]{1,0:T(8,128)(2,1)S(1)} collective-permute-done((bf16[512,128]{1,0:T(8,128)(2,1)S(1)}, bf16[512,128]{1,0:T(8,128)(2,1)S(1)}, u32[]{:S(2)}, u32[]{:S(2)}) %collective-permute-start.11) | collective-permute-done | bytes 131104 | tf_op jit(solution)/shard_map/ppermute | solution.py:39
  28.2 0.0 collective-permute-done.9.v3.refs_2_
  28.2 4.0 %collective-permute-done.4.k3.refs_0_ = bf16[512,128]{1,0:T(8,128)(2,1)S(1)} collective-permute-done((bf16[512,128]{1,0:T(8,128)(2,1)S(1)}, bf16[512,128]{1,0:T(8,128)(2,1)S(1)}, u32[]{:S(2)}, u32[]{:S(2)}) %collective-permute-start.4) | collective-permute-done | bytes 131104 | tf_op jit(solution)/shard_map/ppermute | solution.py:39
  32.2 0.4 collective-permute-done.5.k2.refs_0_
  32.6 0.0 collective-permute-done.6.k1.refs_1_
  32.6 0.0 copy-done.2
  32.6 0.0 copy-done.3
  32.7 0.0 copy-done.10
  32.7 7.7 %fwd.1 = (bf16[8,32,1024]{2,1,0:T(8,128)(2,1)}, f32[8,16,256]{2,1,0:T(8,128)S(1)}) custom-call(s32[12]{0:T(128)S(1)} %concatenate.9.ix, s32[2,8]{1,0:T(2,128)S(1)} %pad_add_fusion.tl, s32[8,8]{1,0:T(8,128)S(1)} %copy-done.10, bf16[256,2048]{1,0:T(8,128)(2,1)S(1)} %copy-done.2, bf16[256,2048]{1,0:T(8,128)(2,1)S(1)} %copy-done.3, ...), custom_call_target="tpu_custom_call" | custom-call | flops 7699999744 | bytes 65536 | tf_op jit(solution)/shard_map/fwd/pallas_call | solution.py:189
  40.4 0.0 copy-done
  40.4 0.0 copy-done.4
  40.4 0.0 copy-done.7
  40.4 0.0 copy-done.8
  40.4 0.0 copy-done.9
  40.5 10.3 %all_to_all.15.st = f32[8,16,256]{2,1,0:T(8,128)S(1)} all-to-all(f32[8,16,256]{2,1,0:T(8,128)S(1)} %get-tuple-element.31), channel_id=1, replica_groups={{0,16,32,48,64,80,96,112},{8,24,40,56,72,88,104,120},{1,17,33,49,65,81,..., dimensions={0} | all-to-all | bytes 262144 | tf_op jit(solution)/shard_map/all_to_all | solution.py:466
  50.8 3.7 %all-to-all-start.1 = ((bf16[8,32,1024]{2,1,0:T(8,128)(2,1)}), bf16[8,32,1024]{2,1,0:T(8,128)(2,1)S(1)}, u32[]{:S(2)}, u32[]{:S(2)}) async-start(bf16[8,32,1024]{2,1,0:T(8,128)(2,1)} %get-tuple-element.32), calls=%async_computation.1 | async-start | bytes 1048576 | tf_op jit(solution)/shard_map/all_to_all | solution.py:466
  54.4 7.0 %grads21.1 = (bf16[512,256]{1,0:T(8,128)(2,1)}, bf16[512,256]{1,0:T(8,128)(2,1)}) custom-call(s32[12]{0:T(128)S(1)} %concatenate.9.ix, s32[2,8]{1,0:T(2,128)S(1)} %pad_add_fusion.tl, s32[8,8]{1,0:T(8,128)S(1)} %copy-done.10, bf16[256,2048]{1,0:T(8,128)(2,1)S(1)} %copy-done.2, bf16[256,2048]{1,0:T(8,128)(2,1)S(1)} %copy-done.3, ...), custom_call_target="tpu_custom_call" | custom-call | flops 6600000000 | bytes 65536 | tf_op jit(solution)/shard_map/grads21/pallas_call | solution.py:310
  61.4 3.1 %collective-permute-start.12 = (bf16[512,256]{1,0:T(8,128)(2,1)}, bf16[512,256]{1,0:T(8,128)(2,1)}, u32[]{:S(2)}, u32[]{:S(2)}) collective-permute-start(bf16[512,256]{1,0:T(8,128)(2,1)} %get-tuple-element.34), channel_id=1, source_target_pairs={{0,2},{1,3},{2,0},{3,1},{4,6},{5,7},{6,4},{7,5},{8,10},{9,11},{10,... | collective-permute-start | bytes 786440 | tf_op jit(solution)/shard_map/ppermute | solution.py:39
  64.5 0.1 collective-permute-start.13
  64.6 0.0 all-to-all-done.1.refs_4_
  64.6 6.8 %grads30.1 = (bf16[512,256]{1,0:T(8,128)(2,1)}, f32[512,256]{1,0:T(8,128)S(1)}, bf16[8,32,1024]{2,1,0:T(8,128)(2,1)}) custom-call(s32[12]{0:T(128)S(1)} %concatenate.9.ix, s32[2,8]{1,0:T(2,128)S(1)} %pad_add_fusion.tl, s32[8,8]{1,0:T(8,128)S(1)} %copy-done.10, bf16[256,2048]{1,0:T(8,128)(2,1)S(1)} %copy-done.2, bf16[256,2048]{1,0:T(8,128)(2,1)S(1)} %copy-done.3, ...), custom_call_target="tpu_custom_call" | custom-call | flops 6600000000 | bytes 65536 | tf_op jit(solution)/shard_map/grads30/pallas_call | solution.py:310
  71.3 0.7 collective-permute-start.14
  72.1 4.9 %all-to-all-start.2 = ((bf16[8,32,1024]{2,1,0:T(8,128)(2,1)}), bf16[8,32,1024]{2,1,0:T(8,128)(2,1)S(1)}, u32[]{:S(2)}, u32[]{:S(2)}) async-start(bf16[8,32,1024]{2,1,0:T(8,128)(2,1)} %get-tuple-element.37), calls=%async_computation.2 | async-start | bytes 1048576 | tf_op jit(solution)/shard_map/all_to_all | solution.py:466
  77.0 0.0 collective-permute-done.12
  77.0 0.0 collective-permute-done.13
  77.0 1.0 collective-permute-done.14
  78.0 1.2 %add_convert_fusion._ = bf16[512,256]{1,0:T(8,128)(2,1)S(1)} fusion(bf16[512,256]{1,0:T(8,128)(2,1)S(1)} %collective-permute-done.14, bf16[512,256]{1,0:T(8,128)(2,1)} %collective-permute-done.13, f32[512,256]{1,0:T(8,128)S(1)} %get-tuple-element.33, bf16[512,256]{1,0:T(8,128)(2,1)} %collective-permute-done.12), kind=kLoop, calls=%fused_computation | loop fusion | flops 917504 | bytes 1572864 | tf_op jit(solution)/shard_map/convert_element_type | solution.py:508
  79.1 4.1 %collective-permute-start.15 = (bf16[256,256]{1,0:T(8,128)(2,1)S(1)}, bf16[256,256]{1,0:T(8,128)(2,1)S(1)}, u32[]{:S(2)}, u32[]{:S(2)}) collective-permute-start(bf16[256,256]{1,0:T(8,128)(2,1)S(1)} %get-tuple-element.44), channel_id=1, source_target_pairs={{0,8},{1,9},{2,10},{3,11},{4,12},{5,13},{6,14},{7,15},{8,0},{9,1},... | collective-permute-start | bytes 393224 | tf_op jit(solution)/shard_map/ppermute | solution.py:39
  83.2 1.7 %collective-permute-start.17 = (bf16[256,256]{1,0:T(8,128)(2,1)S(1)}, bf16[256,256]{1,0:T(8,128)(2,1)S(1)}, u32[]{:S(2)}, u32[]{:S(2)}) collective-permute-start(bf16[256,256]{1,0:T(8,128)(2,1)S(1)} %get-tuple-element.44), channel_id=1, source_target_pairs={{0,12},{1,13},{2,14},{3,15},{4,8},{5,9},{6,10},{7,11},{8,4},{9,5},... | collective-permute-start | bytes 393224 | tf_op jit(solution)/shard_map/ppermute | solution.py:39
  84.9 1.3 %collective-permute-start.16 = (bf16[256,256]{1,0:T(8,128)(2,1)S(1)}, bf16[256,256]{1,0:T(8,128)(2,1)S(1)}, u32[]{:S(2)}, u32[]{:S(2)}) collective-permute-start(bf16[256,256]{1,0:T(8,128)(2,1)S(1)} %get-tuple-element.45.a), channel_id=1, source_target_pairs={{0,4},{1,5},{2,6},{3,7},{4,0},{5,1},{6,2},{7,3},{8,12},{9,13},{10,... | collective-permute-start | bytes 393224 | tf_op jit(solution)/shard_map/ppermute | solution.py:39
  86.2 0.0 collective-permute-done.15.b
  86.2 0.0 all-to-all-done.2
  86.2 2.9 %collective-permute-start.18 = (bf16[256,1024]{1,0:T(8,128)(2,1)S(1)}, bf16[256,1024]{1,0:T(8,128)(2,1)S(1)}, u32[]{:S(2)}, u32[]{:S(2)}) collective-permute-start(bf16[256,1024]{1,0:T(8,128)(2,1)S(1)} %bitcast.6), channel_id=1, source_target_pairs={{0,8},{1,9},{2,10},{3,11},{4,12},{5,13},{6,14},{7,15},{8,0},{9,1},... | collective-permute-start | bytes 1572872 | tf_op jit(solution)/shard_map/ppermute | solution.py:39
  89.1 3.3 %fetch.1 = (bf16[3840,512]{1,0:T(8,128)(2,1)S(1)}, bf16[3840,512]{1,0:T(8,128)(2,1)S(1)}) custom-call(bf16[3840,512]{1,0:T(8,128)(2,1)} %k_hbm.1, bf16[3840,512]{1,0:T(8,128)(2,1)} %v_hbm.1, bf16[512,256]{1,0:T(8,128)(2,1)S(1)} %add_convert_fusion._), custom_call_target="tpu_custom_call" | custom-call | flops 4400000000 | bytes 65536 | tf_op jit(solution)/shard_map/fetch/pallas_call | solution.py:344
  92.4 1.5 %collective-permute-done.16.c_ = bf16[256,256]{1,0:T(8,128)(2,1)S(1)} collective-permute-done((bf16[256,256]{1,0:T(8,128)(2,1)S(1)}, bf16[256,256]{1,0:T(8,128)(2,1)S(1)}, u32[]{:S(2)}, u32[]{:S(2)}) %collective-permute-start.16) | collective-permute-done | bytes 131104 | tf_op jit(solution)/shard_map/ppermute | solution.py:39
  93.9 0.0 collective-permute-done.17.d_
  93.9 3.7 %feats.1 = (bf16[256,3840]{1,0:T(8,128)(2,1)}, bf16[256,2048]{1,0:T(8,128)(2,1)}) custom-call(s32[12]{0:T(128)S(1)} %concatenate.9.ix, bf16[256,256]{1,0:T(8,128)(2,1)S(1)} %get-tuple-element.45.a, bf16[256,256]{1,0:T(8,128)(2,1)S(1)} %collective-permute-done.15.b, bf16[256,256]{1,0:T(8,128)(2,1)S(1)} %collective-permute-done.16.c_, ...), custom_call_target="tpu_custom_call" | custom-call | flops 4400000000 | bytes 65536 | tf_op jit(solution)/shard_map/feats/pallas_call | solution.py:400
  97.6 0.0 collective-permute-done.18.t_ref
  97.6 1.4 %theirs.1 = bf16[256,2048]{1,0:T(8,128)(2,1)} custom-call(s32[12]{0:T(128)S(1)} %concatenate.9.ix, bf16[256,2048]{1,0:T(8,128)(2,1)} %get-tuple-element.42._, bf16[256,1024]{1,0:T(8,128)(2,1)S(1)} %collective-permute-done.18.t_ref), custom_call_target="tpu_custom_call", output_to_operand_aliasing={{}: (1, {})} | custom-call | tf_op jit(solution)/shard_map/theirs/pallas_call | solution.py:441
  (21 shorter events, 0.1 us)
Async XLA Ops:
  1.4 25.4 %copy-start.11 = (s32[8]{0:T(128)S(1)}, s32[8]{0:T(128)}, u32[]{:S(2)}) copy-start(s32[8]{0:T(128)} %param.12) | copy-start | bytes 100
  1.4 31.3 %copy-start.2 = (bf16[256,2048]{1,0:T(8,128)(2,1)S(1)}, bf16[256,2048]{1,0:T(8,128)(2,1)}, u32[]{:S(2)}) copy-start(bf16[256,2048]{1,0:T(8,128)(2,1)} %q.5) | copy-start | bytes 3145732
  1.4 31.3 %copy-start.3 = (bf16[256,2048]{1,0:T(8,128)(2,1)S(1)}, bf16[256,2048]{1,0:T(8,128)(2,1)}, u32[]{:S(2)}) copy-start(bf16[256,2048]{1,0:T(8,128)(2,1)} %g.5) | copy-start | bytes 3145732
  1.4 31.3 %copy-start.10 = (s32[8,8]{1,0:T(8,128)S(1)}, s32[8,8]{1,0:T(8,128)}, u32[]{:S(2)}) copy-start(s32[8,8]{1,0:T(8,128)} %se.5) | copy-start | bytes 772
  6.7 9.1 %collective-permute-start.7 = (bf16[256,128]{1,0:T(8,128)(2,1)S(1)}, bf16[256,128]{1,0:T(8,128)(2,1)S(1)}, u32[]{:S(2)}, u32[]{:S(2)}) collective-permute-start(bf16[256,128]{1,0:T(8,128)(2,1)S(1)} %get-tuple-element.29), channel_id=1, source_target_pairs={{0,4},{1,5},{2,6},{3,7},{4,0},{5,1},{6,2},{7,3},{8,12},{9,13},{10,... | collective-permute-start | bytes 196616 | tf_op jit(solution)/shard_map/ppermute | solution.py:39
  11.2 6.9 %collective-permute-start = (bf16[272,128]{1,0:T(8,128)(2,1)S(1)}, bf16[272,128]{1,0:T(8,128)(2,1)S(1)}, u32[]{:S(2)}, u32[]{:S(2)}) collective-permute-start(bf16[272,128]{1,0:T(8,128)(2,1)S(1)} %get-tuple-element.23), channel_id=1, source_target_pairs={{0,8},{1,9},{2,10},{3,11},{4,12},{5,13},{6,14},{7,15},{8,0},{9,1},... | collective-permute-start | bytes 208904 | tf_op jit(solution)/shard_map/ppermute | solution.py:39
  12.2 5.9 %collective-permute-start.8 = (bf16[256,128]{1,0:T(8,128)(2,1)S(1)}, bf16[256,128]{1,0:T(8,128)(2,1)S(1)}, u32[]{:S(2)}, u32[]{:S(2)}) collective-permute-start(bf16[256,128]{1,0:T(8,128)(2,1)S(1)} %get-tuple-element.30), channel_id=1, source_target_pairs={{0,12},{1,13},{2,14},{3,15},{4,8},{5,9},{6,10},{7,11},{8,4},{9,5},... | collective-permute-start | bytes 196616 | tf_op jit(solution)/shard_map/ppermute | solution.py:39
  12.2 9.4 %collective-permute-start.1 = (f32[256,128]{1,0:T(8,128)S(1)}, f32[256,128]{1,0:T(8,128)S(1)}, u32[]{:S(2)}, u32[]{:S(2)}) collective-permute-start(f32[256,128]{1,0:T(8,128)S(1)} %get-tuple-element.25), channel_id=1, source_target_pairs={{0,4},{1,5},{2,6},{3,7},{4,0},{5,1},{6,2},{7,3},{8,12},{9,13},{10,... | collective-permute-start | bytes 393224 | tf_op jit(solution)/shard_map/ppermute | solution.py:39
  15.0 7.6 %collective-permute-start.2 = (f32[256,128]{1,0:T(8,128)S(1)}, f32[256,128]{1,0:T(8,128)S(1)}, u32[]{:S(2)}, u32[]{:S(2)}) collective-permute-start(f32[256,128]{1,0:T(8,128)S(1)} %get-tuple-element.26), channel_id=1, source_target_pairs={{0,8},{1,9},{2,10},{3,11},{4,12},{5,13},{6,14},{7,15},{8,0},{9,1},... | collective-permute-start | bytes 393224 | tf_op jit(solution)/shard_map/ppermute | solution.py:39
  15.8 7.5 %collective-permute-start.3 = (f32[256,128]{1,0:T(8,128)S(1)}, f32[256,128]{1,0:T(8,128)S(1)}, u32[]{:S(2)}, u32[]{:S(2)}) collective-permute-start(f32[256,128]{1,0:T(8,128)S(1)} %get-tuple-element.27), channel_id=1, source_target_pairs={{0,12},{1,13},{2,14},{3,15},{4,8},{5,9},{6,10},{7,11},{8,4},{9,5},... | collective-permute-start | bytes 393224 | tf_op jit(solution)/shard_map/ppermute | solution.py:39
  18.2 22.2 %copy-start = (bf16[512,128]{1,0:T(8,128)(2,1)}, bf16[512,128]{1,0:T(8,128)(2,1)S(1)}, u32[]{:S(2)}) copy-start(bf16[512,128]{1,0:T(8,128)(2,1)S(1)} %pad_maximum_fusion.1.v0.refs_3_) | copy-start | bytes 393220
  18.2 8.0 %collective-permute-start.10 = (bf16[512,128]{1,0:T(8,128)(2,1)S(1)}, bf16[512,128]{1,0:T(8,128)(2,1)S(1)}, u32[]{:S(2)}, u32[]{:S(2)}) collective-permute-start(bf16[512,128]{1,0:T(8,128)(2,1)S(1)} %pad_maximum_fusion.1.v0.refs_3_), channel_id=1, source_target_pairs={{0,2},{1,3},{2,0},{3,1},{4,6},{5,7},{6,4},{7,5},{8,10},{9,11},{10,... | collective-permute-start | bytes 393224 | tf_op jit(solution)/shard_map/ppermute | solution.py:39
  21.2 7.0 %collective-permute-start.11 = (bf16[512,128]{1,0:T(8,128)(2,1)S(1)}, bf16[512,128]{1,0:T(8,128)(2,1)S(1)}, u32[]{:S(2)}, u32[]{:S(2)}) collective-permute-start(bf16[512,128]{1,0:T(8,128)(2,1)S(1)} %pad_maximum_fusion.1.v0.refs_3_), channel_id=1, source_target_pairs={{0,1},{1,0},{2,3},{3,2},{4,5},{5,4},{6,7},{7,6},{8,9},{9,8},{10,11... | collective-permute-start | bytes 393224 | tf_op jit(solution)/shard_map/ppermute | solution.py:39
  21.6 6.6 %collective-permute-start.9 = (bf16[512,128]{1,0:T(8,128)(2,1)S(1)}, bf16[512,128]{1,0:T(8,128)(2,1)S(1)}, u32[]{:S(2)}, u32[]{:S(2)}) collective-permute-start(bf16[512,128]{1,0:T(8,128)(2,1)S(1)} %pad_maximum_fusion.1.v0.refs_3_), channel_id=1, source_target_pairs={{0,3},{1,2},{2,1},{3,0},{4,7},{5,6},{6,5},{7,4},{8,11},{9,10},{10,... | collective-permute-start | bytes 393224 | tf_op jit(solution)/shard_map/ppermute | solution.py:39
  23.3 17.1 %copy-start.1 = (bf16[512,128]{1,0:T(8,128)(2,1)}, bf16[512,128]{1,0:T(8,128)(2,1)S(1)}, u32[]{:S(2)}) copy-start(bf16[512,128]{1,0:T(8,128)(2,1)S(1)} %pad_maximum_fusion.k0.refs_1_) | copy-start | bytes 393220
  23.3 8.9 %collective-permute-start.4 = (bf16[512,128]{1,0:T(8,128)(2,1)S(1)}, bf16[512,128]{1,0:T(8,128)(2,1)S(1)}, u32[]{:S(2)}, u32[]{:S(2)}) collective-permute-start(bf16[512,128]{1,0:T(8,128)(2,1)S(1)} %pad_maximum_fusion.k0.refs_1_), channel_id=1, source_target_pairs={{0,3},{1,2},{2,1},{3,0},{4,7},{5,6},{6,5},{7,4},{8,11},{9,10},{10,... | collective-permute-start | bytes 393224 | tf_op jit(solution)/shard_map/ppermute | solution.py:39
  26.1 6.5 %collective-permute-start.5 = (bf16[512,128]{1,0:T(8,128)(2,1)S(1)}, bf16[512,128]{1,0:T(8,128)(2,1)S(1)}, u32[]{:S(2)}, u32[]{:S(2)}) collective-permute-start(bf16[512,128]{1,0:T(8,128)(2,1)S(1)} %pad_maximum_fusion.k0.refs_1_), channel_id=1, source_target_pairs={{0,2},{1,3},{2,0},{3,1},{4,6},{5,7},{6,4},{7,5},{8,10},{9,11},{10,... | collective-permute-start | bytes 393224 | tf_op jit(solution)/shard_map/ppermute | solution.py:39
  26.2 14.2 %copy-start.5 = (bf16[512,128]{1,0:T(8,128)(2,1)}, bf16[512,128]{1,0:T(8,128)(2,1)S(1)}, u32[]{:S(2)}) copy-start(bf16[512,128]{1,0:T(8,128)(2,1)S(1)} %collective-permute-done.10.v2.refs_2_) | copy-start | bytes 393220
  26.2 6.4 %collective-permute-start.6 = (bf16[512,128]{1,0:T(8,128)(2,1)S(1)}, bf16[512,128]{1,0:T(8,128)(2,1)S(1)}, u32[]{:S(2)}, u32[]{:S(2)}) collective-permute-start(bf16[512,128]{1,0:T(8,128)(2,1)S(1)} %pad_maximum_fusion.k0.refs_1_), channel_id=1, source_target_pairs={{0,1},{1,0},{2,3},{3,2},{4,5},{5,4},{6,7},{7,6},{8,9},{9,8},{10,11... | collective-permute-start | bytes 393224 | tf_op jit(solution)/shard_map/ppermute | solution.py:39
  28.2 12.2 %copy-start.6 = (bf16[512,128]{1,0:T(8,128)(2,1)}, bf16[512,128]{1,0:T(8,128)(2,1)S(1)}, u32[]{:S(2)}) copy-start(bf16[512,128]{1,0:T(8,128)(2,1)S(1)} %collective-permute-done.11.v1.refs_3_) | copy-start | bytes 393220
  28.2 12.2 %copy-start.4 = (bf16[512,128]{1,0:T(8,128)(2,1)}, bf16[512,128]{1,0:T(8,128)(2,1)S(1)}, u32[]{:S(2)}) copy-start(bf16[512,128]{1,0:T(8,128)(2,1)S(1)} %collective-permute-done.9.v3.refs_2_) | copy-start | bytes 393220
  32.2 8.2 %copy-start.7 = (bf16[512,128]{1,0:T(8,128)(2,1)}, bf16[512,128]{1,0:T(8,128)(2,1)S(1)}, u32[]{:S(2)}) copy-start(bf16[512,128]{1,0:T(8,128)(2,1)S(1)} %collective-permute-done.4.k3.refs_0_) | copy-start | bytes 393220
  32.6 7.8 %copy-start.8 = (bf16[512,128]{1,0:T(8,128)(2,1)}, bf16[512,128]{1,0:T(8,128)(2,1)S(1)}, u32[]{:S(2)}) copy-start(bf16[512,128]{1,0:T(8,128)(2,1)S(1)} %collective-permute-done.5.k2.refs_0_) | copy-start | bytes 393220
  32.7 7.8 %copy-start.9 = (bf16[512,128]{1,0:T(8,128)(2,1)}, bf16[512,128]{1,0:T(8,128)(2,1)S(1)}, u32[]{:S(2)}) copy-start(bf16[512,128]{1,0:T(8,128)(2,1)S(1)} %collective-permute-done.6.k1.refs_1_) | copy-start | bytes 393220
  50.8 13.8 %all-to-all-start.1 = ((bf16[8,32,1024]{2,1,0:T(8,128)(2,1)}), bf16[8,32,1024]{2,1,0:T(8,128)(2,1)S(1)}, u32[]{:S(2)}, u32[]{:S(2)}) async-start(bf16[8,32,1024]{2,1,0:T(8,128)(2,1)} %get-tuple-element.32), calls=%async_computation.1 | async-start | bytes 1048576 | tf_op jit(solution)/shard_map/all_to_all | solution.py:466
  61.4 15.6 %collective-permute-start.12 = (bf16[512,256]{1,0:T(8,128)(2,1)}, bf16[512,256]{1,0:T(8,128)(2,1)}, u32[]{:S(2)}, u32[]{:S(2)}) collective-permute-start(bf16[512,256]{1,0:T(8,128)(2,1)} %get-tuple-element.34), channel_id=1, source_target_pairs={{0,2},{1,3},{2,0},{3,1},{4,6},{5,7},{6,4},{7,5},{8,10},{9,11},{10,... | collective-permute-start | bytes 786440 | tf_op jit(solution)/shard_map/ppermute | solution.py:39
  64.5 12.5 %collective-permute-start.13 = (bf16[512,256]{1,0:T(8,128)(2,1)}, bf16[512,256]{1,0:T(8,128)(2,1)}, u32[]{:S(2)}, u32[]{:S(2)}) collective-permute-start(bf16[512,256]{1,0:T(8,128)(2,1)} %get-tuple-element.35), channel_id=1, source_target_pairs={{0,1},{1,0},{2,3},{3,2},{4,5},{5,4},{6,7},{7,6},{8,9},{9,8},{10,11... | collective-permute-start | bytes 786440 | tf_op jit(solution)/shard_map/ppermute | solution.py:39
  71.3 6.6 %collective-permute-start.14 = (bf16[512,256]{1,0:T(8,128)(2,1)}, bf16[512,256]{1,0:T(8,128)(2,1)S(1)}, u32[]{:S(2)}, u32[]{:S(2)}) collective-permute-start(bf16[512,256]{1,0:T(8,128)(2,1)} %get-tuple-element.36), channel_id=1, source_target_pairs={{0,3},{1,2},{2,1},{3,0},{4,7},{5,6},{6,5},{7,4},{8,11},{9,10},{10,... | collective-permute-start | bytes 786440 | tf_op jit(solution)/shard_map/ppermute | solution.py:39
  72.1 14.1 %all-to-all-start.2 = ((bf16[8,32,1024]{2,1,0:T(8,128)(2,1)}), bf16[8,32,1024]{2,1,0:T(8,128)(2,1)S(1)}, u32[]{:S(2)}, u32[]{:S(2)}) async-start(bf16[8,32,1024]{2,1,0:T(8,128)(2,1)} %get-tuple-element.37), calls=%async_computation.2 | async-start | bytes 1048576 | tf_op jit(solution)/shard_map/all_to_all | solution.py:466
  79.1 7.1 %collective-permute-start.15 = (bf16[256,256]{1,0:T(8,128)(2,1)S(1)}, bf16[256,256]{1,0:T(8,128)(2,1)S(1)}, u32[]{:S(2)}, u32[]{:S(2)}) collective-permute-start(bf16[256,256]{1,0:T(8,128)(2,1)S(1)} %get-tuple-element.44), channel_id=1, source_target_pairs={{0,8},{1,9},{2,10},{3,11},{4,12},{5,13},{6,14},{7,15},{8,0},{9,1},... | collective-permute-start | bytes 393224 | tf_op jit(solution)/shard_map/ppermute | solution.py:39
  83.2 10.7 %collective-permute-start.17 = (bf16[256,256]{1,0:T(8,128)(2,1)S(1)}, bf16[256,256]{1,0:T(8,128)(2,1)S(1)}, u32[]{:S(2)}, u32[]{:S(2)}) collective-permute-start(bf16[256,256]{1,0:T(8,128)(2,1)S(1)} %get-tuple-element.44), channel_id=1, source_target_pairs={{0,12},{1,13},{2,14},{3,15},{4,8},{5,9},{6,10},{7,11},{8,4},{9,5},... | collective-permute-start | bytes 393224 | tf_op jit(solution)/shard_map/ppermute | solution.py:39
  84.9 9.0 %collective-permute-start.16 = (bf16[256,256]{1,0:T(8,128)(2,1)S(1)}, bf16[256,256]{1,0:T(8,128)(2,1)S(1)}, u32[]{:S(2)}, u32[]{:S(2)}) collective-permute-start(bf16[256,256]{1,0:T(8,128)(2,1)S(1)} %get-tuple-element.45.a), channel_id=1, source_target_pairs={{0,4},{1,5},{2,6},{3,7},{4,0},{5,1},{6,2},{7,3},{8,12},{9,13},{10,... | collective-permute-start | bytes 393224 | tf_op jit(solution)/shard_map/ppermute | solution.py:39
  86.2 11.4 %collective-permute-start.18 = (bf16[256,1024]{1,0:T(8,128)(2,1)S(1)}, bf16[256,1024]{1,0:T(8,128)(2,1)S(1)}, u32[]{:S(2)}, u32[]{:S(2)}) collective-permute-start(bf16[256,1024]{1,0:T(8,128)(2,1)S(1)} %bitcast.6), channel_id=1, source_target_pairs={{0,8},{1,9},{2,10},{3,11},{4,12},{5,13},{6,14},{7,15},{8,0},{9,1},... | collective-permute-start | bytes 1572872 | tf_op jit(solution)/shard_map/ppermute | solution.py:39

commit v11 on v8

--- a/solution.py
+++ b/solution.py
@@ -143,7 +143,7 @@
     share = rows // 8
     per = span // TILE
 
-    def body(ix, tl, se, q, g, k3, k2, k1, k0, v3, v2, v1, v0, out, st_out, y_scr, va):
+    def body(ix, tl, se, q, g, k3, k2, k1, k0, v0, v1, v2, v3, out, st_out, y_scr, va):
         ks = (k0, k1, k2, k3)
         vs = (v0, v1, v2, v3)
         for j in range(n):
@@ -205,7 +205,7 @@
         compiler_params=pltpu.CompilerParams(vmem_limit_bytes=24 << 20),
         name="fwd",
         cost_estimate=cost(7),
-    )(idx, tiles, sees, queries, grad_out, *keys[::-1], *values[::-1])
+    )(idx, tiles, sees, queries, grad_out, *keys[::-1], *values)
 
 
 def merge_weights(st, heads):

time: 99.6 us -> 99.6 us (level)
  waiting for transfers between devices: 9.01 us -> 11.1 us
  starting transfers between devices: 41.6 us -> 40.1 us
    ppermute x19, waiting for transfers between devices: 9 us -> 11 us  [moved(): return lambda x: lax.ppermute(x, AXES, pairs)]
    all_to_all x2, starting transfers between devices: 8.57 us -> 7.21 us  [swap8(): return lax.all_to_all(x, 'img', 0, 0, axis_index_groups=chips, tiled=True)]
  transfers between devices with their start and end apart: 21 -> 21, of which waited for: 6 -> 7; matrix products, arithmetic and copies ran while one was open for 1% -> 1% of each run, Pallas kernels for 21% -> 21%
where the time goes in v11:
time: 99.6 us; the launch traced here: 99.2 us
  starting transfers between devices  40.1 us (40%)
  Pallas kernels  35.2 us (35%)
  waiting for transfers between devices  11.1 us (11%)
  blocking collectives  9.83 us (10%)
  other arithmetic  1.26 us (1%)
  between operations  1.03 us (1%)
    ppermute x19, starting transfers between devices, moved(): return lambda x: lax.ppermute(x, AXES, pairs)  32.9 us
    pallas_call x2, Pallas kernels, backward(): pl.pallas_call(body, out_shape=out_shape, grid_spec=pltpu.PrefetchScalarG...  13.8 us
    ppermute x19, waiting for transfers between devices, moved(): return lambda x: lax.ppermute(x, AXES, pairs)  11 us
    all_to_all x1, blocking collectives, swap8(): return lax.all_to_all(x, 'img', 0, 0, axis_index_groups=chips, tiled=True)  9.83 us
    pallas_call x1, Pallas kernels, forward(): pl.pallas_call(body, out_shape=(jax.ShapeDtypeStruct((8, share, width), B...  7.72 us
    all_to_all x2, starting transfers between devices, swap8(): return lax.all_to_all(x, 'img', 0, 0, axis_index_groups=chips, tiled=True)  7.21 us
    pallas_call x1, Pallas kernels, project(): pl.pallas_call(body, out_shape=outs, grid_spec=pltpu.PrefetchScalarGridSp...  5.29 us
    pallas_call x1, Pallas kernels, feature_grad(): pl.pallas_call(body, out_shape=(jax.ShapeDtypeStruct((rows, feat), BF), j...  3.7 us
  transfers between devices with their start and end apart: 21, of which 7 were waited for; matrix products, arithmetic and copies ran while one was open for 1% of the time, Pallas kernels for 21%

profile of v11, /device:TPU:1, one launch (start us, length us, event | category | flops | bytes accessed | tf_op | source)
XLA Modules:
  0.0 99.2 jit_solution(12612088825892134891)
XLA Ops:
  0.6 0.7 concatenate.9.ix
  1.4 0.0 copy-start.10
  1.4 5.3 %project.1 = (f32[256,128]{1,0:T(8,128)S(1)}, f32[256,128]{1,0:T(8,128)S(1)}, f32[256,128]{1,0:T(8,128)S(1)}, f32[256,128]{1,0:T(8,128)S(1)}, f32[256,128]{1,0:T...) custom-call(s32[12]{0:T(128)S(1)} %concatenate.9.ix, ...), custom_call_target="tpu_custom_call" | custom-call | flops 4400000000 | bytes 65536 | tf_op jit(solution)/shard_map/project/pallas_call | solution.py:106
  6.7 4.5 %collective-permute-start.7 = (bf16[256,128]{1,0:T(8,128)(2,1)S(1)}, bf16[256,128]{1,0:T(8,128)(2,1)S(1)}, u32[]{:S(2)}, u32[]{:S(2)}) collective-permute-start(bf16[256,128]{1,0:T(8,128)(2,1)S(1)} %get-tuple-element.29), channel_id=1, source_target_pairs={{0,4},{1,5},{2,6},{3,7},{4,0},{5,1},{6,2},{7,3},{8,12},{9,13},{10,... | collective-permute-start | bytes 196616 | tf_op jit(solution)/shard_map/ppermute | solution.py:39
  11.2 1.0 collective-permute-start
  12.2 0.0 collective-permute-start.8
  12.2 2.9 %collective-permute-start.1 = (f32[256,128]{1,0:T(8,128)S(1)}, f32[256,128]{1,0:T(8,128)S(1)}, u32[]{:S(2)}, u32[]{:S(2)}) collective-permute-start(f32[256,128]{1,0:T(8,128)S(1)} %get-tuple-element.25), channel_id=1, source_target_pairs={{0,4},{1,5},{2,6},{3,7},{4,0},{5,1},{6,2},{7,3},{8,12},{9,13},{10,... | collective-permute-start | bytes 393224 | tf_op jit(solution)/shard_map/ppermute | solution.py:39
  15.0 0.8 collective-permute-start.2
  15.8 0.0 collective-permute-done.7
  15.8 2.3 %collective-permute-start.3 = (f32[256,128]{1,0:T(8,128)S(1)}, f32[256,128]{1,0:T(8,128)S(1)}, u32[]{:S(2)}, u32[]{:S(2)}) collective-permute-start(f32[256,128]{1,0:T(8,128)S(1)} %get-tuple-element.27), channel_id=1, source_target_pairs={{0,12},{1,13},{2,14},{3,15},{4,8},{5,9},{6,10},{7,11},{8,4},{9,5},... | collective-permute-start | bytes 393224 | tf_op jit(solution)/shard_map/ppermute | solution.py:39
  18.1 0.0 collective-permute-done.8
  18.1 0.0 collective-permute-done
  18.2 0.0 copy-start
  18.2 3.0 %collective-permute-start.10 = (bf16[512,128]{1,0:T(8,128)(2,1)S(1)}, bf16[512,128]{1,0:T(8,128)(2,1)S(1)}, u32[]{:S(2)}, u32[]{:S(2)}) collective-permute-start(bf16[512,128]{1,0:T(8,128)(2,1)S(1)} %pad_maximum_fusion.1.v0.refs_3_), channel_id=1, source_target_pairs={{0,2},{1,3},{2,0},{3,1},{4,6},{5,7},{6,4},{7,5},{8,10},{9,11},{10,... | collective-permute-start | bytes 393224 | tf_op jit(solution)/shard_map/ppermute | solution.py:39
  21.2 0.8 collective-permute-start.11
  21.9 0.0 collective-permute-done.1
  21.9 0.0 collective-permute-start.9
  22.0 0.0 collective-permute-done.2
  22.0 1.3 %collective-permute-done.3 = f32[256,128]{1,0:T(8,128)S(1)} collective-permute-done((f32[256,128]{1,0:T(8,128)S(1)}, f32[256,128]{1,0:T(8,128)S(1)}, u32[]{:S(2)}, u32[]{:S(2)}) %collective-permute-start.3) | collective-permute-done | bytes 131104 | tf_op jit(solution)/shard_map/ppermute | solution.py:39
  23.3 0.0 copy-start.1
  23.3 2.8 %collective-permute-start.4 = (bf16[512,128]{1,0:T(8,128)(2,1)S(1)}, bf16[512,128]{1,0:T(8,128)(2,1)S(1)}, u32[]{:S(2)}, u32[]{:S(2)}) collective-permute-start(bf16[512,128]{1,0:T(8,128)(2,1)S(1)} %pad_maximum_fusion.k0.refs_1_), channel_id=1, source_target_pairs={{0,3},{1,2},{2,1},{3,0},{4,7},{5,6},{6,5},{7,4},{8,11},{9,10},{10,... | collective-permute-start | bytes 393224 | tf_op jit(solution)/shard_map/ppermute | solution.py:39
  26.1 0.1 collective-permute-start.5
  26.2 0.0 collective-permute-done.10.v2.refs_2_
  26.2 0.6 collective-permute-start.6
  26.8 0.0 copy-done.11
  26.8 1.0 %collective-permute-done.11.v3.refs_2_ = bf16[512,128]{1,0:T(8,128)(2,1)S(1)} collective-permute-done((bf16[512,128]{1,0:T(8,128)(2,1)S(1)}, bf16[512,128]{1,0:T(8,128)(2,1)S(1)}, u32[]{:S(2)}, u32[]{:S(2)}) %collective-permute-start.11) | collective-permute-done | bytes 131104 | tf_op jit(solution)/shard_map/ppermute | solution.py:39
  27.8 0.4 collective-permute-done.9.v1.refs_3_
  28.2 4.9 %collective-permute-done.4.k3.refs_0_ = bf16[512,128]{1,0:T(8,128)(2,1)S(1)} collective-permute-done((bf16[512,128]{1,0:T(8,128)(2,1)S(1)}, bf16[512,128]{1,0:T(8,128)(2,1)S(1)}, u32[]{:S(2)}, u32[]{:S(2)}) %collective-permute-start.4) | collective-permute-done | bytes 131104 | tf_op jit(solution)/shard_map/ppermute | solution.py:39
  33.1 0.0 collective-permute-done.5.k2.refs_0_
  33.1 0.3 collective-permute-done.6.k1.refs_1_
  33.5 0.0 copy-done.2
  33.5 0.0 copy-done.3
  33.5 0.0 copy-done.10
  33.5 0.0 copy-start.9
  33.5 7.7 %fwd.1 = (bf16[8,32,1024]{2,1,0:T(8,128)(2,1)}, f32[8,16,256]{2,1,0:T(8,128)S(1)}) custom-call(s32[12]{0:T(128)S(1)} %concatenate.9.ix, s32[2,8]{1,0:T(2,128)S(1)} %pad_add_fusion.tl, s32[8,8]{1,0:T(8,128)S(1)} %copy-done.10, bf16[256,2048]{1,0:T(8,128)(2,1)S(1)} %copy-done.2, bf16[256,2048]{1,0:T(8,128)(2,1)S(1)} %copy-done.3, ...), custom_call_target="tpu_custom_call" | custom-call | flops 7699999744 | bytes 65536 | tf_op jit(solution)/shard_map/fwd/pallas_call | solution.py:189
  41.2 0.0 copy-done
  41.2 0.0 copy-done.1
  41.2 0.0 copy-done.5
  41.2 0.0 copy-done.4
  41.2 9.8 %all_to_all.15.st = f32[8,16,256]{2,1,0:T(8,128)S(1)} all-to-all(f32[8,16,256]{2,1,0:T(8,128)S(1)} %get-tuple-element.31), channel_id=1, replica_groups={{0,16,32,48,64,80,96,112},{8,24,40,56,72,88,104,120},{1,17,33,49,65,81,..., dimensions={0} | all-to-all | bytes 262144 | tf_op jit(solution)/shard_map/all_to_all | solution.py:458
  51.1 3.7 %all-to-all-start.1 = ((bf16[8,32,1024]{2,1,0:T(8,128)(2,1)}), bf16[8,32,1024]{2,1,0:T(8,128)(2,1)S(1)}, u32[]{:S(2)}, u32[]{:S(2)}) async-start(bf16[8,32,1024]{2,1,0:T(8,128)(2,1)} %get-tuple-element.32), calls=%async_computation.1 | async-start | bytes 1048576 | tf_op jit(solution)/shard_map/all_to_all | solution.py:458
  54.8 7.0 %grads21.1 = (bf16[512,256]{1,0:T(8,128)(2,1)}, bf16[512,256]{1,0:T(8,128)(2,1)}) custom-call(s32[12]{0:T(128)S(1)} %concatenate.9.ix, s32[2,8]{1,0:T(2,128)S(1)} %pad_add_fusion.tl, s32[8,8]{1,0:T(8,128)S(1)} %copy-done.10, bf16[256,2048]{1,0:T(8,128)(2,1)S(1)} %copy-done.2, bf16[256,2048]{1,0:T(8,128)(2,1)S(1)} %copy-done.3, ...), custom_call_target="tpu_custom_call" | custom-call | flops 6600000000 | bytes 65536 | tf_op jit(solution)/shard_map/grads21/pallas_call | solution.py:310
  61.8 2.3 %collective-permute-start.12 = (bf16[512,256]{1,0:T(8,128)(2,1)}, bf16[512,256]{1,0:T(8,128)(2,1)}, u32[]{:S(2)}, u32[]{:S(2)}) collective-permute-start(bf16[512,256]{1,0:T(8,128)(2,1)} %get-tuple-element.34), channel_id=1, source_target_pairs={{0,2},{1,3},{2,0},{3,1},{4,6},{5,7},{6,4},{7,5},{8,10},{9,11},{10,... | collective-permute-start | bytes 786440 | tf_op jit(solution)/shard_map/ppermute | solution.py:39
  64.1 0.9 collective-permute-start.13
  65.0 0.0 all-to-all-done.1.refs_4_
  65.0 6.8 %grads30.1 = (bf16[512,256]{1,0:T(8,128)(2,1)}, f32[512,256]{1,0:T(8,128)S(1)}, bf16[8,32,1024]{2,1,0:T(8,128)(2,1)}) custom-call(s32[12]{0:T(128)S(1)} %concatenate.9.ix, s32[2,8]{1,0:T(2,128)S(1)} %pad_add_fusion.tl, s32[8,8]{1,0:T(8,128)S(1)} %copy-done.10, bf16[256,2048]{1,0:T(8,128)(2,1)S(1)} %copy-done.2, bf16[256,2048]{1,0:T(8,128)(2,1)S(1)} %copy-done.3, ...), custom_call_target="tpu_custom_call" | custom-call | flops 6600000000 | bytes 65536 | tf_op jit(solution)/shard_map/grads30/pallas_call | solution.py:310
  71.8 1.8 %collective-permute-start.14 = (bf16[512,256]{1,0:T(8,128)(2,1)}, bf16[512,256]{1,0:T(8,128)(2,1)S(1)}, u32[]{:S(2)}, u32[]{:S(2)}) collective-permute-start(bf16[512,256]{1,0:T(8,128)(2,1)} %get-tuple-element.36), channel_id=1, source_target_pairs={{0,3},{1,2},{2,1},{3,0},{4,7},{5,6},{6,5},{7,4},{8,11},{9,10},{10,... | collective-permute-start | bytes 786440 | tf_op jit(solution)/shard_map/ppermute | solution.py:39
  73.6 3.5 %all-to-all-start.2 = ((bf16[8,32,1024]{2,1,0:T(8,128)(2,1)}), bf16[8,32,1024]{2,1,0:T(8,128)(2,1)S(1)}, u32[]{:S(2)}, u32[]{:S(2)}) async-start(bf16[8,32,1024]{2,1,0:T(8,128)(2,1)} %get-tuple-element.37), calls=%async_computation.2 | async-start | bytes 1048576 | tf_op jit(solution)/shard_map/all_to_all | solution.py:458
  77.1 0.0 collective-permute-done.12
  77.1 0.0 collective-permute-done.13
  77.1 1.3 %collective-permute-done.14 = bf16[512,256]{1,0:T(8,128)(2,1)S(1)} collective-permute-done((bf16[512,256]{1,0:T(8,128)(2,1)}, bf16[512,256]{1,0:T(8,128)(2,1)S(1)}, u32[]{:S(2)}, u32[]{:S(2)}) %collective-permute-start.14) | collective-permute-done | bytes 262176 | tf_op jit(solution)/shard_map/ppermute | solution.py:39
  78.5 1.2 %add_convert_fusion._ = bf16[512,256]{1,0:T(8,128)(2,1)S(1)} fusion(bf16[512,256]{1,0:T(8,128)(2,1)S(1)} %collective-permute-done.14, bf16[512,256]{1,0:T(8,128)(2,1)} %collective-permute-done.13, f32[512,256]{1,0:T(8,128)S(1)} %get-tuple-element.33, bf16[512,256]{1,0:T(8,128)(2,1)} %collective-permute-done.12), kind=kLoop, calls=%fused_computation | loop fusion | flops 917504 | bytes 1572864 | tf_op jit(solution)/shard_map/convert_element_type | solution.py:500
  79.6 3.7 %collective-permute-start.15 = (bf16[256,256]{1,0:T(8,128)(2,1)S(1)}, bf16[256,256]{1,0:T(8,128)(2,1)S(1)}, u32[]{:S(2)}, u32[]{:S(2)}) collective-permute-start(bf16[256,256]{1,0:T(8,128)(2,1)S(1)} %get-tuple-element.44), channel_id=1, source_target_pairs={{0,8},{1,9},{2,10},{3,11},{4,12},{5,13},{6,14},{7,15},{8,0},{9,1},... | collective-permute-start | bytes 393224 | tf_op jit(solution)/shard_map/ppermute | solution.py:39
  83.3 1.6 %collective-permute-start.17 = (bf16[256,256]{1,0:T(8,128)(2,1)S(1)}, bf16[256,256]{1,0:T(8,128)(2,1)S(1)}, u32[]{:S(2)}, u32[]{:S(2)}) collective-permute-start(bf16[256,256]{1,0:T(8,128)(2,1)S(1)} %get-tuple-element.44), channel_id=1, source_target_pairs={{0,12},{1,13},{2,14},{3,15},{4,8},{5,9},{6,10},{7,11},{8,4},{9,5},... | collective-permute-start | bytes 393224 | tf_op jit(solution)/shard_map/ppermute | solution.py:39
  85.0 1.3 %collective-permute-start.16 = (bf16[256,256]{1,0:T(8,128)(2,1)S(1)}, bf16[256,256]{1,0:T(8,128)(2,1)S(1)}, u32[]{:S(2)}, u32[]{:S(2)}) collective-permute-start(bf16[256,256]{1,0:T(8,128)(2,1)S(1)} %get-tuple-element.45.a), channel_id=1, source_target_pairs={{0,4},{1,5},{2,6},{3,7},{4,0},{5,1},{6,2},{7,3},{8,12},{9,13},{10,... | collective-permute-start | bytes 393224 | tf_op jit(solution)/shard_map/ppermute | solution.py:39
  86.3 0.0 collective-permute-done.15.b
  86.3 0.0 all-to-all-done.2
  86.3 2.6 %collective-permute-start.18 = (bf16[256,1024]{1,0:T(8,128)(2,1)S(1)}, bf16[256,1024]{1,0:T(8,128)(2,1)S(1)}, u32[]{:S(2)}, u32[]{:S(2)}) collective-permute-start(bf16[256,1024]{1,0:T(8,128)(2,1)S(1)} %bitcast.6), channel_id=1, source_target_pairs={{0,8},{1,9},{2,10},{3,11},{4,12},{5,13},{6,14},{7,15},{8,0},{9,1},... | collective-permute-start | bytes 1572872 | tf_op jit(solution)/shard_map/ppermute | solution.py:39
  88.9 3.3 %fetch.1 = (bf16[3840,512]{1,0:T(8,128)(2,1)S(1)}, bf16[3840,512]{1,0:T(8,128)(2,1)S(1)}) custom-call(bf16[3840,512]{1,0:T(8,128)(2,1)} %k_hbm.1, bf16[3840,512]{1,0:T(8,128)(2,1)} %v_hbm.1, bf16[512,256]{1,0:T(8,128)(2,1)S(1)} %add_convert_fusion._), custom_call_target="tpu_custom_call" | custom-call | flops 4400000000 | bytes 65536 | tf_op jit(solution)/shard_map/fetch/pallas_call | solution.py:344
  92.3 1.8 %collective-permute-done.16.c_ = bf16[256,256]{1,0:T(8,128)(2,1)S(1)} collective-permute-done((bf16[256,256]{1,0:T(8,128)(2,1)S(1)}, bf16[256,256]{1,0:T(8,128)(2,1)S(1)}, u32[]{:S(2)}, u32[]{:S(2)}) %collective-permute-start.16) | collective-permute-done | bytes 131104 | tf_op jit(solution)/shard_map/ppermute | solution.py:39
  94.0 0.0 collective-permute-done.17.d_
  94.0 3.7 %feats.1 = (bf16[256,3840]{1,0:T(8,128)(2,1)}, bf16[256,2048]{1,0:T(8,128)(2,1)}) custom-call(s32[12]{0:T(128)S(1)} %concatenate.9.ix, bf16[256,256]{1,0:T(8,128)(2,1)S(1)} %get-tuple-element.45.a, bf16[256,256]{1,0:T(8,128)(2,1)S(1)} %collective-permute-done.15.b, bf16[256,256]{1,0:T(8,128)(2,1)S(1)} %collective-permute-done.16.c_, ...), custom_call_target="tpu_custom_call" | custom-call | flops 4400000000 | bytes 65536 | tf_op jit(solution)/shard_map/feats/pallas_call | solution.py:400
  97.7 0.0 collective-permute-done.18.t_ref
  97.7 1.4 %theirs.1 = bf16[256,2048]{1,0:T(8,128)(2,1)} custom-call(s32[12]{0:T(128)S(1)} %concatenate.9.ix, bf16[256,2048]{1,0:T(8,128)(2,1)} %get-tuple-element.42._, bf16[256,1024]{1,0:T(8,128)(2,1)S(1)} %collective-permute-done.18.t_ref), custom_call_target="tpu_custom_call", output_to_operand_aliasing={{}: (1, {})} | custom-call | tf_op jit(solution)/shard_map/theirs/pallas_call | solution.py:433
  (21 shorter events, 0.1 us)
Async XLA Ops:
  1.4 25.4 %copy-start.11 = (s32[8]{0:T(128)S(1)}, s32[8]{0:T(128)}, u32[]{:S(2)}) copy-start(s32[8]{0:T(128)} %param.12) | copy-start | bytes 100
  1.4 32.1 %copy-start.2 = (bf16[256,2048]{1,0:T(8,128)(2,1)S(1)}, bf16[256,2048]{1,0:T(8,128)(2,1)}, u32[]{:S(2)}) copy-start(bf16[256,2048]{1,0:T(8,128)(2,1)} %q.5) | copy-start | bytes 3145732
  1.4 32.1 %copy-start.3 = (bf16[256,2048]{1,0:T(8,128)(2,1)S(1)}, bf16[256,2048]{1,0:T(8,128)(2,1)}, u32[]{:S(2)}) copy-start(bf16[256,2048]{1,0:T(8,128)(2,1)} %g.5) | copy-start | bytes 3145732
  1.4 32.1 %copy-start.10 = (s32[8,8]{1,0:T(8,128)S(1)}, s32[8,8]{1,0:T(8,128)}, u32[]{:S(2)}) copy-start(s32[8,8]{1,0:T(8,128)} %se.5) | copy-start | bytes 772
  6.7 9.1 %collective-permute-start.7 = (bf16[256,128]{1,0:T(8,128)(2,1)S(1)}, bf16[256,128]{1,0:T(8,128)(2,1)S(1)}, u32[]{:S(2)}, u32[]{:S(2)}) collective-permute-start(bf16[256,128]{1,0:T(8,128)(2,1)S(1)} %get-tuple-element.29), channel_id=1, source_target_pairs={{0,4},{1,5},{2,6},{3,7},{4,0},{5,1},{6,2},{7,3},{8,12},{9,13},{10,... | collective-permute-start | bytes 196616 | tf_op jit(solution)/shard_map/ppermute | solution.py:39
  11.2 6.9 %collective-permute-start = (bf16[272,128]{1,0:T(8,128)(2,1)S(1)}, bf16[272,128]{1,0:T(8,128)(2,1)S(1)}, u32[]{:S(2)}, u32[]{:S(2)}) collective-permute-start(bf16[272,128]{1,0:T(8,128)(2,1)S(1)} %get-tuple-element.23), channel_id=1, source_target_pairs={{0,8},{1,9},{2,10},{3,11},{4,12},{5,13},{6,14},{7,15},{8,0},{9,1},... | collective-permute-start | bytes 208904 | tf_op jit(solution)/shard_map/ppermute | solution.py:39
  12.2 5.9 %collective-permute-start.8 = (bf16[256,128]{1,0:T(8,128)(2,1)S(1)}, bf16[256,128]{1,0:T(8,128)(2,1)S(1)}, u32[]{:S(2)}, u32[]{:S(2)}) collective-permute-start(bf16[256,128]{1,0:T(8,128)(2,1)S(1)} %get-tuple-element.30), channel_id=1, source_target_pairs={{0,12},{1,13},{2,14},{3,15},{4,8},{5,9},{6,10},{7,11},{8,4},{9,5},... | collective-permute-start | bytes 196616 | tf_op jit(solution)/shard_map/ppermute | solution.py:39
  12.2 9.8 %collective-permute-start.1 = (f32[256,128]{1,0:T(8,128)S(1)}, f32[256,128]{1,0:T(8,128)S(1)}, u32[]{:S(2)}, u32[]{:S(2)}) collective-permute-start(f32[256,128]{1,0:T(8,128)S(1)} %get-tuple-element.25), channel_id=1, source_target_pairs={{0,4},{1,5},{2,6},{3,7},{4,0},{5,1},{6,2},{7,3},{8,12},{9,13},{10,... | collective-permute-start | bytes 393224 | tf_op jit(solution)/shard_map/ppermute | solution.py:39
  15.0 6.9 %collective-permute-start.2 = (f32[256,128]{1,0:T(8,128)S(1)}, f32[256,128]{1,0:T(8,128)S(1)}, u32[]{:S(2)}, u32[]{:S(2)}) collective-permute-start(f32[256,128]{1,0:T(8,128)S(1)} %get-tuple-element.26), channel_id=1, source_target_pairs={{0,8},{1,9},{2,10},{3,11},{4,12},{5,13},{6,14},{7,15},{8,0},{9,1},... | collective-permute-start | bytes 393224 | tf_op jit(solution)/shard_map/ppermute | solution.py:39
  15.8 7.5 %collective-permute-start.3 = (f32[256,128]{1,0:T(8,128)S(1)}, f32[256,128]{1,0:T(8,128)S(1)}, u32[]{:S(2)}, u32[]{:S(2)}) collective-permute-start(f32[256,128]{1,0:T(8,128)S(1)} %get-tuple-element.27), channel_id=1, source_target_pairs={{0,12},{1,13},{2,14},{3,15},{4,8},{5,9},{6,10},{7,11},{8,4},{9,5},... | collective-permute-start | bytes 393224 | tf_op jit(solution)/shard_map/ppermute | solution.py:39
  18.2 23.0 %copy-start = (bf16[512,128]{1,0:T(8,128)(2,1)}, bf16[512,128]{1,0:T(8,128)(2,1)S(1)}, u32[]{:S(2)}) copy-start(bf16[512,128]{1,0:T(8,128)(2,1)S(1)} %pad_maximum_fusion.1.v0.refs_3_) | copy-start | bytes 393220
  18.2 8.0 %collective-permute-start.10 = (bf16[512,128]{1,0:T(8,128)(2,1)S(1)}, bf16[512,128]{1,0:T(8,128)(2,1)S(1)}, u32[]{:S(2)}, u32[]{:S(2)}) collective-permute-start(bf16[512,128]{1,0:T(8,128)(2,1)S(1)} %pad_maximum_fusion.1.v0.refs_3_), channel_id=1, source_target_pairs={{0,2},{1,3},{2,0},{3,1},{4,6},{5,7},{6,4},{7,5},{8,10},{9,11},{10,... | collective-permute-start | bytes 393224 | tf_op jit(solution)/shard_map/ppermute | solution.py:39
  21.2 6.7 %collective-permute-start.11 = (bf16[512,128]{1,0:T(8,128)(2,1)S(1)}, bf16[512,128]{1,0:T(8,128)(2,1)S(1)}, u32[]{:S(2)}, u32[]{:S(2)}) collective-permute-start(bf16[512,128]{1,0:T(8,128)(2,1)S(1)} %pad_maximum_fusion.1.v0.refs_3_), channel_id=1, source_target_pairs={{0,3},{1,2},{2,1},{3,0},{4,7},{5,6},{6,5},{7,4},{8,11},{9,10},{10,... | collective-permute-start | bytes 393224 | tf_op jit(solution)/shard_map/ppermute | solution.py:39
  21.9 6.3 %collective-permute-start.9 = (bf16[512,128]{1,0:T(8,128)(2,1)S(1)}, bf16[512,128]{1,0:T(8,128)(2,1)S(1)}, u32[]{:S(2)}, u32[]{:S(2)}) collective-permute-start(bf16[512,128]{1,0:T(8,128)(2,1)S(1)} %pad_maximum_fusion.1.v0.refs_3_), channel_id=1, source_target_pairs={{0,1},{1,0},{2,3},{3,2},{4,5},{5,4},{6,7},{7,6},{8,9},{9,8},{10,11... | collective-permute-start | bytes 393224 | tf_op jit(solution)/shard_map/ppermute | solution.py:39
  23.3 17.9 %copy-start.1 = (bf16[512,128]{1,0:T(8,128)(2,1)}, bf16[512,128]{1,0:T(8,128)(2,1)S(1)}, u32[]{:S(2)}) copy-start(bf16[512,128]{1,0:T(8,128)(2,1)S(1)} %pad_maximum_fusion.k0.refs_1_) | copy-start | bytes 393220
  23.3 9.8 %collective-permute-start.4 = (bf16[512,128]{1,0:T(8,128)(2,1)S(1)}, bf16[512,128]{1,0:T(8,128)(2,1)S(1)}, u32[]{:S(2)}, u32[]{:S(2)}) collective-permute-start(bf16[512,128]{1,0:T(8,128)(2,1)S(1)} %pad_maximum_fusion.k0.refs_1_), channel_id=1, source_target_pairs={{0,3},{1,2},{2,1},{3,0},{4,7},{5,6},{6,5},{7,4},{8,11},{9,10},{10,... | collective-permute-start | bytes 393224 | tf_op jit(solution)/shard_map/ppermute | solution.py:39
  26.1 7.0 %collective-permute-start.5 = (bf16[512,128]{1,0:T(8,128)(2,1)S(1)}, bf16[512,128]{1,0:T(8,128)(2,1)S(1)}, u32[]{:S(2)}, u32[]{:S(2)}) collective-permute-start(bf16[512,128]{1,0:T(8,128)(2,1)S(1)} %pad_maximum_fusion.k0.refs_1_), channel_id=1, source_target_pairs={{0,2},{1,3},{2,0},{3,1},{4,6},{5,7},{6,4},{7,5},{8,10},{9,11},{10,... | collective-permute-start | bytes 393224 | tf_op jit(solution)/shard_map/ppermute | solution.py:39
  26.2 15.0 %copy-start.5 = (bf16[512,128]{1,0:T(8,128)(2,1)}, bf16[512,128]{1,0:T(8,128)(2,1)S(1)}, u32[]{:S(2)}) copy-start(bf16[512,128]{1,0:T(8,128)(2,1)S(1)} %collective-permute-done.10.v2.refs_2_) | copy-start | bytes 393220
  26.2 7.2 %collective-permute-start.6 = (bf16[512,128]{1,0:T(8,128)(2,1)S(1)}, bf16[512,128]{1,0:T(8,128)(2,1)S(1)}, u32[]{:S(2)}, u32[]{:S(2)}) collective-permute-start(bf16[512,128]{1,0:T(8,128)(2,1)S(1)} %pad_maximum_fusion.k0.refs_1_), channel_id=1, source_target_pairs={{0,1},{1,0},{2,3},{3,2},{4,5},{5,4},{6,7},{7,6},{8,9},{9,8},{10,11... | collective-permute-start | bytes 393224 | tf_op jit(solution)/shard_map/ppermute | solution.py:39
  27.8 13.4 %copy-start.4 = (bf16[512,128]{1,0:T(8,128)(2,1)}, bf16[512,128]{1,0:T(8,128)(2,1)S(1)}, u32[]{:S(2)}) copy-start(bf16[512,128]{1,0:T(8,128)(2,1)S(1)} %collective-permute-done.11.v3.refs_2_) | copy-start | bytes 393220
  28.2 13.0 %copy-start.7 = (bf16[512,128]{1,0:T(8,128)(2,1)}, bf16[512,128]{1,0:T(8,128)(2,1)S(1)}, u32[]{:S(2)}) copy-start(bf16[512,128]{1,0:T(8,128)(2,1)S(1)} %collective-permute-done.9.v1.refs_3_) | copy-start | bytes 393220
  33.1 8.1 %copy-start.6 = (bf16[512,128]{1,0:T(8,128)(2,1)}, bf16[512,128]{1,0:T(8,128)(2,1)S(1)}, u32[]{:S(2)}) copy-start(bf16[512,128]{1,0:T(8,128)(2,1)S(1)} %collective-permute-done.4.k3.refs_0_) | copy-start | bytes 393220
  33.1 8.1 %copy-start.8 = (bf16[512,128]{1,0:T(8,128)(2,1)}, bf16[512,128]{1,0:T(8,128)(2,1)S(1)}, u32[]{:S(2)}) copy-start(bf16[512,128]{1,0:T(8,128)(2,1)S(1)} %collective-permute-done.5.k2.refs_0_) | copy-start | bytes 393220
  33.5 7.8 %copy-start.9 = (bf16[512,128]{1,0:T(8,128)(2,1)}, bf16[512,128]{1,0:T(8,128)(2,1)S(1)}, u32[]{:S(2)}) copy-start(bf16[512,128]{1,0:T(8,128)(2,1)S(1)} %collective-permute-done.6.k1.refs_1_) | copy-start | bytes 393220
  51.1 13.9 %all-to-all-start.1 = ((bf16[8,32,1024]{2,1,0:T(8,128)(2,1)}), bf16[8,32,1024]{2,1,0:T(8,128)(2,1)S(1)}, u32[]{:S(2)}, u32[]{:S(2)}) async-start(bf16[8,32,1024]{2,1,0:T(8,128)(2,1)} %get-tuple-element.32), calls=%async_computation.1 | async-start | bytes 1048576 | tf_op jit(solution)/shard_map/all_to_all | solution.py:458
  61.8 15.3 %collective-permute-start.12 = (bf16[512,256]{1,0:T(8,128)(2,1)}, bf16[512,256]{1,0:T(8,128)(2,1)}, u32[]{:S(2)}, u32[]{:S(2)}) collective-permute-start(bf16[512,256]{1,0:T(8,128)(2,1)} %get-tuple-element.34), channel_id=1, source_target_pairs={{0,2},{1,3},{2,0},{3,1},{4,6},{5,7},{6,4},{7,5},{8,10},{9,11},{10,... | collective-permute-start | bytes 786440 | tf_op jit(solution)/shard_map/ppermute | solution.py:39
  64.1 13.0 %collective-permute-start.13 = (bf16[512,256]{1,0:T(8,128)(2,1)}, bf16[512,256]{1,0:T(8,128)(2,1)}, u32[]{:S(2)}, u32[]{:S(2)}) collective-permute-start(bf16[512,256]{1,0:T(8,128)(2,1)} %get-tuple-element.35), channel_id=1, source_target_pairs={{0,1},{1,0},{2,3},{3,2},{4,5},{5,4},{6,7},{7,6},{8,9},{9,8},{10,11... | collective-permute-start | bytes 786440 | tf_op jit(solution)/shard_map/ppermute | solution.py:39
  71.8 6.6 %collective-permute-start.14 = (bf16[512,256]{1,0:T(8,128)(2,1)}, bf16[512,256]{1,0:T(8,128)(2,1)S(1)}, u32[]{:S(2)}, u32[]{:S(2)}) collective-permute-start(bf16[512,256]{1,0:T(8,128)(2,1)} %get-tuple-element.36), channel_id=1, source_target_pairs={{0,3},{1,2},{2,1},{3,0},{4,7},{5,6},{6,5},{7,4},{8,11},{9,10},{10,... | collective-permute-start | bytes 786440 | tf_op jit(solution)/shard_map/ppermute | solution.py:39
  73.6 12.7 %all-to-all-start.2 = ((bf16[8,32,1024]{2,1,0:T(8,128)(2,1)}), bf16[8,32,1024]{2,1,0:T(8,128)(2,1)S(1)}, u32[]{:S(2)}, u32[]{:S(2)}) async-start(bf16[8,32,1024]{2,1,0:T(8,128)(2,1)} %get-tuple-element.37), calls=%async_computation.2 | async-start | bytes 1048576 | tf_op jit(solution)/shard_map/all_to_all | solution.py:458
  79.6 6.7 %collective-permute-start.15 = (bf16[256,256]{1,0:T(8,128)(2,1)S(1)}, bf16[256,256]{1,0:T(8,128)(2,1)S(1)}, u32[]{:S(2)}, u32[]{:S(2)}) collective-permute-start(bf16[256,256]{1,0:T(8,128)(2,1)S(1)} %get-tuple-element.44), channel_id=1, source_target_pairs={{0,8},{1,9},{2,10},{3,11},{4,12},{5,13},{6,14},{7,15},{8,0},{9,1},... | collective-permute-start | bytes 393224 | tf_op jit(solution)/shard_map/ppermute | solution.py:39
  83.3 10.7 %collective-permute-start.17 = (bf16[256,256]{1,0:T(8,128)(2,1)S(1)}, bf16[256,256]{1,0:T(8,128)(2,1)S(1)}, u32[]{:S(2)}, u32[]{:S(2)}) collective-permute-start(bf16[256,256]{1,0:T(8,128)(2,1)S(1)} %get-tuple-element.44), channel_id=1, source_target_pairs={{0,12},{1,13},{2,14},{3,15},{4,8},{5,9},{6,10},{7,11},{8,4},{9,5},... | collective-permute-start | bytes 393224 | tf_op jit(solution)/shard_map/ppermute | solution.py:39
  85.0 9.0 %collective-permute-start.16 = (bf16[256,256]{1,0:T(8,128)(2,1)S(1)}, bf16[256,256]{1,0:T(8,128)(2,1)S(1)}, u32[]{:S(2)}, u32[]{:S(2)}) collective-permute-start(bf16[256,256]{1,0:T(8,128)(2,1)S(1)} %get-tuple-element.45.a), channel_id=1, source_target_pairs={{0,4},{1,5},{2,6},{3,7},{4,0},{5,1},{6,2},{7,3},{8,12},{9,13},{10,... | collective-permute-start | bytes 393224 | tf_op jit(solution)/shard_map/ppermute | solution.py:39
  86.3 11.4 %collective-permute-start.18 = (bf16[256,1024]{1,0:T(8,128)(2,1)S(1)}, bf16[256,1024]{1,0:T(8,128)(2,1)S(1)}, u32[]{:S(2)}, u32[]{:S(2)}) collective-permute-start(bf16[256,1024]{1,0:T(8,128)(2,1)S(1)} %bitcast.6), channel_id=1, source_target_pairs={{0,8},{1,9},{2,10},{3,11},{4,12},{5,13},{6,14},{7,15},{8,0},{9,1},... | collective-permute-start | bytes 1572872 | tf_op jit(solution)/shard_map/ppermute | solution.py:39
